TPU v7x, 32 devices: a whole 2x2x4 slice. The times are simulated.
32 devices in a mesh: row: 4 (over y, x), col: 8 (over z, core).
Axes of the slice: x: 2, y: 2, z: 4, core: 2. Of those that a mesh axis runs over, the one named last changes fastest.
Arguments:
- rhs: float32 [4, 8, 4608], P('row', 'col'), may hold values from -14 to 14
- friction: float32 [4, 8, 4608], P('row', 'col'), may hold values from 1 to 4
- kernel_tiles: bfloat16 [4, 8, 256, 128, 128], P('row', 'col'), may hold values from -0.1875 to 0.1875
- tile_scale: float32 [4, 8, 256], P('row', 'col'), may hold values from 0.5 to 2
- tile_row: int32 [4, 8, 256], P('row', 'col'), may hold values from 0 to 287, as said below
- tile_col: int32 [4, 8, 256], P('row', 'col'), may hold values from 0 to 143
- tile_counts: int32 [4, 8], P('row', 'col'), may hold values from 64 to 256, as said below
- precond_blocks: bfloat16 [4, 8, 24, 512, 512], P('row', 'col'), may hold values from -3 to 3, as said below
- fault_sizes: int32 [4, 8, 24], P('row', 'col'), may hold values from 1 to 512, 4608 in all within a row
Outputs:
- update: float32 [4, 8, 4608], P('row', 'col')
- residual: float32 [4, 8, 4608], P('row', 'col')
Inputs may be any that keep to these rules, and one draw needn't show every extreme that they name: Row tile within the row group; in every block (r, c), over all 256 slots, at most 64 slots have the same tile_row // 36, and some value of it has exactly 64. `tile_counts`: slots at or beyond the count hold no kernel tile and are ignored; some block has 256 live slots and some 256 // 4. `fault_sizes`: the faults of each (r, c) cover its 4608 elements in order; each (r, c) has a fault of exactly 512 elements. `precond_blocks`: entries of a block outside its fault's size are ignored.
All inputs are finite; a program needn't handle non-finite values.
Results may differ from a plain program's by a relative error of at most 0.012.
Values may be sent and summed in bfloat16 or wider, within the bound.
No kernel may reach another device: no remote copies, remote signals or barrier semaphores. Data moves between devices by JAX's collectives and lax.ppermute only.
A program may use at most 64 MiB of HBM per device.

v0:
```python
import jax
import jax.numpy as jnp
from jax import lax
from jax.sharding import PartitionSpec as P

ITERS = 3


exact_mode = lax.Precision.HIGHEST


def local(
    rhs,
    friction,
    kernel_tiles,
    tile_scale,
    tile_row,
    tile_col,
    tile_counts,
    precond_blocks,
    fault_sizes,
):
    vector_len = rhs.shape[2]
    tile_width = kernel_tiles.shape[3]
    slot_count = kernel_tiles.shape[2]
    fault_width = precond_blocks.shape[3]
    col_devices = lax.axis_size("col")
    row_tiles = col_devices * vector_len // tile_width
    local_tiles = kernel_tiles[0, 0]
    tile_rows = tile_row[0, 0]
    tile_cols = tile_col[0, 0]
    tile_weight = jnp.where(
        jnp.arange(slot_count, dtype=jnp.int32) < tile_counts[0, 0], tile_scale[0, 0], 0.0
    )
    fault_blocks = precond_blocks[0, 0]
    fault_len = fault_sizes[0, 0]
    fault_starts = jnp.cumsum(fault_len) - fault_len
    slot_place = jnp.arange(fault_width, dtype=jnp.int32)
    gather_spot = jnp.clip(fault_starts[:, None] + slot_place[None, :], 0, vector_len - 1)
    slot_live = slot_place[None, :] < fault_len[:, None]
    element_ids = jnp.arange(vector_len, dtype=jnp.int32)
    owner_fault = (
        jnp.sum((fault_starts[None, :] <= element_ids[:, None]).astype(jnp.int32), axis=1) - 1
    )
    flat_spot = owner_fault * fault_width + element_ids - fault_starts[owner_fault]

    def kernel_apply(field):
        low_field = field.astype(jnp.bfloat16).reshape(1, 1, vector_len)
        column = lax.all_gather(low_field, "row", axis=0, tiled=True)
        column_pieces = column.reshape(-1, tile_width)[tile_cols]
        products = (
            jnp.einsum("tij,tj->ti", local_tiles, column_pieces, preferred_element_type=jnp.float32)
            * tile_weight[:, None]
        )
        partial_value = jax.ops.segment_sum(products, tile_rows, num_segments=row_tiles).reshape(-1)
        row_total = lax.psum(partial_value, "col")
        return lax.dynamic_slice_in_dim(row_total, lax.axis_index("col") * vector_len, vector_len)

    rhs_flat = rhs.reshape(-1)
    friction_flat = friction.reshape(-1)

    def operator(field):
        return friction_flat * field + kernel_apply(field)

    def global_norm(field):
        return jnp.sqrt(lax.psum(jnp.sum(field * field), ("row", "col")))

    rhs_norm = global_norm(rhs_flat)
    krylov = [rhs_flat / rhs_norm]
    directions = []
    hessenberg = jnp.zeros((ITERS + 1, ITERS), jnp.float32)
    for step in range(ITERS):
        low_vector = krylov[step].astype(jnp.bfloat16)
        padded = jnp.where(slot_live, low_vector[gather_spot], jnp.zeros((), jnp.bfloat16))
        result = jnp.einsum("fij,fj->fi", fault_blocks, padded, preferred_element_type=jnp.float32)
        direction = result.reshape(-1)[flat_spot]
        directions.append(direction)
        image = operator(direction)
        height_list = []
        for earlier in krylov:
            height = lax.psum(jnp.sum(earlier * image), ("row", "col"))
            image = image - height * earlier
            height_list.append(height)
        heights = jnp.stack(height_list)
        new_norm = global_norm(image)
        hessenberg = hessenberg.at[: step + 1, step].set(heights).at[step + 1, step].set(new_norm)
        krylov.append(image / new_norm)
    gram_matrix = jnp.dot(hessenberg.T, hessenberg, precision=exact_mode)
    target = rhs_norm * hessenberg[0, :]
    lower_factor = jnp.linalg.cholesky(gram_matrix)
    weights_y = jax.scipy.linalg.cho_solve((lower_factor, True), target)
    update = jnp.dot(weights_y, jnp.stack(directions), precision=exact_mode)
    residual = rhs_flat - operator(update)
    return (update.reshape(1, 1, vector_len), residual.reshape(1, 1, vector_len))


def solution(mesh):
    return jax.shard_map(
        local,
        mesh=mesh,
        in_specs=(
            P("row", "col", None),
            P("row", "col", None),
            P("row", "col", None, None, None),
            P("row", "col", None),
            P("row", "col", None),
            P("row", "col", None),
            P("row", "col"),
            P("row", "col", None, None, None),
            P("row", "col", None),
        ),
        out_specs=(P("row", "col", None), P("row", "col", None)),
        check_vma=False,
    )
```

profile of v0, /device:TPU:0, one launch (start us, length us, event | category | flops | bytes accessed | tf_op | source)
XLA Modules:
  0.0 1087.3 jit_solution(13645294912561519744)
XLA Ops:
  7.2 0.7 copy.23
  8.1 0.7 bitcast_subtract_fusion
  8.8 0.7 fusion.63
  9.5 0.7 fusion.64
  10.4 4.5 fusion.50
  14.9 0.9 compare_reduce_fusion.16
  15.8 10.6 select_select_fusion
  26.5 0.8 reduce.28
  27.9 42.2 %psum.98 = f32[]{:T(128)} all-reduce(f32[]{:T(128)} %multiply_reduce_fusion.9), channel_id=1, replica_groups=mesh['row'=4,'col'=8] {'row','col'}, use_global_device_ids=true, to_apply=%region_1.2 | all-reduce | flops 1 | bytes 8 | tf_op jit(solution)/shard_map/psum | solution.py:66
  70.9 75.8 %gather_fusion = bf16[12288]{0:T(1024)(128)(2,1)S(1)} fusion(bf16[4608]{0:T(1024)(128)(2,1)S(1)} %fusion.59, s32[12288]{0:T(1024)S(1)} %broadcast_clamp_fusion), kind=kCustom, calls=%fused_computation | custom fusion | bytes 98304 | tf_op jit(solution)/shard_map/gather | solution.py:74
  146.8 7.9 fusion.4
  154.8 24.1 %gather_fusion.1 = f32[4608]{0:T(1024)S(1)} fusion(f32[12288]{0:T(1024)S(1)} %bitcast.140, s32[5120]{0:T(1024)S(1)} %pad_clamp_fusion), kind=kCustom, calls=%fused_computation.1 | custom fusion | bytes 55296 | tf_op jit(solution)/shard_map/gather | solution.py:76
  179.0 9.3 all-gather.4
  189.1 0.9 gather_fusion.2
  190.0 7.8 fusion.12
  197.8 2.3 scatter_custom_fusion
  200.2 0.7 compare_reduce_fusion.18
  202.1 49.2 %all-reduce.6.cloned.1.call-done = f32[36864]{0:T(1024)} async-done(((f32[36864]{0:T(1024)}), f32[36864]{0:T(1024)}) %all-reduce.6.cloned.1.call-update) | async-done | bytes 147472 | tf_op jit(solution)/shard_map/psum | solution.py:56
  251.3 1.4 multiply_reduce_fusion.8
  252.7 42.0 %psum.100 = f32[]{:T(128)} all-reduce(f32[]{:T(128)} %get-tuple-element.99), channel_id=1, replica_groups=mesh['row'=4,'col'=8] {'row','col'}, use_global_device_ids=true, to_apply=%region_7.8 | all-reduce | flops 1 | bytes 8 | tf_op jit(solution)/shard_map/psum | solution.py:81
  294.7 1.3 multiply_reduce_fusion.7
  296.0 39.7 %psum.101 = f32[]{:T(128)} all-reduce(f32[]{:T(128)} %multiply_reduce_fusion.7), channel_id=1, replica_groups=mesh['row'=4,'col'=8] {'row','col'}, use_global_device_ids=true, to_apply=%region_9.10 | all-reduce | flops 1 | bytes 8 | tf_op jit(solution)/shard_map/psum | solution.py:66
  337.1 75.8 %gather_fusion.3 = bf16[12288]{0:T(1024)(128)(2,1)S(1)} fusion(bf16[4608]{0:T(1024)(128)(2,1)S(1)} %fusion.60, s32[12288]{0:T(1024)S(1)} %broadcast_clamp_fusion), kind=kCustom, calls=%fused_computation.3 | custom fusion | bytes 98304 | tf_op jit(solution)/shard_map/gather | solution.py:74
  413.0 7.9 fusion.2
  421.0 24.1 %gather_fusion.4 = f32[4608]{0:T(1024)S(1)} fusion(f32[12288]{0:T(1024)S(1)} %bitcast.141, s32[5120]{0:T(1024)S(1)} %pad_clamp_fusion), kind=kCustom, calls=%fused_computation.4 | custom fusion | bytes 55296 | tf_op jit(solution)/shard_map/gather | solution.py:76
  445.1 9.3 all-gather.5
  454.6 0.9 gather_fusion.5
  455.4 7.8 fusion.10
  463.2 2.3 scatter_custom_fusion.1
  465.6 0.7 fusion.61
  466.9 49.9 %all-reduce.8.cloned.1.call-done = f32[36864]{0:T(1024)} async-done(((f32[36864]{0:T(1024)}), f32[36864]{0:T(1024)}) %all-reduce.8.cloned.1.call-update) | async-done | bytes 147472 | tf_op jit(solution)/shard_map/psum | solution.py:56
  516.8 1.5 multiply_reduce_fusion.6
  518.3 42.0 %psum.103 = f32[]{:T(128)} all-reduce(f32[]{:T(128)} %get-tuple-element.97), channel_id=1, replica_groups=mesh['row'=4,'col'=8] {'row','col'}, use_global_device_ids=true, to_apply=%region_14.15 | all-reduce | flops 1 | bytes 8 | tf_op jit(solution)/shard_map/psum | solution.py:81
  560.3 2.0 multiply_reduce_fusion.5
  562.4 39.6 %psum.104 = f32[]{:T(128)} all-reduce(f32[]{:T(128)} %multiply_reduce_fusion.5), channel_id=1, replica_groups=mesh['row'=4,'col'=8] {'row','col'}, use_global_device_ids=true, to_apply=%region_16.17 | all-reduce | flops 1 | bytes 8 | tf_op jit(solution)/shard_map/psum | solution.py:81
  602.0 2.6 multiply_reduce_fusion.4
  604.7 41.5 %psum.105 = f32[]{:T(128)} all-reduce(f32[]{:T(128)} %get-tuple-element.95), channel_id=1, replica_groups=mesh['row'=4,'col'=8] {'row','col'}, use_global_device_ids=true, to_apply=%region_18.19 | all-reduce | flops 1 | bytes 8 | tf_op jit(solution)/shard_map/psum | solution.py:66
  646.9 75.8 %gather_fusion.6 = bf16[12288]{0:T(1024)(128)(2,1)S(1)} fusion(bf16[4608]{0:T(1024)(128)(2,1)S(1)} %fusion.58, s32[12288]{0:T(1024)S(1)} %broadcast_clamp_fusion), kind=kCustom, calls=%fused_computation.6 | custom fusion | bytes 98304 | tf_op jit(solution)/shard_map/gather | solution.py:74
  722.8 7.9 fusion
  730.7 24.1 %gather_fusion.7 = f32[4608]{0:T(1024)S(1)} fusion(f32[12288]{0:T(1024)S(1)} %bitcast.139, s32[5120]{0:T(1024)S(1)} %pad_clamp_fusion), kind=kCustom, calls=%fused_computation.7 | custom fusion | bytes 55296 | tf_op jit(solution)/shard_map/gather | solution.py:76
  754.9 9.5 all-gather.6
  764.6 0.9 gather_fusion.8
  765.5 7.8 fusion.8
  773.2 2.3 scatter_custom_fusion.2
  775.6 3.2 broadcast_select_fusion.1
  778.8 48.0 %all-reduce.10.cloned.1.call-done = f32[36864]{0:T(1024)} async-done(((f32[36864]{0:T(1024)}), f32[36864]{0:T(1024)}) %all-reduce.10.cloned.1.call-update) | async-done | bytes 147472 | tf_op jit(solution)/shard_map/psum | solution.py:56
  826.8 1.5 multiply_reduce_fusion.3
  828.3 42.0 %psum.107 = f32[]{:T(128)} all-reduce(f32[]{:T(128)} %get-tuple-element.93), channel_id=1, replica_groups=mesh['row'=4,'col'=8] {'row','col'}, use_global_device_ids=true, to_apply=%region_23.24 | all-reduce | flops 1 | bytes 8 | tf_op jit(solution)/shard_map/psum | solution.py:81
  870.3 1.9 multiply_reduce_fusion.2
  872.2 1.3 scatter.24
  873.6 39.6 %psum.108 = f32[]{:T(128)} all-reduce(f32[]{:T(128)} %multiply_reduce_fusion.2), channel_id=1, replica_groups=mesh['row'=4,'col'=8] {'row','col'}, use_global_device_ids=true, to_apply=%region_25.26 | all-reduce | flops 1 | bytes 8 | tf_op jit(solution)/shard_map/psum | solution.py:81
  913.1 2.5 multiply_reduce_fusion.1
  915.7 41.3 %psum.109 = f32[]{:T(128)} all-reduce(f32[]{:T(128)} %get-tuple-element.91), channel_id=1, replica_groups=mesh['row'=4,'col'=8] {'row','col'}, use_global_device_ids=true, to_apply=%region_27.28 | all-reduce | flops 1 | bytes 8 | tf_op jit(solution)/shard_map/psum | solution.py:81
  957.0 1.3 multiply_reduce_fusion
  958.4 39.6 %psum.110 = f32[]{:T(128)} all-reduce(f32[]{:T(128)} %multiply_reduce_fusion), channel_id=1, replica_groups=mesh['row'=4,'col'=8] {'row','col'}, use_global_device_ids=true, to_apply=%region_29.30 | all-reduce | flops 1 | bytes 8 | tf_op jit(solution)/shard_map/psum | solution.py:66
  998.6 3.9 broadcast_select_fusion
  1002.5 1.5 scatter.26
  1006.7 0.9 fusion.65
  1007.6 9.3 all-gather.7
  1017.1 0.9 gather_fusion.9
  1018.0 7.8 fusion.6
  1025.7 2.3 scatter_custom_fusion.3
  1028.1 51.2 %all-reduce.12.cloned.1.call-done = f32[36864]{0:T(1024)} async-done(((f32[36864]{0:T(1024)}), f32[36864]{0:T(1024)}) %all-reduce.12.cloned.1.call-update) | async-done | bytes 147472 | tf_op jit(solution)/shard_map/psum | solution.py:56
  1079.3 0.8 add_subtract_fusion
  (86 shorter events, 8.8 us)
Async XLA Ops:
  7.2 244.2 %all-reduce.6.cloned.1.call-start = ((), (), s32[]{:S(2)}) async-start(), calls=%async_computation | async-start | bytes 294912 | tf_op jit(solution)/shard_map/psum | solution.py:56
  70.9 75.9 %copy-start.1 = (s32[1,1,24]{2,1,0:T(1,128)S(1)}, s32[1,1,24]{2,1,0:T(1,128)}, u32[]{:S(2)}) copy-start(s32[1,1,24]{2,1,0:T(1,128)} %param.29) | copy-start | bytes 292
  154.8 33.7 %copy-start.2 = (s32[1,1,256]{2,1,0:T(1,128)S(1)}, s32[1,1,256]{2,1,0:T(1,128)}, u32[]{:S(2)}) copy-start(s32[1,1,256]{2,1,0:T(1,128)} %param.26) | copy-start | bytes 3076
  178.9 18.9 %copy-start.3 = (f32[1,1,256]{2,1,0:T(1,128)S(1)}, f32[1,1,256]{2,1,0:T(1,128)}, u32[]{:S(2)}) copy-start(f32[1,1,256]{2,1,0:T(1,128)} %param.24) | copy-start | bytes 3076
  178.9 21.9 %copy-start = (f32[1,1,4608]{2,1,0:T(1,128)S(1)}, f32[1,1,4608]{2,1,0:T(1,128)}, u32[]{:S(2)}) copy-start(f32[1,1,4608]{2,1,0:T(1,128)} %param.22) | copy-start | bytes 55300
  178.9 22.6 %copy-start.4 = (s32[2]{0:T(128)S(1)}, s32[2]{0:T(128)}, u32[]{:S(2)}) copy-start(s32[2]{0:T(128)} %constant.236.clone.1) | copy-start | bytes 28
  200.1 316.7 %all-reduce.8.cloned.1.call-start = ((), (), s32[]{:S(2)}) async-start(), calls=%async_computation.1 | async-start | bytes 294912 | tf_op jit(solution)/shard_map/psum | solution.py:56
  465.5 361.3 %all-reduce.10.cloned.1.call-start = ((), (), s32[]{:S(2)}) async-start(), calls=%async_computation.2 | async-start | bytes 294912 | tf_op jit(solution)/shard_map/psum | solution.py:56
  775.6 303.7 %all-reduce.12.cloned.1.call-start = ((), (), s32[]{:S(2)}) async-start(), calls=%async_computation.3 | async-start | bytes 294912 | tf_op jit(solution)/shard_map/psum | solution.py:56
Sparse Core Ops, SparseCore 0:
  200.2 51.0 all-reduce.5
  465.7 51.1 all-reduce.7
  775.7 51.0 all-reduce.9
  1028.2 51.0 all-reduce.11
where the time goes:
time: 1090 us
  blocking collectives  447 us (41%)
  local copies, waits for them, and re-layouts  311 us (29%)
  waiting for transfers between devices  198 us (18%)
  other arithmetic  56.7 us (5%)
  matrix products  56.1 us (5%)
  between operations  17.6 us (2%)
    psum x6, blocking collectives, local(): height = lax.psum(jnp.sum(earlier * image), ('row', 'col'))  247 us
    gather x6, local copies, waits for them, and re-layouts, local(): low_vector[gather_spot]  228 us
    psum x4, waiting for transfers between devices, kernel_apply(): row_total = lax.psum(partial_value, 'col')  198 us
    psum x4, blocking collectives, global_norm(): return jnp.sqrt(lax.psum(jnp.sum(field * field), ('row', 'col')))  163 us
    gather x3, local copies, waits for them, and re-layouts, local(): direction = result.reshape(-1)[flat_spot]  72.2 us
    all_gather x4, blocking collectives, kernel_apply(): column = lax.all_gather(low_field, 'row', axis=0, tiled=True)  37.3 us
    dot_general x4, matrix products, kernel_apply(): jnp.einsum('tij,tj->ti', local_tiles, column_pieces, preferred_element_ty...  31.1 us
    dot_general x3, matrix products, local(): jnp.einsum('fij,fj->fi', fault_blocks, padded, preferred_element_type=jnp...  23.7 us
  transfers between devices with their start and end apart: 4, of which 4 were waited for; matrix products, arithmetic and copies ran while one was open for 1% of the time, Pallas kernels for 0%

commit v1 on v0

v1 whole, which is shorter than its diff:
```python
import jax
import jax.numpy as jnp
from jax import lax
from jax.experimental import pallas as pl
from jax.experimental.pallas import tpu as pltpu
from jax.sharding import PartitionSpec as P

LANES = 128
F32 = jnp.float32
BF16 = jnp.bfloat16
VMEM = pl.BlockSpec(memory_space=pltpu.VMEM)
SMEM = pl.BlockSpec(memory_space=pltpu.SMEM)
ANY = pl.BlockSpec(memory_space=pl.ANY)
PARAMS = pltpu.CompilerParams(vmem_limit_bytes=48 << 20)


def dot_nt(left, right):
    return lax.dot_general(left, right, (((1,), (1,)), ((), ())), preferred_element_type=F32)


def split(value):
    high = value.astype(BF16)
    low = (value - high.astype(F32)).astype(BF16)
    return high, low


def total(value):
    return jnp.sum(jnp.sum(value, axis=0, keepdims=True), axis=1, keepdims=True)


def lane_row(values):
    lane = lax.broadcasted_iota(jnp.int32, (1, LANES), 1)
    row = jnp.zeros((1, LANES), F32)
    for place, value in enumerate(values):
        row = jnp.where(lane == place, value, row)
    return row


def pick(row, place):
    lane = lax.broadcasted_iota(jnp.int32, (1, LANES), 1)
    return jnp.sum(jnp.where(lane == place, row, 0.0), axis=1, keepdims=True)


def load_rows(ref, count):
    return jnp.concatenate(
        [ref[0, :, pl.ds(k * LANES, LANES)] for k in range(count)], axis=0
    )


def fault_scalars(sizes, faults):
    start = jnp.int32(0)
    scalars = []
    for f in range(faults):
        scalars.append((start // LANES, start % LANES, sizes[0, 0, f]))
        start = start + sizes[0, 0, f]
    return scalars


def precondition(scalars, blocks, field, windows, shifts, lens, stack, ready):
    faults = len(scalars)
    chunks = blocks.shape[1] // LANES
    rows = field.shape[0]
    lane = lax.broadcasted_iota(jnp.int32, (faults, LANES), 1)
    for f, (tile, shift, size) in enumerate(scalars):
        shifts[f : f + 1, :] = jnp.full((1, LANES), shift, jnp.int32)
        lens[f : f + 1, :] = jnp.full((1, LANES), size, jnp.int32)
        for k in range(chunks + 1):
            windows[k, f : f + 1, :] = field[pl.ds(tile + k, 1), :]
    shift = shifts[...]
    size = lens[...]
    bits = [((shift >> b) & 1) == 1 for b in range(7)]
    live = [lane + k * LANES < size for k in range(chunks)]
    parts = [windows[k] for k in range(chunks + 1)]
    for b in range(7):
        step = 1 << b
        rolled = [pltpu.roll(part, LANES - step, 1) for part in parts]
        moved = [
            jnp.where(lane < LANES - step, rolled[k], rolled[min(k + 1, chunks)])
            for k in range(chunks + 1)
        ]
        parts = [jnp.where(bits[b], new, old) for new, old in zip(moved, parts)]
    parts = [jnp.where(live[k], parts[k], 0.0) for k in range(chunks)]
    sub = lax.broadcasted_iota(jnp.int32, (8, LANES), 0)
    products = [[] for _ in range(chunks)]
    for group in range(faults // 8):
        pieces = []
        for k in range(chunks):
            high, low = split(parts[k][group * 8 : group * 8 + 8])
            pieces.append(jnp.concatenate([high, low], axis=0))
        left = jnp.concatenate(pieces, axis=1)
        found = [jnp.zeros((8, LANES), F32) for _ in range(chunks)]
        for place in range(8):
            f = group * 8 + place
            ready(f)
            result = dot_nt(left, blocks[f])
            result = result[:8] + result[8:]
            for k in range(chunks):
                found[k] = jnp.where(
                    sub == place, result[:, k * LANES : (k + 1) * LANES], found[k]
                )
        for k in range(chunks):
            products[k].append(found[k])
    parts = [
        jnp.where(live[k], jnp.concatenate(products[k], axis=0), 0.0) for k in range(chunks)
    ]
    parts.append(jnp.zeros((faults, LANES), F32))
    for b in range(7):
        step = 1 << b
        rolled = [pltpu.roll(part, step, 1) for part in parts]
        moved = [
            jnp.where(lane >= step, rolled[k], rolled[k - 1] if k else 0.0)
            for k in range(chunks + 1)
        ]
        parts = [jnp.where(bits[b], new, old) for new, old in zip(moved, parts)]
    count = faults * (chunks + 1)
    for k in range(chunks + 1):
        stack[k * faults : (k + 1) * faults, :] = parts[k]
    depth = stack.shape[0]
    if depth > count:
        stack[count:depth, :] = jnp.zeros((depth - count, LANES), F32)
    place = lax.broadcasted_iota(jnp.int32, (1, depth), 1)
    chunk = jnp.zeros((1, depth), jnp.int32)
    for k in range(1, chunks + 1):
        chunk = chunk + (place >= k * faults).astype(jnp.int32)
    local = place - chunk * faults
    target = jnp.full((1, depth), -1, jnp.int32)
    for f, (tile, _, _) in enumerate(scalars):
        target = jnp.where(local == f, tile + chunk, target)
    target = jnp.where(place < count, target, -1)
    chosen = (lax.broadcasted_iota(jnp.int32, (rows, depth), 0) == target).astype(BF16)
    high, low = split(stack[...])
    return jnp.dot(chosen, high, preferred_element_type=F32) + jnp.dot(
        chosen, low, preferred_element_type=F32
    )


def always(f):
    pass


def first_kernel(sizes, rhs, friction, blocks, send, blocks_out, field, windows, shifts, lens, stack, sems):
    faults, width = blocks.shape[2], blocks.shape[3]
    tiles = rhs.shape[2] // LANES
    scalars = fault_scalars(sizes, faults)
    copies = []
    for f, (_, _, size) in enumerate(scalars):
        need = pl.multiple_of((size + 15) // 16 * 16, 16)
        copy = pltpu.make_async_copy(
            blocks.at[0, 0, f, pl.ds(0, need)], blocks_out.at[f, pl.ds(0, need)], sems.at[f]
        )
        copy.start()
        copies.append(copy)
    value = load_rows(rhs, tiles)
    field[0:tiles, :] = value
    field[tiles:, :] = jnp.zeros((field.shape[0] - tiles, LANES), F32)
    out = precondition(
        scalars, blocks_out, field, windows, shifts, lens, stack, lambda f: copies[f].wait()
    )
    direction = out[0:tiles]
    scaled = load_rows(friction, tiles) * direction
    send[...] = jnp.zeros_like(send)
    send[0:tiles, :] = direction
    send[tiles : tiles + 1, :] = lane_row([total(value * value), total(value * scaled)])


def gathered(parts, tiles):
    whole = parts[0]
    for c in range(1, parts.shape[0]):
        whole = whole + parts[c]
    return whole[0:tiles], whole[tiles : tiles + 1]


def second_kernel(sizes, rhs, friction, sent, parts, blocks, send, image_out, basis_out, field, windows, shifts, lens, stack):
    tiles = rhs.shape[2] // LANES
    scalars = fault_scalars(sizes, blocks.shape[0])
    start = load_rows(rhs, tiles)
    diagonal = load_rows(friction, tiles)
    product, sums = gathered(parts, tiles)
    norm2 = pick(sums, 0)
    image = diagonal * sent[0:tiles, :] + product
    scale = lax.rsqrt(norm2)
    value = (image - pick(sums, 1) / norm2 * start) * scale
    image_out[...] = image
    basis_out[0:tiles, :] = value
    basis_out[tiles:, :] = jnp.broadcast_to(norm2, (basis_out.shape[0] - tiles, LANES))
    field[0:tiles, :] = value
    field[tiles:, :] = jnp.zeros((field.shape[0] - tiles, LANES), F32)
    direction = precondition(scalars, blocks, field, windows, shifts, lens, stack, always)[0:tiles]
    scaled = diagonal * direction
    send[...] = jnp.zeros_like(send)
    send[0:tiles, :] = direction
    send[tiles : tiles + 1, :] = lane_row(
        [
            total(value * value),
            total(start * value) * scale,
            total(start * scaled) * scale,
            total(value * scaled),
        ]
    )


def third_kernel(sizes, rhs, friction, sent, parts, basis, blocks, send, image_out, field, windows, shifts, lens, stack):
    tiles = rhs.shape[2] // LANES
    scalars = fault_scalars(sizes, blocks.shape[0])
    start = load_rows(rhs, tiles)
    diagonal = load_rows(friction, tiles)
    product, sums = gathered(parts, tiles)
    image = diagonal * sent[0:tiles, :] + product
    value = basis[0:tiles, :]
    scale = lax.rsqrt(basis[tiles : tiles + 1, 0:1])
    norm2, cross, along_start, along = [pick(sums, k) for k in range(4)]
    left = norm2 - cross * cross
    usable = left > 1e-5 * norm2
    along = jnp.where(usable, (along - cross * along_start) / jnp.where(usable, left, 1.0), 0.0)
    along_start = along_start - cross * along
    value = (image - along * value - (along_start * scale) * start) * lax.rsqrt(
        jnp.maximum(norm2, 1e-30)
    )
    image_out[...] = image
    field[0:tiles, :] = value
    field[tiles:, :] = jnp.zeros((field.shape[0] - tiles, LANES), F32)
    direction = precondition(scalars, blocks, field, windows, shifts, lens, stack, always)[0:tiles]
    send[...] = jnp.zeros_like(send)
    send[0:tiles, :] = direction


def fourth_kernel(rhs, friction, sent, parts, image0, image1, image_out, sums_out):
    tiles = rhs.shape[2] // LANES
    start = load_rows(rhs, tiles)
    product, _ = gathered(parts, tiles)
    image = load_rows(friction, tiles) * sent[0:tiles, :] + product
    image_out[...] = image
    images = [image0[...], image1[...], image]
    values = [total(images[i] * images[j]) for i in range(3) for j in range(i + 1)]
    values += [total(start * one) for one in images]
    sums_out[...] = jnp.broadcast_to(lane_row(values), sums_out.shape)


def last_kernel(sums, rhs, image0, image1, image2, sent0, sent1, sent2, update, residual):
    tiles = rhs.shape[2] // LANES
    row = jnp.sum(sums[...], axis=0, keepdims=True)
    entries = [pick(row, k) for k in range(9)]
    scale = [lax.rsqrt(jnp.maximum(entries[k], 1e-30)) for k in (0, 2, 5)]
    gram = {}
    place = 0
    for i in range(3):
        for j in range(i + 1):
            gram[i, j] = entries[place] * scale[i] * scale[j]
            place += 1
    goal = [entries[6 + i] * scale[i] for i in range(3)]
    low10 = gram[1, 0]
    low20 = gram[2, 0]
    pivot1 = 1.0 - low10 * low10
    keep1 = pivot1 > 1e-6
    inverse1 = jnp.where(keep1, 1.0 / jnp.where(keep1, pivot1, 1.0), 0.0)
    cross = gram[2, 1] - low20 * low10
    low21 = cross * inverse1
    pivot2 = 1.0 - low20 * low20 - cross * low21
    keep2 = pivot2 > 1e-6
    inverse2 = jnp.where(keep2, 1.0 / jnp.where(keep2, pivot2, 1.0), 0.0)
    part1 = goal[1] - low10 * goal[0]
    part2 = goal[2] - low20 * goal[0] - low21 * part1
    weight2 = part2 * inverse2
    weight1 = part1 * inverse1 - low21 * weight2
    weight0 = goal[0] - low10 * weight1 - low20 * weight2
    weights = [weight0 * scale[0], weight1 * scale[1], weight2 * scale[2]]
    start = load_rows(rhs, tiles)
    best = (
        weights[0] * sent0[0:tiles, :]
        + weights[1] * sent1[0:tiles, :]
        + weights[2] * sent2[0:tiles, :]
    )
    rest = start - weights[0] * image0[...] - weights[1] * image1[...] - weights[2] * image2[...]
    for k in range(tiles):
        update[0, :, pl.ds(k * LANES, LANES)] = best[k : k + 1]
        residual[0, :, pl.ds(k * LANES, LANES)] = rest[k : k + 1]


def tiles_kernel(spots, rows, weight, blocks, *refs):
    sent, (out, field, found, products) = refs[:-4], refs[-4:]
    slots = blocks.shape[0]
    count, height = out.shape[0], out.shape[1]
    tiles = height - 8 if height % 8 == 0 else height
    sums = None
    for k, one in enumerate(sent):
        field[k * height : (k + 1) * height, :] = one[...]
    for t in range(slots):
        found[t : t + 1, :] = field[pl.ds(spots[0, t], 1), :]
    sub = lax.broadcasted_iota(jnp.int32, (8, LANES), 0)
    blank = jnp.zeros((8, LANES), F32)
    for group in range(slots // 16):
        base = group * 16
        top = jnp.concatenate([found[base : base + 8, :], blank], axis=1)
        bottom = jnp.concatenate([blank, found[base + 8 : base + 16, :]], axis=1)
        left = jnp.concatenate([top, bottom], axis=0).astype(BF16)
        first, second = blank, blank
        for p in range(4):
            a, b = base + 2 * p, base + 2 * p + 1
            right = jnp.concatenate(
                [
                    jnp.concatenate([blocks[a], blocks[a + 8]], axis=1),
                    jnp.concatenate([blocks[b], blocks[b + 8]], axis=1),
                ],
                axis=0,
            )
            result = dot_nt(left, right)
            for spot, half in ((2 * p, slice(0, LANES)), (2 * p + 1, slice(LANES, 2 * LANES))):
                first = jnp.where(sub == spot, result[:8, half], first)
                second = jnp.where(sub == spot, result[8:, half], second)
        products[base : base + 8, :] = first
        products[base + 8 : base + 16, :] = second
    high, low = split(products[...])
    target = rows[...]
    chosen = jnp.where(
        lax.broadcasted_iota(jnp.int32, (count * height, slots), 0) == target, weight[...], 0.0
    )
    chosen_high, chosen_low = split(chosen)
    value = (
        jnp.dot(chosen_high, high, preferred_element_type=F32)
        + jnp.dot(chosen_low, high, preferred_element_type=F32)
        + jnp.dot(chosen_high, low, preferred_element_type=F32)
    )
    out[...] = value.reshape(count, height, LANES)


def scratch(shape, dtype=F32):
    return pltpu.VMEM(shape, dtype)


def local(
    rhs,
    friction,
    kernel_tiles,
    tile_scale,
    tile_row,
    tile_col,
    tile_counts,
    precond_blocks,
    fault_sizes,
):
    length = rhs.shape[2]
    slots = kernel_tiles.shape[2]
    faults, width = precond_blocks.shape[2], precond_blocks.shape[3]
    tiles = length // LANES
    height = (tiles + 8) // 8 * 8
    chunks = width // LANES
    row_count = lax.axis_size("row")
    col_count = lax.axis_size("col")
    my_row = lax.axis_index("row")
    paired = row_count & (row_count - 1) == 0
    rows = (tiles + chunks + 8) // 8 * 8
    depth = (faults * (chunks + 1) + LANES - 1) // LANES * LANES

    source = tile_col[0, 0] // tiles
    order = source ^ my_row if paired else (my_row - source) % row_count
    spots = (order * height + tile_col[0, 0] % tiles).reshape(1, slots)
    target = (tile_row[0, 0] // tiles * height + tile_row[0, 0] % tiles).reshape(1, slots)
    weight = jnp.where(
        jnp.arange(slots, dtype=jnp.int32) < tile_counts[0, 0], tile_scale[0, 0], 0.0
    ).reshape(1, slots)

    grid = jax.ShapeDtypeStruct((height, LANES), F32)
    plain = jax.ShapeDtypeStruct((tiles, LANES), F32)
    work = [
        scratch((rows, LANES)),
        scratch((chunks + 1, faults, LANES)),
        scratch((faults, LANES), jnp.int32),
        scratch((faults, LANES), jnp.int32),
        scratch((depth, LANES)),
    ]

    sent0, blocks = pl.pallas_call(
        first_kernel,
        out_shape=[grid, pltpu.VMEM((faults, width, width), BF16)],
        in_specs=[SMEM, VMEM, VMEM, ANY],
        out_specs=[VMEM, VMEM],
        scratch_shapes=work + [pltpu.SemaphoreType.DMA((faults,))],
        compiler_params=PARAMS,
        name="first",
    )(fault_sizes, rhs, friction, precond_blocks)

    near = pltpu.with_memory_space_constraint(
        kernel_tiles.reshape(slots, LANES, LANES), pltpu.VMEM
    )

    def apply_kernel(sent):
        got = [sent]
        for d in range(1, row_count):
            pairs = [(i, i ^ d if paired else (i + d) % row_count) for i in range(row_count)]
            got.append(lax.ppermute(sent, "row", pairs))
        sums = got[0][tiles]
        for one in got[1:]:
            sums = sums + one[tiles]
        parts = pl.pallas_call(
            tiles_kernel,
            out_shape=jax.ShapeDtypeStruct((col_count, height, LANES), F32),
            in_specs=[SMEM, VMEM, VMEM, VMEM] + [VMEM] * row_count,
            out_specs=VMEM,
            scratch_shapes=[
                scratch((row_count * height, LANES)),
                scratch((slots, LANES)),
                scratch((slots, LANES)),
            ],
            compiler_params=PARAMS,
            name="tiles",
        )(spots, target, weight, near, *got)
        parts = parts.at[:, tiles, :].set(sums)
        return lax.all_to_all(parts, "col", 0, 0, tiled=True)

    parts0 = apply_kernel(sent0)
    sent1, image0, basis = pl.pallas_call(
        second_kernel,
        out_shape=[grid, plain, grid],
        in_specs=[SMEM] + [VMEM] * 5,
        out_specs=[VMEM] * 3,
        scratch_shapes=work,
        compiler_params=PARAMS,
        name="second",
    )(fault_sizes, rhs, friction, sent0, parts0, blocks)
    parts1 = apply_kernel(sent1)
    sent2, image1 = pl.pallas_call(
        third_kernel,
        out_shape=[grid, plain],
        in_specs=[SMEM] + [VMEM] * 6,
        out_specs=[VMEM] * 2,
        scratch_shapes=work,
        compiler_params=PARAMS,
        name="third",
    )(fault_sizes, rhs, friction, sent1, parts1, basis, blocks)
    parts2 = apply_kernel(sent2)
    devices = row_count * col_count
    image2, sums = pl.pallas_call(
        fourth_kernel,
        out_shape=[plain, jax.ShapeDtypeStruct((devices, LANES), F32)],
        in_specs=[VMEM] * 6,
        out_specs=[VMEM] * 2,
        compiler_params=PARAMS,
        name="fourth",
    )(rhs, friction, sent2, parts2, image0, image1)
    sums = lax.all_to_all(sums, ("row", "col"), 0, 0, tiled=True)
    whole = jax.ShapeDtypeStruct((1, 1, length), F32)
    return pl.pallas_call(
        last_kernel,
        out_shape=[whole, whole],
        in_specs=[VMEM] * 8,
        out_specs=[VMEM] * 2,
        compiler_params=PARAMS,
        name="last",
    )(sums, rhs, image0, image1, image2, sent0, sent1, sent2)


def solution(mesh):
    return jax.shard_map(
        local,
        mesh=mesh,
        in_specs=(
            P("row", "col", None),
            P("row", "col", None),
            P("row", "col", None, None, None),
            P("row", "col", None),
            P("row", "col", None),
            P("row", "col", None),
            P("row", "col"),
            P("row", "col", None, None, None),
            P("row", "col", None),
        ),
        out_specs=(P("row", "col", None), P("row", "col", None)),
        check_vma=False,
    )
```

time: 1090 us -> 128 us (0.12)
  blocking collectives: 447 us -> 43.3 us
  local copies, waits for them, and re-layouts: 311 us -> 19.6 us
  waiting for transfers between devices: 198 us -> 7.61 us
  matrix products: 56.1 us -> 0 us
  other arithmetic: 56.7 us -> 1.83 us
  Pallas kernels: 0 us -> 41.3 us
  between operations: 17.6 us -> 1.49 us
  starting transfers between devices: 0.16 us -> 11.5 us
    psum x10 -> x0, blocking collectives: 409 us -> none  [the longest x6 247 us: local(): height = lax.psum(jnp.sum(earlier * image), ('row', 'col'))]
    gather x15 -> x0, local copies, waits for them, and re-layouts: 305 us -> none  [the longest x6 228 us: local(): low_vector[gather_spot]]
    psum x4 -> x0, waiting for transfers between devices: 198 us -> none  [kernel_apply(): row_total = lax.psum(partial_value, 'col')]
    dot_general x9 -> x0, matrix products: 55.9 us -> none  [the longest x4 31.1 us: kernel_apply(): jnp.einsum('tij,tj->ti', local_tiles, column_pieces, preferred_element_ty...]
    all_to_all x0 -> x4, blocking collectives: none -> 43.3 us  [the longest x3 33.3 us: apply_kernel(): return lax.all_to_all(parts, 'col', 0, 0, tiled=True)]
    pallas_call x0 -> x8, Pallas kernels: none -> 41.3 us  [the longest x3 12.3 us: apply_kernel(): pl.pallas_call(tiles_kernel, out_shape=jax.ShapeDtypeStruct((col_count, h...]
    all_gather x4 -> x0, blocking collectives: 37.3 us -> none  [kernel_apply(): column = lax.all_gather(low_field, 'row', axis=0, tiled=True)]
    reduce_sum x11 -> x0, other arithmetic: 16.7 us -> none  [the longest x6 10.8 us: local(): height = lax.psum(jnp.sum(earlier * image), ('row', 'col'))]
  transfers between devices with their start and end apart: 4 -> 9, of which waited for: 4 -> 8; matrix products, arithmetic and copies ran while one was open for 1% -> 1% of each run, Pallas kernels for 0% -> 0%
where the time goes in v1:
time: 128 us; the launch traced here: 127 us
  blocking collectives  43.3 us (34%)
  Pallas kernels  41.3 us (32%)
  local copies, waits for them, and re-layouts  19.6 us (15%)
  starting transfers between devices  11.5 us (9%)
  waiting for transfers between devices  7.61 us (6%)
  other arithmetic  1.83 us (1%)
  between operations  1.49 us (1%)
    all_to_all x3, blocking collectives, apply_kernel(): return lax.all_to_all(parts, 'col', 0, 0, tiled=True)  33.3 us
    unnamed x54, local copies, waits for them, and re-layouts  15.4 us
    pallas_call x3, Pallas kernels, apply_kernel(): pl.pallas_call(tiles_kernel, out_shape=jax.ShapeDtypeStruct((col_count, h...  12.3 us
    ppermute x9, starting transfers between devices, apply_kernel(): got.append(lax.ppermute(sent, 'row', pairs))  11.5 us
    all_to_all x1, blocking collectives, local(): sums = lax.all_to_all(sums, ('row', 'col'), 0, 0, tiled=True)  9.95 us
    pallas_call x1, Pallas kernels, local(): pl.pallas_call(first_kernel, out_shape=[grid, pltpu.VMEM((faults, width,...  9.73 us
    pallas_call x1, Pallas kernels, local(): pl.pallas_call(second_kernel, out_shape=[grid, plain, grid], in_specs=[SM...  9.23 us
    pallas_call x1, Pallas kernels, local(): pl.pallas_call(third_kernel, out_shape=[grid, plain], in_specs=[SMEM] + [...  9.18 us
  transfers between devices with their start and end apart: 9, of which 8 were waited for; matrix products, arithmetic and copies ran while one was open for 1% of the time, Pallas kernels for 0%

profile of v1, /device:TPU:0, one launch (start us, length us, event | category | flops | bytes accessed | tf_op | source)
XLA Modules:
  0.0 126.6 jit_solution(10704767424496406024)
XLA Ops:
  0.6 0.0 copy-start.4
  0.6 0.0 copy-start.5
  0.7 0.0 copy-start.14
  0.7 0.0 copy-start.25
  0.7 0.0 copy-start.26
  0.7 0.0 copy-start.24
  0.7 9.7 %first.1 = (f32[40,128]{1,0:T(8,128)}, bf16[24,512,512]{2,1,0:T(8,128)(2,1)S(1)}) custom-call(s32[1,1,24]{2,1,0:T(1,128)} %sizes.5, f32[1,1,4608]{2,1,0:T(1,128)} %rhs.12, f32[1,1,4608]{2,1,0:T(1,128)} %friction.7, bf16[1,1,24,512,512]{4,3,2,1,0:T(8,128)(2,1)} %blocks.1), custom_call_target="tpu_custom_call" | custom-call | tf_op jit(solution)/shard_map/first/pallas_call | solution.py:372
  10.4 0.0 copy-start.3
  10.4 4.5 %copy-done.3 = bf16[24,512,512]{2,1,0:T(8,128)(2,1)} copy-done((bf16[24,512,512]{2,1,0:T(8,128)(2,1)}, bf16[24,512,512]{2,1,0:T(8,128)(2,1)S(1)}, u32[]{:S(2)}) %copy-start.3) | copy-done | bytes 12582936
  15.0 3.8 %collective-permute-start.2 = (f32[40,128]{1,0:T(8,128)}, f32[40,128]{1,0:T(8,128)S(1)}, u32[]{:S(2)}, u32[]{:S(2)}) collective-permute-start(f32[40,128]{1,0:T(8,128)} %get-tuple-element.47.refs_0_.sent.sent0), channel_id=1, source_target_pairs={{0,24},{8,16},{16,8},{24,0},{1,25},{9,17},{17,9},{25,1},{2,26},{10... | collective-permute-start | bytes 61448 | tf_op jit(solution)/shard_map/ppermute | solution.py:390
  18.8 0.6 collective-permute-start.1
  19.3 0.1 collective-permute-start
  20.1 0.0 copy-done.25
  20.1 0.0 copy-done.26
  20.1 0.6 fusion.2
  20.7 0.0 copy-done.24
  20.7 0.5 compare_select_fusion.weight
  21.2 0.0 collective-permute-done.2.refs_3_
  21.2 1.5 %collective-permute-done.1.refs_2_ = f32[40,128]{1,0:T(8,128)S(1)} collective-permute-done((f32[40,128]{1,0:T(8,128)}, f32[40,128]{1,0:T(8,128)S(1)}, u32[]{:S(2)}, u32[]{:S(2)}) %collective-permute-start.1) | collective-permute-done | bytes 20512 | tf_op jit(solution)/shard_map/ppermute | solution.py:390
  22.8 0.6 collective-permute-done.refs_1_
  23.3 0.7 fusion.6
  24.0 0.0 copy-done.15
  24.0 0.0 copy-done.16
  24.0 0.0 copy-done.17
  24.0 0.0 copy-start
  24.1 3.4 %copy-done = bf16[1,1,256,128,128]{4,3,2,1,0:T(8,128)(2,1)S(1)} copy-done((bf16[1,1,256,128,128]{4,3,2,1,0:T(8,128)(2,1)S(1)}, bf16[1,1,256,128,128]{4,3,2,1,0:T(8,128)(2,1)}, u32[]{:S(2)}) %copy-start) | copy-done | bytes 8388632
  27.4 4.1 %tiles.3 = f32[8,40,128]{2,1,0:T(8,128)} custom-call(s32[1,256]{1,0:T(1,128)} %get-tuple-element.56.spots, s32[1,256]{1,0:T(1,128)} %get-tuple-element.57.rows, f32[1,256]{1,0:T(1,128)} %compare_select_fusion.weight, bf16[256,128,128]{2,1,0:T(8,128)(2,1)S(1)} %bitcast.45, f32[40,128]{1,0:T(8,128)} %get-tuple-element.47.refs_0_.sent.sent0, ...), custom_call_target="tpu_custom_call" | custom-call | tf_op jit(solution)/shard_map/tiles/pallas_call | solution.py:394
  31.5 1.4 %scatter.10 = f32[8,40,128]{2,1,0:T(8,128)} dynamic-update-slice(f32[8,40,128]{2,1,0:T(8,128)} %tiles.3, f32[8,1,128]{2,1,0:T(1,128)S(1)} %broadcast.206, s32[]{:T(128)} %constant.97.clone.1, s32[]{:T(128)} %constant.96.clone.1, s32[]{:T(128)} %constant.97.clone.1) | dynamic-update-slice | bytes 8196 | tf_op jit(solution)/shard_map/scatter | solution.py:407
  32.9 12.3 %all_to_all.26.parts = f32[8,40,128]{2,1,0:T(8,128)S(1)} all-to-all(f32[8,40,128]{2,1,0:T(8,128)} %scatter.10), channel_id=1, replica_groups=mesh['row'=4,'col'=8] {'col'}, dimensions={0} | all-to-all | bytes 327680 | tf_op jit(solution)/shard_map/all_to_all | solution.py:408
  45.2 0.0 copy-done.4
  45.2 0.0 copy-done.5
  45.2 0.0 copy-start.6
  45.3 0.7 copy-done.6
  46.0 9.2 %second.1 = (f32[40,128]{1,0:T(8,128)S(1)}, f32[36,128]{1,0:T(8,128)S(1)}, f32[40,128]{1,0:T(8,128)S(1)}) custom-call(s32[1,1,24]{2,1,0:T(1,128)S(1)} %copy-done.14, f32[1,1,4608]{2,1,0:T(1,128)S(1)} %copy-done.4, f32[1,1,4608]{2,1,0:T(1,128)S(1)} %copy-done.5, f32[40,128]{1,0:T(8,128)S(1)} %copy-done.6, f32[8,40,128]{2,1,0:T(8,128)S(1)} %all_to_all.26.parts, ...), custom_call_target="tpu_custom_call" | custom-call | tf_op jit(solution)/shard_map/second/pallas_call | solution.py:411
  55.2 1.4 %collective-permute-start.5 = (f32[40,128]{1,0:T(8,128)S(1)}, f32[40,128]{1,0:T(8,128)S(1)}, u32[]{:S(2)}, u32[]{:S(2)}) collective-permute-start(f32[40,128]{1,0:T(8,128)S(1)} %get-tuple-element.49.refs_0_.sent.sent1), channel_id=1, source_target_pairs={{0,24},{8,16},{16,8},{24,0},{1,25},{9,17},{17,9},{25,1},{2,26},{10... | collective-permute-start | bytes 61448 | tf_op jit(solution)/shard_map/ppermute | solution.py:390
  56.6 0.6 collective-permute-start.4
  57.2 1.5 %collective-permute-start.3 = (f32[40,128]{1,0:T(8,128)S(1)}, f32[40,128]{1,0:T(8,128)S(1)}, u32[]{:S(2)}, u32[]{:S(2)}) collective-permute-start(f32[40,128]{1,0:T(8,128)S(1)} %get-tuple-element.49.refs_0_.sent.sent1), channel_id=1, source_target_pairs={{0,8},{8,0},{16,24},{24,16},{1,9},{9,1},{17,25},{25,17},{2,10},{10... | collective-permute-start | bytes 61448 | tf_op jit(solution)/shard_map/ppermute | solution.py:390
  58.7 1.2 collective-permute-done.5.refs_3_
  59.9 0.5 collective-permute-done.4.refs_2_
  60.4 0.6 collective-permute-done.3.refs_1_
  61.0 0.6 copy-done.23
  61.6 4.1 %tiles.4 = f32[8,40,128]{2,1,0:T(8,128)} custom-call(s32[1,256]{1,0:T(1,128)} %get-tuple-element.56.spots, s32[1,256]{1,0:T(1,128)} %get-tuple-element.57.rows, f32[1,256]{1,0:T(1,128)} %compare_select_fusion.weight, bf16[256,128,128]{2,1,0:T(8,128)(2,1)S(1)} %bitcast.46, f32[40,128]{1,0:T(8,128)} %copy-done.8, f32[40,128]{1,0:T(8,128)} %copy-done.23, ...), custom_call_target="tpu_custom_call" | custom-call | tf_op jit(solution)/shard_map/tiles/pallas_call | solution.py:394
  65.7 1.4 %scatter.11 = f32[8,40,128]{2,1,0:T(8,128)} dynamic-update-slice(f32[8,40,128]{2,1,0:T(8,128)} %tiles.4, f32[8,1,128]{2,1,0:T(1,128)S(1)} %broadcast.207, s32[]{:T(128)} %constant.97.clone.1, s32[]{:T(128)} %constant.96.clone.1, s32[]{:T(128)} %constant.97.clone.1) | dynamic-update-slice | bytes 8196 | tf_op jit(solution)/shard_map/scatter | solution.py:407
  67.1 10.5 %all_to_all.27.parts = f32[8,40,128]{2,1,0:T(8,128)S(1)} all-to-all(f32[8,40,128]{2,1,0:T(8,128)} %scatter.11), channel_id=1, replica_groups=mesh['row'=4,'col'=8] {'col'}, dimensions={0} | all-to-all | bytes 327680 | tf_op jit(solution)/shard_map/all_to_all | solution.py:408
  77.6 0.7 copy-done.9
  78.3 9.2 %third.1 = (f32[40,128]{1,0:T(8,128)S(1)}, f32[36,128]{1,0:T(8,128)S(1)}) custom-call(s32[1,1,24]{2,1,0:T(1,128)S(1)} %copy-done.14, f32[1,1,4608]{2,1,0:T(1,128)S(1)} %copy-done.4, f32[1,1,4608]{2,1,0:T(1,128)S(1)} %copy-done.5, f32[40,128]{1,0:T(8,128)S(1)} %copy-done.9, f32[8,40,128]{2,1,0:T(8,128)S(1)} %all_to_all.27.parts, ...), custom_call_target="tpu_custom_call" | custom-call | tf_op jit(solution)/shard_map/third/pallas_call | solution.py:421
  87.5 2.5 %collective-permute-start.8 = (f32[40,128]{1,0:T(8,128)S(1)}, f32[40,128]{1,0:T(8,128)S(1)}, u32[]{:S(2)}, u32[]{:S(2)}) collective-permute-start(f32[40,128]{1,0:T(8,128)S(1)} %get-tuple-element.51.refs_0_.sent.sent2), channel_id=1, source_target_pairs={{0,24},{8,16},{16,8},{24,0},{1,25},{9,17},{17,9},{25,1},{2,26},{10... | collective-permute-start | bytes 61448 | tf_op jit(solution)/shard_map/ppermute | solution.py:390
  90.1 0.5 collective-permute-start.7
  90.5 0.5 collective-permute-start.6
  91.1 1.2 collective-permute-done.8.refs_3_
  92.3 1.6 %collective-permute-done.7.refs_2_ = f32[40,128]{1,0:T(8,128)S(1)} collective-permute-done((f32[40,128]{1,0:T(8,128)S(1)}, f32[40,128]{1,0:T(8,128)S(1)}, u32[]{:S(2)}, u32[]{:S(2)}) %collective-permute-start.7) | collective-permute-done | bytes 20512 | tf_op jit(solution)/shard_map/ppermute | solution.py:390
  93.8 0.5 collective-permute-done.6.refs_1_
  94.4 0.1 copy-done.20
  94.4 0.5 copy-done.22
  94.9 3.4 %copy-done.2 = bf16[1,1,256,128,128]{4,3,2,1,0:T(8,128)(2,1)S(1)} copy-done((bf16[1,1,256,128,128]{4,3,2,1,0:T(8,128)(2,1)S(1)}, bf16[1,1,256,128,128]{4,3,2,1,0:T(8,128)(2,1)}, u32[]{:S(2)}) %copy-start.2) | copy-done | bytes 8388632
  98.3 4.1 %tiles.5 = f32[8,40,128]{2,1,0:T(8,128)} custom-call(s32[1,256]{1,0:T(1,128)} %get-tuple-element.56.spots, s32[1,256]{1,0:T(1,128)} %get-tuple-element.57.rows, f32[1,256]{1,0:T(1,128)} %compare_select_fusion.weight, bf16[256,128,128]{2,1,0:T(8,128)(2,1)S(1)} %bitcast.47, f32[40,128]{1,0:T(8,128)} %copy-done.11, f32[40,128]{1,0:T(8,128)} %copy-done.22, ...), custom_call_target="tpu_custom_call" | custom-call | tf_op jit(solution)/shard_map/tiles/pallas_call | solution.py:394
  102.4 1.4 %scatter.14 = f32[8,40,128]{2,1,0:T(8,128)} dynamic-update-slice(f32[8,40,128]{2,1,0:T(8,128)} %tiles.5, f32[8,1,128]{2,1,0:T(1,128)S(1)} %broadcast.208, s32[]{:T(128)} %constant.97.clone.1, s32[]{:T(128)} %constant.96.clone.1, s32[]{:T(128)} %constant.97.clone.1) | dynamic-update-slice | bytes 8196 | tf_op jit(solution)/shard_map/scatter | solution.py:407
  103.8 10.5 %all_to_all.28.parts = f32[8,40,128]{2,1,0:T(8,128)S(1)} all-to-all(f32[8,40,128]{2,1,0:T(8,128)} %scatter.14), channel_id=1, replica_groups=mesh['row'=4,'col'=8] {'col'}, dimensions={0} | all-to-all | bytes 327680 | tf_op jit(solution)/shard_map/all_to_all | solution.py:408
  114.3 0.7 copy-done.12
  115.0 0.1 fourth.1
  115.1 9.9 %all_to_all.29 = f32[32,1,128]{2,1,0:T(1,128)S(1)} all-to-all(f32[32,1,128]{2,1,0:T(1,128)S(1)} %bitcast.49), channel_id=1, replica_groups=mesh['row'=4,'col'=8] {'row','col'}, dimensions={0} | all-to-all | bytes 32768 | tf_op jit(solution)/shard_map/all_to_all | solution.py:440
  125.1 0.0 copy-done.10
  125.1 0.7 copy-done.13
  125.8 0.8 last.1
  (31 shorter events, 0.1 us)
Async XLA Ops:
  0.6 44.6 %copy-start.4 = (f32[1,1,4608]{2,1,0:T(1,128)S(1)}, f32[1,1,4608]{2,1,0:T(1,128)}, u32[]{:S(2)}) copy-start(f32[1,1,4608]{2,1,0:T(1,128)} %rhs.12) | copy-start | bytes 55300
  0.6 44.6 %copy-start.5 = (f32[1,1,4608]{2,1,0:T(1,128)S(1)}, f32[1,1,4608]{2,1,0:T(1,128)}, u32[]{:S(2)}) copy-start(f32[1,1,4608]{2,1,0:T(1,128)} %friction.7) | copy-start | bytes 55300
  0.7 44.6 %copy-start.14 = (s32[1,1,24]{2,1,0:T(1,128)S(1)}, s32[1,1,24]{2,1,0:T(1,128)}, u32[]{:S(2)}) copy-start(s32[1,1,24]{2,1,0:T(1,128)} %sizes.5) | copy-start | bytes 292
  0.7 19.4 %copy-start.25 = (s32[1,1,256]{2,1,0:T(1,128)S(1)}, s32[1,1,256]{2,1,0:T(1,128)}, u32[]{:S(2)}) copy-start(s32[1,1,256]{2,1,0:T(1,128)} %param.20) | copy-start | bytes 3076
  0.7 19.4 %copy-start.26 = (s32[1,1,256]{2,1,0:T(1,128)S(1)}, s32[1,1,256]{2,1,0:T(1,128)}, u32[]{:S(2)}) copy-start(s32[1,1,256]{2,1,0:T(1,128)} %param.19) | copy-start | bytes 3076
  0.7 20.0 %copy-start.24 = (f32[1,1,256]{2,1,0:T(1,128)S(1)}, f32[1,1,256]{2,1,0:T(1,128)}, u32[]{:S(2)}) copy-start(f32[1,1,256]{2,1,0:T(1,128)} %param.18) | copy-start | bytes 3076
  10.4 4.5 %copy-start.3 = (bf16[24,512,512]{2,1,0:T(8,128)(2,1)}, bf16[24,512,512]{2,1,0:T(8,128)(2,1)S(1)}, u32[]{:S(2)}) copy-start(bf16[24,512,512]{2,1,0:T(8,128)(2,1)S(1)} %get-tuple-element.48.blocks) | copy-start | bytes 37748740
  15.0 6.3 %collective-permute-start.2 = (f32[40,128]{1,0:T(8,128)}, f32[40,128]{1,0:T(8,128)S(1)}, u32[]{:S(2)}, u32[]{:S(2)}) collective-permute-start(f32[40,128]{1,0:T(8,128)} %get-tuple-element.47.refs_0_.sent.sent0), channel_id=1, source_target_pairs={{0,24},{8,16},{16,8},{24,0},{1,25},{9,17},{17,9},{25,1},{2,26},{10... | collective-permute-start | bytes 61448 | tf_op jit(solution)/shard_map/ppermute | solution.py:390
  18.8 4.0 %collective-permute-start.1 = (f32[40,128]{1,0:T(8,128)}, f32[40,128]{1,0:T(8,128)S(1)}, u32[]{:S(2)}, u32[]{:S(2)}) collective-permute-start(f32[40,128]{1,0:T(8,128)} %get-tuple-element.47.refs_0_.sent.sent0), channel_id=1, source_target_pairs={{0,16},{8,24},{16,0},{24,8},{1,17},{9,25},{17,1},{25,9},{2,18},{10... | collective-permute-start | bytes 61448 | tf_op jit(solution)/shard_map/ppermute | solution.py:390
  19.3 4.0 %collective-permute-start = (f32[40,128]{1,0:T(8,128)}, f32[40,128]{1,0:T(8,128)S(1)}, u32[]{:S(2)}, u32[]{:S(2)}) collective-permute-start(f32[40,128]{1,0:T(8,128)} %get-tuple-element.47.refs_0_.sent.sent0), channel_id=1, source_target_pairs={{0,8},{8,0},{16,24},{24,16},{1,9},{9,1},{17,25},{25,17},{2,10},{10... | collective-permute-start | bytes 61448 | tf_op jit(solution)/shard_map/ppermute | solution.py:390
  21.2 2.8 %copy-start.15 = (f32[40,128]{1,0:T(8,128)}, f32[40,128]{1,0:T(8,128)S(1)}, u32[]{:S(2)}) copy-start(f32[40,128]{1,0:T(8,128)S(1)} %collective-permute-done.2.refs_3_) | copy-start | bytes 61444
  22.8 1.3 copy-start.16
  23.3 0.7 copy-start.17
  24.0 3.4 %copy-start = (bf16[1,1,256,128,128]{4,3,2,1,0:T(8,128)(2,1)S(1)}, bf16[1,1,256,128,128]{4,3,2,1,0:T(8,128)(2,1)}, u32[]{:S(2)}) copy-start(bf16[1,1,256,128,128]{4,3,2,1,0:T(8,128)(2,1)} %param.17) | copy-start | bytes 25165828
  32.9 28.7 %copy-start.1 = (bf16[1,1,256,128,128]{4,3,2,1,0:T(8,128)(2,1)S(1)}, bf16[1,1,256,128,128]{4,3,2,1,0:T(8,128)(2,1)}, u32[]{:S(2)}) copy-start(bf16[1,1,256,128,128]{4,3,2,1,0:T(8,128)(2,1)} %param.17) | copy-start | bytes 25165828
  45.2 0.7 copy-start.6
  55.2 5.8 %copy-start.8 = (f32[40,128]{1,0:T(8,128)}, f32[40,128]{1,0:T(8,128)S(1)}, u32[]{:S(2)}) copy-start(f32[40,128]{1,0:T(8,128)S(1)} %get-tuple-element.49.refs_0_.sent.sent1) | copy-start | bytes 61444
  55.2 4.7 %collective-permute-start.5 = (f32[40,128]{1,0:T(8,128)S(1)}, f32[40,128]{1,0:T(8,128)S(1)}, u32[]{:S(2)}, u32[]{:S(2)}) collective-permute-start(f32[40,128]{1,0:T(8,128)S(1)} %get-tuple-element.49.refs_0_.sent.sent1), channel_id=1, source_target_pairs={{0,24},{8,16},{16,8},{24,0},{1,25},{9,17},{17,9},{25,1},{2,26},{10... | collective-permute-start | bytes 61448 | tf_op jit(solution)/shard_map/ppermute | solution.py:390
  56.6 3.8 %collective-permute-start.4 = (f32[40,128]{1,0:T(8,128)S(1)}, f32[40,128]{1,0:T(8,128)S(1)}, u32[]{:S(2)}, u32[]{:S(2)}) collective-permute-start(f32[40,128]{1,0:T(8,128)S(1)} %get-tuple-element.49.refs_0_.sent.sent1), channel_id=1, source_target_pairs={{0,16},{8,24},{16,0},{24,8},{1,17},{9,25},{17,1},{25,9},{2,18},{10... | collective-permute-start | bytes 61448 | tf_op jit(solution)/shard_map/ppermute | solution.py:390
  57.2 3.8 %collective-permute-start.3 = (f32[40,128]{1,0:T(8,128)S(1)}, f32[40,128]{1,0:T(8,128)S(1)}, u32[]{:S(2)}, u32[]{:S(2)}) collective-permute-start(f32[40,128]{1,0:T(8,128)S(1)} %get-tuple-element.49.refs_0_.sent.sent1), channel_id=1, source_target_pairs={{0,8},{8,0},{16,24},{24,16},{1,9},{9,1},{17,25},{25,17},{2,10},{10... | collective-permute-start | bytes 61448 | tf_op jit(solution)/shard_map/ppermute | solution.py:390
  59.9 1.1 copy-start.19
  60.4 0.6 copy-start.21
  61.0 0.6 copy-start.23
  65.7 59.4 %copy-start.7 = (f32[40,128]{1,0:T(8,128)S(1)}, f32[40,128]{1,0:T(8,128)}, u32[]{:S(2)}) copy-start(f32[40,128]{1,0:T(8,128)} %get-tuple-element.47.refs_0_.sent.sent0) | copy-start | bytes 61444
  65.7 59.4 %copy-start.10 = (f32[40,128]{1,0:T(8,128)S(1)}, f32[40,128]{1,0:T(8,128)}, u32[]{:S(2)}) copy-start(f32[40,128]{1,0:T(8,128)} %copy-done.8) | copy-start | bytes 61444
  77.6 0.7 copy-start.9
  87.5 6.8 %copy-start.11 = (f32[40,128]{1,0:T(8,128)}, f32[40,128]{1,0:T(8,128)S(1)}, u32[]{:S(2)}) copy-start(f32[40,128]{1,0:T(8,128)S(1)} %get-tuple-element.51.refs_0_.sent.sent2) | copy-start | bytes 61444
  87.5 4.7 %collective-permute-start.8 = (f32[40,128]{1,0:T(8,128)S(1)}, f32[40,128]{1,0:T(8,128)S(1)}, u32[]{:S(2)}, u32[]{:S(2)}) collective-permute-start(f32[40,128]{1,0:T(8,128)S(1)} %get-tuple-element.51.refs_0_.sent.sent2), channel_id=1, source_target_pairs={{0,24},{8,16},{16,8},{24,0},{1,25},{9,17},{17,9},{25,1},{2,26},{10... | collective-permute-start | bytes 61448 | tf_op jit(solution)/shard_map/ppermute | solution.py:390
  90.1 3.8 %collective-permute-start.7 = (f32[40,128]{1,0:T(8,128)S(1)}, f32[40,128]{1,0:T(8,128)S(1)}, u32[]{:S(2)}, u32[]{:S(2)}) collective-permute-start(f32[40,128]{1,0:T(8,128)S(1)} %get-tuple-element.51.refs_0_.sent.sent2), channel_id=1, source_target_pairs={{0,16},{8,24},{16,0},{24,8},{1,17},{9,25},{17,1},{25,9},{2,18},{10... | collective-permute-start | bytes 61448 | tf_op jit(solution)/shard_map/ppermute | solution.py:390
  90.5 3.8 %collective-permute-start.6 = (f32[40,128]{1,0:T(8,128)S(1)}, f32[40,128]{1,0:T(8,128)S(1)}, u32[]{:S(2)}, u32[]{:S(2)}) collective-permute-start(f32[40,128]{1,0:T(8,128)S(1)} %get-tuple-element.51.refs_0_.sent.sent2), channel_id=1, source_target_pairs={{0,8},{8,0},{16,24},{24,16},{1,9},{9,1},{17,25},{25,17},{2,10},{10... | collective-permute-start | bytes 61448 | tf_op jit(solution)/shard_map/ppermute | solution.py:390
  92.3 2.1 %copy-start.18 = (f32[40,128]{1,0:T(8,128)}, f32[40,128]{1,0:T(8,128)S(1)}, u32[]{:S(2)}) copy-start(f32[40,128]{1,0:T(8,128)S(1)} %collective-permute-done.8.refs_3_) | copy-start | bytes 61444
  93.8 0.6 copy-start.20
  94.3 0.6 copy-start.22
  94.9 3.4 %copy-start.2 = (bf16[1,1,256,128,128]{4,3,2,1,0:T(8,128)(2,1)S(1)}, bf16[1,1,256,128,128]{4,3,2,1,0:T(8,128)(2,1)}, u32[]{:S(2)}) copy-start(bf16[1,1,256,128,128]{4,3,2,1,0:T(8,128)(2,1)} %param.17) | copy-start | bytes 25165828
  114.3 0.7 copy-start.12
  125.1 0.7 copy-start.13

commit v2 on v1

--- a/solution.py
+++ b/solution.py
@@ -1,3 +1,5 @@
+import functools
+
 import jax
 import jax.numpy as jnp
 from jax import lax
@@ -6,12 +8,13 @@
 from jax.sharding import PartitionSpec as P
 
 LANES = 128
+UNROLL = 3
 F32 = jnp.float32
 BF16 = jnp.bfloat16
 VMEM = pl.BlockSpec(memory_space=pltpu.VMEM)
 SMEM = pl.BlockSpec(memory_space=pltpu.SMEM)
 ANY = pl.BlockSpec(memory_space=pl.ANY)
-PARAMS = pltpu.CompilerParams(vmem_limit_bytes=48 << 20)
+PARAMS = pltpu.CompilerParams(vmem_limit_bytes=54 << 20)
 
 
 def dot_nt(left, right):
@@ -56,10 +59,25 @@
     return scalars
 
 
-def precondition(scalars, blocks, field, windows, shifts, lens, stack, ready):
-    faults = len(scalars)
+def fetch(scalars, remote, blocks, sems):
+    copies = []
+    for f, (_, _, size) in enumerate(scalars):
+        need = pl.multiple_of((size + 15) // 16 * 16, 16)
+        copy = pltpu.make_async_copy(
+            remote.at[0, 0, f, pl.ds(0, need)], blocks.at[f, pl.ds(0, need)], sems.at[f]
+        )
+        copy.start()
+        copies.append(copy)
+    return copies
+
+
+def precondition(sizes, remote, field, work):
+    blocks, windows, shifts, lens, stack, lefts, found, large, sems = work
+    faults = remote.shape[2]
     chunks = blocks.shape[1] // LANES
     rows = field.shape[0]
+    scalars = fault_scalars(sizes, faults)
+    copies = fetch(scalars, remote, blocks, sems)
     lane = lax.broadcasted_iota(jnp.int32, (faults, LANES), 1)
     for f, (tile, shift, size) in enumerate(scalars):
         shifts[f : f + 1, :] = jnp.full((1, LANES), shift, jnp.int32)
@@ -81,27 +99,50 @@
         parts = [jnp.where(bits[b], new, old) for new, old in zip(moved, parts)]
     parts = [jnp.where(live[k], parts[k], 0.0) for k in range(chunks)]
     sub = lax.broadcasted_iota(jnp.int32, (8, LANES), 0)
-    products = [[] for _ in range(chunks)]
+    half = blocks.shape[1] // 2
+    chunk_half = chunks // 2
     for group in range(faults // 8):
         pieces = []
         for k in range(chunks):
             high, low = split(parts[k][group * 8 : group * 8 + 8])
             pieces.append(jnp.concatenate([high, low], axis=0))
         left = jnp.concatenate(pieces, axis=1)
-        found = [jnp.zeros((8, LANES), F32) for _ in range(chunks)]
+        lefts[group] = left
+        sums = [jnp.zeros((8, LANES), F32) for _ in range(chunk_half)]
         for place in range(8):
             f = group * 8 + place
-            ready(f)
-            result = dot_nt(left, blocks[f])
+            copies[f].wait()
+            result = dot_nt(left[:, :half], blocks[f, :half, :half])
             result = result[:8] + result[8:]
-            for k in range(chunks):
-                found[k] = jnp.where(
-                    sub == place, result[:, k * LANES : (k + 1) * LANES], found[k]
-                )
+            for k in range(chunk_half):
+                sums[k] = jnp.where(sub == place, result[:, k * LANES : (k + 1) * LANES], sums[k])
         for k in range(chunks):
-            products[k].append(found[k])
+            found[k, group] = sums[k] if k < chunk_half else jnp.zeros((8, LANES), F32)
+    count = jnp.int32(0)
+    for f, (_, _, size) in enumerate(scalars):
+        large[count] = f
+        count = count + (size > half).astype(jnp.int32)
+
+    def rest(step, carry):
+        for u in range(UNROLL):
+            place = step * UNROLL + u
+            f = large[jnp.minimum(place, count - 1)]
+            group = f // 8
+            left = lefts[group]
+            above = dot_nt(left[:, half:], blocks[f, :half, half:])
+            below = dot_nt(left, blocks[f, half:, :])
+            above = above[:8] + above[8:]
+            below = below[:8] + below[8:]
+            mine = jnp.logical_and(sub == f % 8, place < count)
+            for k in range(chunk_half):
+                piece = slice(k * LANES, (k + 1) * LANES)
+                found[k, group] += jnp.where(mine, above[:, piece], 0.0)
+                found[chunk_half + k, group] += jnp.where(mine, below[:, piece], 0.0)
+        return carry
+
+    lax.fori_loop(0, (count + UNROLL - 1) // UNROLL, rest, 0)
     parts = [
-        jnp.where(live[k], jnp.concatenate(products[k], axis=0), 0.0) for k in range(chunks)
+        jnp.where(live[k], found[k].reshape(faults, LANES), 0.0) for k in range(chunks)
     ]
     parts.append(jnp.zeros((faults, LANES), F32))
     for b in range(7):
@@ -134,29 +175,17 @@
     )
 
 
-def always(f):
-    pass
-
-
-def first_kernel(sizes, rhs, friction, blocks, send, blocks_out, field, windows, shifts, lens, stack, sems):
-    faults, width = blocks.shape[2], blocks.shape[3]
-    tiles = rhs.shape[2] // LANES
-    scalars = fault_scalars(sizes, faults)
-    copies = []
-    for f, (_, _, size) in enumerate(scalars):
-        need = pl.multiple_of((size + 15) // 16 * 16, 16)
-        copy = pltpu.make_async_copy(
-            blocks.at[0, 0, f, pl.ds(0, need)], blocks_out.at[f, pl.ds(0, need)], sems.at[f]
-        )
-        copy.start()
-        copies.append(copy)
-    value = load_rows(rhs, tiles)
+def set_field(field, value):
+    tiles = value.shape[0]
     field[0:tiles, :] = value
     field[tiles:, :] = jnp.zeros((field.shape[0] - tiles, LANES), F32)
-    out = precondition(
-        scalars, blocks_out, field, windows, shifts, lens, stack, lambda f: copies[f].wait()
-    )
-    direction = out[0:tiles]
+
+
+def first_kernel(sizes, rhs, friction, blocks, send, field, *work):
+    tiles = rhs.shape[2] // LANES
+    value = load_rows(rhs, tiles)
+    set_field(field, value)
+    direction = precondition(sizes, blocks, field, work)[0:tiles]
     scaled = load_rows(friction, tiles) * direction
     send[...] = jnp.zeros_like(send)
     send[0:tiles, :] = direction
@@ -164,15 +193,15 @@
 
 
 def gathered(parts, tiles):
-    whole = parts[0]
-    for c in range(1, parts.shape[0]):
-        whole = whole + parts[c]
+    whole = parts[0][...]
+    for part in parts[1:]:
+        whole = whole + part[...]
     return whole[0:tiles], whole[tiles : tiles + 1]
 
 
-def second_kernel(sizes, rhs, friction, sent, parts, blocks, send, image_out, basis_out, field, windows, shifts, lens, stack):
+def second_kernel(sizes, rhs, friction, blocks, sent, *refs):
+    parts, (send, image_out, basis_out, field, *work) = refs[:-13], refs[-13:]
     tiles = rhs.shape[2] // LANES
-    scalars = fault_scalars(sizes, blocks.shape[0])
     start = load_rows(rhs, tiles)
     diagonal = load_rows(friction, tiles)
     product, sums = gathered(parts, tiles)
@@ -183,9 +212,8 @@
     image_out[...] = image
     basis_out[0:tiles, :] = value
     basis_out[tiles:, :] = jnp.broadcast_to(norm2, (basis_out.shape[0] - tiles, LANES))
-    field[0:tiles, :] = value
-    field[tiles:, :] = jnp.zeros((field.shape[0] - tiles, LANES), F32)
-    direction = precondition(scalars, blocks, field, windows, shifts, lens, stack, always)[0:tiles]
+    set_field(field, value)
+    direction = precondition(sizes, blocks, field, work)[0:tiles]
     scaled = diagonal * direction
     send[...] = jnp.zeros_like(send)
     send[0:tiles, :] = direction
@@ -199,9 +227,9 @@
     )
 
 
-def third_kernel(sizes, rhs, friction, sent, parts, basis, blocks, send, image_out, field, windows, shifts, lens, stack):
+def third_kernel(sizes, rhs, friction, blocks, sent, basis, *refs):
+    parts, (send, image_out, field, *work) = refs[:-12], refs[-12:]
     tiles = rhs.shape[2] // LANES
-    scalars = fault_scalars(sizes, blocks.shape[0])
     start = load_rows(rhs, tiles)
     diagonal = load_rows(friction, tiles)
     product, sums = gathered(parts, tiles)
@@ -217,14 +245,14 @@
         jnp.maximum(norm2, 1e-30)
     )
     image_out[...] = image
-    field[0:tiles, :] = value
-    field[tiles:, :] = jnp.zeros((field.shape[0] - tiles, LANES), F32)
-    direction = precondition(scalars, blocks, field, windows, shifts, lens, stack, always)[0:tiles]
+    set_field(field, value)
+    direction = precondition(sizes, blocks, field, work)[0:tiles]
     send[...] = jnp.zeros_like(send)
     send[0:tiles, :] = direction
 
 
-def fourth_kernel(rhs, friction, sent, parts, image0, image1, image_out, sums_out):
+def fourth_kernel(rhs, friction, sent, image0, image1, *refs):
+    parts, (image_out, sums_out) = refs[:-2], refs[-2:]
     tiles = rhs.shape[2] // LANES
     start = load_rows(rhs, tiles)
     product, _ = gathered(parts, tiles)
@@ -276,19 +304,28 @@
         residual[0, :, pl.ds(k * LANES, LANES)] = rest[k : k + 1]
 
 
-def tiles_kernel(spots, rows, weight, blocks, *refs):
-    sent, (out, field, found, products) = refs[:-4], refs[-4:]
+def tiles_kernel(tail, spots, rows, weight, remote, *refs):
+    sent, (keep, give, blocks, field, found, products, sems) = refs[:-7], refs[-7:]
     slots = blocks.shape[0]
-    count, height = out.shape[0], out.shape[1]
-    tiles = height - 8 if height % 8 == 0 else height
-    sums = None
+    far, height = keep.shape[0], keep.shape[1]
+    groups = slots // 16
+    copies = []
+    for group in range(groups):
+        copy = pltpu.make_async_copy(
+            remote.at[0, 0, pl.ds(group * 16, 16)],
+            blocks.at[pl.ds(group * 16, 16)],
+            sems.at[group],
+        )
+        copy.start()
+        copies.append(copy)
     for k, one in enumerate(sent):
         field[k * height : (k + 1) * height, :] = one[...]
     for t in range(slots):
         found[t : t + 1, :] = field[pl.ds(spots[0, t], 1), :]
     sub = lax.broadcasted_iota(jnp.int32, (8, LANES), 0)
     blank = jnp.zeros((8, LANES), F32)
-    for group in range(slots // 16):
+    for group in range(groups):
+        copies[group].wait()
         base = group * 16
         top = jnp.concatenate([found[base : base + 8, :], blank], axis=1)
         bottom = jnp.concatenate([blank, found[base + 8 : base + 16, :]], axis=1)
@@ -312,7 +349,7 @@
     high, low = split(products[...])
     target = rows[...]
     chosen = jnp.where(
-        lax.broadcasted_iota(jnp.int32, (count * height, slots), 0) == target, weight[...], 0.0
+        lax.broadcasted_iota(jnp.int32, (2 * far * height, slots), 0) == target, weight[...], 0.0
     )
     chosen_high, chosen_low = split(chosen)
     value = (
@@ -320,7 +357,16 @@
         + jnp.dot(chosen_low, high, preferred_element_type=F32)
         + jnp.dot(chosen_high, low, preferred_element_type=F32)
     )
-    out[...] = value.reshape(count, height, LANES)
+    keep[...] = value[: far * height].reshape(far, height, LANES)
+    give[...] = value[far * height :].reshape(far, height, LANES)
+    last = height - 8
+    sums = sent[0][last:height, :]
+    for one in sent[1:]:
+        sums = sums + one[last:height, :]
+    sums = jnp.where(lax.broadcasted_iota(jnp.int32, (8, LANES), 0) == tail, sums, 0.0)
+    for k in range(far):
+        keep[k, last:height, :] += sums
+        give[k, last:height, :] += sums
 
 
 def scratch(shape, dtype=F32):
@@ -347,96 +393,99 @@
     row_count = lax.axis_size("row")
     col_count = lax.axis_size("col")
     my_row = lax.axis_index("row")
-    paired = row_count & (row_count - 1) == 0
+    my_col = lax.axis_index("col")
+    far = col_count // 2
     rows = (tiles + chunks + 8) // 8 * 8
     depth = (faults * (chunks + 1) + LANES - 1) // LANES * LANES
 
-    source = tile_col[0, 0] // tiles
-    order = source ^ my_row if paired else (my_row - source) % row_count
-    spots = (order * height + tile_col[0, 0] % tiles).reshape(1, slots)
-    target = (tile_row[0, 0] // tiles * height + tile_row[0, 0] % tiles).reshape(1, slots)
+    place = tile_col[0, 0] // tiles ^ my_row
+    spots = (place * height + tile_col[0, 0] % tiles).reshape(1, slots)
+    place = tile_row[0, 0] // tiles ^ my_col
+    place = place % 2 * far + place // 2
+    target = (place * height + tile_row[0, 0] % tiles).reshape(1, slots)
     weight = jnp.where(
         jnp.arange(slots, dtype=jnp.int32) < tile_counts[0, 0], tile_scale[0, 0], 0.0
     ).reshape(1, slots)
 
     grid = jax.ShapeDtypeStruct((height, LANES), F32)
     plain = jax.ShapeDtypeStruct((tiles, LANES), F32)
+    half_grid = jax.ShapeDtypeStruct((far, height, LANES), F32)
     work = [
         scratch((rows, LANES)),
+        scratch((faults, width, width), BF16),
         scratch((chunks + 1, faults, LANES)),
         scratch((faults, LANES), jnp.int32),
         scratch((faults, LANES), jnp.int32),
         scratch((depth, LANES)),
+        scratch((faults // 8, 16, width), BF16),
+        scratch((chunks, faults // 8, 8, LANES)),
+        pltpu.SMEM((faults + 1,), jnp.int32),
+        pltpu.SemaphoreType.DMA((faults,)),
     ]
 
-    sent0, blocks = pl.pallas_call(
+    def exchange(value, axis, distance):
+        size = lax.axis_size(axis)
+        return lax.ppermute(value, axis, [(i, i ^ distance) for i in range(size)])
+
+    def apply_kernel(sent):
+        got = [sent] + [exchange(sent, "row", d) for d in range(1, row_count)]
+        keep, give = pl.pallas_call(
+            functools.partial(tiles_kernel, tiles % 8),
+            out_shape=[half_grid, half_grid],
+            in_specs=[SMEM, VMEM, VMEM, ANY] + [VMEM] * row_count,
+            out_specs=[VMEM] * 2,
+            scratch_shapes=[
+                scratch((slots, LANES, LANES), BF16),
+                scratch((row_count * height, LANES)),
+                scratch((slots, LANES)),
+                scratch((slots, LANES)),
+                pltpu.SemaphoreType.DMA((slots // 16,)),
+            ],
+            compiler_params=PARAMS,
+            name="tiles",
+        )(spots, target, weight, kernel_tiles, *got)
+        both = keep + exchange(give, "col", 1)
+        return [both[0]] + [exchange(both[d], "col", 2 * d) for d in range(1, far)]
+
+    sent0 = pl.pallas_call(
         first_kernel,
-        out_shape=[grid, pltpu.VMEM((faults, width, width), BF16)],
+        out_shape=grid,
         in_specs=[SMEM, VMEM, VMEM, ANY],
-        out_specs=[VMEM, VMEM],
-        scratch_shapes=work + [pltpu.SemaphoreType.DMA((faults,))],
+        out_specs=VMEM,
+        scratch_shapes=work,
         compiler_params=PARAMS,
         name="first",
     )(fault_sizes, rhs, friction, precond_blocks)
-
-    near = pltpu.with_memory_space_constraint(
-        kernel_tiles.reshape(slots, LANES, LANES), pltpu.VMEM
-    )
-
-    def apply_kernel(sent):
-        got = [sent]
-        for d in range(1, row_count):
-            pairs = [(i, i ^ d if paired else (i + d) % row_count) for i in range(row_count)]
-            got.append(lax.ppermute(sent, "row", pairs))
-        sums = got[0][tiles]
-        for one in got[1:]:
-            sums = sums + one[tiles]
-        parts = pl.pallas_call(
-            tiles_kernel,
-            out_shape=jax.ShapeDtypeStruct((col_count, height, LANES), F32),
-            in_specs=[SMEM, VMEM, VMEM, VMEM] + [VMEM] * row_count,
-            out_specs=VMEM,
-            scratch_shapes=[
-                scratch((row_count * height, LANES)),
-                scratch((slots, LANES)),
-                scratch((slots, LANES)),
-            ],
-            compiler_params=PARAMS,
-            name="tiles",
-        )(spots, target, weight, near, *got)
-        parts = parts.at[:, tiles, :].set(sums)
-        return lax.all_to_all(parts, "col", 0, 0, tiled=True)
-
     parts0 = apply_kernel(sent0)
     sent1, image0, basis = pl.pallas_call(
         second_kernel,
         out_shape=[grid, plain, grid],
-        in_specs=[SMEM] + [VMEM] * 5,
+        in_specs=[SMEM, VMEM, VMEM, ANY] + [VMEM] * (1 + far),
         out_specs=[VMEM] * 3,
         scratch_shapes=work,
         compiler_params=PARAMS,
         name="second",
-    )(fault_sizes, rhs, friction, sent0, parts0, blocks)
+    )(fault_sizes, rhs, friction, precond_blocks, sent0, *parts0)
     parts1 = apply_kernel(sent1)
     sent2, image1 = pl.pallas_call(
         third_kernel,
         out_shape=[grid, plain],
-        in_specs=[SMEM] + [VMEM] * 6,
+        in_specs=[SMEM, VMEM, VMEM, ANY] + [VMEM] * (2 + far),
         out_specs=[VMEM] * 2,
         scratch_shapes=work,
         compiler_params=PARAMS,
         name="third",
-    )(fault_sizes, rhs, friction, sent1, parts1, basis, blocks)
+    )(fault_sizes, rhs, friction, precond_blocks, sent1, basis, *parts1)
     parts2 = apply_kernel(sent2)
     devices = row_count * col_count
     image2, sums = pl.pallas_call(
         fourth_kernel,
         out_shape=[plain, jax.ShapeDtypeStruct((devices, LANES), F32)],
-        in_specs=[VMEM] * 6,
+        in_specs=[VMEM] * (5 + far),
         out_specs=[VMEM] * 2,
         compiler_params=PARAMS,
         name="fourth",
-    )(rhs, friction, sent2, parts2, image0, image1)
+    )(rhs, friction, sent2, image0, image1, *parts2)
     sums = lax.all_to_all(sums, ("row", "col"), 0, 0, tiled=True)
     whole = jax.ShapeDtypeStruct((1, 1, length), F32)
     return pl.pallas_call(

time: 128 us -> 121 us (0.945)
  blocking collectives: 43.3 us -> 10.4 us
  local copies, waits for them, and re-layouts: 19.6 us -> 5.48 us
  starting transfers between devices: 11.5 us -> 25.1 us
  waiting for transfers between devices: 7.61 us -> 21 us
  Pallas kernels: 41.3 us -> 52.8 us
  other arithmetic: 1.83 us -> 3.89 us
    all_to_all x3 -> x0, blocking collectives: 33.3 us -> none  [apply_kernel(): return lax.all_to_all(parts, 'col', 0, 0, tiled=True)]
    ppermute x9 -> x21, starting transfers between devices: 11.5 us -> 25.1 us  [exchange(): return lax.ppermute(value, axis, [(i, i ^ distance) for i in range(size)])]
    ppermute x9 -> x21, waiting for transfers between devices: 7.61 us -> 21 us  [exchange(): return lax.ppermute(value, axis, [(i, i ^ distance) for i in range(size)])]
    unnamed x54 -> x42, local copies, waits for them, and re-layouts: 15.4 us -> 3.65 us
    pallas_call x5, Pallas kernels: 31.2 us -> 39.9 us  [the longest x3 20.9 us: apply_kernel(): pl.pallas_call(functools.partial(tiles_kernel, tiles % 8), out_shape=[hal...]
    scatter x3 -> x0, local copies, waits for them, and re-layouts: 4.18 us -> none  [apply_kernel(): parts = parts.at[:, tiles, :].set(sums)]
    add x4, other arithmetic: 1.29 us -> 3.3 us  [the longest x3 2.7 us: apply_kernel(): both = keep + exchange(give, 'col', 1)]
    squeeze x0 -> x3, local copies, waits for them, and re-layouts: none -> 1.82 us  [apply_kernel(): return [both[0]] + [exchange(both[d], 'col', 2 * d) for d in range(1, far)]]
  transfers between devices with their start and end apart: 9 -> 21, of which waited for: 8 -> 18; matrix products, arithmetic and copies ran while one was open for 1% -> 1% of each run, Pallas kernels for 0% -> 0%
where the time goes in v2:
time: 121 us; the launch traced here: 120 us
  Pallas kernels  52.8 us (44%)
  starting transfers between devices  25.1 us (21%)
  waiting for transfers between devices  21 us (17%)
  blocking collectives  10.4 us (9%)
  local copies, waits for them, and re-layouts  5.48 us (5%)
  other arithmetic  3.89 us (3%)
  between operations  1.44 us (1%)
    ppermute x21, starting transfers between devices, exchange(): return lax.ppermute(value, axis, [(i, i ^ distance) for i in range(size)])  25.1 us
    ppermute x21, waiting for transfers between devices, exchange(): return lax.ppermute(value, axis, [(i, i ^ distance) for i in range(size)])  21 us
    pallas_call x3, Pallas kernels, apply_kernel(): pl.pallas_call(functools.partial(tiles_kernel, tiles % 8), out_shape=[hal...  20.9 us
    all_to_all x1, blocking collectives, local(): sums = lax.all_to_all(sums, ('row', 'col'), 0, 0, tiled=True)  10.4 us
    pallas_call x1, Pallas kernels, local(): pl.pallas_call(second_kernel, out_shape=[grid, plain, grid], in_specs=[SM...  9.64 us
    pallas_call x1, Pallas kernels, local(): pl.pallas_call(third_kernel, out_shape=[grid, plain], in_specs=[SMEM, VME...  9.58 us
    pallas_call x1, Pallas kernels, local(): pl.pallas_call(first_kernel, out_shape=grid, in_specs=[SMEM, VMEM, VMEM,...  9.43 us
    unnamed x42, local copies, waits for them, and re-layouts  3.65 us
  transfers between devices with their start and end apart: 21, of which 18 were waited for; matrix products, arithmetic and copies ran while one was open for 1% of the time, Pallas kernels for 0%

profile of v2, /device:TPU:0, one launch (start us, length us, event | category | flops | bytes accessed | tf_op | source)
XLA Modules:
  0.0 120.2 jit_solution(2180223896143739503)
XLA Ops:
  0.7 9.4 %first.1.refs_0_.sent.sent0 = f32[40,128]{1,0:T(8,128)} custom-call(s32[1,1,24]{2,1,0:T(1,128)} %sizes.5, f32[1,1,4608]{2,1,0:T(1,128)} %rhs.9, f32[1,1,4608]{2,1,0:T(1,128)} %friction.7, bf16[1,1,24,512,512]{4,3,2,1,0:T(8,128)(2,1)} %blocks.5), custom_call_target="tpu_custom_call" | custom-call | tf_op jit(solution)/shard_map/first/pallas_call | solution.py:450
  10.1 4.0 %collective-permute-start.2 = (f32[40,128]{1,0:T(8,128)}, f32[40,128]{1,0:T(8,128)S(1)}, u32[]{:S(2)}, u32[]{:S(2)}) collective-permute-start(f32[40,128]{1,0:T(8,128)} %first.1.refs_0_.sent.sent0), channel_id=1, source_target_pairs={{0,24},{8,16},{16,8},{24,0},{1,25},{9,17},{17,9},{25,1},{2,26},{10... | collective-permute-start | bytes 61448 | tf_op jit(solution)/shard_map/ppermute | solution.py:428
  14.1 0.5 collective-permute-start.1
  14.6 0.2 collective-permute-start
  15.4 0.6 fusion.2
  16.0 0.6 compare_select_fusion.weight
  16.6 1.5 %collective-permute-done.1.refs_2_ = f32[40,128]{1,0:T(8,128)S(1)} collective-permute-done((f32[40,128]{1,0:T(8,128)}, f32[40,128]{1,0:T(8,128)S(1)}, u32[]{:S(2)}, u32[]{:S(2)}) %collective-permute-start.1) | collective-permute-done | bytes 20512 | tf_op jit(solution)/shard_map/ppermute | solution.py:428
  18.1 0.5 collective-permute-done.refs_1_
  18.6 0.1 copy-done.1
  18.7 0.5 copy-done.2
  19.2 7.0 %tiles.3 = (f32[4,40,128]{2,1,0:T(8,128)}, f32[4,40,128]{2,1,0:T(8,128)}) custom-call(s32[1,256]{1,0:T(1,128)} %get-tuple-element.40.spots, s32[1,256]{1,0:T(1,128)} %get-tuple-element.41.rows, f32[1,256]{1,0:T(1,128)} %compare_select_fusion.weight, bf16[1,1,256,128,128]{4,3,2,1,0:T(8,128)(2,1)} %remote.5, f32[40,128]{1,0:T(8,128)} %first.1.refs_0_.sent.sent0, ...), custom_call_target="tpu_custom_call" | custom-call | tf_op jit(solution)/shard_map/tiles/pallas_call | solution.py:432
  26.1 0.1 collective-permute-start.3
  26.2 1.5 %collective-permute-done.3 = f32[4,40,128]{2,1,0:T(8,128)S(1)} collective-permute-done((f32[4,40,128]{2,1,0:T(8,128)}, f32[4,40,128]{2,1,0:T(8,128)S(1)}, u32[]{:S(2)}, u32[]{:S(2)}) %collective-permute-start.3) | collective-permute-done | bytes 81952 | tf_op jit(solution)/shard_map/ppermute | solution.py:428
  27.7 0.9 add.104
  28.6 0.6 slice_bitcast_fusion.8
  29.2 3.2 %collective-permute-start.6 = (f32[40,128]{1,0:T(8,128)S(1)}, f32[40,128]{1,0:T(8,128)S(1)}, u32[]{:S(2)}, u32[]{:S(2)}) collective-permute-start(f32[40,128]{1,0:T(8,128)S(1)} %get-tuple-element.36), channel_id=1, source_target_pairs={{0,6},{1,7},{2,4},{3,5},{4,2},{5,3},{6,0},{7,1},{8,14},{9,15},{10,... | collective-permute-start | bytes 61448 | tf_op jit(solution)/shard_map/ppermute | solution.py:428
  32.4 1.2 %collective-permute-start.4 = (f32[40,128]{1,0:T(8,128)S(1)}, f32[40,128]{1,0:T(8,128)S(1)}, u32[]{:S(2)}, u32[]{:S(2)}) collective-permute-start(f32[40,128]{1,0:T(8,128)S(1)} %get-tuple-element.38), channel_id=1, source_target_pairs={{0,2},{1,3},{2,0},{3,1},{4,6},{5,7},{6,4},{7,5},{8,10},{9,11},{10,... | collective-permute-start | bytes 61448 | tf_op jit(solution)/shard_map/ppermute | solution.py:428
  33.6 1.2 collective-permute-done.6.refs_3_
  34.8 2.3 %collective-permute-done.5.refs_2_ = f32[40,128]{1,0:T(8,128)S(1)} collective-permute-done((f32[40,128]{1,0:T(8,128)S(1)}, f32[40,128]{1,0:T(8,128)S(1)}, u32[]{:S(2)}, u32[]{:S(2)}) %collective-permute-start.5) | collective-permute-done | bytes 20512 | tf_op jit(solution)/shard_map/ppermute | solution.py:428
  37.1 0.6 copy-done.11
  37.7 9.6 %second.1 = (f32[40,128]{1,0:T(8,128)}, f32[36,128]{1,0:T(8,128)}, f32[40,128]{1,0:T(8,128)}) custom-call(s32[1,1,24]{2,1,0:T(1,128)} %sizes.5, f32[1,1,4608]{2,1,0:T(1,128)} %rhs.9, f32[1,1,4608]{2,1,0:T(1,128)} %friction.7, bf16[1,1,24,512,512]{4,3,2,1,0:T(8,128)(2,1)} %blocks.5, f32[40,128]{1,0:T(8,128)} %first.1.refs_0_.sent.sent0, ...), custom_call_target="tpu_custom_call" | custom-call | tf_op jit(solution)/shard_map/second/pallas_call | solution.py:460
  47.3 1.7 %collective-permute-start.9 = (f32[40,128]{1,0:T(8,128)}, f32[40,128]{1,0:T(8,128)S(1)}, u32[]{:S(2)}, u32[]{:S(2)}) collective-permute-start(f32[40,128]{1,0:T(8,128)} %get-tuple-element.17.refs_0_.sent.sent1), channel_id=1, source_target_pairs={{0,24},{8,16},{16,8},{24,0},{1,25},{9,17},{17,9},{25,1},{2,26},{10... | collective-permute-start | bytes 61448 | tf_op jit(solution)/shard_map/ppermute | solution.py:428
  49.0 0.8 collective-permute-start.8
  49.8 1.1 collective-permute-start.7
  50.9 1.4 %collective-permute-done.9.refs_3_ = f32[40,128]{1,0:T(8,128)S(1)} collective-permute-done((f32[40,128]{1,0:T(8,128)}, f32[40,128]{1,0:T(8,128)S(1)}, u32[]{:S(2)}, u32[]{:S(2)}) %collective-permute-start.9) | collective-permute-done | bytes 20512 | tf_op jit(solution)/shard_map/ppermute | solution.py:428
  52.3 0.7 collective-permute-done.8.refs_2_
  53.0 0.8 collective-permute-done.7.refs_1_
  53.8 0.6 copy-done.8
  54.4 7.0 %tiles.4 = (f32[4,40,128]{2,1,0:T(8,128)}, f32[4,40,128]{2,1,0:T(8,128)}) custom-call(s32[1,256]{1,0:T(1,128)} %get-tuple-element.40.spots, s32[1,256]{1,0:T(1,128)} %get-tuple-element.41.rows, f32[1,256]{1,0:T(1,128)} %compare_select_fusion.weight, bf16[1,1,256,128,128]{4,3,2,1,0:T(8,128)(2,1)} %remote.5, f32[40,128]{1,0:T(8,128)} %get-tuple-element.17.refs_0_.sent.sent1, ...), custom_call_target="tpu_custom_call" | custom-call | tf_op jit(solution)/shard_map/tiles/pallas_call | solution.py:432
  61.4 0.1 collective-permute-start.10
  61.5 1.5 %collective-permute-done.10 = f32[4,40,128]{2,1,0:T(8,128)S(1)} collective-permute-done((f32[4,40,128]{2,1,0:T(8,128)}, f32[4,40,128]{2,1,0:T(8,128)S(1)}, u32[]{:S(2)}, u32[]{:S(2)}) %collective-permute-start.10) | collective-permute-done | bytes 81952 | tf_op jit(solution)/shard_map/ppermute | solution.py:428
  63.0 0.9 add.105
  63.9 0.6 slice_bitcast_fusion.4
  64.5 1.2 %collective-permute-start.13 = (f32[40,128]{1,0:T(8,128)S(1)}, f32[40,128]{1,0:T(8,128)S(1)}, u32[]{:S(2)}, u32[]{:S(2)}) collective-permute-start(f32[40,128]{1,0:T(8,128)S(1)} %get-tuple-element.32), channel_id=1, source_target_pairs={{0,6},{1,7},{2,4},{3,5},{4,2},{5,3},{6,0},{7,1},{8,14},{9,15},{10,... | collective-permute-start | bytes 61448 | tf_op jit(solution)/shard_map/ppermute | solution.py:428
  65.7 0.7 collective-permute-start.12
  66.4 2.5 %collective-permute-start.11 = (f32[40,128]{1,0:T(8,128)S(1)}, f32[40,128]{1,0:T(8,128)S(1)}, u32[]{:S(2)}, u32[]{:S(2)}) collective-permute-start(f32[40,128]{1,0:T(8,128)S(1)} %get-tuple-element.34), channel_id=1, source_target_pairs={{0,2},{1,3},{2,0},{3,1},{4,6},{5,7},{6,4},{7,5},{8,10},{9,11},{10,... | collective-permute-start | bytes 61448 | tf_op jit(solution)/shard_map/ppermute | solution.py:428
  68.9 1.3 %collective-permute-done.13.refs_3_ = f32[40,128]{1,0:T(8,128)S(1)} collective-permute-done((f32[40,128]{1,0:T(8,128)S(1)}, f32[40,128]{1,0:T(8,128)S(1)}, u32[]{:S(2)}, u32[]{:S(2)}) %collective-permute-start.13) | collective-permute-done | bytes 20512 | tf_op jit(solution)/shard_map/ppermute | solution.py:428
  70.2 0.2 collective-permute-done.12.refs_2_
  70.4 0.2 collective-permute-done.11.refs_1_
  70.7 0.2 copy-done.10
  70.8 0.2 copy-done.12
  71.0 0.2 copy-done.14
  71.3 9.6 %third.1 = (f32[40,128]{1,0:T(8,128)}, f32[36,128]{1,0:T(8,128)}) custom-call(s32[1,1,24]{2,1,0:T(1,128)} %sizes.5, f32[1,1,4608]{2,1,0:T(1,128)} %rhs.9, f32[1,1,4608]{2,1,0:T(1,128)} %friction.7, bf16[1,1,24,512,512]{4,3,2,1,0:T(8,128)(2,1)} %blocks.5, f32[40,128]{1,0:T(8,128)} %get-tuple-element.17.refs_0_.sent.sent1, f32[40,128]{1,0:T(8,128)} %get-tuple-element.18.basis, ...), custom_call_target="tpu_custom_call" | custom-call | tf_op jit(solution)/shard_map/third/pallas_call | solution.py:470
  80.8 2.6 %collective-permute-start.16 = (f32[40,128]{1,0:T(8,128)}, f32[40,128]{1,0:T(8,128)S(1)}, u32[]{:S(2)}, u32[]{:S(2)}) collective-permute-start(f32[40,128]{1,0:T(8,128)} %get-tuple-element.21.refs_0_.sent.sent2), channel_id=1, source_target_pairs={{0,24},{8,16},{16,8},{24,0},{1,25},{9,17},{17,9},{25,1},{2,26},{10... | collective-permute-start | bytes 61448 | tf_op jit(solution)/shard_map/ppermute | solution.py:428
  83.4 0.6 collective-permute-start.15
  84.0 0.4 collective-permute-start.14
  84.4 1.4 %collective-permute-done.16.refs_3_ = f32[40,128]{1,0:T(8,128)S(1)} collective-permute-done((f32[40,128]{1,0:T(8,128)}, f32[40,128]{1,0:T(8,128)S(1)}, u32[]{:S(2)}, u32[]{:S(2)}) %collective-permute-start.16) | collective-permute-done | bytes 20512 | tf_op jit(solution)/shard_map/ppermute | solution.py:428
  85.8 1.6 %collective-permute-done.15.refs_2_ = f32[40,128]{1,0:T(8,128)S(1)} collective-permute-done((f32[40,128]{1,0:T(8,128)}, f32[40,128]{1,0:T(8,128)S(1)}, u32[]{:S(2)}, u32[]{:S(2)}) %collective-permute-start.15) | collective-permute-done | bytes 20512 | tf_op jit(solution)/shard_map/ppermute | solution.py:428
  87.4 0.6 collective-permute-done.14.refs_1_
  88.0 0.6 copy-done.7
  88.6 7.0 %tiles.5 = (f32[4,40,128]{2,1,0:T(8,128)}, f32[4,40,128]{2,1,0:T(8,128)}) custom-call(s32[1,256]{1,0:T(1,128)} %get-tuple-element.40.spots, s32[1,256]{1,0:T(1,128)} %get-tuple-element.41.rows, f32[1,256]{1,0:T(1,128)} %compare_select_fusion.weight, bf16[1,1,256,128,128]{4,3,2,1,0:T(8,128)(2,1)} %remote.5, f32[40,128]{1,0:T(8,128)} %get-tuple-element.21.refs_0_.sent.sent2, ...), custom_call_target="tpu_custom_call" | custom-call | tf_op jit(solution)/shard_map/tiles/pallas_call | solution.py:432
  95.6 0.1 collective-permute-start.17
  95.7 1.5 %collective-permute-done.17 = f32[4,40,128]{2,1,0:T(8,128)S(1)} collective-permute-done((f32[4,40,128]{2,1,0:T(8,128)}, f32[4,40,128]{2,1,0:T(8,128)S(1)}, u32[]{:S(2)}, u32[]{:S(2)}) %collective-permute-start.17) | collective-permute-done | bytes 81952 | tf_op jit(solution)/shard_map/ppermute | solution.py:428
  97.2 0.9 add.106
  98.1 0.6 slice_bitcast_fusion
  98.7 2.6 %collective-permute-start.20 = (f32[40,128]{1,0:T(8,128)S(1)}, f32[40,128]{1,0:T(8,128)S(1)}, u32[]{:S(2)}, u32[]{:S(2)}) collective-permute-start(f32[40,128]{1,0:T(8,128)S(1)} %get-tuple-element.28), channel_id=1, source_target_pairs={{0,6},{1,7},{2,4},{3,5},{4,2},{5,3},{6,0},{7,1},{8,14},{9,15},{10,... | collective-permute-start | bytes 61448 | tf_op jit(solution)/shard_map/ppermute | solution.py:428
  101.2 0.6 collective-permute-start.19
  101.8 1.2 %collective-permute-start.18 = (f32[40,128]{1,0:T(8,128)S(1)}, f32[40,128]{1,0:T(8,128)S(1)}, u32[]{:S(2)}, u32[]{:S(2)}) collective-permute-start(f32[40,128]{1,0:T(8,128)S(1)} %get-tuple-element.30), channel_id=1, source_target_pairs={{0,2},{1,3},{2,0},{3,1},{4,6},{5,7},{6,4},{7,5},{8,10},{9,11},{10,... | collective-permute-start | bytes 61448 | tf_op jit(solution)/shard_map/ppermute | solution.py:428
  103.1 1.3 %collective-permute-done.20.refs_3_ = f32[40,128]{1,0:T(8,128)S(1)} collective-permute-done((f32[40,128]{1,0:T(8,128)S(1)}, f32[40,128]{1,0:T(8,128)S(1)}, u32[]{:S(2)}, u32[]{:S(2)}) %collective-permute-start.20) | collective-permute-done | bytes 20512 | tf_op jit(solution)/shard_map/ppermute | solution.py:428
  104.4 1.6 %collective-permute-done.19.refs_2_ = f32[40,128]{1,0:T(8,128)S(1)} collective-permute-done((f32[40,128]{1,0:T(8,128)S(1)}, f32[40,128]{1,0:T(8,128)S(1)}, u32[]{:S(2)}, u32[]{:S(2)}) %collective-permute-start.19) | collective-permute-done | bytes 20512 | tf_op jit(solution)/shard_map/ppermute | solution.py:428
  105.9 0.6 copy-done.16
  106.5 1.6 %fourth.1 = (f32[36,128]{1,0:T(8,128)}, f32[32,128]{1,0:T(8,128)}) custom-call(f32[1,1,4608]{2,1,0:T(1,128)} %rhs.9, f32[1,1,4608]{2,1,0:T(1,128)} %friction.7, f32[40,128]{1,0:T(8,128)} %get-tuple-element.21.refs_0_.sent.sent2, f32[36,128]{1,0:T(8,128)} %get-tuple-element.22.image0, f32[36,128]{1,0:T(8,128)} %get-tuple-element.23.image1, ...), custom_call_target="tpu_custom_call" | custom-call | tf_op jit(solution)/shard_map/fourth/pallas_call | solution.py:481
  108.1 10.4 %all_to_all.11 = f32[32,1,128]{2,1,0:T(1,128)} all-to-all(f32[32,1,128]{2,1,0:T(1,128)} %bitcast.63), channel_id=1, replica_groups=mesh['row'=4,'col'=8] {'row','col'}, dimensions={0} | all-to-all | bytes 32768 | tf_op jit(solution)/shard_map/all_to_all | solution.py:489
  118.6 1.6 %last.1 = (f32[1,1,4608]{2,1,0:T(1,128)}, f32[1,1,4608]{2,1,0:T(1,128)}) custom-call(f32[32,128]{1,0:T(8,128)} %bitcast.62, f32[1,1,4608]{2,1,0:T(1,128)} %rhs.9, f32[36,128]{1,0:T(8,128)} %get-tuple-element.22.image0, f32[36,128]{1,0:T(8,128)} %get-tuple-element.23.image1, f32[36,128]{1,0:T(8,128)} %get-tuple-element.27.image2, ...), custom_call_target="tpu_custom_call" | custom-call | tf_op jit(solution)/shard_map/last/pallas_call | solution.py:491
  (37 shorter events, 0.1 us)
Async XLA Ops:
  0.6 14.7 %copy-start.18 = (s32[1,1,256]{2,1,0:T(1,128)S(1)}, s32[1,1,256]{2,1,0:T(1,128)}, u32[]{:S(2)}) copy-start(s32[1,1,256]{2,1,0:T(1,128)} %param.14) | copy-start | bytes 3076
  0.6 14.7 %copy-start.19 = (s32[1,1,256]{2,1,0:T(1,128)S(1)}, s32[1,1,256]{2,1,0:T(1,128)}, u32[]{:S(2)}) copy-start(s32[1,1,256]{2,1,0:T(1,128)} %param.13) | copy-start | bytes 3076
  0.7 15.3 %copy-start.20 = (f32[1,1,256]{2,1,0:T(1,128)S(1)}, f32[1,1,256]{2,1,0:T(1,128)}, u32[]{:S(2)}) copy-start(f32[1,1,256]{2,1,0:T(1,128)} %param.12) | copy-start | bytes 3076
  10.1 6.5 %collective-permute-start.2 = (f32[40,128]{1,0:T(8,128)}, f32[40,128]{1,0:T(8,128)S(1)}, u32[]{:S(2)}, u32[]{:S(2)}) collective-permute-start(f32[40,128]{1,0:T(8,128)} %first.1.refs_0_.sent.sent0), channel_id=1, source_target_pairs={{0,24},{8,16},{16,8},{24,0},{1,25},{9,17},{17,9},{25,1},{2,26},{10... | collective-permute-start | bytes 61448 | tf_op jit(solution)/shard_map/ppermute | solution.py:428
  14.1 4.0 %collective-permute-start.1 = (f32[40,128]{1,0:T(8,128)}, f32[40,128]{1,0:T(8,128)S(1)}, u32[]{:S(2)}, u32[]{:S(2)}) collective-permute-start(f32[40,128]{1,0:T(8,128)} %first.1.refs_0_.sent.sent0), channel_id=1, source_target_pairs={{0,16},{8,24},{16,0},{24,8},{1,17},{9,25},{17,1},{25,9},{2,18},{10... | collective-permute-start | bytes 61448 | tf_op jit(solution)/shard_map/ppermute | solution.py:428
  14.6 4.0 %collective-permute-start = (f32[40,128]{1,0:T(8,128)}, f32[40,128]{1,0:T(8,128)S(1)}, u32[]{:S(2)}, u32[]{:S(2)}) collective-permute-start(f32[40,128]{1,0:T(8,128)} %first.1.refs_0_.sent.sent0), channel_id=1, source_target_pairs={{0,8},{8,0},{16,24},{24,16},{1,9},{9,1},{17,25},{25,17},{2,10},{10... | collective-permute-start | bytes 61448 | tf_op jit(solution)/shard_map/ppermute | solution.py:428
  16.6 2.0 %copy-start = (f32[40,128]{1,0:T(8,128)}, f32[40,128]{1,0:T(8,128)S(1)}, u32[]{:S(2)}) copy-start(f32[40,128]{1,0:T(8,128)S(1)} %collective-permute-done.2.refs_3_) | copy-start | bytes 61444
  18.1 0.6 copy-start.1
  18.6 0.6 copy-start.2
  26.1 1.6 %collective-permute-start.3 = (f32[4,40,128]{2,1,0:T(8,128)}, f32[4,40,128]{2,1,0:T(8,128)S(1)}, u32[]{:S(2)}, u32[]{:S(2)}) collective-permute-start(f32[4,40,128]{2,1,0:T(8,128)} %get-tuple-element.16), channel_id=1, source_target_pairs={{0,1},{1,0},{2,3},{3,2},{4,5},{5,4},{6,7},{7,6},{8,9},{9,8},{10,11... | collective-permute-start | bytes 245768 | tf_op jit(solution)/shard_map/ppermute | solution.py:428
  29.2 5.6 %collective-permute-start.6 = (f32[40,128]{1,0:T(8,128)S(1)}, f32[40,128]{1,0:T(8,128)S(1)}, u32[]{:S(2)}, u32[]{:S(2)}) collective-permute-start(f32[40,128]{1,0:T(8,128)S(1)} %get-tuple-element.36), channel_id=1, source_target_pairs={{0,6},{1,7},{2,4},{3,5},{4,2},{5,3},{6,0},{7,1},{8,14},{9,15},{10,... | collective-permute-start | bytes 61448 | tf_op jit(solution)/shard_map/ppermute | solution.py:428
  32.4 4.7 %collective-permute-start.5 = (f32[40,128]{1,0:T(8,128)S(1)}, f32[40,128]{1,0:T(8,128)S(1)}, u32[]{:S(2)}, u32[]{:S(2)}) collective-permute-start(f32[40,128]{1,0:T(8,128)S(1)} %get-tuple-element.37), channel_id=1, source_target_pairs={{0,4},{1,5},{2,6},{3,7},{4,0},{5,1},{6,2},{7,3},{8,12},{9,13},{10,... | collective-permute-start | bytes 61448 | tf_op jit(solution)/shard_map/ppermute | solution.py:428
  32.4 4.7 %collective-permute-start.4 = (f32[40,128]{1,0:T(8,128)S(1)}, f32[40,128]{1,0:T(8,128)S(1)}, u32[]{:S(2)}, u32[]{:S(2)}) collective-permute-start(f32[40,128]{1,0:T(8,128)S(1)} %get-tuple-element.38), channel_id=1, source_target_pairs={{0,2},{1,3},{2,0},{3,1},{4,6},{5,7},{6,4},{7,5},{8,10},{9,11},{10,... | collective-permute-start | bytes 61448 | tf_op jit(solution)/shard_map/ppermute | solution.py:428
  34.8 2.3 %copy-start.9 = (f32[40,128]{1,0:T(8,128)}, f32[40,128]{1,0:T(8,128)S(1)}, u32[]{:S(2)}) copy-start(f32[40,128]{1,0:T(8,128)S(1)} %collective-permute-done.6.refs_3_) | copy-start | bytes 61444
  37.0 0.6 copy-start.11
  37.1 0.6 copy-start.13
  47.3 5.0 %collective-permute-start.9 = (f32[40,128]{1,0:T(8,128)}, f32[40,128]{1,0:T(8,128)S(1)}, u32[]{:S(2)}, u32[]{:S(2)}) collective-permute-start(f32[40,128]{1,0:T(8,128)} %get-tuple-element.17.refs_0_.sent.sent1), channel_id=1, source_target_pairs={{0,24},{8,16},{16,8},{24,0},{1,25},{9,17},{17,9},{25,1},{2,26},{10... | collective-permute-start | bytes 61448 | tf_op jit(solution)/shard_map/ppermute | solution.py:428
  49.0 4.0 %collective-permute-start.8 = (f32[40,128]{1,0:T(8,128)}, f32[40,128]{1,0:T(8,128)S(1)}, u32[]{:S(2)}, u32[]{:S(2)}) collective-permute-start(f32[40,128]{1,0:T(8,128)} %get-tuple-element.17.refs_0_.sent.sent1), channel_id=1, source_target_pairs={{0,16},{8,24},{16,0},{24,8},{1,17},{9,25},{17,1},{25,9},{2,18},{10... | collective-permute-start | bytes 61448 | tf_op jit(solution)/shard_map/ppermute | solution.py:428
  49.8 4.0 %collective-permute-start.7 = (f32[40,128]{1,0:T(8,128)}, f32[40,128]{1,0:T(8,128)S(1)}, u32[]{:S(2)}, u32[]{:S(2)}) collective-permute-start(f32[40,128]{1,0:T(8,128)} %get-tuple-element.17.refs_0_.sent.sent1), channel_id=1, source_target_pairs={{0,8},{8,0},{16,24},{24,16},{1,9},{9,1},{17,25},{25,17},{2,10},{10... | collective-permute-start | bytes 61448 | tf_op jit(solution)/shard_map/ppermute | solution.py:428
  52.3 1.6 %copy-start.4 = (f32[40,128]{1,0:T(8,128)}, f32[40,128]{1,0:T(8,128)S(1)}, u32[]{:S(2)}) copy-start(f32[40,128]{1,0:T(8,128)S(1)} %collective-permute-done.9.refs_3_) | copy-start | bytes 61444
  53.0 0.8 copy-start.6
  53.8 0.6 copy-start.8
  61.4 1.6 %collective-permute-start.10 = (f32[4,40,128]{2,1,0:T(8,128)}, f32[4,40,128]{2,1,0:T(8,128)S(1)}, u32[]{:S(2)}, u32[]{:S(2)}) collective-permute-start(f32[4,40,128]{2,1,0:T(8,128)} %get-tuple-element.20), channel_id=1, source_target_pairs={{0,1},{1,0},{2,3},{3,2},{4,5},{5,4},{6,7},{7,6},{8,9},{9,8},{10,11... | collective-permute-start | bytes 245768 | tf_op jit(solution)/shard_map/ppermute | solution.py:428
  64.5 5.7 %collective-permute-start.13 = (f32[40,128]{1,0:T(8,128)S(1)}, f32[40,128]{1,0:T(8,128)S(1)}, u32[]{:S(2)}, u32[]{:S(2)}) collective-permute-start(f32[40,128]{1,0:T(8,128)S(1)} %get-tuple-element.32), channel_id=1, source_target_pairs={{0,6},{1,7},{2,4},{3,5},{4,2},{5,3},{6,0},{7,1},{8,14},{9,15},{10,... | collective-permute-start | bytes 61448 | tf_op jit(solution)/shard_map/ppermute | solution.py:428
  65.7 4.7 %collective-permute-start.12 = (f32[40,128]{1,0:T(8,128)S(1)}, f32[40,128]{1,0:T(8,128)S(1)}, u32[]{:S(2)}, u32[]{:S(2)}) collective-permute-start(f32[40,128]{1,0:T(8,128)S(1)} %get-tuple-element.33), channel_id=1, source_target_pairs={{0,4},{1,5},{2,6},{3,7},{4,0},{5,1},{6,2},{7,3},{8,12},{9,13},{10,... | collective-permute-start | bytes 61448 | tf_op jit(solution)/shard_map/ppermute | solution.py:428
  66.4 4.2 %collective-permute-start.11 = (f32[40,128]{1,0:T(8,128)S(1)}, f32[40,128]{1,0:T(8,128)S(1)}, u32[]{:S(2)}, u32[]{:S(2)}) collective-permute-start(f32[40,128]{1,0:T(8,128)S(1)} %get-tuple-element.34), channel_id=1, source_target_pairs={{0,2},{1,3},{2,0},{3,1},{4,6},{5,7},{6,4},{7,5},{8,10},{9,11},{10,... | collective-permute-start | bytes 61448 | tf_op jit(solution)/shard_map/ppermute | solution.py:428
  70.2 0.6 copy-start.10
  70.4 0.6 copy-start.12
  70.7 0.6 copy-start.14
  80.8 5.0 %collective-permute-start.16 = (f32[40,128]{1,0:T(8,128)}, f32[40,128]{1,0:T(8,128)S(1)}, u32[]{:S(2)}, u32[]{:S(2)}) collective-permute-start(f32[40,128]{1,0:T(8,128)} %get-tuple-element.21.refs_0_.sent.sent2), channel_id=1, source_target_pairs={{0,24},{8,16},{16,8},{24,0},{1,25},{9,17},{17,9},{25,1},{2,26},{10... | collective-permute-start | bytes 61448 | tf_op jit(solution)/shard_map/ppermute | solution.py:428
  83.4 4.0 %collective-permute-start.15 = (f32[40,128]{1,0:T(8,128)}, f32[40,128]{1,0:T(8,128)S(1)}, u32[]{:S(2)}, u32[]{:S(2)}) collective-permute-start(f32[40,128]{1,0:T(8,128)} %get-tuple-element.21.refs_0_.sent.sent2), channel_id=1, source_target_pairs={{0,16},{8,24},{16,0},{24,8},{1,17},{9,25},{17,1},{25,9},{2,18},{10... | collective-permute-start | bytes 61448 | tf_op jit(solution)/shard_map/ppermute | solution.py:428
  84.0 4.0 %collective-permute-start.14 = (f32[40,128]{1,0:T(8,128)}, f32[40,128]{1,0:T(8,128)S(1)}, u32[]{:S(2)}, u32[]{:S(2)}) collective-permute-start(f32[40,128]{1,0:T(8,128)} %get-tuple-element.21.refs_0_.sent.sent2), channel_id=1, source_target_pairs={{0,8},{8,0},{16,24},{24,16},{1,9},{9,1},{17,25},{25,17},{2,10},{10... | collective-permute-start | bytes 61448 | tf_op jit(solution)/shard_map/ppermute | solution.py:428
  85.8 2.2 %copy-start.3 = (f32[40,128]{1,0:T(8,128)}, f32[40,128]{1,0:T(8,128)S(1)}, u32[]{:S(2)}) copy-start(f32[40,128]{1,0:T(8,128)S(1)} %collective-permute-done.16.refs_3_) | copy-start | bytes 61444
  87.4 0.6 copy-start.5
  88.0 0.6 copy-start.7
  95.6 1.6 %collective-permute-start.17 = (f32[4,40,128]{2,1,0:T(8,128)}, f32[4,40,128]{2,1,0:T(8,128)S(1)}, u32[]{:S(2)}, u32[]{:S(2)}) collective-permute-start(f32[4,40,128]{2,1,0:T(8,128)} %get-tuple-element.25), channel_id=1, source_target_pairs={{0,1},{1,0},{2,3},{3,2},{4,5},{5,4},{6,7},{7,6},{8,9},{9,8},{10,11... | collective-permute-start | bytes 245768 | tf_op jit(solution)/shard_map/ppermute | solution.py:428
  98.7 5.7 %collective-permute-start.20 = (f32[40,128]{1,0:T(8,128)S(1)}, f32[40,128]{1,0:T(8,128)S(1)}, u32[]{:S(2)}, u32[]{:S(2)}) collective-permute-start(f32[40,128]{1,0:T(8,128)S(1)} %get-tuple-element.28), channel_id=1, source_target_pairs={{0,6},{1,7},{2,4},{3,5},{4,2},{5,3},{6,0},{7,1},{8,14},{9,15},{10,... | collective-permute-start | bytes 61448 | tf_op jit(solution)/shard_map/ppermute | solution.py:428
  101.2 4.7 %collective-permute-start.19 = (f32[40,128]{1,0:T(8,128)S(1)}, f32[40,128]{1,0:T(8,128)S(1)}, u32[]{:S(2)}, u32[]{:S(2)}) collective-permute-start(f32[40,128]{1,0:T(8,128)S(1)} %get-tuple-element.29), channel_id=1, source_target_pairs={{0,4},{1,5},{2,6},{3,7},{4,0},{5,1},{6,2},{7,3},{8,12},{9,13},{10,... | collective-permute-start | bytes 61448 | tf_op jit(solution)/shard_map/ppermute | solution.py:428
  101.8 4.1 %collective-permute-start.18 = (f32[40,128]{1,0:T(8,128)S(1)}, f32[40,128]{1,0:T(8,128)S(1)}, u32[]{:S(2)}, u32[]{:S(2)}) collective-permute-start(f32[40,128]{1,0:T(8,128)S(1)} %get-tuple-element.30), channel_id=1, source_target_pairs={{0,2},{1,3},{2,0},{3,1},{4,6},{5,7},{6,4},{7,5},{8,10},{9,11},{10,... | collective-permute-start | bytes 61448 | tf_op jit(solution)/shard_map/ppermute | solution.py:428
  104.4 1.6 %copy-start.15 = (f32[40,128]{1,0:T(8,128)}, f32[40,128]{1,0:T(8,128)S(1)}, u32[]{:S(2)}) copy-start(f32[40,128]{1,0:T(8,128)S(1)} %collective-permute-done.20.refs_3_) | copy-start | bytes 61444
  105.9 0.6 copy-start.16
  105.9 0.6 copy-start.17

commit v3 on v2

--- a/solution.py
+++ b/solution.py
@@ -9,12 +9,13 @@
 
 LANES = 128
 UNROLL = 3
+AHEAD = 6
 F32 = jnp.float32
 BF16 = jnp.bfloat16
 VMEM = pl.BlockSpec(memory_space=pltpu.VMEM)
 SMEM = pl.BlockSpec(memory_space=pltpu.SMEM)
-ANY = pl.BlockSpec(memory_space=pl.ANY)
-PARAMS = pltpu.CompilerParams(vmem_limit_bytes=54 << 20)
+HBM = pl.BlockSpec(memory_space=pltpu.HBM)
+PARAMS = pltpu.CompilerParams(vmem_limit_bytes=24 << 20)
 
 
 def dot_nt(left, right):
@@ -66,18 +67,27 @@
         copy = pltpu.make_async_copy(
             remote.at[0, 0, f, pl.ds(0, need)], blocks.at[f, pl.ds(0, need)], sems.at[f]
         )
+        copies.append(copy)
+    for copy in copies[:AHEAD]:
         copy.start()
-        copies.append(copy)
     return copies
 
 
-def precondition(sizes, remote, field, work):
+def await_copy(copies, place):
+    copies[place].wait()
+    if place + AHEAD < len(copies):
+        copies[place + AHEAD].start()
+
+
+def precondition(sizes, remote, field, work, begin=None):
     blocks, windows, shifts, lens, stack, lefts, found, large, sems = work
     faults = remote.shape[2]
     chunks = blocks.shape[1] // LANES
     rows = field.shape[0]
     scalars = fault_scalars(sizes, faults)
     copies = fetch(scalars, remote, blocks, sems)
+    if begin is not None:
+        begin()
     lane = lax.broadcasted_iota(jnp.int32, (faults, LANES), 1)
     for f, (tile, shift, size) in enumerate(scalars):
         shifts[f : f + 1, :] = jnp.full((1, LANES), shift, jnp.int32)
@@ -111,7 +121,7 @@
         sums = [jnp.zeros((8, LANES), F32) for _ in range(chunk_half)]
         for place in range(8):
             f = group * 8 + place
-            copies[f].wait()
+            await_copy(copies, f)
             result = dot_nt(left[:, :half], blocks[f, :half, :half])
             result = result[:8] + result[8:]
             for k in range(chunk_half):
@@ -181,11 +191,21 @@
     field[tiles:, :] = jnp.zeros((field.shape[0] - tiles, LANES), F32)
 
 
-def first_kernel(sizes, rhs, friction, blocks, send, field, *work):
+def first_kernel(far_sizes, far_rhs, far_friction, blocks, send, sizes, rhs, friction, sems, field, *work):
     tiles = rhs.shape[2] // LANES
-    value = load_rows(rhs, tiles)
-    set_field(field, value)
-    direction = precondition(sizes, blocks, field, work)[0:tiles]
+    pairs = [(far_sizes, sizes), (far_rhs, rhs), (far_friction, friction)]
+    copies = [pltpu.make_async_copy(a, b, sems.at[i]) for i, (a, b) in enumerate(pairs)]
+    for copy in copies:
+        copy.start()
+    copies[0].wait()
+
+    def value_to_field():
+        copies[1].wait()
+        set_field(field, load_rows(rhs, tiles))
+
+    direction = precondition(sizes, blocks, field, work, value_to_field)[0:tiles]
+    copies[2].wait()
+    value = field[0:tiles, :]
     scaled = load_rows(friction, tiles) * direction
     send[...] = jnp.zeros_like(send)
     send[0:tiles, :] = direction
@@ -316,8 +336,9 @@
             blocks.at[pl.ds(group * 16, 16)],
             sems.at[group],
         )
+        copies.append(copy)
+    for copy in copies[:AHEAD]:
         copy.start()
-        copies.append(copy)
     for k, one in enumerate(sent):
         field[k * height : (k + 1) * height, :] = one[...]
     for t in range(slots):
@@ -325,7 +346,7 @@
     sub = lax.broadcasted_iota(jnp.int32, (8, LANES), 0)
     blank = jnp.zeros((8, LANES), F32)
     for group in range(groups):
-        copies[group].wait()
+        await_copy(copies, group)
         base = group * 16
         top = jnp.concatenate([found[base : base + 8, :], blank], axis=1)
         bottom = jnp.concatenate([blank, found[base + 8 : base + 16, :]], axis=1)
@@ -407,6 +428,8 @@
         jnp.arange(slots, dtype=jnp.int32) < tile_counts[0, 0], tile_scale[0, 0], 0.0
     ).reshape(1, slots)
 
+    kernel_tiles = pltpu.with_memory_space_constraint(kernel_tiles, pltpu.HBM)
+    precond_blocks = pltpu.with_memory_space_constraint(precond_blocks, pltpu.HBM)
     grid = jax.ShapeDtypeStruct((height, LANES), F32)
     plain = jax.ShapeDtypeStruct((tiles, LANES), F32)
     half_grid = jax.ShapeDtypeStruct((far, height, LANES), F32)
@@ -432,7 +455,7 @@
         keep, give = pl.pallas_call(
             functools.partial(tiles_kernel, tiles % 8),
             out_shape=[half_grid, half_grid],
-            in_specs=[SMEM, VMEM, VMEM, ANY] + [VMEM] * row_count,
+            in_specs=[SMEM, VMEM, VMEM, HBM] + [VMEM] * row_count,
             out_specs=[VMEM] * 2,
             scratch_shapes=[
                 scratch((slots, LANES, LANES), BF16),
@@ -450,17 +473,23 @@
     sent0 = pl.pallas_call(
         first_kernel,
         out_shape=grid,
-        in_specs=[SMEM, VMEM, VMEM, ANY],
+        in_specs=[HBM] * 4,
         out_specs=VMEM,
-        scratch_shapes=work,
+        scratch_shapes=[
+            pltpu.SMEM(fault_sizes.shape, jnp.int32),
+            scratch(rhs.shape),
+            scratch(friction.shape),
+            pltpu.SemaphoreType.DMA((3,)),
+        ]
+        + work,
         compiler_params=PARAMS,
         name="first",
-    )(fault_sizes, rhs, friction, precond_blocks)
+    )(*[pltpu.with_memory_space_constraint(a, pltpu.HBM) for a in (fault_sizes, rhs, friction)], precond_blocks)
     parts0 = apply_kernel(sent0)
     sent1, image0, basis = pl.pallas_call(
         second_kernel,
         out_shape=[grid, plain, grid],
-        in_specs=[SMEM, VMEM, VMEM, ANY] + [VMEM] * (1 + far),
+        in_specs=[SMEM, VMEM, VMEM, HBM] + [VMEM] * (1 + far),
         out_specs=[VMEM] * 3,
         scratch_shapes=work,
         compiler_params=PARAMS,
@@ -470,7 +499,7 @@
     sent2, image1 = pl.pallas_call(
         third_kernel,
         out_shape=[grid, plain],
-        in_specs=[SMEM, VMEM, VMEM, ANY] + [VMEM] * (2 + far),
+        in_specs=[SMEM, VMEM, VMEM, HBM] + [VMEM] * (2 + far),
         out_specs=[VMEM] * 2,
         scratch_shapes=work,
         compiler_params=PARAMS,

time: 121 us -> 104 us (0.86)
  Pallas kernels: 52.8 us -> 45.6 us
  local copies, waits for them, and re-layouts: 5.48 us -> 0.05 us
  other arithmetic: 3.89 us -> 0.08 us
    unnamed x42 -> x12, local copies, waits for them, and re-layouts: 3.65 us -> 0.03 us
    pallas_call x3, Pallas kernels: 20.9 us -> 18.2 us  [apply_kernel(): pl.pallas_call(functools.partial(tiles_kernel, tiles % 8), out_shape=[hal...]
    add x3, other arithmetic: 2.7 us -> 0.03 us  [apply_kernel(): both = keep + exchange(give, 'col', 1)]
    squeeze x3, local copies, waits for them, and re-layouts: 1.82 us -> 0.03 us  [apply_kernel(): return [both[0]] + [exchange(both[d], 'col', 2 * d) for d in range(1, far)]]
    pallas_call x1, Pallas kernels: 1.59 us -> 0.11 us  [local(): pl.pallas_call(fourth_kernel, out_shape=[plain, jax.ShapeDtypeStruct((dev...]
  transfers between devices with their start and end apart: 21 -> 21, of which waited for: 18 -> 20; matrix products, arithmetic and copies ran while one was open for 1% -> 0% of each run, Pallas kernels for 0% -> 0%
where the time goes in v3:
time: 104 us
  Pallas kernels  45.6 us (44%)
  starting transfers between devices  25.3 us (24%)
  waiting for transfers between devices  20.5 us (20%)
  blocking collectives  10.6 us (10%)
  between operations  1.5 us (1%)
    ppermute x21, starting transfers between devices, exchange(): return lax.ppermute(value, axis, [(i, i ^ distance) for i in range(size)])  25.3 us
    ppermute x21, waiting for transfers between devices, exchange(): return lax.ppermute(value, axis, [(i, i ^ distance) for i in range(size)])  20.5 us
    pallas_call x3, Pallas kernels, apply_kernel(): pl.pallas_call(functools.partial(tiles_kernel, tiles % 8), out_shape=[hal...  18.2 us
    all_to_all x1, blocking collectives, local(): sums = lax.all_to_all(sums, ('row', 'col'), 0, 0, tiled=True)  10.6 us
    pallas_call x1, Pallas kernels, local(): pl.pallas_call(third_kernel, out_shape=[grid, plain], in_specs=[SMEM, VME...  9 us
    pallas_call x1, Pallas kernels, local(): pl.pallas_call(second_kernel, out_shape=[grid, plain, grid], in_specs=[SM...  8.94 us
    pallas_call x1, Pallas kernels, local(): pl.pallas_call(first_kernel, out_shape=grid, in_specs=[HBM] * 4, out_spec...  8.55 us
  transfers between devices with their start and end apart: 21, of which 20 were waited for; matrix products, arithmetic and copies ran while one was open for 0% of the time, Pallas kernels for 0%

profile of v3, /device:TPU:0, one launch (start us, length us, event | category | flops | bytes accessed | tf_op | source)
XLA Modules:
  0.0 103.6 jit_solution(11288446647365888816)
XLA Ops:
  0.6 0.0 copy-start
  0.6 0.0 copy-start.1
  0.7 0.0 copy-start.2
  0.7 0.0 copy-start.3
  0.7 0.0 copy-start.4
  0.7 0.0 copy-start.5
  0.7 8.6 %first.1.refs_0_.sent.sent0 = f32[40,128]{1,0:T(8,128)S(1)} custom-call(s32[1,1,24]{2,1,0:T(1,128)} %sizes.3, f32[1,1,4608]{2,1,0:T(1,128)} %rhs.7, f32[1,1,4608]{2,1,0:T(1,128)} %friction.5, bf16[1,1,24,512,512]{4,3,2,1,0:T(8,128)(2,1)} %blocks.5), custom_call_target="tpu_custom_call" | custom-call | tf_op jit(solution)/shard_map/first/pallas_call | solution.py:473
  9.3 4.0 %collective-permute-start.2 = (f32[40,128]{1,0:T(8,128)S(1)}, f32[40,128]{1,0:T(8,128)S(1)}, u32[]{:S(2)}, u32[]{:S(2)}) collective-permute-start(f32[40,128]{1,0:T(8,128)S(1)} %first.1.refs_0_.sent.sent0), channel_id=1, source_target_pairs={{0,24},{8,16},{16,8},{24,0},{1,25},{9,17},{17,9},{25,1},{2,26},{10... | collective-permute-start | bytes 61448 | tf_op jit(solution)/shard_map/ppermute | solution.py:451
  13.3 0.5 collective-permute-start.1
  13.8 0.1 collective-permute-start
  14.6 0.0 copy-done.3
  14.6 0.0 copy-done.4
  14.6 0.0 copy-done.5
  14.7 0.4 collective-permute-done.2.refs_3_
  15.0 2.0 %collective-permute-done.1.refs_2_ = f32[40,128]{1,0:T(8,128)S(1)} collective-permute-done((f32[40,128]{1,0:T(8,128)S(1)}, f32[40,128]{1,0:T(8,128)S(1)}, u32[]{:S(2)}, u32[]{:S(2)}) %collective-permute-start.1) | collective-permute-done | bytes 20512 | tf_op jit(solution)/shard_map/ppermute | solution.py:451
  17.1 0.5 collective-permute-done.refs_1_
  17.6 6.1 %tiles.3 = (f32[4,40,128]{2,1,0:T(8,128)S(1)}, f32[4,40,128]{2,1,0:T(8,128)S(1)}) custom-call(s32[1,256]{1,0:T(1,128)S(1)} %get-tuple-element.40.spots, s32[1,256]{1,0:T(1,128)S(1)} %get-tuple-element.41.rows, f32[1,256]{1,0:T(1,128)S(1)} %compare_select_fusion.weight, bf16[1,1,256,128,128]{4,3,2,1,0:T(8,128)(2,1)} %remote.5, ...), custom_call_target="tpu_custom_call" | custom-call | tf_op jit(solution)/shard_map/tiles/pallas_call | solution.py:455
  23.7 0.1 collective-permute-start.3
  23.7 1.3 %collective-permute-done.3 = f32[4,40,128]{2,1,0:T(8,128)S(1)} collective-permute-done((f32[4,40,128]{2,1,0:T(8,128)S(1)}, f32[4,40,128]{2,1,0:T(8,128)S(1)}, u32[]{:S(2)}, u32[]{:S(2)}) %collective-permute-start.3) | collective-permute-done | bytes 81952 | tf_op jit(solution)/shard_map/ppermute | solution.py:451
  25.0 3.2 %collective-permute-start.6 = (f32[40,128]{1,0:T(8,128)S(1)}, f32[40,128]{1,0:T(8,128)S(1)}, u32[]{:S(2)}, u32[]{:S(2)}) collective-permute-start(f32[40,128]{1,0:T(8,128)S(1)} %get-tuple-element.36), channel_id=1, source_target_pairs={{0,6},{1,7},{2,4},{3,5},{4,2},{5,3},{6,0},{7,1},{8,14},{9,15},{10,... | collective-permute-start | bytes 61448 | tf_op jit(solution)/shard_map/ppermute | solution.py:451
  28.2 0.0 collective-permute-start.5
  28.2 1.3 %collective-permute-start.4 = (f32[40,128]{1,0:T(8,128)S(1)}, f32[40,128]{1,0:T(8,128)S(1)}, u32[]{:S(2)}, u32[]{:S(2)}) collective-permute-start(f32[40,128]{1,0:T(8,128)S(1)} %get-tuple-element.38), channel_id=1, source_target_pairs={{0,2},{1,3},{2,0},{3,1},{4,6},{5,7},{6,4},{7,5},{8,10},{9,11},{10,... | collective-permute-start | bytes 61448 | tf_op jit(solution)/shard_map/ppermute | solution.py:451
  29.5 1.2 %collective-permute-done.6.refs_3_ = f32[40,128]{1,0:T(8,128)S(1)} collective-permute-done((f32[40,128]{1,0:T(8,128)S(1)}, f32[40,128]{1,0:T(8,128)S(1)}, u32[]{:S(2)}, u32[]{:S(2)}) %collective-permute-start.6) | collective-permute-done | bytes 20512 | tf_op jit(solution)/shard_map/ppermute | solution.py:451
  30.7 2.2 %collective-permute-done.5.refs_2_ = f32[40,128]{1,0:T(8,128)S(1)} collective-permute-done((f32[40,128]{1,0:T(8,128)S(1)}, f32[40,128]{1,0:T(8,128)S(1)}, u32[]{:S(2)}, u32[]{:S(2)}) %collective-permute-start.5) | collective-permute-done | bytes 20512 | tf_op jit(solution)/shard_map/ppermute | solution.py:451
  32.9 0.0 collective-permute-done.4.refs_1_
  32.9 0.0 copy-done
  32.9 0.0 copy-done.1
  32.9 0.0 copy-done.2
  32.9 8.9 %second.1 = (f32[40,128]{1,0:T(8,128)S(1)}, f32[36,128]{1,0:T(8,128)S(1)}, f32[40,128]{1,0:T(8,128)S(1)}) custom-call(s32[1,1,24]{2,1,0:T(1,128)S(1)} %copy-done.2, f32[1,1,4608]{2,1,0:T(1,128)S(1)} %copy-done, f32[1,1,4608]{2,1,0:T(1,128)S(1)} %copy-done.1, bf16[1,1,24,512,512]{4,3,2,1,0:T(8,128)(2,1)} %blocks.5, f32[40,128]{1,0:T(8,128)S(1)} %first.1.refs_0_.sent.sent0, ...), custom_call_target="tpu_custom_call" | custom-call | tf_op jit(solution)/shard_map/second/pallas_call | solution.py:489
  41.9 1.7 %collective-permute-start.9 = (f32[40,128]{1,0:T(8,128)S(1)}, f32[40,128]{1,0:T(8,128)S(1)}, u32[]{:S(2)}, u32[]{:S(2)}) collective-permute-start(f32[40,128]{1,0:T(8,128)S(1)} %get-tuple-element.17.refs_0_.sent.sent1), channel_id=1, source_target_pairs={{0,24},{8,16},{16,8},{24,0},{1,25},{9,17},{17,9},{25,1},{2,26},{10... | collective-permute-start | bytes 61448 | tf_op jit(solution)/shard_map/ppermute | solution.py:451
  43.6 1.0 collective-permute-start.8
  44.5 0.9 collective-permute-start.7
  45.4 1.4 %collective-permute-done.9.refs_3_ = f32[40,128]{1,0:T(8,128)S(1)} collective-permute-done((f32[40,128]{1,0:T(8,128)S(1)}, f32[40,128]{1,0:T(8,128)S(1)}, u32[]{:S(2)}, u32[]{:S(2)}) %collective-permute-start.9) | collective-permute-done | bytes 20512 | tf_op jit(solution)/shard_map/ppermute | solution.py:451
  46.8 0.6 collective-permute-done.8.refs_2_
  47.4 1.0 collective-permute-done.7.refs_1_
  48.3 6.1 %tiles.4 = (f32[4,40,128]{2,1,0:T(8,128)S(1)}, f32[4,40,128]{2,1,0:T(8,128)S(1)}) custom-call(s32[1,256]{1,0:T(1,128)S(1)} %get-tuple-element.40.spots, s32[1,256]{1,0:T(1,128)S(1)} %get-tuple-element.41.rows, f32[1,256]{1,0:T(1,128)S(1)} %compare_select_fusion.weight, bf16[1,1,256,128,128]{4,3,2,1,0:T(8,128)(2,1)} %remote.5, ...), custom_call_target="tpu_custom_call" | custom-call | tf_op jit(solution)/shard_map/tiles/pallas_call | solution.py:455
  54.4 0.1 collective-permute-start.10
  54.5 1.3 %collective-permute-done.10 = f32[4,40,128]{2,1,0:T(8,128)S(1)} collective-permute-done((f32[4,40,128]{2,1,0:T(8,128)S(1)}, f32[4,40,128]{2,1,0:T(8,128)S(1)}, u32[]{:S(2)}, u32[]{:S(2)}) %collective-permute-start.10) | collective-permute-done | bytes 81952 | tf_op jit(solution)/shard_map/ppermute | solution.py:451
  55.8 1.0 collective-permute-start.13
  56.7 1.1 %collective-permute-start.12 = (f32[40,128]{1,0:T(8,128)S(1)}, f32[40,128]{1,0:T(8,128)S(1)}, u32[]{:S(2)}, u32[]{:S(2)}) collective-permute-start(f32[40,128]{1,0:T(8,128)S(1)} %get-tuple-element.33), channel_id=1, source_target_pairs={{0,4},{1,5},{2,6},{3,7},{4,0},{5,1},{6,2},{7,3},{8,12},{9,13},{10,... | collective-permute-start | bytes 61448 | tf_op jit(solution)/shard_map/ppermute | solution.py:451
  57.9 2.3 %collective-permute-start.11 = (f32[40,128]{1,0:T(8,128)S(1)}, f32[40,128]{1,0:T(8,128)S(1)}, u32[]{:S(2)}, u32[]{:S(2)}) collective-permute-start(f32[40,128]{1,0:T(8,128)S(1)} %get-tuple-element.34), channel_id=1, source_target_pairs={{0,2},{1,3},{2,0},{3,1},{4,6},{5,7},{6,4},{7,5},{8,10},{9,11},{10,... | collective-permute-start | bytes 61448 | tf_op jit(solution)/shard_map/ppermute | solution.py:451
  60.2 1.4 %collective-permute-done.13.refs_3_ = f32[40,128]{1,0:T(8,128)S(1)} collective-permute-done((f32[40,128]{1,0:T(8,128)S(1)}, f32[40,128]{1,0:T(8,128)S(1)}, u32[]{:S(2)}, u32[]{:S(2)}) %collective-permute-start.13) | collective-permute-done | bytes 20512 | tf_op jit(solution)/shard_map/ppermute | solution.py:451
  61.7 0.2 collective-permute-done.12.refs_2_
  61.8 0.2 collective-permute-done.11.refs_1_
  62.1 9.0 %third.1 = (f32[40,128]{1,0:T(8,128)S(1)}, f32[36,128]{1,0:T(8,128)S(1)}) custom-call(s32[1,1,24]{2,1,0:T(1,128)S(1)} %copy-done.2, f32[1,1,4608]{2,1,0:T(1,128)S(1)} %copy-done, f32[1,1,4608]{2,1,0:T(1,128)S(1)} %copy-done.1, bf16[1,1,24,512,512]{4,3,2,1,0:T(8,128)(2,1)} %blocks.5, f32[40,128]{1,0:T(8,128)S(1)} %get-tuple-element.17.refs_0_.sent.sent1, ...), custom_call_target="tpu_custom_call" | custom-call | tf_op jit(solution)/shard_map/third/pallas_call | solution.py:499
  71.1 2.2 %collective-permute-start.16 = (f32[40,128]{1,0:T(8,128)S(1)}, f32[40,128]{1,0:T(8,128)S(1)}, u32[]{:S(2)}, u32[]{:S(2)}) collective-permute-start(f32[40,128]{1,0:T(8,128)S(1)} %get-tuple-element.21.refs_0_.sent.sent2), channel_id=1, source_target_pairs={{0,24},{8,16},{16,8},{24,0},{1,25},{9,17},{17,9},{25,1},{2,26},{10... | collective-permute-start | bytes 61448 | tf_op jit(solution)/shard_map/ppermute | solution.py:451
  73.3 0.4 collective-permute-start.15
  73.7 0.9 collective-permute-start.14
  74.6 1.2 %collective-permute-done.16.refs_3_ = f32[40,128]{1,0:T(8,128)S(1)} collective-permute-done((f32[40,128]{1,0:T(8,128)S(1)}, f32[40,128]{1,0:T(8,128)S(1)}, u32[]{:S(2)}, u32[]{:S(2)}) %collective-permute-start.16) | collective-permute-done | bytes 20512 | tf_op jit(solution)/shard_map/ppermute | solution.py:451
  75.8 1.2 %collective-permute-done.15.refs_2_ = f32[40,128]{1,0:T(8,128)S(1)} collective-permute-done((f32[40,128]{1,0:T(8,128)S(1)}, f32[40,128]{1,0:T(8,128)S(1)}, u32[]{:S(2)}, u32[]{:S(2)}) %collective-permute-start.15) | collective-permute-done | bytes 20512 | tf_op jit(solution)/shard_map/ppermute | solution.py:451
  77.1 0.4 collective-permute-done.14.refs_1_
  77.5 6.1 %tiles.5 = (f32[4,40,128]{2,1,0:T(8,128)S(1)}, f32[4,40,128]{2,1,0:T(8,128)S(1)}) custom-call(s32[1,256]{1,0:T(1,128)S(1)} %get-tuple-element.40.spots, s32[1,256]{1,0:T(1,128)S(1)} %get-tuple-element.41.rows, f32[1,256]{1,0:T(1,128)S(1)} %compare_select_fusion.weight, bf16[1,1,256,128,128]{4,3,2,1,0:T(8,128)(2,1)} %remote.5, ...), custom_call_target="tpu_custom_call" | custom-call | tf_op jit(solution)/shard_map/tiles/pallas_call | solution.py:455
  83.6 0.1 collective-permute-start.17
  83.7 1.3 %collective-permute-done.17 = f32[4,40,128]{2,1,0:T(8,128)S(1)} collective-permute-done((f32[4,40,128]{2,1,0:T(8,128)S(1)}, f32[4,40,128]{2,1,0:T(8,128)S(1)}, u32[]{:S(2)}, u32[]{:S(2)}) %collective-permute-start.17) | collective-permute-done | bytes 81952 | tf_op jit(solution)/shard_map/ppermute | solution.py:451
  85.0 2.3 %collective-permute-start.20 = (f32[40,128]{1,0:T(8,128)S(1)}, f32[40,128]{1,0:T(8,128)S(1)}, u32[]{:S(2)}, u32[]{:S(2)}) collective-permute-start(f32[40,128]{1,0:T(8,128)S(1)} %get-tuple-element.28), channel_id=1, source_target_pairs={{0,6},{1,7},{2,4},{3,5},{4,2},{5,3},{6,0},{7,1},{8,14},{9,15},{10,... | collective-permute-start | bytes 61448 | tf_op jit(solution)/shard_map/ppermute | solution.py:451
  87.2 1.0 collective-permute-start.19
  88.2 1.2 %collective-permute-start.18 = (f32[40,128]{1,0:T(8,128)S(1)}, f32[40,128]{1,0:T(8,128)S(1)}, u32[]{:S(2)}, u32[]{:S(2)}) collective-permute-start(f32[40,128]{1,0:T(8,128)S(1)} %get-tuple-element.30), channel_id=1, source_target_pairs={{0,2},{1,3},{2,0},{3,1},{4,6},{5,7},{6,4},{7,5},{8,10},{9,11},{10,... | collective-permute-start | bytes 61448 | tf_op jit(solution)/shard_map/ppermute | solution.py:451
  89.4 1.4 %collective-permute-done.20.refs_3_ = f32[40,128]{1,0:T(8,128)S(1)} collective-permute-done((f32[40,128]{1,0:T(8,128)S(1)}, f32[40,128]{1,0:T(8,128)S(1)}, u32[]{:S(2)}, u32[]{:S(2)}) %collective-permute-start.20) | collective-permute-done | bytes 20512 | tf_op jit(solution)/shard_map/ppermute | solution.py:451
  90.8 1.1 %collective-permute-done.19.refs_2_ = f32[40,128]{1,0:T(8,128)S(1)} collective-permute-done((f32[40,128]{1,0:T(8,128)S(1)}, f32[40,128]{1,0:T(8,128)S(1)}, u32[]{:S(2)}, u32[]{:S(2)}) %collective-permute-start.19) | collective-permute-done | bytes 20512 | tf_op jit(solution)/shard_map/ppermute | solution.py:451
  91.9 0.2 collective-permute-done.18.refs_1_
  92.1 0.1 fourth.1
  92.3 10.6 %all_to_all.11 = f32[32,1,128]{2,1,0:T(1,128)S(1)} all-to-all(f32[32,1,128]{2,1,0:T(1,128)S(1)} %bitcast.63), channel_id=1, replica_groups=mesh['row'=4,'col'=8] {'row','col'}, dimensions={0} | all-to-all | bytes 32768 | tf_op jit(solution)/shard_map/all_to_all | solution.py:518
  102.8 0.8 last.1
  (8 shorter events, 0.1 us)
Async XLA Ops:
  0.6 32.3 %copy-start = (f32[1,1,4608]{2,1,0:T(1,128)S(1)}, f32[1,1,4608]{2,1,0:T(1,128)}, u32[]{:S(2)}) copy-start(f32[1,1,4608]{2,1,0:T(1,128)} %rhs.7) | copy-start | bytes 55300
  0.6 32.3 %copy-start.1 = (f32[1,1,4608]{2,1,0:T(1,128)S(1)}, f32[1,1,4608]{2,1,0:T(1,128)}, u32[]{:S(2)}) copy-start(f32[1,1,4608]{2,1,0:T(1,128)} %friction.5) | copy-start | bytes 55300
  0.7 32.3 %copy-start.2 = (s32[1,1,24]{2,1,0:T(1,128)S(1)}, s32[1,1,24]{2,1,0:T(1,128)}, u32[]{:S(2)}) copy-start(s32[1,1,24]{2,1,0:T(1,128)} %sizes.3) | copy-start | bytes 292
  0.7 13.9 %copy-start.3 = (s32[1,1,256]{2,1,0:T(1,128)S(1)}, s32[1,1,256]{2,1,0:T(1,128)}, u32[]{:S(2)}) copy-start(s32[1,1,256]{2,1,0:T(1,128)} %param.14) | copy-start | bytes 3076
  0.7 13.9 %copy-start.4 = (s32[1,1,256]{2,1,0:T(1,128)S(1)}, s32[1,1,256]{2,1,0:T(1,128)}, u32[]{:S(2)}) copy-start(s32[1,1,256]{2,1,0:T(1,128)} %param.13) | copy-start | bytes 3076
  0.7 13.9 %copy-start.5 = (f32[1,1,256]{2,1,0:T(1,128)S(1)}, f32[1,1,256]{2,1,0:T(1,128)}, u32[]{:S(2)}) copy-start(f32[1,1,256]{2,1,0:T(1,128)} %param.12) | copy-start | bytes 3076
  9.3 5.8 %collective-permute-start.2 = (f32[40,128]{1,0:T(8,128)S(1)}, f32[40,128]{1,0:T(8,128)S(1)}, u32[]{:S(2)}, u32[]{:S(2)}) collective-permute-start(f32[40,128]{1,0:T(8,128)S(1)} %first.1.refs_0_.sent.sent0), channel_id=1, source_target_pairs={{0,24},{8,16},{16,8},{24,0},{1,25},{9,17},{17,9},{25,1},{2,26},{10... | collective-permute-start | bytes 61448 | tf_op jit(solution)/shard_map/ppermute | solution.py:451
  13.3 3.8 %collective-permute-start.1 = (f32[40,128]{1,0:T(8,128)S(1)}, f32[40,128]{1,0:T(8,128)S(1)}, u32[]{:S(2)}, u32[]{:S(2)}) collective-permute-start(f32[40,128]{1,0:T(8,128)S(1)} %first.1.refs_0_.sent.sent0), channel_id=1, source_target_pairs={{0,16},{8,24},{16,0},{24,8},{1,17},{9,25},{17,1},{25,9},{2,18},{10... | collective-permute-start | bytes 61448 | tf_op jit(solution)/shard_map/ppermute | solution.py:451
  13.8 3.8 %collective-permute-start = (f32[40,128]{1,0:T(8,128)S(1)}, f32[40,128]{1,0:T(8,128)S(1)}, u32[]{:S(2)}, u32[]{:S(2)}) collective-permute-start(f32[40,128]{1,0:T(8,128)S(1)} %first.1.refs_0_.sent.sent0), channel_id=1, source_target_pairs={{0,8},{8,0},{16,24},{24,16},{1,9},{9,1},{17,25},{25,17},{2,10},{10... | collective-permute-start | bytes 61448 | tf_op jit(solution)/shard_map/ppermute | solution.py:451
  23.7 1.3 %collective-permute-start.3 = (f32[4,40,128]{2,1,0:T(8,128)S(1)}, f32[4,40,128]{2,1,0:T(8,128)S(1)}, u32[]{:S(2)}, u32[]{:S(2)}) collective-permute-start(f32[4,40,128]{2,1,0:T(8,128)S(1)} %get-tuple-element.16), channel_id=1, source_target_pairs={{0,1},{1,0},{2,3},{3,2},{4,5},{5,4},{6,7},{7,6},{8,9},{9,8},{10,11... | collective-permute-start | bytes 245768 | tf_op jit(solution)/shard_map/ppermute | solution.py:451
  25.0 5.6 %collective-permute-start.6 = (f32[40,128]{1,0:T(8,128)S(1)}, f32[40,128]{1,0:T(8,128)S(1)}, u32[]{:S(2)}, u32[]{:S(2)}) collective-permute-start(f32[40,128]{1,0:T(8,128)S(1)} %get-tuple-element.36), channel_id=1, source_target_pairs={{0,6},{1,7},{2,4},{3,5},{4,2},{5,3},{6,0},{7,1},{8,14},{9,15},{10,... | collective-permute-start | bytes 61448 | tf_op jit(solution)/shard_map/ppermute | solution.py:451
  28.2 4.7 %collective-permute-start.5 = (f32[40,128]{1,0:T(8,128)S(1)}, f32[40,128]{1,0:T(8,128)S(1)}, u32[]{:S(2)}, u32[]{:S(2)}) collective-permute-start(f32[40,128]{1,0:T(8,128)S(1)} %get-tuple-element.37), channel_id=1, source_target_pairs={{0,4},{1,5},{2,6},{3,7},{4,0},{5,1},{6,2},{7,3},{8,12},{9,13},{10,... | collective-permute-start | bytes 61448 | tf_op jit(solution)/shard_map/ppermute | solution.py:451
  28.2 4.7 %collective-permute-start.4 = (f32[40,128]{1,0:T(8,128)S(1)}, f32[40,128]{1,0:T(8,128)S(1)}, u32[]{:S(2)}, u32[]{:S(2)}) collective-permute-start(f32[40,128]{1,0:T(8,128)S(1)} %get-tuple-element.38), channel_id=1, source_target_pairs={{0,2},{1,3},{2,0},{3,1},{4,6},{5,7},{6,4},{7,5},{8,10},{9,11},{10,... | collective-permute-start | bytes 61448 | tf_op jit(solution)/shard_map/ppermute | solution.py:451
  41.9 4.9 %collective-permute-start.9 = (f32[40,128]{1,0:T(8,128)S(1)}, f32[40,128]{1,0:T(8,128)S(1)}, u32[]{:S(2)}, u32[]{:S(2)}) collective-permute-start(f32[40,128]{1,0:T(8,128)S(1)} %get-tuple-element.17.refs_0_.sent.sent1), channel_id=1, source_target_pairs={{0,24},{8,16},{16,8},{24,0},{1,25},{9,17},{17,9},{25,1},{2,26},{10... | collective-permute-start | bytes 61448 | tf_op jit(solution)/shard_map/ppermute | solution.py:451
  43.6 3.8 %collective-permute-start.8 = (f32[40,128]{1,0:T(8,128)S(1)}, f32[40,128]{1,0:T(8,128)S(1)}, u32[]{:S(2)}, u32[]{:S(2)}) collective-permute-start(f32[40,128]{1,0:T(8,128)S(1)} %get-tuple-element.17.refs_0_.sent.sent1), channel_id=1, source_target_pairs={{0,16},{8,24},{16,0},{24,8},{1,17},{9,25},{17,1},{25,9},{2,18},{10... | collective-permute-start | bytes 61448 | tf_op jit(solution)/shard_map/ppermute | solution.py:451
  44.5 3.8 %collective-permute-start.7 = (f32[40,128]{1,0:T(8,128)S(1)}, f32[40,128]{1,0:T(8,128)S(1)}, u32[]{:S(2)}, u32[]{:S(2)}) collective-permute-start(f32[40,128]{1,0:T(8,128)S(1)} %get-tuple-element.17.refs_0_.sent.sent1), channel_id=1, source_target_pairs={{0,8},{8,0},{16,24},{24,16},{1,9},{9,1},{17,25},{25,17},{2,10},{10... | collective-permute-start | bytes 61448 | tf_op jit(solution)/shard_map/ppermute | solution.py:451
  54.4 1.3 %collective-permute-start.10 = (f32[4,40,128]{2,1,0:T(8,128)S(1)}, f32[4,40,128]{2,1,0:T(8,128)S(1)}, u32[]{:S(2)}, u32[]{:S(2)}) collective-permute-start(f32[4,40,128]{2,1,0:T(8,128)S(1)} %get-tuple-element.20), channel_id=1, source_target_pairs={{0,1},{1,0},{2,3},{3,2},{4,5},{5,4},{6,7},{7,6},{8,9},{9,8},{10,11... | collective-permute-start | bytes 245768 | tf_op jit(solution)/shard_map/ppermute | solution.py:451
  55.8 5.9 %collective-permute-start.13 = (f32[40,128]{1,0:T(8,128)S(1)}, f32[40,128]{1,0:T(8,128)S(1)}, u32[]{:S(2)}, u32[]{:S(2)}) collective-permute-start(f32[40,128]{1,0:T(8,128)S(1)} %get-tuple-element.32), channel_id=1, source_target_pairs={{0,6},{1,7},{2,4},{3,5},{4,2},{5,3},{6,0},{7,1},{8,14},{9,15},{10,... | collective-permute-start | bytes 61448 | tf_op jit(solution)/shard_map/ppermute | solution.py:451
  56.7 5.1 %collective-permute-start.12 = (f32[40,128]{1,0:T(8,128)S(1)}, f32[40,128]{1,0:T(8,128)S(1)}, u32[]{:S(2)}, u32[]{:S(2)}) collective-permute-start(f32[40,128]{1,0:T(8,128)S(1)} %get-tuple-element.33), channel_id=1, source_target_pairs={{0,4},{1,5},{2,6},{3,7},{4,0},{5,1},{6,2},{7,3},{8,12},{9,13},{10,... | collective-permute-start | bytes 61448 | tf_op jit(solution)/shard_map/ppermute | solution.py:451
  57.9 4.2 %collective-permute-start.11 = (f32[40,128]{1,0:T(8,128)S(1)}, f32[40,128]{1,0:T(8,128)S(1)}, u32[]{:S(2)}, u32[]{:S(2)}) collective-permute-start(f32[40,128]{1,0:T(8,128)S(1)} %get-tuple-element.34), channel_id=1, source_target_pairs={{0,2},{1,3},{2,0},{3,1},{4,6},{5,7},{6,4},{7,5},{8,10},{9,11},{10,... | collective-permute-start | bytes 61448 | tf_op jit(solution)/shard_map/ppermute | solution.py:451
  71.1 4.8 %collective-permute-start.16 = (f32[40,128]{1,0:T(8,128)S(1)}, f32[40,128]{1,0:T(8,128)S(1)}, u32[]{:S(2)}, u32[]{:S(2)}) collective-permute-start(f32[40,128]{1,0:T(8,128)S(1)} %get-tuple-element.21.refs_0_.sent.sent2), channel_id=1, source_target_pairs={{0,24},{8,16},{16,8},{24,0},{1,25},{9,17},{17,9},{25,1},{2,26},{10... | collective-permute-start | bytes 61448 | tf_op jit(solution)/shard_map/ppermute | solution.py:451
  73.3 3.8 %collective-permute-start.15 = (f32[40,128]{1,0:T(8,128)S(1)}, f32[40,128]{1,0:T(8,128)S(1)}, u32[]{:S(2)}, u32[]{:S(2)}) collective-permute-start(f32[40,128]{1,0:T(8,128)S(1)} %get-tuple-element.21.refs_0_.sent.sent2), channel_id=1, source_target_pairs={{0,16},{8,24},{16,0},{24,8},{1,17},{9,25},{17,1},{25,9},{2,18},{10... | collective-permute-start | bytes 61448 | tf_op jit(solution)/shard_map/ppermute | solution.py:451
  73.7 3.8 %collective-permute-start.14 = (f32[40,128]{1,0:T(8,128)S(1)}, f32[40,128]{1,0:T(8,128)S(1)}, u32[]{:S(2)}, u32[]{:S(2)}) collective-permute-start(f32[40,128]{1,0:T(8,128)S(1)} %get-tuple-element.21.refs_0_.sent.sent2), channel_id=1, source_target_pairs={{0,8},{8,0},{16,24},{24,16},{1,9},{9,1},{17,25},{25,17},{2,10},{10... | collective-permute-start | bytes 61448 | tf_op jit(solution)/shard_map/ppermute | solution.py:451
  83.6 1.3 %collective-permute-start.17 = (f32[4,40,128]{2,1,0:T(8,128)S(1)}, f32[4,40,128]{2,1,0:T(8,128)S(1)}, u32[]{:S(2)}, u32[]{:S(2)}) collective-permute-start(f32[4,40,128]{2,1,0:T(8,128)S(1)} %get-tuple-element.25), channel_id=1, source_target_pairs={{0,1},{1,0},{2,3},{3,2},{4,5},{5,4},{6,7},{7,6},{8,9},{9,8},{10,11... | collective-permute-start | bytes 245768 | tf_op jit(solution)/shard_map/ppermute | solution.py:451
  85.0 5.8 %collective-permute-start.20 = (f32[40,128]{1,0:T(8,128)S(1)}, f32[40,128]{1,0:T(8,128)S(1)}, u32[]{:S(2)}, u32[]{:S(2)}) collective-permute-start(f32[40,128]{1,0:T(8,128)S(1)} %get-tuple-element.28), channel_id=1, source_target_pairs={{0,6},{1,7},{2,4},{3,5},{4,2},{5,3},{6,0},{7,1},{8,14},{9,15},{10,... | collective-permute-start | bytes 61448 | tf_op jit(solution)/shard_map/ppermute | solution.py:451
  87.2 4.7 %collective-permute-start.19 = (f32[40,128]{1,0:T(8,128)S(1)}, f32[40,128]{1,0:T(8,128)S(1)}, u32[]{:S(2)}, u32[]{:S(2)}) collective-permute-start(f32[40,128]{1,0:T(8,128)S(1)} %get-tuple-element.29), channel_id=1, source_target_pairs={{0,4},{1,5},{2,6},{3,7},{4,0},{5,1},{6,2},{7,3},{8,12},{9,13},{10,... | collective-permute-start | bytes 61448 | tf_op jit(solution)/shard_map/ppermute | solution.py:451
  88.2 3.9 %collective-permute-start.18 = (f32[40,128]{1,0:T(8,128)S(1)}, f32[40,128]{1,0:T(8,128)S(1)}, u32[]{:S(2)}, u32[]{:S(2)}) collective-permute-start(f32[40,128]{1,0:T(8,128)S(1)} %get-tuple-element.30), channel_id=1, source_target_pairs={{0,2},{1,3},{2,0},{3,1},{4,6},{5,7},{6,4},{7,5},{8,10},{9,11},{10,... | collective-permute-start | bytes 61448 | tf_op jit(solution)/shard_map/ppermute | solution.py:451

commit v4 on v3

--- a/solution.py
+++ b/solution.py
@@ -9,13 +9,12 @@
 
 LANES = 128
 UNROLL = 3
-AHEAD = 6
 F32 = jnp.float32
 BF16 = jnp.bfloat16
 VMEM = pl.BlockSpec(memory_space=pltpu.VMEM)
 SMEM = pl.BlockSpec(memory_space=pltpu.SMEM)
 HBM = pl.BlockSpec(memory_space=pltpu.HBM)
-PARAMS = pltpu.CompilerParams(vmem_limit_bytes=24 << 20)
+PARAMS = pltpu.CompilerParams(vmem_limit_bytes=6 << 20)
 
 
 def dot_nt(left, right):
@@ -60,32 +59,39 @@
     return scalars
 
 
+def quarters(remote, blocks, sems, f, which):
+    half = blocks.shape[1] // 2
+    near, far = pl.ds(0, half), pl.ds(half, half)
+    return [
+        pltpu.make_async_copy(
+            remote.at[(0, 0, f) + part], blocks.at[(f,) + part], sems.at[place, f]
+        )
+        for place, part in list(enumerate([(near, near), (near, far), (far,)]))[which]
+    ]
+
+
 def fetch(scalars, remote, blocks, sems):
-    copies = []
+    half = blocks.shape[1] // 2
+    for f in range(len(scalars)):
+        quarters(remote, blocks, sems, f, slice(0, 1))[0].start()
     for f, (_, _, size) in enumerate(scalars):
-        need = pl.multiple_of((size + 15) // 16 * 16, 16)
-        copy = pltpu.make_async_copy(
-            remote.at[0, 0, f, pl.ds(0, need)], blocks.at[f, pl.ds(0, need)], sems.at[f]
-        )
-        copies.append(copy)
-    for copy in copies[:AHEAD]:
-        copy.start()
-    return copies
-
-
-def await_copy(copies, place):
-    copies[place].wait()
-    if place + AHEAD < len(copies):
-        copies[place + AHEAD].start()
+
+        @pl.when(size > half)
+        def _():
+            for copy in quarters(remote, blocks, sems, f, slice(1, 3)):
+                copy.start()
 
 
 def precondition(sizes, remote, field, work, begin=None):
-    blocks, windows, shifts, lens, stack, lefts, found, large, sems = work
-    faults = remote.shape[2]
+    windows, shifts, lens, stack, lefts, found, large = work[:7]
+    local = len(work) == 7
+    blocks, sems = (remote, None) if local else work[7:]
+    faults = blocks.shape[0]
     chunks = blocks.shape[1] // LANES
     rows = field.shape[0]
     scalars = fault_scalars(sizes, faults)
-    copies = fetch(scalars, remote, blocks, sems)
+    if not local:
+        fetch(scalars, remote, blocks, sems)
     if begin is not None:
         begin()
     lane = lax.broadcasted_iota(jnp.int32, (faults, LANES), 1)
@@ -121,7 +127,8 @@
         sums = [jnp.zeros((8, LANES), F32) for _ in range(chunk_half)]
         for place in range(8):
             f = group * 8 + place
-            await_copy(copies, f)
+            if not local:
+                quarters(remote, blocks, sems, f, slice(0, 1))[0].wait()
             result = dot_nt(left[:, :half], blocks[f, :half, :half])
             result = result[:8] + result[8:]
             for k in range(chunk_half):
@@ -139,6 +146,13 @@
             f = large[jnp.minimum(place, count - 1)]
             group = f // 8
             left = lefts[group]
+            if not local:
+
+                @pl.when(place < count)
+                def _():
+                    for copy in quarters(remote, blocks, sems, f, slice(1, 3)):
+                        copy.wait()
+
             above = dot_nt(left[:, half:], blocks[f, :half, half:])
             below = dot_nt(left, blocks[f, half:, :])
             above = above[:8] + above[8:]
@@ -191,20 +205,46 @@
     field[tiles:, :] = jnp.zeros((field.shape[0] - tiles, LANES), F32)
 
 
-def first_kernel(far_sizes, far_rhs, far_friction, blocks, send, sizes, rhs, friction, sems, field, *work):
+def owner(index, each, count):
+    found = jnp.zeros(index.shape, jnp.int32)
+    for c in range(1, count):
+        found = found + (index >= c * each).astype(jnp.int32)
+    return found
+
+
+def first_kernel(shape, *refs):
+    (blocks, far_tiles, send, near_blocks, near_tiles, spots, target) = refs[5:12]
+    (sizes, rhs, friction, tile_row, tile_col) = refs[12:17]
+    (sems, tiles_sem, block_sems, field, *work) = refs[17:]
+    work = work + [near_blocks, block_sems]
+    row_count, col_count = shape
     tiles = rhs.shape[2] // LANES
-    pairs = [(far_sizes, sizes), (far_rhs, rhs), (far_friction, friction)]
+    height = send.shape[0]
+    pairs = list(zip(refs[:5], refs[12:17]))
     copies = [pltpu.make_async_copy(a, b, sems.at[i]) for i, (a, b) in enumerate(pairs)]
     for copy in copies:
         copy.start()
+    whole = pltpu.make_async_copy(far_tiles.at[0, 0], near_tiles, tiles_sem)
     copies[0].wait()
 
     def value_to_field():
+        whole.start()
         copies[1].wait()
         set_field(field, load_rows(rhs, tiles))
+        for copy in copies[3:]:
+            copy.wait()
+        column = tile_col[0]
+        source = owner(column, tiles, row_count)
+        spots[...] = (source ^ lax.axis_index("row")) * height + column - source * tiles
+        row = tile_row[0]
+        source = owner(row, tiles, col_count)
+        place = source ^ lax.axis_index("col")
+        place = (place & 1) * (col_count // 2) + (place >> 1)
+        target[...] = place * height + row - source * tiles
 
     direction = precondition(sizes, blocks, field, work, value_to_field)[0:tiles]
     copies[2].wait()
+    whole.wait()
     value = field[0:tiles, :]
     scaled = load_rows(friction, tiles) * direction
     send[...] = jnp.zeros_like(send)
@@ -220,7 +260,7 @@
 
 
 def second_kernel(sizes, rhs, friction, blocks, sent, *refs):
-    parts, (send, image_out, basis_out, field, *work) = refs[:-13], refs[-13:]
+    parts, (send, image_out, basis_out, field, *work) = refs[:-11], refs[-11:]
     tiles = rhs.shape[2] // LANES
     start = load_rows(rhs, tiles)
     diagonal = load_rows(friction, tiles)
@@ -248,7 +288,7 @@
 
 
 def third_kernel(sizes, rhs, friction, blocks, sent, basis, *refs):
-    parts, (send, image_out, field, *work) = refs[:-12], refs[-12:]
+    parts, (send, image_out, field, *work) = refs[:-10], refs[-10:]
     tiles = rhs.shape[2] // LANES
     start = load_rows(rhs, tiles)
     diagonal = load_rows(friction, tiles)
@@ -324,21 +364,11 @@
         residual[0, :, pl.ds(k * LANES, LANES)] = rest[k : k + 1]
 
 
-def tiles_kernel(tail, spots, rows, weight, remote, *refs):
-    sent, (keep, give, blocks, field, found, products, sems) = refs[:-7], refs[-7:]
+def tiles_kernel(tail, counts, spots, rows, scale, blocks, *refs):
+    sent, (keep, give, field, found, products) = refs[:-5], refs[-5:]
     slots = blocks.shape[0]
     far, height = keep.shape[0], keep.shape[1]
     groups = slots // 16
-    copies = []
-    for group in range(groups):
-        copy = pltpu.make_async_copy(
-            remote.at[0, 0, pl.ds(group * 16, 16)],
-            blocks.at[pl.ds(group * 16, 16)],
-            sems.at[group],
-        )
-        copies.append(copy)
-    for copy in copies[:AHEAD]:
-        copy.start()
     for k, one in enumerate(sent):
         field[k * height : (k + 1) * height, :] = one[...]
     for t in range(slots):
@@ -346,7 +376,6 @@
     sub = lax.broadcasted_iota(jnp.int32, (8, LANES), 0)
     blank = jnp.zeros((8, LANES), F32)
     for group in range(groups):
-        await_copy(copies, group)
         base = group * 16
         top = jnp.concatenate([found[base : base + 8, :], blank], axis=1)
         bottom = jnp.concatenate([blank, found[base + 8 : base + 16, :]], axis=1)
@@ -369,8 +398,10 @@
         products[base + 8 : base + 16, :] = second
     high, low = split(products[...])
     target = rows[...]
+    slot = lax.broadcasted_iota(jnp.int32, target.shape, 1)
+    weight = jnp.where(slot < counts[0, 0], scale[0], 0.0)
     chosen = jnp.where(
-        lax.broadcasted_iota(jnp.int32, (2 * far * height, slots), 0) == target, weight[...], 0.0
+        lax.broadcasted_iota(jnp.int32, (2 * far * height, slots), 0) == target, weight, 0.0
     )
     chosen_high, chosen_low = split(chosen)
     value = (
@@ -413,29 +444,15 @@
     chunks = width // LANES
     row_count = lax.axis_size("row")
     col_count = lax.axis_size("col")
-    my_row = lax.axis_index("row")
-    my_col = lax.axis_index("col")
     far = col_count // 2
     rows = (tiles + chunks + 8) // 8 * 8
     depth = (faults * (chunks + 1) + LANES - 1) // LANES * LANES
 
-    place = tile_col[0, 0] // tiles ^ my_row
-    spots = (place * height + tile_col[0, 0] % tiles).reshape(1, slots)
-    place = tile_row[0, 0] // tiles ^ my_col
-    place = place % 2 * far + place // 2
-    target = (place * height + tile_row[0, 0] % tiles).reshape(1, slots)
-    weight = jnp.where(
-        jnp.arange(slots, dtype=jnp.int32) < tile_counts[0, 0], tile_scale[0, 0], 0.0
-    ).reshape(1, slots)
-
-    kernel_tiles = pltpu.with_memory_space_constraint(kernel_tiles, pltpu.HBM)
-    precond_blocks = pltpu.with_memory_space_constraint(precond_blocks, pltpu.HBM)
     grid = jax.ShapeDtypeStruct((height, LANES), F32)
     plain = jax.ShapeDtypeStruct((tiles, LANES), F32)
     half_grid = jax.ShapeDtypeStruct((far, height, LANES), F32)
     work = [
         scratch((rows, LANES)),
-        scratch((faults, width, width), BF16),
         scratch((chunks + 1, faults, LANES)),
         scratch((faults, LANES), jnp.int32),
         scratch((faults, LANES), jnp.int32),
@@ -443,68 +460,78 @@
         scratch((faults // 8, 16, width), BF16),
         scratch((chunks, faults // 8, 8, LANES)),
         pltpu.SMEM((faults + 1,), jnp.int32),
-        pltpu.SemaphoreType.DMA((faults,)),
     ]
 
     def exchange(value, axis, distance):
         size = lax.axis_size(axis)
         return lax.ppermute(value, axis, [(i, i ^ distance) for i in range(size)])
+
+    inputs = (fault_sizes, rhs, friction, tile_row, tile_col, precond_blocks, kernel_tiles)
+    places = jax.ShapeDtypeStruct((1, slots), jnp.int32)
+    sent0, near_blocks, near_tiles, spots, target = pl.pallas_call(
+        functools.partial(first_kernel, (row_count, col_count)),
+        out_shape=[
+            grid,
+            pltpu.VMEM((faults, width, width), BF16),
+            pltpu.VMEM((slots, LANES, LANES), BF16),
+            places,
+            places,
+        ],
+        in_specs=[HBM] * 7,
+        out_specs=[VMEM] * 5,
+        scratch_shapes=[
+            pltpu.SMEM(fault_sizes.shape, jnp.int32),
+            scratch(rhs.shape),
+            scratch(friction.shape),
+            scratch(tile_row.shape, jnp.int32),
+            scratch(tile_col.shape, jnp.int32),
+            pltpu.SemaphoreType.DMA((5,)),
+            pltpu.SemaphoreType.DMA,
+            pltpu.SemaphoreType.DMA((3, faults)),
+        ]
+        + work,
+        compiler_params=PARAMS,
+        name="first",
+    )(*[pltpu.with_memory_space_constraint(a, pltpu.HBM) for a in inputs])
 
     def apply_kernel(sent):
         got = [sent] + [exchange(sent, "row", d) for d in range(1, row_count)]
         keep, give = pl.pallas_call(
             functools.partial(tiles_kernel, tiles % 8),
             out_shape=[half_grid, half_grid],
-            in_specs=[SMEM, VMEM, VMEM, HBM] + [VMEM] * row_count,
+            in_specs=[SMEM, SMEM, VMEM, VMEM, VMEM] + [VMEM] * row_count,
             out_specs=[VMEM] * 2,
             scratch_shapes=[
-                scratch((slots, LANES, LANES), BF16),
                 scratch((row_count * height, LANES)),
                 scratch((slots, LANES)),
                 scratch((slots, LANES)),
-                pltpu.SemaphoreType.DMA((slots // 16,)),
             ],
             compiler_params=PARAMS,
             name="tiles",
-        )(spots, target, weight, kernel_tiles, *got)
+        )(tile_counts, spots, target, tile_scale, near_tiles, *got)
         both = keep + exchange(give, "col", 1)
         return [both[0]] + [exchange(both[d], "col", 2 * d) for d in range(1, far)]
 
-    sent0 = pl.pallas_call(
-        first_kernel,
-        out_shape=grid,
-        in_specs=[HBM] * 4,
-        out_specs=VMEM,
-        scratch_shapes=[
-            pltpu.SMEM(fault_sizes.shape, jnp.int32),
-            scratch(rhs.shape),
-            scratch(friction.shape),
-            pltpu.SemaphoreType.DMA((3,)),
-        ]
-        + work,
-        compiler_params=PARAMS,
-        name="first",
-    )(*[pltpu.with_memory_space_constraint(a, pltpu.HBM) for a in (fault_sizes, rhs, friction)], precond_blocks)
     parts0 = apply_kernel(sent0)
     sent1, image0, basis = pl.pallas_call(
         second_kernel,
         out_shape=[grid, plain, grid],
-        in_specs=[SMEM, VMEM, VMEM, HBM] + [VMEM] * (1 + far),
+        in_specs=[SMEM, VMEM, VMEM, VMEM] + [VMEM] * (1 + far),
         out_specs=[VMEM] * 3,
         scratch_shapes=work,
         compiler_params=PARAMS,
         name="second",
-    )(fault_sizes, rhs, friction, precond_blocks, sent0, *parts0)
+    )(fault_sizes, rhs, friction, near_blocks, sent0, *parts0)
     parts1 = apply_kernel(sent1)
     sent2, image1 = pl.pallas_call(
         third_kernel,
         out_shape=[grid, plain],
-        in_specs=[SMEM, VMEM, VMEM, HBM] + [VMEM] * (2 + far),
+        in_specs=[SMEM, VMEM, VMEM, VMEM] + [VMEM] * (2 + far),
         out_specs=[VMEM] * 2,
         scratch_shapes=work,
         compiler_params=PARAMS,
         name="third",
-    )(fault_sizes, rhs, friction, precond_blocks, sent1, basis, *parts1)
+    )(fault_sizes, rhs, friction, near_blocks, sent1, basis, *parts1)
     parts2 = apply_kernel(sent2)
     devices = row_count * col_count
     image2, sums = pl.pallas_call(

time: 104 us -> 86.9 us (0.84)
  Pallas kernels: 45.6 us -> 29.4 us
  blocking collectives: 10.6 us -> 9.34 us
    pallas_call x3, Pallas kernels: 18.2 us -> 9.4 us  [apply_kernel(): pl.pallas_call(functools.partial(tiles_kernel, tiles % 8), out_shape=[hal...]
    pallas_call x1, Pallas kernels: 9 us -> 4.36 us  [local(): pl.pallas_call(third_kernel, out_shape=[grid, plain], in_specs=[SMEM, VME...]
    pallas_call x1, Pallas kernels: 8.94 us -> 4.43 us  [local(): pl.pallas_call(second_kernel, out_shape=[grid, plain, grid], in_specs=[SM...]
    pallas_call x1, Pallas kernels: 8.55 us -> 10.3 us  [local(): pl.pallas_call(functools.partial(first_kernel, (row_count, col_count)), o...]
    all_to_all x1, blocking collectives: 10.6 us -> 9.34 us  [local(): sums = lax.all_to_all(sums, ('row', 'col'), 0, 0, tiled=True)]
  transfers between devices with their start and end apart: 21 -> 21, of which waited for: 20 -> 17; matrix products, arithmetic and copies ran while one was open for 0% -> 0% of each run, Pallas kernels for 0% -> 0%
where the time goes in v4:
time: 86.9 us; the launch traced here: 86.3 us
  Pallas kernels  29.4 us (34%)
  starting transfers between devices  25.1 us (29%)
  waiting for transfers between devices  21 us (24%)
  blocking collectives  9.34 us (11%)
  between operations  1.45 us (2%)
    ppermute x21, starting transfers between devices, exchange(): return lax.ppermute(value, axis, [(i, i ^ distance) for i in range(size)])  25.1 us
    ppermute x21, waiting for transfers between devices, exchange(): return lax.ppermute(value, axis, [(i, i ^ distance) for i in range(size)])  21 us
    pallas_call x1, Pallas kernels, local(): pl.pallas_call(functools.partial(first_kernel, (row_count, col_count)), o...  10.3 us
    pallas_call x3, Pallas kernels, apply_kernel(): pl.pallas_call(functools.partial(tiles_kernel, tiles % 8), out_shape=[hal...  9.4 us
    all_to_all x1, blocking collectives, local(): sums = lax.all_to_all(sums, ('row', 'col'), 0, 0, tiled=True)  9.34 us
    pallas_call x1, Pallas kernels, local(): pl.pallas_call(second_kernel, out_shape=[grid, plain, grid], in_specs=[SM...  4.43 us
    pallas_call x1, Pallas kernels, local(): pl.pallas_call(third_kernel, out_shape=[grid, plain], in_specs=[SMEM, VME...  4.36 us
  transfers between devices with their start and end apart: 21, of which 17 were waited for; matrix products, arithmetic and copies ran while one was open for 0% of the time, Pallas kernels for 0%

profile of v4, /device:TPU:0, one launch (start us, length us, event | category | flops | bytes accessed | tf_op | source)
XLA Modules:
  0.0 86.3 jit_solution(17295147376767556722)
XLA Ops:
  0.6 0.0 copy-start
  0.6 0.0 copy-start.1
  0.7 0.0 copy-start.3
  0.7 0.0 copy-start.2
  0.7 10.3 %first.1 = (f32[40,128]{1,0:T(8,128)S(1)}, bf16[24,512,512]{2,1,0:T(8,128)(2,1)S(1)}, bf16[256,128,128]{2,1,0:T(8,128)(2,1)S(1)}, s32[1,256]{1,0:T(1,128)S(1)}, s32[1,256]{1,0:T(1,128)S(1)}) custom-call(s32[1,1,24]{2,1,0:T(1,128)} %sizes.3, f32[1,1,4608]{2,1,0:T(1,128)} %rhs.7, f32[1,1,4608]{2,1,0:T(1,128)} %friction.5, s32[1,1,256]{2,1,0:T(1,128)} %refs_3_.1, ...), custom_call_target="tpu_custom_call" | custom-call | tf_op jit(solution)/shard_map/first/pallas_call | solution.py:471
  11.0 3.1 %collective-permute-start.2 = (f32[40,128]{1,0:T(8,128)S(1)}, f32[40,128]{1,0:T(8,128)S(1)}, u32[]{:S(2)}, u32[]{:S(2)}) collective-permute-start(f32[40,128]{1,0:T(8,128)S(1)} %get-tuple-element.21.refs_0_.sent.sent0), channel_id=1, source_target_pairs={{0,24},{8,16},{16,8},{24,0},{1,25},{9,17},{17,9},{25,1},{2,26},{10... | collective-permute-start | bytes 61448 | tf_op jit(solution)/shard_map/ppermute | solution.py:467
  14.0 1.4 %collective-permute-start.1 = (f32[40,128]{1,0:T(8,128)S(1)}, f32[40,128]{1,0:T(8,128)S(1)}, u32[]{:S(2)}, u32[]{:S(2)}) collective-permute-start(f32[40,128]{1,0:T(8,128)S(1)} %get-tuple-element.21.refs_0_.sent.sent0), channel_id=1, source_target_pairs={{0,16},{8,24},{16,0},{24,8},{1,17},{9,25},{17,1},{25,9},{2,18},{10... | collective-permute-start | bytes 61448 | tf_op jit(solution)/shard_map/ppermute | solution.py:467
  15.5 0.0 collective-permute-start
  16.1 0.0 collective-permute-done.2.refs_3_
  16.1 1.7 %collective-permute-done.1.refs_2_ = f32[40,128]{1,0:T(8,128)S(1)} collective-permute-done((f32[40,128]{1,0:T(8,128)S(1)}, f32[40,128]{1,0:T(8,128)S(1)}, u32[]{:S(2)}, u32[]{:S(2)}) %collective-permute-start.1) | collective-permute-done | bytes 20512 | tf_op jit(solution)/shard_map/ppermute | solution.py:467
  17.8 1.4 %collective-permute-done.refs_1_ = f32[40,128]{1,0:T(8,128)S(1)} collective-permute-done((f32[40,128]{1,0:T(8,128)S(1)}, f32[40,128]{1,0:T(8,128)S(1)}, u32[]{:S(2)}, u32[]{:S(2)}) %collective-permute-start) | collective-permute-done | bytes 20512 | tf_op jit(solution)/shard_map/ppermute | solution.py:467
  19.2 0.0 copy-done.2
  19.2 3.1 %tiles.3 = (f32[4,40,128]{2,1,0:T(8,128)S(1)}, f32[4,40,128]{2,1,0:T(8,128)S(1)}) custom-call(s32[1,1]{1,0:T(1,128)S(6)} %copy.12.counts, s32[1,256]{1,0:T(1,128)S(1)} %get-tuple-element.22.spots, s32[1,256]{1,0:T(1,128)S(1)} %get-tuple-element.23.rows, f32[1,1,256]{2,1,0:T(1,128)S(1)} %copy-done.2, bf16[256,128,128]{2,1,0:T(8,128)(2,1)S(1)} %get-tuple-element.24.blocks, ...), custom_call_target="tpu_custom_call" | custom-call | tf_op jit(solution)/shard_map/tiles/pallas_call | solution.py:499
  22.4 0.1 collective-permute-start.3
  22.5 1.3 %collective-permute-done.3 = f32[4,40,128]{2,1,0:T(8,128)S(1)} collective-permute-done((f32[4,40,128]{2,1,0:T(8,128)S(1)}, f32[4,40,128]{2,1,0:T(8,128)S(1)}, u32[]{:S(2)}, u32[]{:S(2)}) %collective-permute-start.3) | collective-permute-done | bytes 81952 | tf_op jit(solution)/shard_map/ppermute | solution.py:467
  23.8 3.7 %collective-permute-start.6 = (f32[40,128]{1,0:T(8,128)S(1)}, f32[40,128]{1,0:T(8,128)S(1)}, u32[]{:S(2)}, u32[]{:S(2)}) collective-permute-start(f32[40,128]{1,0:T(8,128)S(1)} %get-tuple-element.46), channel_id=1, source_target_pairs={{0,6},{1,7},{2,4},{3,5},{4,2},{5,3},{6,0},{7,1},{8,14},{9,15},{10,... | collective-permute-start | bytes 61448 | tf_op jit(solution)/shard_map/ppermute | solution.py:467
  27.4 0.0 collective-permute-start.5
  27.4 0.8 collective-permute-start.4
  28.2 1.2 %collective-permute-done.6.refs_3_ = f32[40,128]{1,0:T(8,128)S(1)} collective-permute-done((f32[40,128]{1,0:T(8,128)S(1)}, f32[40,128]{1,0:T(8,128)S(1)}, u32[]{:S(2)}, u32[]{:S(2)}) %collective-permute-start.6) | collective-permute-done | bytes 20512 | tf_op jit(solution)/shard_map/ppermute | solution.py:467
  29.4 2.7 %collective-permute-done.5.refs_2_ = f32[40,128]{1,0:T(8,128)S(1)} collective-permute-done((f32[40,128]{1,0:T(8,128)S(1)}, f32[40,128]{1,0:T(8,128)S(1)}, u32[]{:S(2)}, u32[]{:S(2)}) %collective-permute-start.5) | collective-permute-done | bytes 20512 | tf_op jit(solution)/shard_map/ppermute | solution.py:467
  32.1 0.0 collective-permute-done.4.refs_1_
  32.1 0.0 copy-done
  32.1 0.0 copy-done.1
  32.1 0.0 copy-done.3
  32.1 4.4 %second.1 = (f32[40,128]{1,0:T(8,128)S(1)}, f32[36,128]{1,0:T(8,128)S(1)}, f32[40,128]{1,0:T(8,128)S(1)}) custom-call(s32[1,1,24]{2,1,0:T(1,128)S(1)} %copy-done.3, f32[1,1,4608]{2,1,0:T(1,128)S(1)} %copy-done, f32[1,1,4608]{2,1,0:T(1,128)S(1)} %copy-done.1, bf16[24,512,512]{2,1,0:T(8,128)(2,1)S(1)} %get-tuple-element.20.blocks, ...), custom_call_target="tpu_custom_call" | custom-call | tf_op jit(solution)/shard_map/second/pallas_call | solution.py:516
  36.6 0.2 collective-permute-start.9
  36.8 1.2 %collective-permute-start.8 = (f32[40,128]{1,0:T(8,128)S(1)}, f32[40,128]{1,0:T(8,128)S(1)}, u32[]{:S(2)}, u32[]{:S(2)}) collective-permute-start(f32[40,128]{1,0:T(8,128)S(1)} %get-tuple-element.27.refs_0_.sent.sent1), channel_id=1, source_target_pairs={{0,16},{8,24},{16,0},{24,8},{1,17},{9,25},{17,1},{25,9},{2,18},{10... | collective-permute-start | bytes 61448 | tf_op jit(solution)/shard_map/ppermute | solution.py:467
  38.0 2.0 %collective-permute-start.7 = (f32[40,128]{1,0:T(8,128)S(1)}, f32[40,128]{1,0:T(8,128)S(1)}, u32[]{:S(2)}, u32[]{:S(2)}) collective-permute-start(f32[40,128]{1,0:T(8,128)S(1)} %get-tuple-element.27.refs_0_.sent.sent1), channel_id=1, source_target_pairs={{0,8},{8,0},{16,24},{24,16},{1,9},{9,1},{17,25},{25,17},{2,10},{10... | collective-permute-start | bytes 61448 | tf_op jit(solution)/shard_map/ppermute | solution.py:467
  40.1 1.2 %collective-permute-done.9.refs_3_ = f32[40,128]{1,0:T(8,128)S(1)} collective-permute-done((f32[40,128]{1,0:T(8,128)S(1)}, f32[40,128]{1,0:T(8,128)S(1)}, u32[]{:S(2)}, u32[]{:S(2)}) %collective-permute-start.9) | collective-permute-done | bytes 20512 | tf_op jit(solution)/shard_map/ppermute | solution.py:467
  41.2 0.0 collective-permute-done.8.refs_2_
  41.2 0.6 collective-permute-done.7.refs_1_
  41.8 3.1 %tiles.4 = (f32[4,40,128]{2,1,0:T(8,128)S(1)}, f32[4,40,128]{2,1,0:T(8,128)S(1)}) custom-call(s32[1,1]{1,0:T(1,128)S(6)} %copy.12.counts, s32[1,256]{1,0:T(1,128)S(1)} %get-tuple-element.22.spots, s32[1,256]{1,0:T(1,128)S(1)} %get-tuple-element.23.rows, f32[1,1,256]{2,1,0:T(1,128)S(1)} %copy-done.2, bf16[256,128,128]{2,1,0:T(8,128)(2,1)S(1)} %get-tuple-element.24.blocks, ...), custom_call_target="tpu_custom_call" | custom-call | tf_op jit(solution)/shard_map/tiles/pallas_call | solution.py:499
  45.0 0.1 collective-permute-start.10
  45.0 1.3 %collective-permute-done.10 = f32[4,40,128]{2,1,0:T(8,128)S(1)} collective-permute-done((f32[4,40,128]{2,1,0:T(8,128)S(1)}, f32[4,40,128]{2,1,0:T(8,128)S(1)}, u32[]{:S(2)}, u32[]{:S(2)}) %collective-permute-start.10) | collective-permute-done | bytes 81952 | tf_op jit(solution)/shard_map/ppermute | solution.py:467
  46.3 1.6 %collective-permute-start.13 = (f32[40,128]{1,0:T(8,128)S(1)}, f32[40,128]{1,0:T(8,128)S(1)}, u32[]{:S(2)}, u32[]{:S(2)}) collective-permute-start(f32[40,128]{1,0:T(8,128)S(1)} %get-tuple-element.42), channel_id=1, source_target_pairs={{0,6},{1,7},{2,4},{3,5},{4,2},{5,3},{6,0},{7,1},{8,14},{9,15},{10,... | collective-permute-start | bytes 61448 | tf_op jit(solution)/shard_map/ppermute | solution.py:467
  47.9 0.6 collective-permute-start.12
  48.5 2.3 %collective-permute-start.11 = (f32[40,128]{1,0:T(8,128)S(1)}, f32[40,128]{1,0:T(8,128)S(1)}, u32[]{:S(2)}, u32[]{:S(2)}) collective-permute-start(f32[40,128]{1,0:T(8,128)S(1)} %get-tuple-element.44), channel_id=1, source_target_pairs={{0,2},{1,3},{2,0},{3,1},{4,6},{5,7},{6,4},{7,5},{8,10},{9,11},{10,... | collective-permute-start | bytes 61448 | tf_op jit(solution)/shard_map/ppermute | solution.py:467
  50.8 1.4 %collective-permute-done.13.refs_3_ = f32[40,128]{1,0:T(8,128)S(1)} collective-permute-done((f32[40,128]{1,0:T(8,128)S(1)}, f32[40,128]{1,0:T(8,128)S(1)}, u32[]{:S(2)}, u32[]{:S(2)}) %collective-permute-start.13) | collective-permute-done | bytes 20512 | tf_op jit(solution)/shard_map/ppermute | solution.py:467
  52.2 0.5 collective-permute-done.12.refs_2_
  52.6 0.1 collective-permute-done.11.refs_1_
  52.8 4.4 %third.1 = (f32[40,128]{1,0:T(8,128)S(1)}, f32[36,128]{1,0:T(8,128)S(1)}) custom-call(s32[1,1,24]{2,1,0:T(1,128)S(1)} %copy-done.3, f32[1,1,4608]{2,1,0:T(1,128)S(1)} %copy-done, f32[1,1,4608]{2,1,0:T(1,128)S(1)} %copy-done.1, bf16[24,512,512]{2,1,0:T(8,128)(2,1)S(1)} %get-tuple-element.20.blocks, f32[40,128]{1,0:T(8,128)S(1)} %get-tuple-element.27.refs_0_.sent.sent1, ...), custom_call_target="tpu_custom_call" | custom-call | tf_op jit(solution)/shard_map/third/pallas_call | solution.py:526
  57.1 1.4 %collective-permute-start.16 = (f32[40,128]{1,0:T(8,128)S(1)}, f32[40,128]{1,0:T(8,128)S(1)}, u32[]{:S(2)}, u32[]{:S(2)}) collective-permute-start(f32[40,128]{1,0:T(8,128)S(1)} %get-tuple-element.31.refs_0_.sent.sent2), channel_id=1, source_target_pairs={{0,24},{8,16},{16,8},{24,0},{1,25},{9,17},{17,9},{25,1},{2,26},{10... | collective-permute-start | bytes 61448 | tf_op jit(solution)/shard_map/ppermute | solution.py:467
  58.5 2.1 %collective-permute-start.15 = (f32[40,128]{1,0:T(8,128)S(1)}, f32[40,128]{1,0:T(8,128)S(1)}, u32[]{:S(2)}, u32[]{:S(2)}) collective-permute-start(f32[40,128]{1,0:T(8,128)S(1)} %get-tuple-element.31.refs_0_.sent.sent2), channel_id=1, source_target_pairs={{0,16},{8,24},{16,0},{24,8},{1,17},{9,25},{17,1},{25,9},{2,18},{10... | collective-permute-start | bytes 61448 | tf_op jit(solution)/shard_map/ppermute | solution.py:467
  60.6 0.1 collective-permute-start.14
  60.7 1.2 %collective-permute-done.16.refs_3_ = f32[40,128]{1,0:T(8,128)S(1)} collective-permute-done((f32[40,128]{1,0:T(8,128)S(1)}, f32[40,128]{1,0:T(8,128)S(1)}, u32[]{:S(2)}, u32[]{:S(2)}) %collective-permute-start.16) | collective-permute-done | bytes 20512 | tf_op jit(solution)/shard_map/ppermute | solution.py:467
  61.9 0.4 collective-permute-done.15.refs_2_
  62.3 2.0 %collective-permute-done.14.refs_1_ = f32[40,128]{1,0:T(8,128)S(1)} collective-permute-done((f32[40,128]{1,0:T(8,128)S(1)}, f32[40,128]{1,0:T(8,128)S(1)}, u32[]{:S(2)}, u32[]{:S(2)}) %collective-permute-start.14) | collective-permute-done | bytes 20512 | tf_op jit(solution)/shard_map/ppermute | solution.py:467
  64.3 3.1 %tiles.5 = (f32[4,40,128]{2,1,0:T(8,128)S(1)}, f32[4,40,128]{2,1,0:T(8,128)S(1)}) custom-call(s32[1,1]{1,0:T(1,128)S(6)} %copy.12.counts, s32[1,256]{1,0:T(1,128)S(1)} %get-tuple-element.22.spots, s32[1,256]{1,0:T(1,128)S(1)} %get-tuple-element.23.rows, f32[1,1,256]{2,1,0:T(1,128)S(1)} %copy-done.2, bf16[256,128,128]{2,1,0:T(8,128)(2,1)S(1)} %get-tuple-element.24.blocks, ...), custom_call_target="tpu_custom_call" | custom-call | tf_op jit(solution)/shard_map/tiles/pallas_call | solution.py:499
  67.5 0.1 collective-permute-start.17
  67.6 1.3 %collective-permute-done.17 = f32[4,40,128]{2,1,0:T(8,128)S(1)} collective-permute-done((f32[4,40,128]{2,1,0:T(8,128)S(1)}, f32[4,40,128]{2,1,0:T(8,128)S(1)}, u32[]{:S(2)}, u32[]{:S(2)}) %collective-permute-start.17) | collective-permute-done | bytes 81952 | tf_op jit(solution)/shard_map/ppermute | solution.py:467
  68.9 2.6 %collective-permute-start.20 = (f32[40,128]{1,0:T(8,128)S(1)}, f32[40,128]{1,0:T(8,128)S(1)}, u32[]{:S(2)}, u32[]{:S(2)}) collective-permute-start(f32[40,128]{1,0:T(8,128)S(1)} %get-tuple-element.38), channel_id=1, source_target_pairs={{0,6},{1,7},{2,4},{3,5},{4,2},{5,3},{6,0},{7,1},{8,14},{9,15},{10,... | collective-permute-start | bytes 61448 | tf_op jit(solution)/shard_map/ppermute | solution.py:467
  71.4 0.5 collective-permute-start.19
  71.9 1.5 %collective-permute-start.18 = (f32[40,128]{1,0:T(8,128)S(1)}, f32[40,128]{1,0:T(8,128)S(1)}, u32[]{:S(2)}, u32[]{:S(2)}) collective-permute-start(f32[40,128]{1,0:T(8,128)S(1)} %get-tuple-element.40), channel_id=1, source_target_pairs={{0,2},{1,3},{2,0},{3,1},{4,6},{5,7},{6,4},{7,5},{8,10},{9,11},{10,... | collective-permute-start | bytes 61448 | tf_op jit(solution)/shard_map/ppermute | solution.py:467
  73.3 1.2 %collective-permute-done.20.refs_3_ = f32[40,128]{1,0:T(8,128)S(1)} collective-permute-done((f32[40,128]{1,0:T(8,128)S(1)}, f32[40,128]{1,0:T(8,128)S(1)}, u32[]{:S(2)}, u32[]{:S(2)}) %collective-permute-start.20) | collective-permute-done | bytes 20512 | tf_op jit(solution)/shard_map/ppermute | solution.py:467
  74.5 1.6 %collective-permute-done.19.refs_2_ = f32[40,128]{1,0:T(8,128)S(1)} collective-permute-done((f32[40,128]{1,0:T(8,128)S(1)}, f32[40,128]{1,0:T(8,128)S(1)}, u32[]{:S(2)}, u32[]{:S(2)}) %collective-permute-start.19) | collective-permute-done | bytes 20512 | tf_op jit(solution)/shard_map/ppermute | solution.py:467
  76.1 0.0 collective-permute-done.18.refs_1_
  76.1 0.1 fourth.1
  76.2 9.3 %all_to_all.11 = f32[32,1,128]{2,1,0:T(1,128)S(1)} all-to-all(f32[32,1,128]{2,1,0:T(1,128)S(1)} %bitcast.29), channel_id=1, replica_groups=mesh['row'=4,'col'=8] {'row','col'}, dimensions={0} | all-to-all | bytes 32768 | tf_op jit(solution)/shard_map/all_to_all | solution.py:545
  85.5 0.8 last.1
  (6 shorter events, 0.1 us)
Async XLA Ops:
  0.6 31.5 %copy-start = (f32[1,1,4608]{2,1,0:T(1,128)S(1)}, f32[1,1,4608]{2,1,0:T(1,128)}, u32[]{:S(2)}) copy-start(f32[1,1,4608]{2,1,0:T(1,128)} %rhs.7) | copy-start | bytes 55300
  0.6 31.5 %copy-start.1 = (f32[1,1,4608]{2,1,0:T(1,128)S(1)}, f32[1,1,4608]{2,1,0:T(1,128)}, u32[]{:S(2)}) copy-start(f32[1,1,4608]{2,1,0:T(1,128)} %friction.5) | copy-start | bytes 55300
  0.7 31.5 %copy-start.3 = (s32[1,1,24]{2,1,0:T(1,128)S(1)}, s32[1,1,24]{2,1,0:T(1,128)}, u32[]{:S(2)}) copy-start(s32[1,1,24]{2,1,0:T(1,128)} %sizes.3) | copy-start | bytes 292
  0.7 18.6 %copy-start.2 = (f32[1,1,256]{2,1,0:T(1,128)S(1)}, f32[1,1,256]{2,1,0:T(1,128)}, u32[]{:S(2)}) copy-start(f32[1,1,256]{2,1,0:T(1,128)} %scale.5) | copy-start | bytes 3076
  11.0 5.1 %collective-permute-start.2 = (f32[40,128]{1,0:T(8,128)S(1)}, f32[40,128]{1,0:T(8,128)S(1)}, u32[]{:S(2)}, u32[]{:S(2)}) collective-permute-start(f32[40,128]{1,0:T(8,128)S(1)} %get-tuple-element.21.refs_0_.sent.sent0), channel_id=1, source_target_pairs={{0,24},{8,16},{16,8},{24,0},{1,25},{9,17},{17,9},{25,1},{2,26},{10... | collective-permute-start | bytes 61448 | tf_op jit(solution)/shard_map/ppermute | solution.py:467
  14.0 3.8 %collective-permute-start.1 = (f32[40,128]{1,0:T(8,128)S(1)}, f32[40,128]{1,0:T(8,128)S(1)}, u32[]{:S(2)}, u32[]{:S(2)}) collective-permute-start(f32[40,128]{1,0:T(8,128)S(1)} %get-tuple-element.21.refs_0_.sent.sent0), channel_id=1, source_target_pairs={{0,16},{8,24},{16,0},{24,8},{1,17},{9,25},{17,1},{25,9},{2,18},{10... | collective-permute-start | bytes 61448 | tf_op jit(solution)/shard_map/ppermute | solution.py:467
  15.5 3.8 %collective-permute-start = (f32[40,128]{1,0:T(8,128)S(1)}, f32[40,128]{1,0:T(8,128)S(1)}, u32[]{:S(2)}, u32[]{:S(2)}) collective-permute-start(f32[40,128]{1,0:T(8,128)S(1)} %get-tuple-element.21.refs_0_.sent.sent0), channel_id=1, source_target_pairs={{0,8},{8,0},{16,24},{24,16},{1,9},{9,1},{17,25},{25,17},{2,10},{10... | collective-permute-start | bytes 61448 | tf_op jit(solution)/shard_map/ppermute | solution.py:467
  22.4 1.3 %collective-permute-start.3 = (f32[4,40,128]{2,1,0:T(8,128)S(1)}, f32[4,40,128]{2,1,0:T(8,128)S(1)}, u32[]{:S(2)}, u32[]{:S(2)}) collective-permute-start(f32[4,40,128]{2,1,0:T(8,128)S(1)} %get-tuple-element.26), channel_id=1, source_target_pairs={{0,1},{1,0},{2,3},{3,2},{4,5},{5,4},{6,7},{7,6},{8,9},{9,8},{10,11... | collective-permute-start | bytes 245768 | tf_op jit(solution)/shard_map/ppermute | solution.py:467
  23.8 5.6 %collective-permute-start.6 = (f32[40,128]{1,0:T(8,128)S(1)}, f32[40,128]{1,0:T(8,128)S(1)}, u32[]{:S(2)}, u32[]{:S(2)}) collective-permute-start(f32[40,128]{1,0:T(8,128)S(1)} %get-tuple-element.46), channel_id=1, source_target_pairs={{0,6},{1,7},{2,4},{3,5},{4,2},{5,3},{6,0},{7,1},{8,14},{9,15},{10,... | collective-permute-start | bytes 61448 | tf_op jit(solution)/shard_map/ppermute | solution.py:467
  27.4 4.7 %collective-permute-start.5 = (f32[40,128]{1,0:T(8,128)S(1)}, f32[40,128]{1,0:T(8,128)S(1)}, u32[]{:S(2)}, u32[]{:S(2)}) collective-permute-start(f32[40,128]{1,0:T(8,128)S(1)} %get-tuple-element.47), channel_id=1, source_target_pairs={{0,4},{1,5},{2,6},{3,7},{4,0},{5,1},{6,2},{7,3},{8,12},{9,13},{10,... | collective-permute-start | bytes 61448 | tf_op jit(solution)/shard_map/ppermute | solution.py:467
  27.4 4.7 %collective-permute-start.4 = (f32[40,128]{1,0:T(8,128)S(1)}, f32[40,128]{1,0:T(8,128)S(1)}, u32[]{:S(2)}, u32[]{:S(2)}) collective-permute-start(f32[40,128]{1,0:T(8,128)S(1)} %get-tuple-element.48), channel_id=1, source_target_pairs={{0,2},{1,3},{2,0},{3,1},{4,6},{5,7},{6,4},{7,5},{8,10},{9,11},{10,... | collective-permute-start | bytes 61448 | tf_op jit(solution)/shard_map/ppermute | solution.py:467
  36.6 4.7 %collective-permute-start.9 = (f32[40,128]{1,0:T(8,128)S(1)}, f32[40,128]{1,0:T(8,128)S(1)}, u32[]{:S(2)}, u32[]{:S(2)}) collective-permute-start(f32[40,128]{1,0:T(8,128)S(1)} %get-tuple-element.27.refs_0_.sent.sent1), channel_id=1, source_target_pairs={{0,24},{8,16},{16,8},{24,0},{1,25},{9,17},{17,9},{25,1},{2,26},{10... | collective-permute-start | bytes 61448 | tf_op jit(solution)/shard_map/ppermute | solution.py:467
  36.8 4.4 %collective-permute-start.8 = (f32[40,128]{1,0:T(8,128)S(1)}, f32[40,128]{1,0:T(8,128)S(1)}, u32[]{:S(2)}, u32[]{:S(2)}) collective-permute-start(f32[40,128]{1,0:T(8,128)S(1)} %get-tuple-element.27.refs_0_.sent.sent1), channel_id=1, source_target_pairs={{0,16},{8,24},{16,0},{24,8},{1,17},{9,25},{17,1},{25,9},{2,18},{10... | collective-permute-start | bytes 61448 | tf_op jit(solution)/shard_map/ppermute | solution.py:467
  38.0 3.8 %collective-permute-start.7 = (f32[40,128]{1,0:T(8,128)S(1)}, f32[40,128]{1,0:T(8,128)S(1)}, u32[]{:S(2)}, u32[]{:S(2)}) collective-permute-start(f32[40,128]{1,0:T(8,128)S(1)} %get-tuple-element.27.refs_0_.sent.sent1), channel_id=1, source_target_pairs={{0,8},{8,0},{16,24},{24,16},{1,9},{9,1},{17,25},{25,17},{2,10},{10... | collective-permute-start | bytes 61448 | tf_op jit(solution)/shard_map/ppermute | solution.py:467
  45.0 1.3 %collective-permute-start.10 = (f32[4,40,128]{2,1,0:T(8,128)S(1)}, f32[4,40,128]{2,1,0:T(8,128)S(1)}, u32[]{:S(2)}, u32[]{:S(2)}) collective-permute-start(f32[4,40,128]{2,1,0:T(8,128)S(1)} %get-tuple-element.30), channel_id=1, source_target_pairs={{0,1},{1,0},{2,3},{3,2},{4,5},{5,4},{6,7},{7,6},{8,9},{9,8},{10,11... | collective-permute-start | bytes 245768 | tf_op jit(solution)/shard_map/ppermute | solution.py:467
  46.3 5.8 %collective-permute-start.13 = (f32[40,128]{1,0:T(8,128)S(1)}, f32[40,128]{1,0:T(8,128)S(1)}, u32[]{:S(2)}, u32[]{:S(2)}) collective-permute-start(f32[40,128]{1,0:T(8,128)S(1)} %get-tuple-element.42), channel_id=1, source_target_pairs={{0,6},{1,7},{2,4},{3,5},{4,2},{5,3},{6,0},{7,1},{8,14},{9,15},{10,... | collective-permute-start | bytes 61448 | tf_op jit(solution)/shard_map/ppermute | solution.py:467
  47.9 4.7 %collective-permute-start.12 = (f32[40,128]{1,0:T(8,128)S(1)}, f32[40,128]{1,0:T(8,128)S(1)}, u32[]{:S(2)}, u32[]{:S(2)}) collective-permute-start(f32[40,128]{1,0:T(8,128)S(1)} %get-tuple-element.43), channel_id=1, source_target_pairs={{0,4},{1,5},{2,6},{3,7},{4,0},{5,1},{6,2},{7,3},{8,12},{9,13},{10,... | collective-permute-start | bytes 61448 | tf_op jit(solution)/shard_map/ppermute | solution.py:467
  48.5 4.3 %collective-permute-start.11 = (f32[40,128]{1,0:T(8,128)S(1)}, f32[40,128]{1,0:T(8,128)S(1)}, u32[]{:S(2)}, u32[]{:S(2)}) collective-permute-start(f32[40,128]{1,0:T(8,128)S(1)} %get-tuple-element.44), channel_id=1, source_target_pairs={{0,2},{1,3},{2,0},{3,1},{4,6},{5,7},{6,4},{7,5},{8,10},{9,11},{10,... | collective-permute-start | bytes 61448 | tf_op jit(solution)/shard_map/ppermute | solution.py:467
  57.1 4.7 %collective-permute-start.16 = (f32[40,128]{1,0:T(8,128)S(1)}, f32[40,128]{1,0:T(8,128)S(1)}, u32[]{:S(2)}, u32[]{:S(2)}) collective-permute-start(f32[40,128]{1,0:T(8,128)S(1)} %get-tuple-element.31.refs_0_.sent.sent2), channel_id=1, source_target_pairs={{0,24},{8,16},{16,8},{24,0},{1,25},{9,17},{17,9},{25,1},{2,26},{10... | collective-permute-start | bytes 61448 | tf_op jit(solution)/shard_map/ppermute | solution.py:467
  58.5 3.8 %collective-permute-start.15 = (f32[40,128]{1,0:T(8,128)S(1)}, f32[40,128]{1,0:T(8,128)S(1)}, u32[]{:S(2)}, u32[]{:S(2)}) collective-permute-start(f32[40,128]{1,0:T(8,128)S(1)} %get-tuple-element.31.refs_0_.sent.sent2), channel_id=1, source_target_pairs={{0,16},{8,24},{16,0},{24,8},{1,17},{9,25},{17,1},{25,9},{2,18},{10... | collective-permute-start | bytes 61448 | tf_op jit(solution)/shard_map/ppermute | solution.py:467
  60.6 3.8 %collective-permute-start.14 = (f32[40,128]{1,0:T(8,128)S(1)}, f32[40,128]{1,0:T(8,128)S(1)}, u32[]{:S(2)}, u32[]{:S(2)}) collective-permute-start(f32[40,128]{1,0:T(8,128)S(1)} %get-tuple-element.31.refs_0_.sent.sent2), channel_id=1, source_target_pairs={{0,8},{8,0},{16,24},{24,16},{1,9},{9,1},{17,25},{25,17},{2,10},{10... | collective-permute-start | bytes 61448 | tf_op jit(solution)/shard_map/ppermute | solution.py:467
  67.5 1.3 %collective-permute-start.17 = (f32[4,40,128]{2,1,0:T(8,128)S(1)}, f32[4,40,128]{2,1,0:T(8,128)S(1)}, u32[]{:S(2)}, u32[]{:S(2)}) collective-permute-start(f32[4,40,128]{2,1,0:T(8,128)S(1)} %get-tuple-element.35), channel_id=1, source_target_pairs={{0,1},{1,0},{2,3},{3,2},{4,5},{5,4},{6,7},{7,6},{8,9},{9,8},{10,11... | collective-permute-start | bytes 245768 | tf_op jit(solution)/shard_map/ppermute | solution.py:467
  68.9 5.6 %collective-permute-start.20 = (f32[40,128]{1,0:T(8,128)S(1)}, f32[40,128]{1,0:T(8,128)S(1)}, u32[]{:S(2)}, u32[]{:S(2)}) collective-permute-start(f32[40,128]{1,0:T(8,128)S(1)} %get-tuple-element.38), channel_id=1, source_target_pairs={{0,6},{1,7},{2,4},{3,5},{4,2},{5,3},{6,0},{7,1},{8,14},{9,15},{10,... | collective-permute-start | bytes 61448 | tf_op jit(solution)/shard_map/ppermute | solution.py:467
  71.4 4.7 %collective-permute-start.19 = (f32[40,128]{1,0:T(8,128)S(1)}, f32[40,128]{1,0:T(8,128)S(1)}, u32[]{:S(2)}, u32[]{:S(2)}) collective-permute-start(f32[40,128]{1,0:T(8,128)S(1)} %get-tuple-element.39), channel_id=1, source_target_pairs={{0,4},{1,5},{2,6},{3,7},{4,0},{5,1},{6,2},{7,3},{8,12},{9,13},{10,... | collective-permute-start | bytes 61448 | tf_op jit(solution)/shard_map/ppermute | solution.py:467
  71.9 4.2 %collective-permute-start.18 = (f32[40,128]{1,0:T(8,128)S(1)}, f32[40,128]{1,0:T(8,128)S(1)}, u32[]{:S(2)}, u32[]{:S(2)}) collective-permute-start(f32[40,128]{1,0:T(8,128)S(1)} %get-tuple-element.40), channel_id=1, source_target_pairs={{0,2},{1,3},{2,0},{3,1},{4,6},{5,7},{6,4},{7,5},{8,10},{9,11},{10,... | collective-permute-start | bytes 61448 | tf_op jit(solution)/shard_map/ppermute | solution.py:467

commit v5 on v4

--- a/solution.py
+++ b/solution.py
@@ -213,22 +213,20 @@
 
 
 def first_kernel(shape, *refs):
-    (blocks, far_tiles, send, near_blocks, near_tiles, spots, target) = refs[5:12]
-    (sizes, rhs, friction, tile_row, tile_col) = refs[12:17]
-    (sems, tiles_sem, block_sems, field, *work) = refs[17:]
+    (blocks, send, near_blocks, spots, target) = refs[5:10]
+    (sizes, rhs, friction, tile_row, tile_col) = refs[10:15]
+    (sems, block_sems, field, *work) = refs[15:]
     work = work + [near_blocks, block_sems]
     row_count, col_count = shape
     tiles = rhs.shape[2] // LANES
     height = send.shape[0]
-    pairs = list(zip(refs[:5], refs[12:17]))
+    pairs = list(zip(refs[:5], refs[10:15]))
     copies = [pltpu.make_async_copy(a, b, sems.at[i]) for i, (a, b) in enumerate(pairs)]
     for copy in copies:
         copy.start()
-    whole = pltpu.make_async_copy(far_tiles.at[0, 0], near_tiles, tiles_sem)
     copies[0].wait()
 
     def value_to_field():
-        whole.start()
         copies[1].wait()
         set_field(field, load_rows(rhs, tiles))
         for copy in copies[3:]:
@@ -244,7 +242,6 @@
 
     direction = precondition(sizes, blocks, field, work, value_to_field)[0:tiles]
     copies[2].wait()
-    whole.wait()
     value = field[0:tiles, :]
     scaled = load_rows(friction, tiles) * direction
     send[...] = jnp.zeros_like(send)
@@ -466,19 +463,19 @@
         size = lax.axis_size(axis)
         return lax.ppermute(value, axis, [(i, i ^ distance) for i in range(size)])
 
-    inputs = (fault_sizes, rhs, friction, tile_row, tile_col, precond_blocks, kernel_tiles)
+    near_tiles = kernel_tiles.reshape(slots, LANES, LANES)
+    inputs = (fault_sizes, rhs, friction, tile_row, tile_col, precond_blocks)
     places = jax.ShapeDtypeStruct((1, slots), jnp.int32)
-    sent0, near_blocks, near_tiles, spots, target = pl.pallas_call(
+    sent0, near_blocks, spots, target = pl.pallas_call(
         functools.partial(first_kernel, (row_count, col_count)),
         out_shape=[
             grid,
             pltpu.VMEM((faults, width, width), BF16),
-            pltpu.VMEM((slots, LANES, LANES), BF16),
             places,
             places,
         ],
-        in_specs=[HBM] * 7,
-        out_specs=[VMEM] * 5,
+        in_specs=[HBM] * 6,
+        out_specs=[VMEM] * 4,
         scratch_shapes=[
             pltpu.SMEM(fault_sizes.shape, jnp.int32),
             scratch(rhs.shape),
@@ -486,7 +483,6 @@
             scratch(tile_row.shape, jnp.int32),
             scratch(tile_col.shape, jnp.int32),
             pltpu.SemaphoreType.DMA((5,)),
-            pltpu.SemaphoreType.DMA,
             pltpu.SemaphoreType.DMA((3, faults)),
         ]
         + work,

time: 86.9 us -> 87.8 us (1.010)
  blocking collectives: 9.34 us -> 10.3 us
    all_to_all x1, blocking collectives: 9.34 us -> 10.3 us  [local(): sums = lax.all_to_all(sums, ('row', 'col'), 0, 0, tiled=True)]
  transfers between devices with their start and end apart: 21 -> 21, of which waited for: 17 -> 19; matrix products, arithmetic and copies ran while one was open for 0% -> 0% of each run, Pallas kernels for 0% -> 0%
where the time goes in v5:
time: 87.8 us; the launch traced here: 87.7 us
  Pallas kernels  29.8 us (34%)
  starting transfers between devices  25.2 us (29%)
  waiting for transfers between devices  20.9 us (24%)
  blocking collectives  10.3 us (12%)
  between operations  1.45 us (2%)
    ppermute x21, starting transfers between devices, exchange(): return lax.ppermute(value, axis, [(i, i ^ distance) for i in range(size)])  25.2 us
    ppermute x21, waiting for transfers between devices, exchange(): return lax.ppermute(value, axis, [(i, i ^ distance) for i in range(size)])  20.9 us
    pallas_call x1, Pallas kernels, local(): pl.pallas_call(functools.partial(first_kernel, (row_count, col_count)), o...  10.7 us
    all_to_all x1, blocking collectives, local(): sums = lax.all_to_all(sums, ('row', 'col'), 0, 0, tiled=True)  10.3 us
    pallas_call x3, Pallas kernels, apply_kernel(): pl.pallas_call(functools.partial(tiles_kernel, tiles % 8), out_shape=[hal...  9.41 us
    pallas_call x1, Pallas kernels, local(): pl.pallas_call(second_kernel, out_shape=[grid, plain, grid], in_specs=[SM...  4.43 us
    pallas_call x1, Pallas kernels, local(): pl.pallas_call(third_kernel, out_shape=[grid, plain], in_specs=[SMEM, VME...  4.36 us
  transfers between devices with their start and end apart: 21, of which 19 were waited for; matrix products, arithmetic and copies ran while one was open for 0% of the time, Pallas kernels for 0%

profile of v5, /device:TPU:0, one launch (start us, length us, event | category | flops | bytes accessed | tf_op | source)
XLA Modules:
  0.0 87.7 jit_solution(2716262869250232007)
XLA Ops:
  0.6 0.0 copy-start.1
  0.6 0.0 copy-start.2
  0.7 0.0 copy-start.4
  0.7 0.0 copy-start.3
  0.7 0.0 copy-start
  0.7 10.7 %first.1 = (f32[40,128]{1,0:T(8,128)S(1)}, bf16[24,512,512]{2,1,0:T(8,128)(2,1)S(1)}, s32[1,256]{1,0:T(1,128)S(1)}, s32[1,256]{1,0:T(1,128)S(1)}) custom-call(s32[1,1,24]{2,1,0:T(1,128)} %sizes.3, f32[1,1,4608]{2,1,0:T(1,128)} %rhs.7, f32[1,1,4608]{2,1,0:T(1,128)} %friction.5, s32[1,1,256]{2,1,0:T(1,128)} %refs_3_.1, s32[1,1,256]{2,1,0:T(1,128)} %refs_4_.1, ...), custom_call_target="tpu_custom_call" | custom-call | tf_op jit(solution)/shard_map/first/pallas_call | solution.py:469
  11.4 4.0 %collective-permute-start.2 = (f32[40,128]{1,0:T(8,128)S(1)}, f32[40,128]{1,0:T(8,128)S(1)}, u32[]{:S(2)}, u32[]{:S(2)}) collective-permute-start(f32[40,128]{1,0:T(8,128)S(1)} %get-tuple-element.20.refs_0_.sent.sent0), channel_id=1, source_target_pairs={{0,24},{8,16},{16,8},{24,0},{1,25},{9,17},{17,9},{25,1},{2,26},{10... | collective-permute-start | bytes 61448 | tf_op jit(solution)/shard_map/ppermute | solution.py:464
  15.4 0.5 collective-permute-start.1
  15.9 0.1 collective-permute-start
  16.7 0.5 collective-permute-done.2.refs_3_
  17.1 2.0 %collective-permute-done.1.refs_2_ = f32[40,128]{1,0:T(8,128)S(1)} collective-permute-done((f32[40,128]{1,0:T(8,128)S(1)}, f32[40,128]{1,0:T(8,128)S(1)}, u32[]{:S(2)}, u32[]{:S(2)}) %collective-permute-start.1) | collective-permute-done | bytes 20512 | tf_op jit(solution)/shard_map/ppermute | solution.py:464
  19.2 0.5 collective-permute-done.refs_1_
  19.7 0.0 copy-done.3
  19.7 0.0 copy-done
  19.7 3.1 %tiles.3 = (f32[4,40,128]{2,1,0:T(8,128)S(1)}, f32[4,40,128]{2,1,0:T(8,128)S(1)}) custom-call(s32[1,1]{1,0:T(1,128)S(6)} %copy.12.counts, s32[1,256]{1,0:T(1,128)S(1)} %get-tuple-element.21.spots, s32[1,256]{1,0:T(1,128)S(1)} %get-tuple-element.22.rows, f32[1,1,256]{2,1,0:T(1,128)S(1)} %copy-done.3, bf16[256,128,128]{2,1,0:T(8,128)(2,1)S(1)} %bitcast.29, ...), custom_call_target="tpu_custom_call" | custom-call | tf_op jit(solution)/shard_map/tiles/pallas_call | solution.py:495
  22.8 0.1 collective-permute-start.3
  22.9 1.3 %collective-permute-done.3 = f32[4,40,128]{2,1,0:T(8,128)S(1)} collective-permute-done((f32[4,40,128]{2,1,0:T(8,128)S(1)}, f32[4,40,128]{2,1,0:T(8,128)S(1)}, u32[]{:S(2)}, u32[]{:S(2)}) %collective-permute-start.3) | collective-permute-done | bytes 81952 | tf_op jit(solution)/shard_map/ppermute | solution.py:464
  24.2 3.7 %collective-permute-start.6 = (f32[40,128]{1,0:T(8,128)S(1)}, f32[40,128]{1,0:T(8,128)S(1)}, u32[]{:S(2)}, u32[]{:S(2)}) collective-permute-start(f32[40,128]{1,0:T(8,128)S(1)} %get-tuple-element.44), channel_id=1, source_target_pairs={{0,6},{1,7},{2,4},{3,5},{4,2},{5,3},{6,0},{7,1},{8,14},{9,15},{10,... | collective-permute-start | bytes 61448 | tf_op jit(solution)/shard_map/ppermute | solution.py:464
  27.9 0.0 collective-permute-start.5
  27.9 0.8 collective-permute-start.4
  28.6 1.2 %collective-permute-done.6.refs_3_ = f32[40,128]{1,0:T(8,128)S(1)} collective-permute-done((f32[40,128]{1,0:T(8,128)S(1)}, f32[40,128]{1,0:T(8,128)S(1)}, u32[]{:S(2)}, u32[]{:S(2)}) %collective-permute-start.6) | collective-permute-done | bytes 20512 | tf_op jit(solution)/shard_map/ppermute | solution.py:464
  29.8 2.7 %collective-permute-done.5.refs_2_ = f32[40,128]{1,0:T(8,128)S(1)} collective-permute-done((f32[40,128]{1,0:T(8,128)S(1)}, f32[40,128]{1,0:T(8,128)S(1)}, u32[]{:S(2)}, u32[]{:S(2)}) %collective-permute-start.5) | collective-permute-done | bytes 20512 | tf_op jit(solution)/shard_map/ppermute | solution.py:464
  32.5 0.0 collective-permute-done.4.refs_1_
  32.5 0.0 copy-done.1
  32.5 0.0 copy-done.2
  32.5 0.0 copy-done.4
  32.6 4.4 %second.1 = (f32[40,128]{1,0:T(8,128)S(1)}, f32[36,128]{1,0:T(8,128)S(1)}, f32[40,128]{1,0:T(8,128)S(1)}) custom-call(s32[1,1,24]{2,1,0:T(1,128)S(1)} %copy-done.4, f32[1,1,4608]{2,1,0:T(1,128)S(1)} %copy-done.1, f32[1,1,4608]{2,1,0:T(1,128)S(1)} %copy-done.2, bf16[24,512,512]{2,1,0:T(8,128)(2,1)S(1)} %get-tuple-element.19.blocks, ...), custom_call_target="tpu_custom_call" | custom-call | tf_op jit(solution)/shard_map/second/pallas_call | solution.py:512
  37.0 1.5 %collective-permute-start.9 = (f32[40,128]{1,0:T(8,128)S(1)}, f32[40,128]{1,0:T(8,128)S(1)}, u32[]{:S(2)}, u32[]{:S(2)}) collective-permute-start(f32[40,128]{1,0:T(8,128)S(1)} %get-tuple-element.25.refs_0_.sent.sent1), channel_id=1, source_target_pairs={{0,24},{8,16},{16,8},{24,0},{1,25},{9,17},{17,9},{25,1},{2,26},{10... | collective-permute-start | bytes 61448 | tf_op jit(solution)/shard_map/ppermute | solution.py:464
  38.5 0.5 collective-permute-start.8
  39.0 1.5 %collective-permute-start.7 = (f32[40,128]{1,0:T(8,128)S(1)}, f32[40,128]{1,0:T(8,128)S(1)}, u32[]{:S(2)}, u32[]{:S(2)}) collective-permute-start(f32[40,128]{1,0:T(8,128)S(1)} %get-tuple-element.25.refs_0_.sent.sent1), channel_id=1, source_target_pairs={{0,8},{8,0},{16,24},{24,16},{1,9},{9,1},{17,25},{25,17},{2,10},{10... | collective-permute-start | bytes 61448 | tf_op jit(solution)/shard_map/ppermute | solution.py:464
  40.5 1.2 %collective-permute-done.9.refs_3_ = f32[40,128]{1,0:T(8,128)S(1)} collective-permute-done((f32[40,128]{1,0:T(8,128)S(1)}, f32[40,128]{1,0:T(8,128)S(1)}, u32[]{:S(2)}, u32[]{:S(2)}) %collective-permute-start.9) | collective-permute-done | bytes 20512 | tf_op jit(solution)/shard_map/ppermute | solution.py:464
  41.7 0.6 collective-permute-done.8.refs_2_
  42.3 0.5 collective-permute-done.7.refs_1_
  42.8 3.1 %tiles.4 = (f32[4,40,128]{2,1,0:T(8,128)S(1)}, f32[4,40,128]{2,1,0:T(8,128)S(1)}) custom-call(s32[1,1]{1,0:T(1,128)S(6)} %copy.12.counts, s32[1,256]{1,0:T(1,128)S(1)} %get-tuple-element.21.spots, s32[1,256]{1,0:T(1,128)S(1)} %get-tuple-element.22.rows, f32[1,1,256]{2,1,0:T(1,128)S(1)} %copy-done.3, bf16[256,128,128]{2,1,0:T(8,128)(2,1)S(1)} %bitcast.30, ...), custom_call_target="tpu_custom_call" | custom-call | tf_op jit(solution)/shard_map/tiles/pallas_call | solution.py:495
  45.9 0.1 collective-permute-start.10
  46.0 1.3 %collective-permute-done.10 = f32[4,40,128]{2,1,0:T(8,128)S(1)} collective-permute-done((f32[4,40,128]{2,1,0:T(8,128)S(1)}, f32[4,40,128]{2,1,0:T(8,128)S(1)}, u32[]{:S(2)}, u32[]{:S(2)}) %collective-permute-start.10) | collective-permute-done | bytes 81952 | tf_op jit(solution)/shard_map/ppermute | solution.py:464
  47.3 1.5 %collective-permute-start.13 = (f32[40,128]{1,0:T(8,128)S(1)}, f32[40,128]{1,0:T(8,128)S(1)}, u32[]{:S(2)}, u32[]{:S(2)}) collective-permute-start(f32[40,128]{1,0:T(8,128)S(1)} %get-tuple-element.40), channel_id=1, source_target_pairs={{0,6},{1,7},{2,4},{3,5},{4,2},{5,3},{6,0},{7,1},{8,14},{9,15},{10,... | collective-permute-start | bytes 61448 | tf_op jit(solution)/shard_map/ppermute | solution.py:464
  48.8 0.6 collective-permute-start.12
  49.4 2.3 %collective-permute-start.11 = (f32[40,128]{1,0:T(8,128)S(1)}, f32[40,128]{1,0:T(8,128)S(1)}, u32[]{:S(2)}, u32[]{:S(2)}) collective-permute-start(f32[40,128]{1,0:T(8,128)S(1)} %get-tuple-element.42), channel_id=1, source_target_pairs={{0,2},{1,3},{2,0},{3,1},{4,6},{5,7},{6,4},{7,5},{8,10},{9,11},{10,... | collective-permute-start | bytes 61448 | tf_op jit(solution)/shard_map/ppermute | solution.py:464
  51.7 1.4 %collective-permute-done.13.refs_3_ = f32[40,128]{1,0:T(8,128)S(1)} collective-permute-done((f32[40,128]{1,0:T(8,128)S(1)}, f32[40,128]{1,0:T(8,128)S(1)}, u32[]{:S(2)}, u32[]{:S(2)}) %collective-permute-start.13) | collective-permute-done | bytes 20512 | tf_op jit(solution)/shard_map/ppermute | solution.py:464
  53.1 0.4 collective-permute-done.12.refs_2_
  53.5 0.2 collective-permute-done.11.refs_1_
  53.7 4.4 %third.1 = (f32[40,128]{1,0:T(8,128)S(1)}, f32[36,128]{1,0:T(8,128)S(1)}) custom-call(s32[1,1,24]{2,1,0:T(1,128)S(1)} %copy-done.4, f32[1,1,4608]{2,1,0:T(1,128)S(1)} %copy-done.1, f32[1,1,4608]{2,1,0:T(1,128)S(1)} %copy-done.2, bf16[24,512,512]{2,1,0:T(8,128)(2,1)S(1)} %get-tuple-element.19.blocks, f32[40,128]{1,0:T(8,128)S(1)} %get-tuple-element.25.refs_0_.sent.sent1, ...), custom_call_target="tpu_custom_call" | custom-call | tf_op jit(solution)/shard_map/third/pallas_call | solution.py:522
  58.1 2.5 %collective-permute-start.16 = (f32[40,128]{1,0:T(8,128)S(1)}, f32[40,128]{1,0:T(8,128)S(1)}, u32[]{:S(2)}, u32[]{:S(2)}) collective-permute-start(f32[40,128]{1,0:T(8,128)S(1)} %get-tuple-element.29.refs_0_.sent.sent2), channel_id=1, source_target_pairs={{0,24},{8,16},{16,8},{24,0},{1,25},{9,17},{17,9},{25,1},{2,26},{10... | collective-permute-start | bytes 61448 | tf_op jit(solution)/shard_map/ppermute | solution.py:464
  60.6 0.5 collective-permute-start.15
  61.1 0.5 collective-permute-start.14
  61.6 1.4 %collective-permute-done.16.refs_3_ = f32[40,128]{1,0:T(8,128)S(1)} collective-permute-done((f32[40,128]{1,0:T(8,128)S(1)}, f32[40,128]{1,0:T(8,128)S(1)}, u32[]{:S(2)}, u32[]{:S(2)}) %collective-permute-start.16) | collective-permute-done | bytes 20512 | tf_op jit(solution)/shard_map/ppermute | solution.py:464
  63.0 1.4 %collective-permute-done.15.refs_2_ = f32[40,128]{1,0:T(8,128)S(1)} collective-permute-done((f32[40,128]{1,0:T(8,128)S(1)}, f32[40,128]{1,0:T(8,128)S(1)}, u32[]{:S(2)}, u32[]{:S(2)}) %collective-permute-start.15) | collective-permute-done | bytes 20512 | tf_op jit(solution)/shard_map/ppermute | solution.py:464
  64.4 0.5 collective-permute-done.14.refs_1_
  64.9 3.1 %tiles.5 = (f32[4,40,128]{2,1,0:T(8,128)S(1)}, f32[4,40,128]{2,1,0:T(8,128)S(1)}) custom-call(s32[1,1]{1,0:T(1,128)S(6)} %copy.12.counts, s32[1,256]{1,0:T(1,128)S(1)} %get-tuple-element.21.spots, s32[1,256]{1,0:T(1,128)S(1)} %get-tuple-element.22.rows, f32[1,1,256]{2,1,0:T(1,128)S(1)} %copy-done.3, bf16[256,128,128]{2,1,0:T(8,128)(2,1)S(1)} %bitcast.31, ...), custom_call_target="tpu_custom_call" | custom-call | tf_op jit(solution)/shard_map/tiles/pallas_call | solution.py:495
  68.0 0.1 collective-permute-start.17
  68.1 1.3 %collective-permute-done.17 = f32[4,40,128]{2,1,0:T(8,128)S(1)} collective-permute-done((f32[4,40,128]{2,1,0:T(8,128)S(1)}, f32[4,40,128]{2,1,0:T(8,128)S(1)}, u32[]{:S(2)}, u32[]{:S(2)}) %collective-permute-start.17) | collective-permute-done | bytes 81952 | tf_op jit(solution)/shard_map/ppermute | solution.py:464
  69.4 2.4 %collective-permute-start.20 = (f32[40,128]{1,0:T(8,128)S(1)}, f32[40,128]{1,0:T(8,128)S(1)}, u32[]{:S(2)}, u32[]{:S(2)}) collective-permute-start(f32[40,128]{1,0:T(8,128)S(1)} %get-tuple-element.36), channel_id=1, source_target_pairs={{0,6},{1,7},{2,4},{3,5},{4,2},{5,3},{6,0},{7,1},{8,14},{9,15},{10,... | collective-permute-start | bytes 61448 | tf_op jit(solution)/shard_map/ppermute | solution.py:464
  71.8 0.4 collective-permute-start.19
  72.3 1.6 %collective-permute-start.18 = (f32[40,128]{1,0:T(8,128)S(1)}, f32[40,128]{1,0:T(8,128)S(1)}, u32[]{:S(2)}, u32[]{:S(2)}) collective-permute-start(f32[40,128]{1,0:T(8,128)S(1)} %get-tuple-element.38), channel_id=1, source_target_pairs={{0,2},{1,3},{2,0},{3,1},{4,6},{5,7},{6,4},{7,5},{8,10},{9,11},{10,... | collective-permute-start | bytes 61448 | tf_op jit(solution)/shard_map/ppermute | solution.py:464
  73.8 1.2 %collective-permute-done.20.refs_3_ = f32[40,128]{1,0:T(8,128)S(1)} collective-permute-done((f32[40,128]{1,0:T(8,128)S(1)}, f32[40,128]{1,0:T(8,128)S(1)}, u32[]{:S(2)}, u32[]{:S(2)}) %collective-permute-start.20) | collective-permute-done | bytes 20512 | tf_op jit(solution)/shard_map/ppermute | solution.py:464
  75.1 1.4 %collective-permute-done.19.refs_2_ = f32[40,128]{1,0:T(8,128)S(1)} collective-permute-done((f32[40,128]{1,0:T(8,128)S(1)}, f32[40,128]{1,0:T(8,128)S(1)}, u32[]{:S(2)}, u32[]{:S(2)}) %collective-permute-start.19) | collective-permute-done | bytes 20512 | tf_op jit(solution)/shard_map/ppermute | solution.py:464
  76.5 0.0 collective-permute-done.18.refs_1_
  76.5 0.1 fourth.1
  76.6 10.3 %all_to_all.11 = f32[32,1,128]{2,1,0:T(1,128)S(1)} all-to-all(f32[32,1,128]{2,1,0:T(1,128)S(1)} %bitcast.33), channel_id=1, replica_groups=mesh['row'=4,'col'=8] {'row','col'}, dimensions={0} | all-to-all | bytes 32768 | tf_op jit(solution)/shard_map/all_to_all | solution.py:541
  86.9 0.8 last.1
  (6 shorter events, 0.1 us)
Async XLA Ops:
  0.6 31.9 %copy-start.1 = (f32[1,1,4608]{2,1,0:T(1,128)S(1)}, f32[1,1,4608]{2,1,0:T(1,128)}, u32[]{:S(2)}) copy-start(f32[1,1,4608]{2,1,0:T(1,128)} %rhs.7) | copy-start | bytes 55300
  0.6 31.9 %copy-start.2 = (f32[1,1,4608]{2,1,0:T(1,128)S(1)}, f32[1,1,4608]{2,1,0:T(1,128)}, u32[]{:S(2)}) copy-start(f32[1,1,4608]{2,1,0:T(1,128)} %friction.5) | copy-start | bytes 55300
  0.7 31.9 %copy-start.4 = (s32[1,1,24]{2,1,0:T(1,128)S(1)}, s32[1,1,24]{2,1,0:T(1,128)}, u32[]{:S(2)}) copy-start(s32[1,1,24]{2,1,0:T(1,128)} %sizes.3) | copy-start | bytes 292
  0.7 19.0 %copy-start.3 = (f32[1,1,256]{2,1,0:T(1,128)S(1)}, f32[1,1,256]{2,1,0:T(1,128)}, u32[]{:S(2)}) copy-start(f32[1,1,256]{2,1,0:T(1,128)} %scale.5) | copy-start | bytes 3076
  0.7 19.0 %copy-start = (bf16[1,1,256,128,128]{4,3,2,1,0:T(8,128)(2,1)S(1)}, bf16[1,1,256,128,128]{4,3,2,1,0:T(8,128)(2,1)}, u32[]{:S(2)}) copy-start(bf16[1,1,256,128,128]{4,3,2,1,0:T(8,128)(2,1)} %param.11) | copy-start | bytes 25165828
  11.4 5.7 %collective-permute-start.2 = (f32[40,128]{1,0:T(8,128)S(1)}, f32[40,128]{1,0:T(8,128)S(1)}, u32[]{:S(2)}, u32[]{:S(2)}) collective-permute-start(f32[40,128]{1,0:T(8,128)S(1)} %get-tuple-element.20.refs_0_.sent.sent0), channel_id=1, source_target_pairs={{0,24},{8,16},{16,8},{24,0},{1,25},{9,17},{17,9},{25,1},{2,26},{10... | collective-permute-start | bytes 61448 | tf_op jit(solution)/shard_map/ppermute | solution.py:464
  15.4 3.8 %collective-permute-start.1 = (f32[40,128]{1,0:T(8,128)S(1)}, f32[40,128]{1,0:T(8,128)S(1)}, u32[]{:S(2)}, u32[]{:S(2)}) collective-permute-start(f32[40,128]{1,0:T(8,128)S(1)} %get-tuple-element.20.refs_0_.sent.sent0), channel_id=1, source_target_pairs={{0,16},{8,24},{16,0},{24,8},{1,17},{9,25},{17,1},{25,9},{2,18},{10... | collective-permute-start | bytes 61448 | tf_op jit(solution)/shard_map/ppermute | solution.py:464
  15.9 3.8 %collective-permute-start = (f32[40,128]{1,0:T(8,128)S(1)}, f32[40,128]{1,0:T(8,128)S(1)}, u32[]{:S(2)}, u32[]{:S(2)}) collective-permute-start(f32[40,128]{1,0:T(8,128)S(1)} %get-tuple-element.20.refs_0_.sent.sent0), channel_id=1, source_target_pairs={{0,8},{8,0},{16,24},{24,16},{1,9},{9,1},{17,25},{25,17},{2,10},{10... | collective-permute-start | bytes 61448 | tf_op jit(solution)/shard_map/ppermute | solution.py:464
  22.8 1.3 %collective-permute-start.3 = (f32[4,40,128]{2,1,0:T(8,128)S(1)}, f32[4,40,128]{2,1,0:T(8,128)S(1)}, u32[]{:S(2)}, u32[]{:S(2)}) collective-permute-start(f32[4,40,128]{2,1,0:T(8,128)S(1)} %get-tuple-element.24), channel_id=1, source_target_pairs={{0,1},{1,0},{2,3},{3,2},{4,5},{5,4},{6,7},{7,6},{8,9},{9,8},{10,11... | collective-permute-start | bytes 245768 | tf_op jit(solution)/shard_map/ppermute | solution.py:464
  24.2 5.6 %collective-permute-start.6 = (f32[40,128]{1,0:T(8,128)S(1)}, f32[40,128]{1,0:T(8,128)S(1)}, u32[]{:S(2)}, u32[]{:S(2)}) collective-permute-start(f32[40,128]{1,0:T(8,128)S(1)} %get-tuple-element.44), channel_id=1, source_target_pairs={{0,6},{1,7},{2,4},{3,5},{4,2},{5,3},{6,0},{7,1},{8,14},{9,15},{10,... | collective-permute-start | bytes 61448 | tf_op jit(solution)/shard_map/ppermute | solution.py:464
  27.9 4.7 %collective-permute-start.5 = (f32[40,128]{1,0:T(8,128)S(1)}, f32[40,128]{1,0:T(8,128)S(1)}, u32[]{:S(2)}, u32[]{:S(2)}) collective-permute-start(f32[40,128]{1,0:T(8,128)S(1)} %get-tuple-element.45), channel_id=1, source_target_pairs={{0,4},{1,5},{2,6},{3,7},{4,0},{5,1},{6,2},{7,3},{8,12},{9,13},{10,... | collective-permute-start | bytes 61448 | tf_op jit(solution)/shard_map/ppermute | solution.py:464
  27.9 4.7 %collective-permute-start.4 = (f32[40,128]{1,0:T(8,128)S(1)}, f32[40,128]{1,0:T(8,128)S(1)}, u32[]{:S(2)}, u32[]{:S(2)}) collective-permute-start(f32[40,128]{1,0:T(8,128)S(1)} %get-tuple-element.46), channel_id=1, source_target_pairs={{0,2},{1,3},{2,0},{3,1},{4,6},{5,7},{6,4},{7,5},{8,10},{9,11},{10,... | collective-permute-start | bytes 61448 | tf_op jit(solution)/shard_map/ppermute | solution.py:464
  37.0 4.7 %collective-permute-start.9 = (f32[40,128]{1,0:T(8,128)S(1)}, f32[40,128]{1,0:T(8,128)S(1)}, u32[]{:S(2)}, u32[]{:S(2)}) collective-permute-start(f32[40,128]{1,0:T(8,128)S(1)} %get-tuple-element.25.refs_0_.sent.sent1), channel_id=1, source_target_pairs={{0,24},{8,16},{16,8},{24,0},{1,25},{9,17},{17,9},{25,1},{2,26},{10... | collective-permute-start | bytes 61448 | tf_op jit(solution)/shard_map/ppermute | solution.py:464
  38.5 3.8 %collective-permute-start.8 = (f32[40,128]{1,0:T(8,128)S(1)}, f32[40,128]{1,0:T(8,128)S(1)}, u32[]{:S(2)}, u32[]{:S(2)}) collective-permute-start(f32[40,128]{1,0:T(8,128)S(1)} %get-tuple-element.25.refs_0_.sent.sent1), channel_id=1, source_target_pairs={{0,16},{8,24},{16,0},{24,8},{1,17},{9,25},{17,1},{25,9},{2,18},{10... | collective-permute-start | bytes 61448 | tf_op jit(solution)/shard_map/ppermute | solution.py:464
  39.0 3.8 %collective-permute-start.7 = (f32[40,128]{1,0:T(8,128)S(1)}, f32[40,128]{1,0:T(8,128)S(1)}, u32[]{:S(2)}, u32[]{:S(2)}) collective-permute-start(f32[40,128]{1,0:T(8,128)S(1)} %get-tuple-element.25.refs_0_.sent.sent1), channel_id=1, source_target_pairs={{0,8},{8,0},{16,24},{24,16},{1,9},{9,1},{17,25},{25,17},{2,10},{10... | collective-permute-start | bytes 61448 | tf_op jit(solution)/shard_map/ppermute | solution.py:464
  45.9 1.3 %collective-permute-start.10 = (f32[4,40,128]{2,1,0:T(8,128)S(1)}, f32[4,40,128]{2,1,0:T(8,128)S(1)}, u32[]{:S(2)}, u32[]{:S(2)}) collective-permute-start(f32[4,40,128]{2,1,0:T(8,128)S(1)} %get-tuple-element.28), channel_id=1, source_target_pairs={{0,1},{1,0},{2,3},{3,2},{4,5},{5,4},{6,7},{7,6},{8,9},{9,8},{10,11... | collective-permute-start | bytes 245768 | tf_op jit(solution)/shard_map/ppermute | solution.py:464
  47.3 5.8 %collective-permute-start.13 = (f32[40,128]{1,0:T(8,128)S(1)}, f32[40,128]{1,0:T(8,128)S(1)}, u32[]{:S(2)}, u32[]{:S(2)}) collective-permute-start(f32[40,128]{1,0:T(8,128)S(1)} %get-tuple-element.40), channel_id=1, source_target_pairs={{0,6},{1,7},{2,4},{3,5},{4,2},{5,3},{6,0},{7,1},{8,14},{9,15},{10,... | collective-permute-start | bytes 61448 | tf_op jit(solution)/shard_map/ppermute | solution.py:464
  48.8 4.7 %collective-permute-start.12 = (f32[40,128]{1,0:T(8,128)S(1)}, f32[40,128]{1,0:T(8,128)S(1)}, u32[]{:S(2)}, u32[]{:S(2)}) collective-permute-start(f32[40,128]{1,0:T(8,128)S(1)} %get-tuple-element.41), channel_id=1, source_target_pairs={{0,4},{1,5},{2,6},{3,7},{4,0},{5,1},{6,2},{7,3},{8,12},{9,13},{10,... | collective-permute-start | bytes 61448 | tf_op jit(solution)/shard_map/ppermute | solution.py:464
  49.4 4.3 %collective-permute-start.11 = (f32[40,128]{1,0:T(8,128)S(1)}, f32[40,128]{1,0:T(8,128)S(1)}, u32[]{:S(2)}, u32[]{:S(2)}) collective-permute-start(f32[40,128]{1,0:T(8,128)S(1)} %get-tuple-element.42), channel_id=1, source_target_pairs={{0,2},{1,3},{2,0},{3,1},{4,6},{5,7},{6,4},{7,5},{8,10},{9,11},{10,... | collective-permute-start | bytes 61448 | tf_op jit(solution)/shard_map/ppermute | solution.py:464
  58.1 4.9 %collective-permute-start.16 = (f32[40,128]{1,0:T(8,128)S(1)}, f32[40,128]{1,0:T(8,128)S(1)}, u32[]{:S(2)}, u32[]{:S(2)}) collective-permute-start(f32[40,128]{1,0:T(8,128)S(1)} %get-tuple-element.29.refs_0_.sent.sent2), channel_id=1, source_target_pairs={{0,24},{8,16},{16,8},{24,0},{1,25},{9,17},{17,9},{25,1},{2,26},{10... | collective-permute-start | bytes 61448 | tf_op jit(solution)/shard_map/ppermute | solution.py:464
  60.6 3.8 %collective-permute-start.15 = (f32[40,128]{1,0:T(8,128)S(1)}, f32[40,128]{1,0:T(8,128)S(1)}, u32[]{:S(2)}, u32[]{:S(2)}) collective-permute-start(f32[40,128]{1,0:T(8,128)S(1)} %get-tuple-element.29.refs_0_.sent.sent2), channel_id=1, source_target_pairs={{0,16},{8,24},{16,0},{24,8},{1,17},{9,25},{17,1},{25,9},{2,18},{10... | collective-permute-start | bytes 61448 | tf_op jit(solution)/shard_map/ppermute | solution.py:464
  61.1 3.8 %collective-permute-start.14 = (f32[40,128]{1,0:T(8,128)S(1)}, f32[40,128]{1,0:T(8,128)S(1)}, u32[]{:S(2)}, u32[]{:S(2)}) collective-permute-start(f32[40,128]{1,0:T(8,128)S(1)} %get-tuple-element.29.refs_0_.sent.sent2), channel_id=1, source_target_pairs={{0,8},{8,0},{16,24},{24,16},{1,9},{9,1},{17,25},{25,17},{2,10},{10... | collective-permute-start | bytes 61448 | tf_op jit(solution)/shard_map/ppermute | solution.py:464
  68.0 1.3 %collective-permute-start.17 = (f32[4,40,128]{2,1,0:T(8,128)S(1)}, f32[4,40,128]{2,1,0:T(8,128)S(1)}, u32[]{:S(2)}, u32[]{:S(2)}) collective-permute-start(f32[4,40,128]{2,1,0:T(8,128)S(1)} %get-tuple-element.33), channel_id=1, source_target_pairs={{0,1},{1,0},{2,3},{3,2},{4,5},{5,4},{6,7},{7,6},{8,9},{9,8},{10,11... | collective-permute-start | bytes 245768 | tf_op jit(solution)/shard_map/ppermute | solution.py:464
  69.4 5.7 %collective-permute-start.20 = (f32[40,128]{1,0:T(8,128)S(1)}, f32[40,128]{1,0:T(8,128)S(1)}, u32[]{:S(2)}, u32[]{:S(2)}) collective-permute-start(f32[40,128]{1,0:T(8,128)S(1)} %get-tuple-element.36), channel_id=1, source_target_pairs={{0,6},{1,7},{2,4},{3,5},{4,2},{5,3},{6,0},{7,1},{8,14},{9,15},{10,... | collective-permute-start | bytes 61448 | tf_op jit(solution)/shard_map/ppermute | solution.py:464
  71.8 4.7 %collective-permute-start.19 = (f32[40,128]{1,0:T(8,128)S(1)}, f32[40,128]{1,0:T(8,128)S(1)}, u32[]{:S(2)}, u32[]{:S(2)}) collective-permute-start(f32[40,128]{1,0:T(8,128)S(1)} %get-tuple-element.37), channel_id=1, source_target_pairs={{0,4},{1,5},{2,6},{3,7},{4,0},{5,1},{6,2},{7,3},{8,12},{9,13},{10,... | collective-permute-start | bytes 61448 | tf_op jit(solution)/shard_map/ppermute | solution.py:464
  72.3 4.2 %collective-permute-start.18 = (f32[40,128]{1,0:T(8,128)S(1)}, f32[40,128]{1,0:T(8,128)S(1)}, u32[]{:S(2)}, u32[]{:S(2)}) collective-permute-start(f32[40,128]{1,0:T(8,128)S(1)} %get-tuple-element.38), channel_id=1, source_target_pairs={{0,2},{1,3},{2,0},{3,1},{4,6},{5,7},{6,4},{7,5},{8,10},{9,11},{10,... | collective-permute-start | bytes 61448 | tf_op jit(solution)/shard_map/ppermute | solution.py:464

commit v6 on v5

--- a/solution.py
+++ b/solution.py
@@ -82,29 +82,47 @@
                 copy.start()
 
 
-def precondition(sizes, remote, field, work, begin=None):
-    windows, shifts, lens, stack, lefts, found, large = work[:7]
-    local = len(work) == 7
-    blocks, sems = (remote, None) if local else work[7:]
-    faults = blocks.shape[0]
-    chunks = blocks.shape[1] // LANES
-    rows = field.shape[0]
-    scalars = fault_scalars(sizes, faults)
-    if not local:
-        fetch(scalars, remote, blocks, sems)
-    if begin is not None:
-        begin()
-    lane = lax.broadcasted_iota(jnp.int32, (faults, LANES), 1)
+def make_plan(scalars, plan, column):
+    chosen, chosen_t, shifts, lens = plan
+    faults = len(scalars)
+    depth, rows = chosen_t.shape
+    chunks = depth // faults - 1
+    column[...] = jnp.full(column.shape, -1, jnp.int32)
+    place = lax.broadcasted_iota(jnp.int32, (1, depth), 1)
+    target = jnp.full((1, depth), -1, jnp.int32)
     for f, (tile, shift, size) in enumerate(scalars):
         shifts[f : f + 1, :] = jnp.full((1, LANES), shift, jnp.int32)
         lens[f : f + 1, :] = jnp.full((1, LANES), size, jnp.int32)
         for k in range(chunks + 1):
-            windows[k, f : f + 1, :] = field[pl.ds(tile + k, 1), :]
+            spot = k * faults + f
+            column[spot : spot + 1, :] = jnp.full((1, LANES), tile + k, jnp.int32)
+            target = jnp.where(place == spot, tile + k, target)
+    chosen[...] = (lax.broadcasted_iota(jnp.int32, (rows, depth), 0) == target).astype(BF16)
+    chosen_t[...] = (
+        lax.broadcasted_iota(jnp.int32, (depth, rows), 1) == column[:, 0:1]
+    ).astype(BF16)
+
+
+def select(chosen, value):
+    high, low = split(value)
+    return jnp.dot(chosen, high, preferred_element_type=F32) + jnp.dot(
+        chosen, low, preferred_element_type=F32
+    )
+
+
+def precondition(sizes, plan, field, blocks, work, remote=None, sems=None):
+    chosen, chosen_t, shifts, lens = plan
+    stack, lefts, found, large = work
+    faults = blocks.shape[0]
+    chunks = blocks.shape[1] // LANES
+    local = remote is None
+    lane = lax.broadcasted_iota(jnp.int32, (faults, LANES), 1)
+    windows = select(chosen_t[...], field[...])
     shift = shifts[...]
     size = lens[...]
     bits = [((shift >> b) & 1) == 1 for b in range(7)]
     live = [lane + k * LANES < size for k in range(chunks)]
-    parts = [windows[k] for k in range(chunks + 1)]
+    parts = [windows[k * faults : (k + 1) * faults] for k in range(chunks + 1)]
     for b in range(7):
         step = 1 << b
         rolled = [pltpu.roll(part, LANES - step, 1) for part in parts]
@@ -136,9 +154,9 @@
         for k in range(chunks):
             found[k, group] = sums[k] if k < chunk_half else jnp.zeros((8, LANES), F32)
     count = jnp.int32(0)
-    for f, (_, _, size) in enumerate(scalars):
+    for f in range(faults):
         large[count] = f
-        count = count + (size > half).astype(jnp.int32)
+        count = count + (sizes[0, 0, f] > half).astype(jnp.int32)
 
     def rest(step, carry):
         for u in range(UNROLL):
@@ -183,20 +201,7 @@
     depth = stack.shape[0]
     if depth > count:
         stack[count:depth, :] = jnp.zeros((depth - count, LANES), F32)
-    place = lax.broadcasted_iota(jnp.int32, (1, depth), 1)
-    chunk = jnp.zeros((1, depth), jnp.int32)
-    for k in range(1, chunks + 1):
-        chunk = chunk + (place >= k * faults).astype(jnp.int32)
-    local = place - chunk * faults
-    target = jnp.full((1, depth), -1, jnp.int32)
-    for f, (tile, _, _) in enumerate(scalars):
-        target = jnp.where(local == f, tile + chunk, target)
-    target = jnp.where(place < count, target, -1)
-    chosen = (lax.broadcasted_iota(jnp.int32, (rows, depth), 0) == target).astype(BF16)
-    high, low = split(stack[...])
-    return jnp.dot(chosen, high, preferred_element_type=F32) + jnp.dot(
-        chosen, low, preferred_element_type=F32
-    )
+    return select(chosen[...], stack[...])
 
 
 def set_field(field, value):
@@ -212,35 +217,20 @@
     return found
 
 
-def first_kernel(shape, *refs):
-    (blocks, send, near_blocks, spots, target) = refs[5:10]
-    (sizes, rhs, friction, tile_row, tile_col) = refs[10:15]
-    (sems, block_sems, field, *work) = refs[15:]
-    work = work + [near_blocks, block_sems]
-    row_count, col_count = shape
+def first_kernel(far_sizes, far_rhs, far_friction, remote, send, blocks, *refs):
+    plan, (sizes, rhs, friction, column, sems, block_sems, field, *work) = refs[:4], refs[4:]
     tiles = rhs.shape[2] // LANES
-    height = send.shape[0]
-    pairs = list(zip(refs[:5], refs[10:15]))
+    pairs = [(far_sizes, sizes), (far_rhs, rhs), (far_friction, friction)]
     copies = [pltpu.make_async_copy(a, b, sems.at[i]) for i, (a, b) in enumerate(pairs)]
     for copy in copies:
         copy.start()
     copies[0].wait()
-
-    def value_to_field():
-        copies[1].wait()
-        set_field(field, load_rows(rhs, tiles))
-        for copy in copies[3:]:
-            copy.wait()
-        column = tile_col[0]
-        source = owner(column, tiles, row_count)
-        spots[...] = (source ^ lax.axis_index("row")) * height + column - source * tiles
-        row = tile_row[0]
-        source = owner(row, tiles, col_count)
-        place = source ^ lax.axis_index("col")
-        place = (place & 1) * (col_count // 2) + (place >> 1)
-        target[...] = place * height + row - source * tiles
-
-    direction = precondition(sizes, blocks, field, work, value_to_field)[0:tiles]
+    scalars = fault_scalars(sizes, blocks.shape[0])
+    fetch(scalars, remote, blocks, block_sems)
+    make_plan(scalars, plan, column)
+    copies[1].wait()
+    set_field(field, load_rows(rhs, tiles))
+    direction = precondition(sizes, plan, field, blocks, work, remote, block_sems)[0:tiles]
     copies[2].wait()
     value = field[0:tiles, :]
     scaled = load_rows(friction, tiles) * direction
@@ -256,8 +246,9 @@
     return whole[0:tiles], whole[tiles : tiles + 1]
 
 
-def second_kernel(sizes, rhs, friction, blocks, sent, *refs):
-    parts, (send, image_out, basis_out, field, *work) = refs[:-11], refs[-11:]
+def second_kernel(sizes, rhs, friction, blocks, *refs):
+    plan, sent, parts = refs[:4], refs[4], refs[5:-8]
+    send, image_out, basis_out, field, *work = refs[-8:]
     tiles = rhs.shape[2] // LANES
     start = load_rows(rhs, tiles)
     diagonal = load_rows(friction, tiles)
@@ -270,7 +261,7 @@
     basis_out[0:tiles, :] = value
     basis_out[tiles:, :] = jnp.broadcast_to(norm2, (basis_out.shape[0] - tiles, LANES))
     set_field(field, value)
-    direction = precondition(sizes, blocks, field, work)[0:tiles]
+    direction = precondition(sizes, plan, field, blocks, work)[0:tiles]
     scaled = diagonal * direction
     send[...] = jnp.zeros_like(send)
     send[0:tiles, :] = direction
@@ -284,8 +275,9 @@
     )
 
 
-def third_kernel(sizes, rhs, friction, blocks, sent, basis, *refs):
-    parts, (send, image_out, field, *work) = refs[:-10], refs[-10:]
+def third_kernel(sizes, rhs, friction, blocks, *refs):
+    plan, sent, basis, parts = refs[:4], refs[4], refs[5], refs[6:-7]
+    send, image_out, field, *work = refs[-7:]
     tiles = rhs.shape[2] // LANES
     start = load_rows(rhs, tiles)
     diagonal = load_rows(friction, tiles)
@@ -303,7 +295,7 @@
     )
     image_out[...] = image
     set_field(field, value)
-    direction = precondition(sizes, blocks, field, work)[0:tiles]
+    direction = precondition(sizes, plan, field, blocks, work)[0:tiles]
     send[...] = jnp.zeros_like(send)
     send[0:tiles, :] = direction
 
@@ -361,15 +353,50 @@
         residual[0, :, pl.ds(k * LANES, LANES)] = rest[k : k + 1]
 
 
-def tiles_kernel(tail, counts, spots, rows, scale, blocks, *refs):
-    sent, (keep, give, field, found, products) = refs[:-5], refs[-5:]
+def prepare_kernel(shape, after, counts, tile_row, tile_col, scale, remote, blocks, *refs):
+    gather, high, low, sems = refs
+    tiles, height, row_count, col_count = shape
+    slots = blocks.shape[0]
+    pieces = sems.shape[0]
+    copies = []
+    for p in range(pieces):
+        part = pl.ds(p * (slots // pieces), slots // pieces)
+        copies.append(
+            pltpu.make_async_copy(remote.at[0, 0, part], blocks.at[part], sems.at[p])
+        )
+        copies[-1].start()
+    column = tile_col[0]
+    source = owner(column, tiles, row_count)
+    spots = (source ^ lax.axis_index("row")) * height + column - source * tiles
+    ones = jnp.ones((LANES, LANES), BF16)
+    for base in range(0, slots, LANES):
+        mine = spots[:, base : base + LANES].astype(F32)
+        square = lax.broadcasted_iota(jnp.int32, (LANES, LANES), 0)
+        across = lax.broadcasted_iota(jnp.int32, (LANES, LANES), 1)
+        square = jnp.where(square == across, mine, 0.0).astype(BF16)
+        down = jnp.dot(square, ones, preferred_element_type=F32)[:, 0:1].astype(jnp.int32)
+        wide = lax.broadcasted_iota(jnp.int32, (LANES, gather.shape[1]), 1)
+        gather[base : base + LANES, :] = (wide == down).astype(BF16)
+    row = tile_row[0]
+    source = owner(row, tiles, col_count)
+    place = source ^ lax.axis_index("col")
+    place = (place & 1) * (col_count // 2) + (place >> 1)
+    target = place * height + row - source * tiles
+    slot = lax.broadcasted_iota(jnp.int32, target.shape, 1)
+    weight = jnp.where(slot < counts[0, 0], scale[0], 0.0)
+    chosen = jnp.where(lax.broadcasted_iota(jnp.int32, high.shape, 0) == target, weight, 0.0)
+    high[...], low[...] = split(chosen)
+    for copy in copies:
+        copy.wait()
+
+
+def tiles_kernel(tail, gather, chosen_high, chosen_low, blocks, *refs):
+    sent, (keep, give, found, products) = refs[:-4], refs[-4:]
     slots = blocks.shape[0]
     far, height = keep.shape[0], keep.shape[1]
     groups = slots // 16
-    for k, one in enumerate(sent):
-        field[k * height : (k + 1) * height, :] = one[...]
-    for t in range(slots):
-        found[t : t + 1, :] = field[pl.ds(spots[0, t], 1), :]
+    field = jnp.concatenate([one[...] for one in sent], axis=0).astype(BF16)
+    found[...] = jnp.dot(gather[...], field, preferred_element_type=F32)
     sub = lax.broadcasted_iota(jnp.int32, (8, LANES), 0)
     blank = jnp.zeros((8, LANES), F32)
     for group in range(groups):
@@ -394,17 +421,10 @@
         products[base : base + 8, :] = first
         products[base + 8 : base + 16, :] = second
     high, low = split(products[...])
-    target = rows[...]
-    slot = lax.broadcasted_iota(jnp.int32, target.shape, 1)
-    weight = jnp.where(slot < counts[0, 0], scale[0], 0.0)
-    chosen = jnp.where(
-        lax.broadcasted_iota(jnp.int32, (2 * far * height, slots), 0) == target, weight, 0.0
-    )
-    chosen_high, chosen_low = split(chosen)
     value = (
-        jnp.dot(chosen_high, high, preferred_element_type=F32)
-        + jnp.dot(chosen_low, high, preferred_element_type=F32)
-        + jnp.dot(chosen_high, low, preferred_element_type=F32)
+        jnp.dot(chosen_high[...], high, preferred_element_type=F32)
+        + jnp.dot(chosen_low[...], high, preferred_element_type=F32)
+        + jnp.dot(chosen_high[...], low, preferred_element_type=F32)
     )
     keep[...] = value[: far * height].reshape(far, height, LANES)
     give[...] = value[far * height :].reshape(far, height, LANES)
@@ -450,9 +470,6 @@
     half_grid = jax.ShapeDtypeStruct((far, height, LANES), F32)
     work = [
         scratch((rows, LANES)),
-        scratch((chunks + 1, faults, LANES)),
-        scratch((faults, LANES), jnp.int32),
-        scratch((faults, LANES), jnp.int32),
         scratch((depth, LANES)),
         scratch((faults // 8, 16, width), BF16),
         scratch((chunks, faults // 8, 8, LANES)),
@@ -463,48 +480,63 @@
         size = lax.axis_size(axis)
         return lax.ppermute(value, axis, [(i, i ^ distance) for i in range(size)])
 
-    near_tiles = kernel_tiles.reshape(slots, LANES, LANES)
-    inputs = (fault_sizes, rhs, friction, tile_row, tile_col, precond_blocks)
-    places = jax.ShapeDtypeStruct((1, slots), jnp.int32)
-    sent0, near_blocks, spots, target = pl.pallas_call(
-        functools.partial(first_kernel, (row_count, col_count)),
+    def pinned(value):
+        return pltpu.with_memory_space_constraint(value, pltpu.HBM)
+
+    sent0, near_blocks, *plan = pl.pallas_call(
+        first_kernel,
         out_shape=[
             grid,
             pltpu.VMEM((faults, width, width), BF16),
-            places,
-            places,
+            jax.ShapeDtypeStruct((rows, depth), BF16),
+            jax.ShapeDtypeStruct((depth, rows), BF16),
+            jax.ShapeDtypeStruct((faults, LANES), jnp.int32),
+            jax.ShapeDtypeStruct((faults, LANES), jnp.int32),
         ],
-        in_specs=[HBM] * 6,
-        out_specs=[VMEM] * 4,
+        in_specs=[HBM] * 4,
+        out_specs=[VMEM] * 6,
         scratch_shapes=[
             pltpu.SMEM(fault_sizes.shape, jnp.int32),
             scratch(rhs.shape),
             scratch(friction.shape),
-            scratch(tile_row.shape, jnp.int32),
-            scratch(tile_col.shape, jnp.int32),
-            pltpu.SemaphoreType.DMA((5,)),
+            scratch((depth, LANES), jnp.int32),
+            pltpu.SemaphoreType.DMA((3,)),
             pltpu.SemaphoreType.DMA((3, faults)),
         ]
         + work,
         compiler_params=PARAMS,
         name="first",
-    )(*[pltpu.with_memory_space_constraint(a, pltpu.HBM) for a in inputs])
+    )(pinned(fault_sizes), pinned(rhs), pinned(friction), pinned(precond_blocks))
+    spread = (2 * far * height, slots)
+    near_tiles, *selections = pl.pallas_call(
+        functools.partial(prepare_kernel, (tiles, height, row_count, col_count)),
+        out_shape=[
+            pltpu.VMEM((slots, LANES, LANES), BF16),
+            jax.ShapeDtypeStruct((slots, row_count * height), BF16),
+            jax.ShapeDtypeStruct(spread, BF16),
+            jax.ShapeDtypeStruct(spread, BF16),
+        ],
+        in_specs=[VMEM, SMEM, VMEM, VMEM, VMEM, HBM],
+        out_specs=[VMEM] * 4,
+        scratch_shapes=[pltpu.SemaphoreType.DMA((4,))],
+        compiler_params=PARAMS,
+        name="prepare",
+    )(plan[3], tile_counts, tile_row, tile_col, tile_scale, pinned(kernel_tiles))
 
     def apply_kernel(sent):
         got = [sent] + [exchange(sent, "row", d) for d in range(1, row_count)]
         keep, give = pl.pallas_call(
             functools.partial(tiles_kernel, tiles % 8),
             out_shape=[half_grid, half_grid],
-            in_specs=[SMEM, SMEM, VMEM, VMEM, VMEM] + [VMEM] * row_count,
+            in_specs=[VMEM] * (4 + row_count),
             out_specs=[VMEM] * 2,
             scratch_shapes=[
-                scratch((row_count * height, LANES)),
                 scratch((slots, LANES)),
                 scratch((slots, LANES)),
             ],
             compiler_params=PARAMS,
             name="tiles",
-        )(tile_counts, spots, target, tile_scale, near_tiles, *got)
+        )(*selections, near_tiles, *got)
         both = keep + exchange(give, "col", 1)
         return [both[0]] + [exchange(both[d], "col", 2 * d) for d in range(1, far)]
 
@@ -512,22 +544,22 @@
     sent1, image0, basis = pl.pallas_call(
         second_kernel,
         out_shape=[grid, plain, grid],
-        in_specs=[SMEM, VMEM, VMEM, VMEM] + [VMEM] * (1 + far),
+        in_specs=[SMEM, VMEM, VMEM, VMEM] + [VMEM] * (5 + far),
         out_specs=[VMEM] * 3,
         scratch_shapes=work,
         compiler_params=PARAMS,
         name="second",
-    )(fault_sizes, rhs, friction, near_blocks, sent0, *parts0)
+    )(fault_sizes, rhs, friction, near_blocks, *plan, sent0, *parts0)
     parts1 = apply_kernel(sent1)
     sent2, image1 = pl.pallas_call(
         third_kernel,
         out_shape=[grid, plain],
-        in_specs=[SMEM, VMEM, VMEM, VMEM] + [VMEM] * (2 + far),
+        in_specs=[SMEM, VMEM, VMEM, VMEM] + [VMEM] * (6 + far),
         out_specs=[VMEM] * 2,
         scratch_shapes=work,
         compiler_params=PARAMS,
         name="third",
-    )(fault_sizes, rhs, friction, near_blocks, sent1, basis, *parts1)
+    )(fault_sizes, rhs, friction, near_blocks, *plan, sent1, basis, *parts1)
     parts2 = apply_kernel(sent2)
     devices = row_count * col_count
     image2, sums = pl.pallas_call(

time: 87.8 us -> 87.9 us (level)
  waiting for transfers between devices: 20.9 us -> 18 us
  Pallas kernels: 29.8 us -> 31.8 us
    pallas_call x1 -> x2, Pallas kernels: 10.7 us -> 14 us  [the longest x1 10.4 us: local(): pl.pallas_call(first_kernel, out_shape=[grid, pltpu.VMEM((faults, width,...]
    ppermute x21, waiting for transfers between devices: 20.9 us -> 18 us  [exchange(): return lax.ppermute(value, axis, [(i, i ^ distance) for i in range(size)])]
    pallas_call x3, Pallas kernels: 9.41 us -> 7.92 us  [apply_kernel(): pl.pallas_call(functools.partial(tiles_kernel, tiles % 8), out_shape=[hal...]
  transfers between devices with their start and end apart: 21 -> 21, of which waited for: 19 -> 17; matrix products, arithmetic and copies ran while one was open for 0% -> 0% of each run, Pallas kernels for 0% -> 4%
where the time goes in v6:
time: 87.9 us; the launch traced here: 87.7 us
  Pallas kernels  31.8 us (36%)
  starting transfers between devices  25.5 us (29%)
  waiting for transfers between devices  18 us (20%)
  blocking collectives  10.9 us (12%)
  between operations  1.51 us (2%)
    ppermute x21, starting transfers between devices, exchange(): return lax.ppermute(value, axis, [(i, i ^ distance) for i in range(size)])  25.5 us
    ppermute x21, waiting for transfers between devices, exchange(): return lax.ppermute(value, axis, [(i, i ^ distance) for i in range(size)])  18 us
    all_to_all x1, blocking collectives, local(): sums = lax.all_to_all(sums, ('row', 'col'), 0, 0, tiled=True)  10.9 us
    pallas_call x1, Pallas kernels, local(): pl.pallas_call(first_kernel, out_shape=[grid, pltpu.VMEM((faults, width,...  10.4 us
    pallas_call x3, Pallas kernels, apply_kernel(): pl.pallas_call(functools.partial(tiles_kernel, tiles % 8), out_shape=[hal...  7.92 us
    pallas_call x1, Pallas kernels, local(): pl.pallas_call(second_kernel, out_shape=[grid, plain, grid], in_specs=[SM...  4.53 us
    pallas_call x1, Pallas kernels, local(): pl.pallas_call(third_kernel, out_shape=[grid, plain], in_specs=[SMEM, VME...  4.47 us
    pallas_call x1, Pallas kernels, local(): pl.pallas_call(functools.partial(prepare_kernel, (tiles, height, row_coun...  3.54 us
  transfers between devices with their start and end apart: 21, of which 17 were waited for; matrix products, arithmetic and copies ran while one was open for 0% of the time, Pallas kernels for 4%

profile of v6, /device:TPU:0, one launch (start us, length us, event | category | flops | bytes accessed | tf_op | source)
XLA Modules:
  0.0 87.7 jit_solution(15007508464743935431)
XLA Ops:
  0.6 0.0 copy-start
  0.6 0.0 copy-start.1
  0.7 0.0 copy-start.2
  0.7 0.0 copy-start.4
  0.7 0.0 copy-start.3
  0.7 0.0 copy-start.5
  0.7 10.4 %first.1 = (f32[40,128]{1,0:T(8,128)S(1)}, bf16[24,512,512]{2,1,0:T(8,128)(2,1)S(1)}, bf16[48,128]{1,0:T(8,128)(2,1)S(1)}, bf16[128,48]{1,0:T(8,128)(2,1)S(1)}, ...) custom-call(s32[1,1,24]{2,1,0:T(1,128)} %sizes.3, f32[1,1,4608]{2,1,0:T(1,128)} %rhs.7, f32[1,1,4608]{2,1,0:T(1,128)} %friction.5, ...), custom_call_target="tpu_custom_call" | custom-call | tf_op jit(solution)/shard_map/first/pallas_call | solution.py:486
  11.1 3.1 %collective-permute-start.2 = (f32[40,128]{1,0:T(8,128)S(1)}, f32[40,128]{1,0:T(8,128)S(1)}, u32[]{:S(2)}, u32[]{:S(2)}) collective-permute-start(f32[40,128]{1,0:T(8,128)S(1)} %get-tuple-element.30.refs_0_.refs_4_.sent0), channel_id=1, source_target_pairs={{0,24},{8,16},{16,8},{24,0},{1,25},{9,17},{17,9},{25,1},{2,26},{10... | collective-permute-start | bytes 61448 | tf_op jit(solution)/shard_map/ppermute | solution.py:481
  14.2 1.4 %collective-permute-start.1 = (f32[40,128]{1,0:T(8,128)S(1)}, f32[40,128]{1,0:T(8,128)S(1)}, u32[]{:S(2)}, u32[]{:S(2)}) collective-permute-start(f32[40,128]{1,0:T(8,128)S(1)} %get-tuple-element.30.refs_0_.refs_4_.sent0), channel_id=1, source_target_pairs={{0,16},{8,24},{16,0},{24,8},{1,17},{9,25},{17,1},{25,9},{2,18},{10... | collective-permute-start | bytes 61448 | tf_op jit(solution)/shard_map/ppermute | solution.py:481
  15.6 0.0 collective-permute-start
  16.3 0.0 copy-done.4
  16.3 0.0 copy-done.3
  16.3 0.0 copy-done.5
  16.3 3.5 %prepare.1 = (bf16[256,128,128]{2,1,0:T(8,128)(2,1)S(1)}, bf16[256,160]{1,0:T(8,128)(2,1)S(1)}, bf16[320,256]{1,0:T(8,128)(2,1)S(1)}, bf16[320,256]{1,0:T(8,128)(2,1)S(1)}) custom-call(s32[24,128]{1,0:T(8,128)S(1)} %get-tuple-element.29.after.refs_3_, s32[1,1]{1,0:T(1,128)S(6)} %copy.12.counts, s32[1,1,256]{2,1,0:T(1,128)S(1)} %copy-done.3, ...), custom_call_target="tpu_custom_call" | custom-call | tf_op jit(solution)/shard_map/prepare/pallas_call | solution.py:511
  19.9 0.0 collective-permute-done.2.refs_3_
  19.9 0.0 collective-permute-done.1.refs_2_
  19.9 0.0 collective-permute-done.refs_1_
  19.9 2.6 %tiles.3 = (f32[4,40,128]{2,1,0:T(8,128)S(1)}, f32[4,40,128]{2,1,0:T(8,128)S(1)}) custom-call(bf16[256,160]{1,0:T(8,128)(2,1)S(1)} %get-tuple-element.31.gather, bf16[320,256]{1,0:T(8,128)(2,1)S(1)} %get-tuple-element.32.chosen_high, bf16[320,256]{1,0:T(8,128)(2,1)S(1)} %get-tuple-element.33.chosen_low, bf16[256,128,128]{2,1,0:T(8,128)(2,1)S(1)} %get-tuple-element.34.blocks, ...), custom_call_target="tpu_custom_call" | custom-call | tf_op jit(solution)/shard_map/tiles/pallas_call | solution.py:528
  22.5 0.1 collective-permute-start.3
  22.6 1.3 %collective-permute-done.3 = f32[4,40,128]{2,1,0:T(8,128)S(1)} collective-permute-done((f32[4,40,128]{2,1,0:T(8,128)S(1)}, f32[4,40,128]{2,1,0:T(8,128)S(1)}, u32[]{:S(2)}, u32[]{:S(2)}) %collective-permute-start.3) | collective-permute-done | bytes 81952 | tf_op jit(solution)/shard_map/ppermute | solution.py:481
  23.9 4.2 %collective-permute-start.6 = (f32[40,128]{1,0:T(8,128)S(1)}, f32[40,128]{1,0:T(8,128)S(1)}, u32[]{:S(2)}, u32[]{:S(2)}) collective-permute-start(f32[40,128]{1,0:T(8,128)S(1)} %get-tuple-element.56), channel_id=1, source_target_pairs={{0,6},{1,7},{2,4},{3,5},{4,2},{5,3},{6,0},{7,1},{8,14},{9,15},{10,... | collective-permute-start | bytes 61448 | tf_op jit(solution)/shard_map/ppermute | solution.py:481
  28.1 0.0 collective-permute-start.5
  28.1 0.6 collective-permute-start.4
  28.7 1.1 %collective-permute-done.6.refs_8_ = f32[40,128]{1,0:T(8,128)S(1)} collective-permute-done((f32[40,128]{1,0:T(8,128)S(1)}, f32[40,128]{1,0:T(8,128)S(1)}, u32[]{:S(2)}, u32[]{:S(2)}) %collective-permute-start.6) | collective-permute-done | bytes 20512 | tf_op jit(solution)/shard_map/ppermute | solution.py:481
  29.9 2.9 %collective-permute-done.5.refs_7_ = f32[40,128]{1,0:T(8,128)S(1)} collective-permute-done((f32[40,128]{1,0:T(8,128)S(1)}, f32[40,128]{1,0:T(8,128)S(1)}, u32[]{:S(2)}, u32[]{:S(2)}) %collective-permute-start.5) | collective-permute-done | bytes 20512 | tf_op jit(solution)/shard_map/ppermute | solution.py:481
  32.8 0.0 collective-permute-done.4.refs_6_
  32.8 0.0 copy-done
  32.8 0.0 copy-done.1
  32.8 0.0 copy-done.2
  32.8 4.5 %second.1 = (f32[40,128]{1,0:T(8,128)S(1)}, f32[36,128]{1,0:T(8,128)S(1)}, f32[40,128]{1,0:T(8,128)S(1)}) custom-call(s32[1,1,24]{2,1,0:T(1,128)S(1)} %copy-done.2, f32[1,1,4608]{2,1,0:T(1,128)S(1)} %copy-done, f32[1,1,4608]{2,1,0:T(1,128)S(1)} %copy-done.1, bf16[24,512,512]{2,1,0:T(8,128)(2,1)S(1)} %get-tuple-element.25.blocks, ...), custom_call_target="tpu_custom_call" | custom-call | tf_op jit(solution)/shard_map/second/pallas_call | solution.py:544
  37.3 2.0 %collective-permute-start.9 = (f32[40,128]{1,0:T(8,128)S(1)}, f32[40,128]{1,0:T(8,128)S(1)}, u32[]{:S(2)}, u32[]{:S(2)}) collective-permute-start(f32[40,128]{1,0:T(8,128)S(1)} %get-tuple-element.37.refs_0_.refs_4_.sent1), channel_id=1, source_target_pairs={{0,24},{8,16},{16,8},{24,0},{1,25},{9,17},{17,9},{25,1},{2,26},{10... | collective-permute-start | bytes 61448 | tf_op jit(solution)/shard_map/ppermute | solution.py:481
  39.3 0.5 collective-permute-start.8
  39.8 1.0 %collective-permute-start.7 = (f32[40,128]{1,0:T(8,128)S(1)}, f32[40,128]{1,0:T(8,128)S(1)}, u32[]{:S(2)}, u32[]{:S(2)}) collective-permute-start(f32[40,128]{1,0:T(8,128)S(1)} %get-tuple-element.37.refs_0_.refs_4_.sent1), channel_id=1, source_target_pairs={{0,8},{8,0},{16,24},{24,16},{1,9},{9,1},{17,25},{25,17},{2,10},{10... | collective-permute-start | bytes 61448 | tf_op jit(solution)/shard_map/ppermute | solution.py:481
  40.8 1.2 %collective-permute-done.9.refs_3_ = f32[40,128]{1,0:T(8,128)S(1)} collective-permute-done((f32[40,128]{1,0:T(8,128)S(1)}, f32[40,128]{1,0:T(8,128)S(1)}, u32[]{:S(2)}, u32[]{:S(2)}) %collective-permute-start.9) | collective-permute-done | bytes 20512 | tf_op jit(solution)/shard_map/ppermute | solution.py:481
  42.0 1.1 %collective-permute-done.8.refs_2_ = f32[40,128]{1,0:T(8,128)S(1)} collective-permute-done((f32[40,128]{1,0:T(8,128)S(1)}, f32[40,128]{1,0:T(8,128)S(1)}, u32[]{:S(2)}, u32[]{:S(2)}) %collective-permute-start.8) | collective-permute-done | bytes 20512 | tf_op jit(solution)/shard_map/ppermute | solution.py:481
  43.1 0.5 collective-permute-done.7.refs_1_
  43.6 2.6 %tiles.4 = (f32[4,40,128]{2,1,0:T(8,128)S(1)}, f32[4,40,128]{2,1,0:T(8,128)S(1)}) custom-call(bf16[256,160]{1,0:T(8,128)(2,1)S(1)} %get-tuple-element.31.gather, bf16[320,256]{1,0:T(8,128)(2,1)S(1)} %get-tuple-element.32.chosen_high, bf16[320,256]{1,0:T(8,128)(2,1)S(1)} %get-tuple-element.33.chosen_low, bf16[256,128,128]{2,1,0:T(8,128)(2,1)S(1)} %get-tuple-element.34.blocks, ...), custom_call_target="tpu_custom_call" | custom-call | tf_op jit(solution)/shard_map/tiles/pallas_call | solution.py:528
  46.2 0.1 collective-permute-start.10
  46.3 1.3 %collective-permute-done.10 = f32[4,40,128]{2,1,0:T(8,128)S(1)} collective-permute-done((f32[4,40,128]{2,1,0:T(8,128)S(1)}, f32[4,40,128]{2,1,0:T(8,128)S(1)}, u32[]{:S(2)}, u32[]{:S(2)}) %collective-permute-start.10) | collective-permute-done | bytes 81952 | tf_op jit(solution)/shard_map/ppermute | solution.py:481
  47.6 1.5 %collective-permute-start.13 = (f32[40,128]{1,0:T(8,128)S(1)}, f32[40,128]{1,0:T(8,128)S(1)}, u32[]{:S(2)}, u32[]{:S(2)}) collective-permute-start(f32[40,128]{1,0:T(8,128)S(1)} %get-tuple-element.52), channel_id=1, source_target_pairs={{0,6},{1,7},{2,4},{3,5},{4,2},{5,3},{6,0},{7,1},{8,14},{9,15},{10,... | collective-permute-start | bytes 61448 | tf_op jit(solution)/shard_map/ppermute | solution.py:481
  49.1 0.4 collective-permute-start.12
  49.5 2.5 %collective-permute-start.11 = (f32[40,128]{1,0:T(8,128)S(1)}, f32[40,128]{1,0:T(8,128)S(1)}, u32[]{:S(2)}, u32[]{:S(2)}) collective-permute-start(f32[40,128]{1,0:T(8,128)S(1)} %get-tuple-element.54), channel_id=1, source_target_pairs={{0,2},{1,3},{2,0},{3,1},{4,6},{5,7},{6,4},{7,5},{8,10},{9,11},{10,... | collective-permute-start | bytes 61448 | tf_op jit(solution)/shard_map/ppermute | solution.py:481
  52.0 1.2 %collective-permute-done.13.refs_9_ = f32[40,128]{1,0:T(8,128)S(1)} collective-permute-done((f32[40,128]{1,0:T(8,128)S(1)}, f32[40,128]{1,0:T(8,128)S(1)}, u32[]{:S(2)}, u32[]{:S(2)}) %collective-permute-start.13) | collective-permute-done | bytes 20512 | tf_op jit(solution)/shard_map/ppermute | solution.py:481
  53.2 0.7 collective-permute-done.12.refs_8_
  53.9 0.1 collective-permute-done.11.refs_7_
  54.0 4.5 %third.1 = (f32[40,128]{1,0:T(8,128)S(1)}, f32[36,128]{1,0:T(8,128)S(1)}) custom-call(s32[1,1,24]{2,1,0:T(1,128)S(1)} %copy-done.2, f32[1,1,4608]{2,1,0:T(1,128)S(1)} %copy-done, f32[1,1,4608]{2,1,0:T(1,128)S(1)} %copy-done.1, bf16[24,512,512]{2,1,0:T(8,128)(2,1)S(1)} %get-tuple-element.25.blocks, bf16[48,128]{1,0:T(8,128)(2,1)S(1)} %get-tuple-element.26.refs_0_, ...), custom_call_target="tpu_custom_call" | custom-call | tf_op jit(solution)/shard_map/third/pallas_call | solution.py:554
  58.5 1.1 %collective-permute-start.16 = (f32[40,128]{1,0:T(8,128)S(1)}, f32[40,128]{1,0:T(8,128)S(1)}, u32[]{:S(2)}, u32[]{:S(2)}) collective-permute-start(f32[40,128]{1,0:T(8,128)S(1)} %get-tuple-element.41.refs_0_.sent.sent2), channel_id=1, source_target_pairs={{0,24},{8,16},{16,8},{24,0},{1,25},{9,17},{17,9},{25,1},{2,26},{10... | collective-permute-start | bytes 61448 | tf_op jit(solution)/shard_map/ppermute | solution.py:481
  59.6 1.5 %collective-permute-start.15 = (f32[40,128]{1,0:T(8,128)S(1)}, f32[40,128]{1,0:T(8,128)S(1)}, u32[]{:S(2)}, u32[]{:S(2)}) collective-permute-start(f32[40,128]{1,0:T(8,128)S(1)} %get-tuple-element.41.refs_0_.sent.sent2), channel_id=1, source_target_pairs={{0,16},{8,24},{16,0},{24,8},{1,17},{9,25},{17,1},{25,9},{2,18},{10... | collective-permute-start | bytes 61448 | tf_op jit(solution)/shard_map/ppermute | solution.py:481
  61.1 1.0 %collective-permute-start.14 = (f32[40,128]{1,0:T(8,128)S(1)}, f32[40,128]{1,0:T(8,128)S(1)}, u32[]{:S(2)}, u32[]{:S(2)}) collective-permute-start(f32[40,128]{1,0:T(8,128)S(1)} %get-tuple-element.41.refs_0_.sent.sent2), channel_id=1, source_target_pairs={{0,8},{8,0},{16,24},{24,16},{1,9},{9,1},{17,25},{25,17},{2,10},{10... | collective-permute-start | bytes 61448 | tf_op jit(solution)/shard_map/ppermute | solution.py:481
  62.0 1.2 %collective-permute-done.16.refs_3_ = f32[40,128]{1,0:T(8,128)S(1)} collective-permute-done((f32[40,128]{1,0:T(8,128)S(1)}, f32[40,128]{1,0:T(8,128)S(1)}, u32[]{:S(2)}, u32[]{:S(2)}) %collective-permute-start.16) | collective-permute-done | bytes 20512 | tf_op jit(solution)/shard_map/ppermute | solution.py:481
  63.3 0.2 collective-permute-done.15.refs_2_
  63.5 1.4 %collective-permute-done.14.refs_1_ = f32[40,128]{1,0:T(8,128)S(1)} collective-permute-done((f32[40,128]{1,0:T(8,128)S(1)}, f32[40,128]{1,0:T(8,128)S(1)}, u32[]{:S(2)}, u32[]{:S(2)}) %collective-permute-start.14) | collective-permute-done | bytes 20512 | tf_op jit(solution)/shard_map/ppermute | solution.py:481
  64.8 2.6 %tiles.5 = (f32[4,40,128]{2,1,0:T(8,128)S(1)}, f32[4,40,128]{2,1,0:T(8,128)S(1)}) custom-call(bf16[256,160]{1,0:T(8,128)(2,1)S(1)} %get-tuple-element.31.gather, bf16[320,256]{1,0:T(8,128)(2,1)S(1)} %get-tuple-element.32.chosen_high, bf16[320,256]{1,0:T(8,128)(2,1)S(1)} %get-tuple-element.33.chosen_low, bf16[256,128,128]{2,1,0:T(8,128)(2,1)S(1)} %get-tuple-element.34.blocks, ...), custom_call_target="tpu_custom_call" | custom-call | tf_op jit(solution)/shard_map/tiles/pallas_call | solution.py:528
  67.5 0.1 collective-permute-start.17
  67.6 1.3 %collective-permute-done.17 = f32[4,40,128]{2,1,0:T(8,128)S(1)} collective-permute-done((f32[4,40,128]{2,1,0:T(8,128)S(1)}, f32[4,40,128]{2,1,0:T(8,128)S(1)}, u32[]{:S(2)}, u32[]{:S(2)}) %collective-permute-start.17) | collective-permute-done | bytes 81952 | tf_op jit(solution)/shard_map/ppermute | solution.py:481
  68.9 1.8 %collective-permute-start.20 = (f32[40,128]{1,0:T(8,128)S(1)}, f32[40,128]{1,0:T(8,128)S(1)}, u32[]{:S(2)}, u32[]{:S(2)}) collective-permute-start(f32[40,128]{1,0:T(8,128)S(1)} %get-tuple-element.48), channel_id=1, source_target_pairs={{0,6},{1,7},{2,4},{3,5},{4,2},{5,3},{6,0},{7,1},{8,14},{9,15},{10,... | collective-permute-start | bytes 61448 | tf_op jit(solution)/shard_map/ppermute | solution.py:481
  70.6 1.6 %collective-permute-start.19 = (f32[40,128]{1,0:T(8,128)S(1)}, f32[40,128]{1,0:T(8,128)S(1)}, u32[]{:S(2)}, u32[]{:S(2)}) collective-permute-start(f32[40,128]{1,0:T(8,128)S(1)} %get-tuple-element.49), channel_id=1, source_target_pairs={{0,4},{1,5},{2,6},{3,7},{4,0},{5,1},{6,2},{7,3},{8,12},{9,13},{10,... | collective-permute-start | bytes 61448 | tf_op jit(solution)/shard_map/ppermute | solution.py:481
  72.2 1.1 %collective-permute-start.18 = (f32[40,128]{1,0:T(8,128)S(1)}, f32[40,128]{1,0:T(8,128)S(1)}, u32[]{:S(2)}, u32[]{:S(2)}) collective-permute-start(f32[40,128]{1,0:T(8,128)S(1)} %get-tuple-element.50), channel_id=1, source_target_pairs={{0,2},{1,3},{2,0},{3,1},{4,6},{5,7},{6,4},{7,5},{8,10},{9,11},{10,... | collective-permute-start | bytes 61448 | tf_op jit(solution)/shard_map/ppermute | solution.py:481
  73.3 1.2 %collective-permute-done.20.refs_3_ = f32[40,128]{1,0:T(8,128)S(1)} collective-permute-done((f32[40,128]{1,0:T(8,128)S(1)}, f32[40,128]{1,0:T(8,128)S(1)}, u32[]{:S(2)}, u32[]{:S(2)}) %collective-permute-start.20) | collective-permute-done | bytes 20512 | tf_op jit(solution)/shard_map/ppermute | solution.py:481
  74.5 0.8 collective-permute-done.19.refs_2_
  75.3 0.7 collective-permute-done.18.refs_1_
  76.0 0.1 fourth.1
  76.1 10.9 %all_to_all.11 = f32[32,1,128]{2,1,0:T(1,128)S(1)} all-to-all(f32[32,1,128]{2,1,0:T(1,128)S(1)} %bitcast.29), channel_id=1, replica_groups=mesh['row'=4,'col'=8] {'row','col'}, dimensions={0} | all-to-all | bytes 32768 | tf_op jit(solution)/shard_map/all_to_all | solution.py:573
  87.0 0.8 last.1
  (6 shorter events, 0.1 us)
Async XLA Ops:
  0.6 32.2 %copy-start = (f32[1,1,4608]{2,1,0:T(1,128)S(1)}, f32[1,1,4608]{2,1,0:T(1,128)}, u32[]{:S(2)}) copy-start(f32[1,1,4608]{2,1,0:T(1,128)} %rhs.7) | copy-start | bytes 55300
  0.6 32.1 %copy-start.1 = (f32[1,1,4608]{2,1,0:T(1,128)S(1)}, f32[1,1,4608]{2,1,0:T(1,128)}, u32[]{:S(2)}) copy-start(f32[1,1,4608]{2,1,0:T(1,128)} %friction.5) | copy-start | bytes 55300
  0.7 32.1 %copy-start.2 = (s32[1,1,24]{2,1,0:T(1,128)S(1)}, s32[1,1,24]{2,1,0:T(1,128)}, u32[]{:S(2)}) copy-start(s32[1,1,24]{2,1,0:T(1,128)} %sizes.3) | copy-start | bytes 292
  0.7 15.6 %copy-start.4 = (s32[1,1,256]{2,1,0:T(1,128)S(1)}, s32[1,1,256]{2,1,0:T(1,128)}, u32[]{:S(2)}) copy-start(s32[1,1,256]{2,1,0:T(1,128)} %tile_col.1) | copy-start | bytes 3076
  0.7 15.6 %copy-start.3 = (s32[1,1,256]{2,1,0:T(1,128)S(1)}, s32[1,1,256]{2,1,0:T(1,128)}, u32[]{:S(2)}) copy-start(s32[1,1,256]{2,1,0:T(1,128)} %tile_row.1) | copy-start | bytes 3076
  0.7 15.6 %copy-start.5 = (f32[1,1,256]{2,1,0:T(1,128)S(1)}, f32[1,1,256]{2,1,0:T(1,128)}, u32[]{:S(2)}) copy-start(f32[1,1,256]{2,1,0:T(1,128)} %scale.1) | copy-start | bytes 3076
  11.1 8.7 %collective-permute-start.2 = (f32[40,128]{1,0:T(8,128)S(1)}, f32[40,128]{1,0:T(8,128)S(1)}, u32[]{:S(2)}, u32[]{:S(2)}) collective-permute-start(f32[40,128]{1,0:T(8,128)S(1)} %get-tuple-element.30.refs_0_.refs_4_.sent0), channel_id=1, source_target_pairs={{0,24},{8,16},{16,8},{24,0},{1,25},{9,17},{17,9},{25,1},{2,26},{10... | collective-permute-start | bytes 61448 | tf_op jit(solution)/shard_map/ppermute | solution.py:481
  14.2 5.7 %collective-permute-start.1 = (f32[40,128]{1,0:T(8,128)S(1)}, f32[40,128]{1,0:T(8,128)S(1)}, u32[]{:S(2)}, u32[]{:S(2)}) collective-permute-start(f32[40,128]{1,0:T(8,128)S(1)} %get-tuple-element.30.refs_0_.refs_4_.sent0), channel_id=1, source_target_pairs={{0,16},{8,24},{16,0},{24,8},{1,17},{9,25},{17,1},{25,9},{2,18},{10... | collective-permute-start | bytes 61448 | tf_op jit(solution)/shard_map/ppermute | solution.py:481
  15.6 4.3 %collective-permute-start = (f32[40,128]{1,0:T(8,128)S(1)}, f32[40,128]{1,0:T(8,128)S(1)}, u32[]{:S(2)}, u32[]{:S(2)}) collective-permute-start(f32[40,128]{1,0:T(8,128)S(1)} %get-tuple-element.30.refs_0_.refs_4_.sent0), channel_id=1, source_target_pairs={{0,8},{8,0},{16,24},{24,16},{1,9},{9,1},{17,25},{25,17},{2,10},{10... | collective-permute-start | bytes 61448 | tf_op jit(solution)/shard_map/ppermute | solution.py:481
  22.5 1.3 %collective-permute-start.3 = (f32[4,40,128]{2,1,0:T(8,128)S(1)}, f32[4,40,128]{2,1,0:T(8,128)S(1)}, u32[]{:S(2)}, u32[]{:S(2)}) collective-permute-start(f32[4,40,128]{2,1,0:T(8,128)S(1)} %get-tuple-element.36), channel_id=1, source_target_pairs={{0,1},{1,0},{2,3},{3,2},{4,5},{5,4},{6,7},{7,6},{8,9},{9,8},{10,11... | collective-permute-start | bytes 245768 | tf_op jit(solution)/shard_map/ppermute | solution.py:481
  23.9 5.9 %collective-permute-start.6 = (f32[40,128]{1,0:T(8,128)S(1)}, f32[40,128]{1,0:T(8,128)S(1)}, u32[]{:S(2)}, u32[]{:S(2)}) collective-permute-start(f32[40,128]{1,0:T(8,128)S(1)} %get-tuple-element.56), channel_id=1, source_target_pairs={{0,6},{1,7},{2,4},{3,5},{4,2},{5,3},{6,0},{7,1},{8,14},{9,15},{10,... | collective-permute-start | bytes 61448 | tf_op jit(solution)/shard_map/ppermute | solution.py:481
  28.1 4.7 %collective-permute-start.5 = (f32[40,128]{1,0:T(8,128)S(1)}, f32[40,128]{1,0:T(8,128)S(1)}, u32[]{:S(2)}, u32[]{:S(2)}) collective-permute-start(f32[40,128]{1,0:T(8,128)S(1)} %get-tuple-element.57), channel_id=1, source_target_pairs={{0,4},{1,5},{2,6},{3,7},{4,0},{5,1},{6,2},{7,3},{8,12},{9,13},{10,... | collective-permute-start | bytes 61448 | tf_op jit(solution)/shard_map/ppermute | solution.py:481
  28.1 4.7 %collective-permute-start.4 = (f32[40,128]{1,0:T(8,128)S(1)}, f32[40,128]{1,0:T(8,128)S(1)}, u32[]{:S(2)}, u32[]{:S(2)}) collective-permute-start(f32[40,128]{1,0:T(8,128)S(1)} %get-tuple-element.58), channel_id=1, source_target_pairs={{0,2},{1,3},{2,0},{3,1},{4,6},{5,7},{6,4},{7,5},{8,10},{9,11},{10,... | collective-permute-start | bytes 61448 | tf_op jit(solution)/shard_map/ppermute | solution.py:481
  37.3 4.7 %collective-permute-start.9 = (f32[40,128]{1,0:T(8,128)S(1)}, f32[40,128]{1,0:T(8,128)S(1)}, u32[]{:S(2)}, u32[]{:S(2)}) collective-permute-start(f32[40,128]{1,0:T(8,128)S(1)} %get-tuple-element.37.refs_0_.refs_4_.sent1), channel_id=1, source_target_pairs={{0,24},{8,16},{16,8},{24,0},{1,25},{9,17},{17,9},{25,1},{2,26},{10... | collective-permute-start | bytes 61448 | tf_op jit(solution)/shard_map/ppermute | solution.py:481
  39.3 3.8 %collective-permute-start.8 = (f32[40,128]{1,0:T(8,128)S(1)}, f32[40,128]{1,0:T(8,128)S(1)}, u32[]{:S(2)}, u32[]{:S(2)}) collective-permute-start(f32[40,128]{1,0:T(8,128)S(1)} %get-tuple-element.37.refs_0_.refs_4_.sent1), channel_id=1, source_target_pairs={{0,16},{8,24},{16,0},{24,8},{1,17},{9,25},{17,1},{25,9},{2,18},{10... | collective-permute-start | bytes 61448 | tf_op jit(solution)/shard_map/ppermute | solution.py:481
  39.8 3.8 %collective-permute-start.7 = (f32[40,128]{1,0:T(8,128)S(1)}, f32[40,128]{1,0:T(8,128)S(1)}, u32[]{:S(2)}, u32[]{:S(2)}) collective-permute-start(f32[40,128]{1,0:T(8,128)S(1)} %get-tuple-element.37.refs_0_.refs_4_.sent1), channel_id=1, source_target_pairs={{0,8},{8,0},{16,24},{24,16},{1,9},{9,1},{17,25},{25,17},{2,10},{10... | collective-permute-start | bytes 61448 | tf_op jit(solution)/shard_map/ppermute | solution.py:481
  46.2 1.3 %collective-permute-start.10 = (f32[4,40,128]{2,1,0:T(8,128)S(1)}, f32[4,40,128]{2,1,0:T(8,128)S(1)}, u32[]{:S(2)}, u32[]{:S(2)}) collective-permute-start(f32[4,40,128]{2,1,0:T(8,128)S(1)} %get-tuple-element.40), channel_id=1, source_target_pairs={{0,1},{1,0},{2,3},{3,2},{4,5},{5,4},{6,7},{7,6},{8,9},{9,8},{10,11... | collective-permute-start | bytes 245768 | tf_op jit(solution)/shard_map/ppermute | solution.py:481
  47.6 5.6 %collective-permute-start.13 = (f32[40,128]{1,0:T(8,128)S(1)}, f32[40,128]{1,0:T(8,128)S(1)}, u32[]{:S(2)}, u32[]{:S(2)}) collective-permute-start(f32[40,128]{1,0:T(8,128)S(1)} %get-tuple-element.52), channel_id=1, source_target_pairs={{0,6},{1,7},{2,4},{3,5},{4,2},{5,3},{6,0},{7,1},{8,14},{9,15},{10,... | collective-permute-start | bytes 61448 | tf_op jit(solution)/shard_map/ppermute | solution.py:481
  49.1 4.8 %collective-permute-start.12 = (f32[40,128]{1,0:T(8,128)S(1)}, f32[40,128]{1,0:T(8,128)S(1)}, u32[]{:S(2)}, u32[]{:S(2)}) collective-permute-start(f32[40,128]{1,0:T(8,128)S(1)} %get-tuple-element.53), channel_id=1, source_target_pairs={{0,4},{1,5},{2,6},{3,7},{4,0},{5,1},{6,2},{7,3},{8,12},{9,13},{10,... | collective-permute-start | bytes 61448 | tf_op jit(solution)/shard_map/ppermute | solution.py:481
  49.5 4.5 %collective-permute-start.11 = (f32[40,128]{1,0:T(8,128)S(1)}, f32[40,128]{1,0:T(8,128)S(1)}, u32[]{:S(2)}, u32[]{:S(2)}) collective-permute-start(f32[40,128]{1,0:T(8,128)S(1)} %get-tuple-element.54), channel_id=1, source_target_pairs={{0,2},{1,3},{2,0},{3,1},{4,6},{5,7},{6,4},{7,5},{8,10},{9,11},{10,... | collective-permute-start | bytes 61448 | tf_op jit(solution)/shard_map/ppermute | solution.py:481
  58.5 4.8 %collective-permute-start.16 = (f32[40,128]{1,0:T(8,128)S(1)}, f32[40,128]{1,0:T(8,128)S(1)}, u32[]{:S(2)}, u32[]{:S(2)}) collective-permute-start(f32[40,128]{1,0:T(8,128)S(1)} %get-tuple-element.41.refs_0_.sent.sent2), channel_id=1, source_target_pairs={{0,24},{8,16},{16,8},{24,0},{1,25},{9,17},{17,9},{25,1},{2,26},{10... | collective-permute-start | bytes 61448 | tf_op jit(solution)/shard_map/ppermute | solution.py:481
  59.6 3.9 %collective-permute-start.15 = (f32[40,128]{1,0:T(8,128)S(1)}, f32[40,128]{1,0:T(8,128)S(1)}, u32[]{:S(2)}, u32[]{:S(2)}) collective-permute-start(f32[40,128]{1,0:T(8,128)S(1)} %get-tuple-element.41.refs_0_.sent.sent2), channel_id=1, source_target_pairs={{0,16},{8,24},{16,0},{24,8},{1,17},{9,25},{17,1},{25,9},{2,18},{10... | collective-permute-start | bytes 61448 | tf_op jit(solution)/shard_map/ppermute | solution.py:481
  61.1 3.8 %collective-permute-start.14 = (f32[40,128]{1,0:T(8,128)S(1)}, f32[40,128]{1,0:T(8,128)S(1)}, u32[]{:S(2)}, u32[]{:S(2)}) collective-permute-start(f32[40,128]{1,0:T(8,128)S(1)} %get-tuple-element.41.refs_0_.sent.sent2), channel_id=1, source_target_pairs={{0,8},{8,0},{16,24},{24,16},{1,9},{9,1},{17,25},{25,17},{2,10},{10... | collective-permute-start | bytes 61448 | tf_op jit(solution)/shard_map/ppermute | solution.py:481
  67.5 1.3 %collective-permute-start.17 = (f32[4,40,128]{2,1,0:T(8,128)S(1)}, f32[4,40,128]{2,1,0:T(8,128)S(1)}, u32[]{:S(2)}, u32[]{:S(2)}) collective-permute-start(f32[4,40,128]{2,1,0:T(8,128)S(1)} %get-tuple-element.45), channel_id=1, source_target_pairs={{0,1},{1,0},{2,3},{3,2},{4,5},{5,4},{6,7},{7,6},{8,9},{9,8},{10,11... | collective-permute-start | bytes 245768 | tf_op jit(solution)/shard_map/ppermute | solution.py:481
  68.9 5.7 %collective-permute-start.20 = (f32[40,128]{1,0:T(8,128)S(1)}, f32[40,128]{1,0:T(8,128)S(1)}, u32[]{:S(2)}, u32[]{:S(2)}) collective-permute-start(f32[40,128]{1,0:T(8,128)S(1)} %get-tuple-element.48), channel_id=1, source_target_pairs={{0,6},{1,7},{2,4},{3,5},{4,2},{5,3},{6,0},{7,1},{8,14},{9,15},{10,... | collective-permute-start | bytes 61448 | tf_op jit(solution)/shard_map/ppermute | solution.py:481
  70.6 4.7 %collective-permute-start.19 = (f32[40,128]{1,0:T(8,128)S(1)}, f32[40,128]{1,0:T(8,128)S(1)}, u32[]{:S(2)}, u32[]{:S(2)}) collective-permute-start(f32[40,128]{1,0:T(8,128)S(1)} %get-tuple-element.49), channel_id=1, source_target_pairs={{0,4},{1,5},{2,6},{3,7},{4,0},{5,1},{6,2},{7,3},{8,12},{9,13},{10,... | collective-permute-start | bytes 61448 | tf_op jit(solution)/shard_map/ppermute | solution.py:481
  72.2 3.8 %collective-permute-start.18 = (f32[40,128]{1,0:T(8,128)S(1)}, f32[40,128]{1,0:T(8,128)S(1)}, u32[]{:S(2)}, u32[]{:S(2)}) collective-permute-start(f32[40,128]{1,0:T(8,128)S(1)} %get-tuple-element.50), channel_id=1, source_target_pairs={{0,2},{1,3},{2,0},{3,1},{4,6},{5,7},{6,4},{7,5},{8,10},{9,11},{10,... | collective-permute-start | bytes 61448 | tf_op jit(solution)/shard_map/ppermute | solution.py:481

commit v7 on v6

--- a/solution.py
+++ b/solution.py
@@ -59,26 +59,31 @@
     return scalars
 
 
-def quarters(remote, blocks, sems, f, which):
+def leading(remote, blocks, sems, group):
+    near = pl.ds(0, blocks.shape[1] // 2)
+    part = (pl.ds(group * 8, 8), near, near)
+    return pltpu.make_async_copy(remote.at[(0, 0) + part], blocks.at[part], sems.at[0, group])
+
+
+def beyond(remote, blocks, sems, f):
     half = blocks.shape[1] // 2
-    near, far = pl.ds(0, half), pl.ds(half, half)
     return [
         pltpu.make_async_copy(
             remote.at[(0, 0, f) + part], blocks.at[(f,) + part], sems.at[place, f]
         )
-        for place, part in list(enumerate([(near, near), (near, far), (far,)]))[which]
+        for place, part in [(1, (pl.ds(0, half), pl.ds(half, half))), (2, (pl.ds(half, half),))]
     ]
 
 
 def fetch(scalars, remote, blocks, sems):
     half = blocks.shape[1] // 2
-    for f in range(len(scalars)):
-        quarters(remote, blocks, sems, f, slice(0, 1))[0].start()
+    for group in range(len(scalars) // 8):
+        leading(remote, blocks, sems, group).start()
     for f, (_, _, size) in enumerate(scalars):
 
         @pl.when(size > half)
         def _():
-            for copy in quarters(remote, blocks, sems, f, slice(1, 3)):
+            for copy in beyond(remote, blocks, sems, f):
                 copy.start()
 
 
@@ -145,8 +150,8 @@
         sums = [jnp.zeros((8, LANES), F32) for _ in range(chunk_half)]
         for place in range(8):
             f = group * 8 + place
-            if not local:
-                quarters(remote, blocks, sems, f, slice(0, 1))[0].wait()
+            if not local and place == 0:
+                leading(remote, blocks, sems, group).wait()
             result = dot_nt(left[:, :half], blocks[f, :half, :half])
             result = result[:8] + result[8:]
             for k in range(chunk_half):
@@ -168,7 +173,7 @@
 
                 @pl.when(place < count)
                 def _():
-                    for copy in quarters(remote, blocks, sems, f, slice(1, 3)):
+                    for copy in beyond(remote, blocks, sems, f):
                         copy.wait()
 
             above = dot_nt(left[:, half:], blocks[f, :half, half:])

time: 87.9 us -> 84.6 us (0.962)
  Pallas kernels: 31.8 us -> 26.9 us
  starting transfers between devices: 25.5 us -> 26.6 us
    pallas_call x1, Pallas kernels: 10.4 us -> 6.47 us  [local(): pl.pallas_call(first_kernel, out_shape=[grid, pltpu.VMEM((faults, width,...]
    ppermute x21, starting transfers between devices: 25.5 us -> 26.6 us  [exchange(): return lax.ppermute(value, axis, [(i, i ^ distance) for i in range(size)])]
  transfers between devices with their start and end apart: 21 -> 21, of which waited for: 17 -> 15; matrix products, arithmetic and copies ran while one was open for 0% -> 0% of each run, Pallas kernels for 4% -> 4%
where the time goes in v7:
time: 84.6 us; the launch traced here: 84.2 us
  Pallas kernels  26.9 us (32%)
  starting transfers between devices  26.6 us (31%)
  waiting for transfers between devices  18.4 us (22%)
  blocking collectives  10.7 us (13%)
  between operations  1.51 us (2%)
    ppermute x21, starting transfers between devices, exchange(): return lax.ppermute(value, axis, [(i, i ^ distance) for i in range(size)])  26.6 us
    ppermute x21, waiting for transfers between devices, exchange(): return lax.ppermute(value, axis, [(i, i ^ distance) for i in range(size)])  18.4 us
    all_to_all x1, blocking collectives, local(): sums = lax.all_to_all(sums, ('row', 'col'), 0, 0, tiled=True)  10.7 us
    pallas_call x3, Pallas kernels, apply_kernel(): pl.pallas_call(functools.partial(tiles_kernel, tiles % 8), out_shape=[hal...  7.92 us
    pallas_call x1, Pallas kernels, local(): pl.pallas_call(first_kernel, out_shape=[grid, pltpu.VMEM((faults, width,...  6.47 us
    pallas_call x1, Pallas kernels, local(): pl.pallas_call(second_kernel, out_shape=[grid, plain, grid], in_specs=[SM...  4.07 us
    pallas_call x1, Pallas kernels, local(): pl.pallas_call(third_kernel, out_shape=[grid, plain], in_specs=[SMEM, VME...  4.01 us
    pallas_call x1, Pallas kernels, local(): pl.pallas_call(functools.partial(prepare_kernel, (tiles, height, row_coun...  3.54 us
  transfers between devices with their start and end apart: 21, of which 15 were waited for; matrix products, arithmetic and copies ran while one was open for 0% of the time, Pallas kernels for 4%

profile of v7, /device:TPU:0, one launch (start us, length us, event | category | flops | bytes accessed | tf_op | source)
XLA Modules:
  0.0 84.2 jit_solution(16098372733044388337)
XLA Ops:
  0.6 0.0 copy-start
  0.6 0.0 copy-start.1
  0.7 0.0 copy-start.2
  0.7 0.0 copy-start.4
  0.7 0.0 copy-start.3
  0.7 0.0 copy-start.5
  0.7 6.5 %first.1 = (f32[40,128]{1,0:T(8,128)S(1)}, bf16[24,512,512]{2,1,0:T(8,128)(2,1)S(1)}, bf16[48,128]{1,0:T(8,128)(2,1)S(1)}, bf16[128,48]{1,0:T(8,128)(2,1)S(1)}, ...) custom-call(s32[1,1,24]{2,1,0:T(1,128)} %sizes.3, f32[1,1,4608]{2,1,0:T(1,128)} %rhs.7, f32[1,1,4608]{2,1,0:T(1,128)} %friction.5, ...), custom_call_target="tpu_custom_call" | custom-call | tf_op jit(solution)/shard_map/first/pallas_call | solution.py:491
  7.2 4.9 %collective-permute-start.2 = (f32[40,128]{1,0:T(8,128)S(1)}, f32[40,128]{1,0:T(8,128)S(1)}, u32[]{:S(2)}, u32[]{:S(2)}) collective-permute-start(f32[40,128]{1,0:T(8,128)S(1)} %get-tuple-element.30.refs_0_.refs_4_.sent0), channel_id=1, source_target_pairs={{0,24},{8,16},{16,8},{24,0},{1,25},{9,17},{17,9},{25,1},{2,26},{10... | collective-permute-start | bytes 61448 | tf_op jit(solution)/shard_map/ppermute | solution.py:486
  12.0 0.0 collective-permute-start.1
  12.0 0.6 collective-permute-start
  13.3 0.0 copy-done.4
  13.3 0.0 copy-done.3
  13.4 0.0 copy-done.5
  13.4 3.5 %prepare.1 = (bf16[256,128,128]{2,1,0:T(8,128)(2,1)S(1)}, bf16[256,160]{1,0:T(8,128)(2,1)S(1)}, bf16[320,256]{1,0:T(8,128)(2,1)S(1)}, bf16[320,256]{1,0:T(8,128)(2,1)S(1)}) custom-call(s32[24,128]{1,0:T(8,128)S(1)} %get-tuple-element.29.after.refs_3_, s32[1,1]{1,0:T(1,128)S(6)} %copy.12.counts, s32[1,1,256]{2,1,0:T(1,128)S(1)} %copy-done.3, ...), custom_call_target="tpu_custom_call" | custom-call | tf_op jit(solution)/shard_map/prepare/pallas_call | solution.py:516
  16.9 0.0 collective-permute-done.2.refs_3_
  16.9 0.0 collective-permute-done.1.refs_2_
  16.9 0.0 collective-permute-done.refs_1_
  16.9 2.6 %tiles.3 = (f32[4,40,128]{2,1,0:T(8,128)S(1)}, f32[4,40,128]{2,1,0:T(8,128)S(1)}) custom-call(bf16[256,160]{1,0:T(8,128)(2,1)S(1)} %get-tuple-element.31.gather, bf16[320,256]{1,0:T(8,128)(2,1)S(1)} %get-tuple-element.32.chosen_high, bf16[320,256]{1,0:T(8,128)(2,1)S(1)} %get-tuple-element.33.chosen_low, bf16[256,128,128]{2,1,0:T(8,128)(2,1)S(1)} %get-tuple-element.34.blocks, ...), custom_call_target="tpu_custom_call" | custom-call | tf_op jit(solution)/shard_map/tiles/pallas_call | solution.py:533
  19.6 0.1 collective-permute-start.3
  19.7 1.3 %collective-permute-done.3 = f32[4,40,128]{2,1,0:T(8,128)S(1)} collective-permute-done((f32[4,40,128]{2,1,0:T(8,128)S(1)}, f32[4,40,128]{2,1,0:T(8,128)S(1)}, u32[]{:S(2)}, u32[]{:S(2)}) %collective-permute-start.3) | collective-permute-done | bytes 81952 | tf_op jit(solution)/shard_map/ppermute | solution.py:486
  21.0 3.6 %collective-permute-start.6 = (f32[40,128]{1,0:T(8,128)S(1)}, f32[40,128]{1,0:T(8,128)S(1)}, u32[]{:S(2)}, u32[]{:S(2)}) collective-permute-start(f32[40,128]{1,0:T(8,128)S(1)} %get-tuple-element.56), channel_id=1, source_target_pairs={{0,6},{1,7},{2,4},{3,5},{4,2},{5,3},{6,0},{7,1},{8,14},{9,15},{10,... | collective-permute-start | bytes 61448 | tf_op jit(solution)/shard_map/ppermute | solution.py:486
  24.5 0.0 collective-permute-start.5
  24.5 0.9 %collective-permute-start.4 = (f32[40,128]{1,0:T(8,128)S(1)}, f32[40,128]{1,0:T(8,128)S(1)}, u32[]{:S(2)}, u32[]{:S(2)}) collective-permute-start(f32[40,128]{1,0:T(8,128)S(1)} %get-tuple-element.58), channel_id=1, source_target_pairs={{0,2},{1,3},{2,0},{3,1},{4,6},{5,7},{6,4},{7,5},{8,10},{9,11},{10,... | collective-permute-start | bytes 61448 | tf_op jit(solution)/shard_map/ppermute | solution.py:486
  25.4 1.2 %collective-permute-done.6.refs_8_ = f32[40,128]{1,0:T(8,128)S(1)} collective-permute-done((f32[40,128]{1,0:T(8,128)S(1)}, f32[40,128]{1,0:T(8,128)S(1)}, u32[]{:S(2)}, u32[]{:S(2)}) %collective-permute-start.6) | collective-permute-done | bytes 20512 | tf_op jit(solution)/shard_map/ppermute | solution.py:486
  26.6 2.6 %collective-permute-done.5.refs_7_ = f32[40,128]{1,0:T(8,128)S(1)} collective-permute-done((f32[40,128]{1,0:T(8,128)S(1)}, f32[40,128]{1,0:T(8,128)S(1)}, u32[]{:S(2)}, u32[]{:S(2)}) %collective-permute-start.5) | collective-permute-done | bytes 20512 | tf_op jit(solution)/shard_map/ppermute | solution.py:486
  29.2 0.0 collective-permute-done.4.refs_6_
  29.2 0.0 copy-done
  29.2 0.0 copy-done.1
  29.2 0.0 copy-done.2
  29.2 4.1 %second.1 = (f32[40,128]{1,0:T(8,128)S(1)}, f32[36,128]{1,0:T(8,128)S(1)}, f32[40,128]{1,0:T(8,128)S(1)}) custom-call(s32[1,1,24]{2,1,0:T(1,128)S(1)} %copy-done.2, f32[1,1,4608]{2,1,0:T(1,128)S(1)} %copy-done, f32[1,1,4608]{2,1,0:T(1,128)S(1)} %copy-done.1, bf16[24,512,512]{2,1,0:T(8,128)(2,1)S(1)} %get-tuple-element.25.blocks, ...), custom_call_target="tpu_custom_call" | custom-call | tf_op jit(solution)/shard_map/second/pallas_call | solution.py:549
  33.3 2.6 %collective-permute-start.9 = (f32[40,128]{1,0:T(8,128)S(1)}, f32[40,128]{1,0:T(8,128)S(1)}, u32[]{:S(2)}, u32[]{:S(2)}) collective-permute-start(f32[40,128]{1,0:T(8,128)S(1)} %get-tuple-element.37.refs_0_.refs_4_.sent1), channel_id=1, source_target_pairs={{0,24},{8,16},{16,8},{24,0},{1,25},{9,17},{17,9},{25,1},{2,26},{10... | collective-permute-start | bytes 61448 | tf_op jit(solution)/shard_map/ppermute | solution.py:486
  35.9 0.8 collective-permute-start.8
  36.8 0.5 collective-permute-start.7
  37.3 0.7 collective-permute-done.9.refs_3_
  38.0 1.7 %collective-permute-done.8.refs_2_ = f32[40,128]{1,0:T(8,128)S(1)} collective-permute-done((f32[40,128]{1,0:T(8,128)S(1)}, f32[40,128]{1,0:T(8,128)S(1)}, u32[]{:S(2)}, u32[]{:S(2)}) %collective-permute-start.8) | collective-permute-done | bytes 20512 | tf_op jit(solution)/shard_map/ppermute | solution.py:486
  39.7 0.8 collective-permute-done.7.refs_1_
  40.5 2.6 %tiles.4 = (f32[4,40,128]{2,1,0:T(8,128)S(1)}, f32[4,40,128]{2,1,0:T(8,128)S(1)}) custom-call(bf16[256,160]{1,0:T(8,128)(2,1)S(1)} %get-tuple-element.31.gather, bf16[320,256]{1,0:T(8,128)(2,1)S(1)} %get-tuple-element.32.chosen_high, bf16[320,256]{1,0:T(8,128)(2,1)S(1)} %get-tuple-element.33.chosen_low, bf16[256,128,128]{2,1,0:T(8,128)(2,1)S(1)} %get-tuple-element.34.blocks, ...), custom_call_target="tpu_custom_call" | custom-call | tf_op jit(solution)/shard_map/tiles/pallas_call | solution.py:533
  43.2 0.1 collective-permute-start.10
  43.3 1.3 %collective-permute-done.10 = f32[4,40,128]{2,1,0:T(8,128)S(1)} collective-permute-done((f32[4,40,128]{2,1,0:T(8,128)S(1)}, f32[4,40,128]{2,1,0:T(8,128)S(1)}, u32[]{:S(2)}, u32[]{:S(2)}) %collective-permute-start.10) | collective-permute-done | bytes 81952 | tf_op jit(solution)/shard_map/ppermute | solution.py:486
  44.6 2.0 %collective-permute-start.13 = (f32[40,128]{1,0:T(8,128)S(1)}, f32[40,128]{1,0:T(8,128)S(1)}, u32[]{:S(2)}, u32[]{:S(2)}) collective-permute-start(f32[40,128]{1,0:T(8,128)S(1)} %get-tuple-element.52), channel_id=1, source_target_pairs={{0,6},{1,7},{2,4},{3,5},{4,2},{5,3},{6,0},{7,1},{8,14},{9,15},{10,... | collective-permute-start | bytes 61448 | tf_op jit(solution)/shard_map/ppermute | solution.py:486
  46.5 0.6 collective-permute-start.12
  47.2 1.8 %collective-permute-start.11 = (f32[40,128]{1,0:T(8,128)S(1)}, f32[40,128]{1,0:T(8,128)S(1)}, u32[]{:S(2)}, u32[]{:S(2)}) collective-permute-start(f32[40,128]{1,0:T(8,128)S(1)} %get-tuple-element.54), channel_id=1, source_target_pairs={{0,2},{1,3},{2,0},{3,1},{4,6},{5,7},{6,4},{7,5},{8,10},{9,11},{10,... | collective-permute-start | bytes 61448 | tf_op jit(solution)/shard_map/ppermute | solution.py:486
  49.0 1.3 %collective-permute-done.13.refs_9_ = f32[40,128]{1,0:T(8,128)S(1)} collective-permute-done((f32[40,128]{1,0:T(8,128)S(1)}, f32[40,128]{1,0:T(8,128)S(1)}, u32[]{:S(2)}, u32[]{:S(2)}) %collective-permute-start.13) | collective-permute-done | bytes 20512 | tf_op jit(solution)/shard_map/ppermute | solution.py:486
  50.3 0.9 %collective-permute-done.12.refs_8_ = f32[40,128]{1,0:T(8,128)S(1)} collective-permute-done((f32[40,128]{1,0:T(8,128)S(1)}, f32[40,128]{1,0:T(8,128)S(1)}, u32[]{:S(2)}, u32[]{:S(2)}) %collective-permute-start.12) | collective-permute-done | bytes 20512 | tf_op jit(solution)/shard_map/ppermute | solution.py:486
  51.2 0.0 collective-permute-done.11.refs_7_
  51.2 4.0 %third.1 = (f32[40,128]{1,0:T(8,128)S(1)}, f32[36,128]{1,0:T(8,128)S(1)}) custom-call(s32[1,1,24]{2,1,0:T(1,128)S(1)} %copy-done.2, f32[1,1,4608]{2,1,0:T(1,128)S(1)} %copy-done, f32[1,1,4608]{2,1,0:T(1,128)S(1)} %copy-done.1, bf16[24,512,512]{2,1,0:T(8,128)(2,1)S(1)} %get-tuple-element.25.blocks, bf16[48,128]{1,0:T(8,128)(2,1)S(1)} %get-tuple-element.26.refs_0_, ...), custom_call_target="tpu_custom_call" | custom-call | tf_op jit(solution)/shard_map/third/pallas_call | solution.py:559
  55.3 2.2 %collective-permute-start.16 = (f32[40,128]{1,0:T(8,128)S(1)}, f32[40,128]{1,0:T(8,128)S(1)}, u32[]{:S(2)}, u32[]{:S(2)}) collective-permute-start(f32[40,128]{1,0:T(8,128)S(1)} %get-tuple-element.41.refs_0_.sent.sent2), channel_id=1, source_target_pairs={{0,24},{8,16},{16,8},{24,0},{1,25},{9,17},{17,9},{25,1},{2,26},{10... | collective-permute-start | bytes 61448 | tf_op jit(solution)/shard_map/ppermute | solution.py:486
  57.5 0.0 collective-permute-start.15
  57.5 1.3 %collective-permute-start.14 = (f32[40,128]{1,0:T(8,128)S(1)}, f32[40,128]{1,0:T(8,128)S(1)}, u32[]{:S(2)}, u32[]{:S(2)}) collective-permute-start(f32[40,128]{1,0:T(8,128)S(1)} %get-tuple-element.41.refs_0_.sent.sent2), channel_id=1, source_target_pairs={{0,8},{8,0},{16,24},{24,16},{1,9},{9,1},{17,25},{25,17},{2,10},{10... | collective-permute-start | bytes 61448 | tf_op jit(solution)/shard_map/ppermute | solution.py:486
  58.8 1.2 %collective-permute-done.16.refs_3_ = f32[40,128]{1,0:T(8,128)S(1)} collective-permute-done((f32[40,128]{1,0:T(8,128)S(1)}, f32[40,128]{1,0:T(8,128)S(1)}, u32[]{:S(2)}, u32[]{:S(2)}) %collective-permute-start.16) | collective-permute-done | bytes 20512 | tf_op jit(solution)/shard_map/ppermute | solution.py:486
  60.0 1.3 %collective-permute-done.15.refs_2_ = f32[40,128]{1,0:T(8,128)S(1)} collective-permute-done((f32[40,128]{1,0:T(8,128)S(1)}, f32[40,128]{1,0:T(8,128)S(1)}, u32[]{:S(2)}, u32[]{:S(2)}) %collective-permute-start.15) | collective-permute-done | bytes 20512 | tf_op jit(solution)/shard_map/ppermute | solution.py:486
  61.3 0.0 collective-permute-done.14.refs_1_
  61.3 2.6 %tiles.5 = (f32[4,40,128]{2,1,0:T(8,128)S(1)}, f32[4,40,128]{2,1,0:T(8,128)S(1)}) custom-call(bf16[256,160]{1,0:T(8,128)(2,1)S(1)} %get-tuple-element.31.gather, bf16[320,256]{1,0:T(8,128)(2,1)S(1)} %get-tuple-element.32.chosen_high, bf16[320,256]{1,0:T(8,128)(2,1)S(1)} %get-tuple-element.33.chosen_low, bf16[256,128,128]{2,1,0:T(8,128)(2,1)S(1)} %get-tuple-element.34.blocks, ...), custom_call_target="tpu_custom_call" | custom-call | tf_op jit(solution)/shard_map/tiles/pallas_call | solution.py:533
  63.9 0.1 collective-permute-start.17
  64.0 1.3 %collective-permute-done.17 = f32[4,40,128]{2,1,0:T(8,128)S(1)} collective-permute-done((f32[4,40,128]{2,1,0:T(8,128)S(1)}, f32[4,40,128]{2,1,0:T(8,128)S(1)}, u32[]{:S(2)}, u32[]{:S(2)}) %collective-permute-start.17) | collective-permute-done | bytes 81952 | tf_op jit(solution)/shard_map/ppermute | solution.py:486
  65.3 2.4 %collective-permute-start.20 = (f32[40,128]{1,0:T(8,128)S(1)}, f32[40,128]{1,0:T(8,128)S(1)}, u32[]{:S(2)}, u32[]{:S(2)}) collective-permute-start(f32[40,128]{1,0:T(8,128)S(1)} %get-tuple-element.48), channel_id=1, source_target_pairs={{0,6},{1,7},{2,4},{3,5},{4,2},{5,3},{6,0},{7,1},{8,14},{9,15},{10,... | collective-permute-start | bytes 61448 | tf_op jit(solution)/shard_map/ppermute | solution.py:486
  67.7 0.9 %collective-permute-start.19 = (f32[40,128]{1,0:T(8,128)S(1)}, f32[40,128]{1,0:T(8,128)S(1)}, u32[]{:S(2)}, u32[]{:S(2)}) collective-permute-start(f32[40,128]{1,0:T(8,128)S(1)} %get-tuple-element.49), channel_id=1, source_target_pairs={{0,4},{1,5},{2,6},{3,7},{4,0},{5,1},{6,2},{7,3},{8,12},{9,13},{10,... | collective-permute-start | bytes 61448 | tf_op jit(solution)/shard_map/ppermute | solution.py:486
  68.6 1.1 %collective-permute-start.18 = (f32[40,128]{1,0:T(8,128)S(1)}, f32[40,128]{1,0:T(8,128)S(1)}, u32[]{:S(2)}, u32[]{:S(2)}) collective-permute-start(f32[40,128]{1,0:T(8,128)S(1)} %get-tuple-element.50), channel_id=1, source_target_pairs={{0,2},{1,3},{2,0},{3,1},{4,6},{5,7},{6,4},{7,5},{8,10},{9,11},{10,... | collective-permute-start | bytes 61448 | tf_op jit(solution)/shard_map/ppermute | solution.py:486
  69.8 1.2 %collective-permute-done.20.refs_3_ = f32[40,128]{1,0:T(8,128)S(1)} collective-permute-done((f32[40,128]{1,0:T(8,128)S(1)}, f32[40,128]{1,0:T(8,128)S(1)}, u32[]{:S(2)}, u32[]{:S(2)}) %collective-permute-start.20) | collective-permute-done | bytes 20512 | tf_op jit(solution)/shard_map/ppermute | solution.py:486
  71.0 1.4 %collective-permute-done.19.refs_2_ = f32[40,128]{1,0:T(8,128)S(1)} collective-permute-done((f32[40,128]{1,0:T(8,128)S(1)}, f32[40,128]{1,0:T(8,128)S(1)}, u32[]{:S(2)}, u32[]{:S(2)}) %collective-permute-start.19) | collective-permute-done | bytes 20512 | tf_op jit(solution)/shard_map/ppermute | solution.py:486
  72.4 0.2 collective-permute-done.18.refs_1_
  72.6 0.1 fourth.1
  72.7 10.7 %all_to_all.11 = f32[32,1,128]{2,1,0:T(1,128)S(1)} all-to-all(f32[32,1,128]{2,1,0:T(1,128)S(1)} %bitcast.29), channel_id=1, replica_groups=mesh['row'=4,'col'=8] {'row','col'}, dimensions={0} | all-to-all | bytes 32768 | tf_op jit(solution)/shard_map/all_to_all | solution.py:578
  83.5 0.8 last.1
  (6 shorter events, 0.1 us)
Async XLA Ops:
  0.6 28.6 %copy-start = (f32[1,1,4608]{2,1,0:T(1,128)S(1)}, f32[1,1,4608]{2,1,0:T(1,128)}, u32[]{:S(2)}) copy-start(f32[1,1,4608]{2,1,0:T(1,128)} %rhs.7) | copy-start | bytes 55300
  0.6 28.6 %copy-start.1 = (f32[1,1,4608]{2,1,0:T(1,128)S(1)}, f32[1,1,4608]{2,1,0:T(1,128)}, u32[]{:S(2)}) copy-start(f32[1,1,4608]{2,1,0:T(1,128)} %friction.5) | copy-start | bytes 55300
  0.7 28.6 %copy-start.2 = (s32[1,1,24]{2,1,0:T(1,128)S(1)}, s32[1,1,24]{2,1,0:T(1,128)}, u32[]{:S(2)}) copy-start(s32[1,1,24]{2,1,0:T(1,128)} %sizes.3) | copy-start | bytes 292
  0.7 12.7 %copy-start.4 = (s32[1,1,256]{2,1,0:T(1,128)S(1)}, s32[1,1,256]{2,1,0:T(1,128)}, u32[]{:S(2)}) copy-start(s32[1,1,256]{2,1,0:T(1,128)} %tile_col.1) | copy-start | bytes 3076
  0.7 12.7 %copy-start.3 = (s32[1,1,256]{2,1,0:T(1,128)S(1)}, s32[1,1,256]{2,1,0:T(1,128)}, u32[]{:S(2)}) copy-start(s32[1,1,256]{2,1,0:T(1,128)} %tile_row.1) | copy-start | bytes 3076
  0.7 12.7 %copy-start.5 = (f32[1,1,256]{2,1,0:T(1,128)S(1)}, f32[1,1,256]{2,1,0:T(1,128)}, u32[]{:S(2)}) copy-start(f32[1,1,256]{2,1,0:T(1,128)} %scale.1) | copy-start | bytes 3076
  7.2 9.7 %collective-permute-start.2 = (f32[40,128]{1,0:T(8,128)S(1)}, f32[40,128]{1,0:T(8,128)S(1)}, u32[]{:S(2)}, u32[]{:S(2)}) collective-permute-start(f32[40,128]{1,0:T(8,128)S(1)} %get-tuple-element.30.refs_0_.refs_4_.sent0), channel_id=1, source_target_pairs={{0,24},{8,16},{16,8},{24,0},{1,25},{9,17},{17,9},{25,1},{2,26},{10... | collective-permute-start | bytes 61448 | tf_op jit(solution)/shard_map/ppermute | solution.py:486
  12.0 4.9 %collective-permute-start.1 = (f32[40,128]{1,0:T(8,128)S(1)}, f32[40,128]{1,0:T(8,128)S(1)}, u32[]{:S(2)}, u32[]{:S(2)}) collective-permute-start(f32[40,128]{1,0:T(8,128)S(1)} %get-tuple-element.30.refs_0_.refs_4_.sent0), channel_id=1, source_target_pairs={{0,16},{8,24},{16,0},{24,8},{1,17},{9,25},{17,1},{25,9},{2,18},{10... | collective-permute-start | bytes 61448 | tf_op jit(solution)/shard_map/ppermute | solution.py:486
  12.0 4.9 %collective-permute-start = (f32[40,128]{1,0:T(8,128)S(1)}, f32[40,128]{1,0:T(8,128)S(1)}, u32[]{:S(2)}, u32[]{:S(2)}) collective-permute-start(f32[40,128]{1,0:T(8,128)S(1)} %get-tuple-element.30.refs_0_.refs_4_.sent0), channel_id=1, source_target_pairs={{0,8},{8,0},{16,24},{24,16},{1,9},{9,1},{17,25},{25,17},{2,10},{10... | collective-permute-start | bytes 61448 | tf_op jit(solution)/shard_map/ppermute | solution.py:486
  19.6 1.3 %collective-permute-start.3 = (f32[4,40,128]{2,1,0:T(8,128)S(1)}, f32[4,40,128]{2,1,0:T(8,128)S(1)}, u32[]{:S(2)}, u32[]{:S(2)}) collective-permute-start(f32[4,40,128]{2,1,0:T(8,128)S(1)} %get-tuple-element.36), channel_id=1, source_target_pairs={{0,1},{1,0},{2,3},{3,2},{4,5},{5,4},{6,7},{7,6},{8,9},{9,8},{10,11... | collective-permute-start | bytes 245768 | tf_op jit(solution)/shard_map/ppermute | solution.py:486
  21.0 5.6 %collective-permute-start.6 = (f32[40,128]{1,0:T(8,128)S(1)}, f32[40,128]{1,0:T(8,128)S(1)}, u32[]{:S(2)}, u32[]{:S(2)}) collective-permute-start(f32[40,128]{1,0:T(8,128)S(1)} %get-tuple-element.56), channel_id=1, source_target_pairs={{0,6},{1,7},{2,4},{3,5},{4,2},{5,3},{6,0},{7,1},{8,14},{9,15},{10,... | collective-permute-start | bytes 61448 | tf_op jit(solution)/shard_map/ppermute | solution.py:486
  24.5 4.7 %collective-permute-start.5 = (f32[40,128]{1,0:T(8,128)S(1)}, f32[40,128]{1,0:T(8,128)S(1)}, u32[]{:S(2)}, u32[]{:S(2)}) collective-permute-start(f32[40,128]{1,0:T(8,128)S(1)} %get-tuple-element.57), channel_id=1, source_target_pairs={{0,4},{1,5},{2,6},{3,7},{4,0},{5,1},{6,2},{7,3},{8,12},{9,13},{10,... | collective-permute-start | bytes 61448 | tf_op jit(solution)/shard_map/ppermute | solution.py:486
  24.5 4.7 %collective-permute-start.4 = (f32[40,128]{1,0:T(8,128)S(1)}, f32[40,128]{1,0:T(8,128)S(1)}, u32[]{:S(2)}, u32[]{:S(2)}) collective-permute-start(f32[40,128]{1,0:T(8,128)S(1)} %get-tuple-element.58), channel_id=1, source_target_pairs={{0,2},{1,3},{2,0},{3,1},{4,6},{5,7},{6,4},{7,5},{8,10},{9,11},{10,... | collective-permute-start | bytes 61448 | tf_op jit(solution)/shard_map/ppermute | solution.py:486
  33.3 4.7 %collective-permute-start.9 = (f32[40,128]{1,0:T(8,128)S(1)}, f32[40,128]{1,0:T(8,128)S(1)}, u32[]{:S(2)}, u32[]{:S(2)}) collective-permute-start(f32[40,128]{1,0:T(8,128)S(1)} %get-tuple-element.37.refs_0_.refs_4_.sent1), channel_id=1, source_target_pairs={{0,24},{8,16},{16,8},{24,0},{1,25},{9,17},{17,9},{25,1},{2,26},{10... | collective-permute-start | bytes 61448 | tf_op jit(solution)/shard_map/ppermute | solution.py:486
  35.9 3.8 %collective-permute-start.8 = (f32[40,128]{1,0:T(8,128)S(1)}, f32[40,128]{1,0:T(8,128)S(1)}, u32[]{:S(2)}, u32[]{:S(2)}) collective-permute-start(f32[40,128]{1,0:T(8,128)S(1)} %get-tuple-element.37.refs_0_.refs_4_.sent1), channel_id=1, source_target_pairs={{0,16},{8,24},{16,0},{24,8},{1,17},{9,25},{17,1},{25,9},{2,18},{10... | collective-permute-start | bytes 61448 | tf_op jit(solution)/shard_map/ppermute | solution.py:486
  36.8 3.8 %collective-permute-start.7 = (f32[40,128]{1,0:T(8,128)S(1)}, f32[40,128]{1,0:T(8,128)S(1)}, u32[]{:S(2)}, u32[]{:S(2)}) collective-permute-start(f32[40,128]{1,0:T(8,128)S(1)} %get-tuple-element.37.refs_0_.refs_4_.sent1), channel_id=1, source_target_pairs={{0,8},{8,0},{16,24},{24,16},{1,9},{9,1},{17,25},{25,17},{2,10},{10... | collective-permute-start | bytes 61448 | tf_op jit(solution)/shard_map/ppermute | solution.py:486
  43.2 1.3 %collective-permute-start.10 = (f32[4,40,128]{2,1,0:T(8,128)S(1)}, f32[4,40,128]{2,1,0:T(8,128)S(1)}, u32[]{:S(2)}, u32[]{:S(2)}) collective-permute-start(f32[4,40,128]{2,1,0:T(8,128)S(1)} %get-tuple-element.40), channel_id=1, source_target_pairs={{0,1},{1,0},{2,3},{3,2},{4,5},{5,4},{6,7},{7,6},{8,9},{9,8},{10,11... | collective-permute-start | bytes 245768 | tf_op jit(solution)/shard_map/ppermute | solution.py:486
  44.6 5.7 %collective-permute-start.13 = (f32[40,128]{1,0:T(8,128)S(1)}, f32[40,128]{1,0:T(8,128)S(1)}, u32[]{:S(2)}, u32[]{:S(2)}) collective-permute-start(f32[40,128]{1,0:T(8,128)S(1)} %get-tuple-element.52), channel_id=1, source_target_pairs={{0,6},{1,7},{2,4},{3,5},{4,2},{5,3},{6,0},{7,1},{8,14},{9,15},{10,... | collective-permute-start | bytes 61448 | tf_op jit(solution)/shard_map/ppermute | solution.py:486
  46.5 4.7 %collective-permute-start.12 = (f32[40,128]{1,0:T(8,128)S(1)}, f32[40,128]{1,0:T(8,128)S(1)}, u32[]{:S(2)}, u32[]{:S(2)}) collective-permute-start(f32[40,128]{1,0:T(8,128)S(1)} %get-tuple-element.53), channel_id=1, source_target_pairs={{0,4},{1,5},{2,6},{3,7},{4,0},{5,1},{6,2},{7,3},{8,12},{9,13},{10,... | collective-permute-start | bytes 61448 | tf_op jit(solution)/shard_map/ppermute | solution.py:486
  47.2 4.0 %collective-permute-start.11 = (f32[40,128]{1,0:T(8,128)S(1)}, f32[40,128]{1,0:T(8,128)S(1)}, u32[]{:S(2)}, u32[]{:S(2)}) collective-permute-start(f32[40,128]{1,0:T(8,128)S(1)} %get-tuple-element.54), channel_id=1, source_target_pairs={{0,2},{1,3},{2,0},{3,1},{4,6},{5,7},{6,4},{7,5},{8,10},{9,11},{10,... | collective-permute-start | bytes 61448 | tf_op jit(solution)/shard_map/ppermute | solution.py:486
  55.3 4.7 %collective-permute-start.16 = (f32[40,128]{1,0:T(8,128)S(1)}, f32[40,128]{1,0:T(8,128)S(1)}, u32[]{:S(2)}, u32[]{:S(2)}) collective-permute-start(f32[40,128]{1,0:T(8,128)S(1)} %get-tuple-element.41.refs_0_.sent.sent2), channel_id=1, source_target_pairs={{0,24},{8,16},{16,8},{24,0},{1,25},{9,17},{17,9},{25,1},{2,26},{10... | collective-permute-start | bytes 61448 | tf_op jit(solution)/shard_map/ppermute | solution.py:486
  57.5 3.8 %collective-permute-start.15 = (f32[40,128]{1,0:T(8,128)S(1)}, f32[40,128]{1,0:T(8,128)S(1)}, u32[]{:S(2)}, u32[]{:S(2)}) collective-permute-start(f32[40,128]{1,0:T(8,128)S(1)} %get-tuple-element.41.refs_0_.sent.sent2), channel_id=1, source_target_pairs={{0,16},{8,24},{16,0},{24,8},{1,17},{9,25},{17,1},{25,9},{2,18},{10... | collective-permute-start | bytes 61448 | tf_op jit(solution)/shard_map/ppermute | solution.py:486
  57.5 3.8 %collective-permute-start.14 = (f32[40,128]{1,0:T(8,128)S(1)}, f32[40,128]{1,0:T(8,128)S(1)}, u32[]{:S(2)}, u32[]{:S(2)}) collective-permute-start(f32[40,128]{1,0:T(8,128)S(1)} %get-tuple-element.41.refs_0_.sent.sent2), channel_id=1, source_target_pairs={{0,8},{8,0},{16,24},{24,16},{1,9},{9,1},{17,25},{25,17},{2,10},{10... | collective-permute-start | bytes 61448 | tf_op jit(solution)/shard_map/ppermute | solution.py:486
  63.9 1.3 %collective-permute-start.17 = (f32[4,40,128]{2,1,0:T(8,128)S(1)}, f32[4,40,128]{2,1,0:T(8,128)S(1)}, u32[]{:S(2)}, u32[]{:S(2)}) collective-permute-start(f32[4,40,128]{2,1,0:T(8,128)S(1)} %get-tuple-element.45), channel_id=1, source_target_pairs={{0,1},{1,0},{2,3},{3,2},{4,5},{5,4},{6,7},{7,6},{8,9},{9,8},{10,11... | collective-permute-start | bytes 245768 | tf_op jit(solution)/shard_map/ppermute | solution.py:486
  65.3 5.7 %collective-permute-start.20 = (f32[40,128]{1,0:T(8,128)S(1)}, f32[40,128]{1,0:T(8,128)S(1)}, u32[]{:S(2)}, u32[]{:S(2)}) collective-permute-start(f32[40,128]{1,0:T(8,128)S(1)} %get-tuple-element.48), channel_id=1, source_target_pairs={{0,6},{1,7},{2,4},{3,5},{4,2},{5,3},{6,0},{7,1},{8,14},{9,15},{10,... | collective-permute-start | bytes 61448 | tf_op jit(solution)/shard_map/ppermute | solution.py:486
  67.7 4.7 %collective-permute-start.19 = (f32[40,128]{1,0:T(8,128)S(1)}, f32[40,128]{1,0:T(8,128)S(1)}, u32[]{:S(2)}, u32[]{:S(2)}) collective-permute-start(f32[40,128]{1,0:T(8,128)S(1)} %get-tuple-element.49), channel_id=1, source_target_pairs={{0,4},{1,5},{2,6},{3,7},{4,0},{5,1},{6,2},{7,3},{8,12},{9,13},{10,... | collective-permute-start | bytes 61448 | tf_op jit(solution)/shard_map/ppermute | solution.py:486
  68.6 4.0 %collective-permute-start.18 = (f32[40,128]{1,0:T(8,128)S(1)}, f32[40,128]{1,0:T(8,128)S(1)}, u32[]{:S(2)}, u32[]{:S(2)}) collective-permute-start(f32[40,128]{1,0:T(8,128)S(1)} %get-tuple-element.50), channel_id=1, source_target_pairs={{0,2},{1,3},{2,0},{3,1},{4,6},{5,7},{6,4},{7,5},{8,10},{9,11},{10,... | collective-permute-start | bytes 61448 | tf_op jit(solution)/shard_map/ppermute | solution.py:486

commit v8 on v7

--- a/solution.py
+++ b/solution.py
@@ -8,7 +8,7 @@
 from jax.sharding import PartitionSpec as P
 
 LANES = 128
-UNROLL = 3
+UNROLL = 4
 F32 = jnp.float32
 BF16 = jnp.bfloat16
 VMEM = pl.BlockSpec(memory_space=pltpu.VMEM)

time: 84.6 us -> 84.5 us (level)
  Pallas kernels: 26.9 us -> 28 us
  starting transfers between devices: 26.6 us -> 25.5 us
    ppermute x21, starting transfers between devices: 26.6 us -> 25.5 us  [exchange(): return lax.ppermute(value, axis, [(i, i ^ distance) for i in range(size)])]
  transfers between devices with their start and end apart: 21 -> 21, of which waited for: 15 -> 17; matrix products, arithmetic and copies ran while one was open for 0% -> 0% of each run, Pallas kernels for 4% -> 4%
where the time goes in v8:
time: 84.5 us; the launch traced here: 84.3 us
  Pallas kernels  28 us (33%)
  starting transfers between devices  25.5 us (30%)
  waiting for transfers between devices  18.2 us (22%)
  blocking collectives  11 us (13%)
  between operations  1.51 us (2%)
    ppermute x21, starting transfers between devices, exchange(): return lax.ppermute(value, axis, [(i, i ^ distance) for i in range(size)])  25.5 us
    ppermute x21, waiting for transfers between devices, exchange(): return lax.ppermute(value, axis, [(i, i ^ distance) for i in range(size)])  18.2 us
    all_to_all x1, blocking collectives, local(): sums = lax.all_to_all(sums, ('row', 'col'), 0, 0, tiled=True)  11 us
    pallas_call x3, Pallas kernels, apply_kernel(): pl.pallas_call(functools.partial(tiles_kernel, tiles % 8), out_shape=[hal...  7.92 us
    pallas_call x1, Pallas kernels, local(): pl.pallas_call(first_kernel, out_shape=[grid, pltpu.VMEM((faults, width,...  7.26 us
    pallas_call x1, Pallas kernels, local(): pl.pallas_call(second_kernel, out_shape=[grid, plain, grid], in_specs=[SM...  4.22 us
    pallas_call x1, Pallas kernels, local(): pl.pallas_call(third_kernel, out_shape=[grid, plain], in_specs=[SMEM, VME...  4.16 us
    pallas_call x1, Pallas kernels, local(): pl.pallas_call(functools.partial(prepare_kernel, (tiles, height, row_coun...  3.54 us
  transfers between devices with their start and end apart: 21, of which 17 were waited for; matrix products, arithmetic and copies ran while one was open for 0% of the time, Pallas kernels for 4%

profile of v8, /device:TPU:0, one launch (start us, length us, event | category | flops | bytes accessed | tf_op | source)
XLA Modules:
  0.0 84.3 jit_solution(4324780055181173076)
XLA Ops:
  0.6 0.0 copy-start
  0.6 0.0 copy-start.1
  0.7 0.0 copy-start.2
  0.7 0.0 copy-start.4
  0.7 0.0 copy-start.3
  0.7 0.0 copy-start.5
  0.7 7.3 %first.1 = (f32[40,128]{1,0:T(8,128)S(1)}, bf16[24,512,512]{2,1,0:T(8,128)(2,1)S(1)}, bf16[48,128]{1,0:T(8,128)(2,1)S(1)}, bf16[128,48]{1,0:T(8,128)(2,1)S(1)}, ...) custom-call(s32[1,1,24]{2,1,0:T(1,128)} %sizes.3, f32[1,1,4608]{2,1,0:T(1,128)} %rhs.7, f32[1,1,4608]{2,1,0:T(1,128)} %friction.5, ...), custom_call_target="tpu_custom_call" | custom-call | tf_op jit(solution)/shard_map/first/pallas_call | solution.py:491
  8.0 4.0 %collective-permute-start.2 = (f32[40,128]{1,0:T(8,128)S(1)}, f32[40,128]{1,0:T(8,128)S(1)}, u32[]{:S(2)}, u32[]{:S(2)}) collective-permute-start(f32[40,128]{1,0:T(8,128)S(1)} %get-tuple-element.30.refs_0_.refs_4_.sent0), channel_id=1, source_target_pairs={{0,24},{8,16},{16,8},{24,0},{1,25},{9,17},{17,9},{25,1},{2,26},{10... | collective-permute-start | bytes 61448 | tf_op jit(solution)/shard_map/ppermute | solution.py:486
  11.9 0.5 collective-permute-start.1
  12.4 0.1 collective-permute-start
  13.2 0.0 copy-done.4
  13.2 0.0 copy-done.3
  13.2 0.0 copy-done.5
  13.2 3.5 %prepare.1 = (bf16[256,128,128]{2,1,0:T(8,128)(2,1)S(1)}, bf16[256,160]{1,0:T(8,128)(2,1)S(1)}, bf16[320,256]{1,0:T(8,128)(2,1)S(1)}, bf16[320,256]{1,0:T(8,128)(2,1)S(1)}) custom-call(s32[24,128]{1,0:T(8,128)S(1)} %get-tuple-element.29.after.refs_3_, s32[1,1]{1,0:T(1,128)S(6)} %copy.12.counts, s32[1,1,256]{2,1,0:T(1,128)S(1)} %copy-done.3, ...), custom_call_target="tpu_custom_call" | custom-call | tf_op jit(solution)/shard_map/prepare/pallas_call | solution.py:516
  16.8 0.0 collective-permute-done.2.refs_3_
  16.8 0.0 collective-permute-done.1.refs_2_
  16.8 0.0 collective-permute-done.refs_1_
  16.8 2.6 %tiles.3 = (f32[4,40,128]{2,1,0:T(8,128)S(1)}, f32[4,40,128]{2,1,0:T(8,128)S(1)}) custom-call(bf16[256,160]{1,0:T(8,128)(2,1)S(1)} %get-tuple-element.31.gather, bf16[320,256]{1,0:T(8,128)(2,1)S(1)} %get-tuple-element.32.chosen_high, bf16[320,256]{1,0:T(8,128)(2,1)S(1)} %get-tuple-element.33.chosen_low, bf16[256,128,128]{2,1,0:T(8,128)(2,1)S(1)} %get-tuple-element.34.blocks, ...), custom_call_target="tpu_custom_call" | custom-call | tf_op jit(solution)/shard_map/tiles/pallas_call | solution.py:533
  19.5 0.1 collective-permute-start.3
  19.5 1.3 %collective-permute-done.3 = f32[4,40,128]{2,1,0:T(8,128)S(1)} collective-permute-done((f32[4,40,128]{2,1,0:T(8,128)S(1)}, f32[4,40,128]{2,1,0:T(8,128)S(1)}, u32[]{:S(2)}, u32[]{:S(2)}) %collective-permute-start.3) | collective-permute-done | bytes 81952 | tf_op jit(solution)/shard_map/ppermute | solution.py:486
  20.8 4.1 %collective-permute-start.6 = (f32[40,128]{1,0:T(8,128)S(1)}, f32[40,128]{1,0:T(8,128)S(1)}, u32[]{:S(2)}, u32[]{:S(2)}) collective-permute-start(f32[40,128]{1,0:T(8,128)S(1)} %get-tuple-element.56), channel_id=1, source_target_pairs={{0,6},{1,7},{2,4},{3,5},{4,2},{5,3},{6,0},{7,1},{8,14},{9,15},{10,... | collective-permute-start | bytes 61448 | tf_op jit(solution)/shard_map/ppermute | solution.py:486
  24.9 0.0 collective-permute-start.5
  24.9 0.6 collective-permute-start.4
  25.6 1.1 %collective-permute-done.6.refs_8_ = f32[40,128]{1,0:T(8,128)S(1)} collective-permute-done((f32[40,128]{1,0:T(8,128)S(1)}, f32[40,128]{1,0:T(8,128)S(1)}, u32[]{:S(2)}, u32[]{:S(2)}) %collective-permute-start.6) | collective-permute-done | bytes 20512 | tf_op jit(solution)/shard_map/ppermute | solution.py:486
  26.7 2.9 %collective-permute-done.5.refs_7_ = f32[40,128]{1,0:T(8,128)S(1)} collective-permute-done((f32[40,128]{1,0:T(8,128)S(1)}, f32[40,128]{1,0:T(8,128)S(1)}, u32[]{:S(2)}, u32[]{:S(2)}) %collective-permute-start.5) | collective-permute-done | bytes 20512 | tf_op jit(solution)/shard_map/ppermute | solution.py:486
  29.6 0.0 collective-permute-done.4.refs_6_
  29.6 0.0 copy-done
  29.6 0.0 copy-done.1
  29.6 0.0 copy-done.2
  29.6 4.2 %second.1 = (f32[40,128]{1,0:T(8,128)S(1)}, f32[36,128]{1,0:T(8,128)S(1)}, f32[40,128]{1,0:T(8,128)S(1)}) custom-call(s32[1,1,24]{2,1,0:T(1,128)S(1)} %copy-done.2, f32[1,1,4608]{2,1,0:T(1,128)S(1)} %copy-done, f32[1,1,4608]{2,1,0:T(1,128)S(1)} %copy-done.1, bf16[24,512,512]{2,1,0:T(8,128)(2,1)S(1)} %get-tuple-element.25.blocks, ...), custom_call_target="tpu_custom_call" | custom-call | tf_op jit(solution)/shard_map/second/pallas_call | solution.py:549
  33.8 2.4 %collective-permute-start.9 = (f32[40,128]{1,0:T(8,128)S(1)}, f32[40,128]{1,0:T(8,128)S(1)}, u32[]{:S(2)}, u32[]{:S(2)}) collective-permute-start(f32[40,128]{1,0:T(8,128)S(1)} %get-tuple-element.37.refs_0_.refs_4_.sent1), channel_id=1, source_target_pairs={{0,24},{8,16},{16,8},{24,0},{1,25},{9,17},{17,9},{25,1},{2,26},{10... | collective-permute-start | bytes 61448 | tf_op jit(solution)/shard_map/ppermute | solution.py:486
  36.3 0.5 collective-permute-start.8
  36.8 0.5 collective-permute-start.7
  37.3 1.2 %collective-permute-done.9.refs_3_ = f32[40,128]{1,0:T(8,128)S(1)} collective-permute-done((f32[40,128]{1,0:T(8,128)S(1)}, f32[40,128]{1,0:T(8,128)S(1)}, u32[]{:S(2)}, u32[]{:S(2)}) %collective-permute-start.9) | collective-permute-done | bytes 20512 | tf_op jit(solution)/shard_map/ppermute | solution.py:486
  38.5 1.5 %collective-permute-done.8.refs_2_ = f32[40,128]{1,0:T(8,128)S(1)} collective-permute-done((f32[40,128]{1,0:T(8,128)S(1)}, f32[40,128]{1,0:T(8,128)S(1)}, u32[]{:S(2)}, u32[]{:S(2)}) %collective-permute-start.8) | collective-permute-done | bytes 20512 | tf_op jit(solution)/shard_map/ppermute | solution.py:486
  40.1 0.5 collective-permute-done.7.refs_1_
  40.6 2.6 %tiles.4 = (f32[4,40,128]{2,1,0:T(8,128)S(1)}, f32[4,40,128]{2,1,0:T(8,128)S(1)}) custom-call(bf16[256,160]{1,0:T(8,128)(2,1)S(1)} %get-tuple-element.31.gather, bf16[320,256]{1,0:T(8,128)(2,1)S(1)} %get-tuple-element.32.chosen_high, bf16[320,256]{1,0:T(8,128)(2,1)S(1)} %get-tuple-element.33.chosen_low, bf16[256,128,128]{2,1,0:T(8,128)(2,1)S(1)} %get-tuple-element.34.blocks, ...), custom_call_target="tpu_custom_call" | custom-call | tf_op jit(solution)/shard_map/tiles/pallas_call | solution.py:533
  43.2 0.1 collective-permute-start.10
  43.3 1.3 %collective-permute-done.10 = f32[4,40,128]{2,1,0:T(8,128)S(1)} collective-permute-done((f32[4,40,128]{2,1,0:T(8,128)S(1)}, f32[4,40,128]{2,1,0:T(8,128)S(1)}, u32[]{:S(2)}, u32[]{:S(2)}) %collective-permute-start.10) | collective-permute-done | bytes 81952 | tf_op jit(solution)/shard_map/ppermute | solution.py:486
  44.6 1.5 %collective-permute-start.13 = (f32[40,128]{1,0:T(8,128)S(1)}, f32[40,128]{1,0:T(8,128)S(1)}, u32[]{:S(2)}, u32[]{:S(2)}) collective-permute-start(f32[40,128]{1,0:T(8,128)S(1)} %get-tuple-element.52), channel_id=1, source_target_pairs={{0,6},{1,7},{2,4},{3,5},{4,2},{5,3},{6,0},{7,1},{8,14},{9,15},{10,... | collective-permute-start | bytes 61448 | tf_op jit(solution)/shard_map/ppermute | solution.py:486
  46.1 0.6 collective-permute-start.12
  46.8 2.3 %collective-permute-start.11 = (f32[40,128]{1,0:T(8,128)S(1)}, f32[40,128]{1,0:T(8,128)S(1)}, u32[]{:S(2)}, u32[]{:S(2)}) collective-permute-start(f32[40,128]{1,0:T(8,128)S(1)} %get-tuple-element.54), channel_id=1, source_target_pairs={{0,2},{1,3},{2,0},{3,1},{4,6},{5,7},{6,4},{7,5},{8,10},{9,11},{10,... | collective-permute-start | bytes 61448 | tf_op jit(solution)/shard_map/ppermute | solution.py:486
  49.0 1.4 %collective-permute-done.13.refs_9_ = f32[40,128]{1,0:T(8,128)S(1)} collective-permute-done((f32[40,128]{1,0:T(8,128)S(1)}, f32[40,128]{1,0:T(8,128)S(1)}, u32[]{:S(2)}, u32[]{:S(2)}) %collective-permute-start.13) | collective-permute-done | bytes 20512 | tf_op jit(solution)/shard_map/ppermute | solution.py:486
  50.4 0.4 collective-permute-done.12.refs_8_
  50.8 0.2 collective-permute-done.11.refs_7_
  51.0 4.2 %third.1 = (f32[40,128]{1,0:T(8,128)S(1)}, f32[36,128]{1,0:T(8,128)S(1)}) custom-call(s32[1,1,24]{2,1,0:T(1,128)S(1)} %copy-done.2, f32[1,1,4608]{2,1,0:T(1,128)S(1)} %copy-done, f32[1,1,4608]{2,1,0:T(1,128)S(1)} %copy-done.1, bf16[24,512,512]{2,1,0:T(8,128)(2,1)S(1)} %get-tuple-element.25.blocks, bf16[48,128]{1,0:T(8,128)(2,1)S(1)} %get-tuple-element.26.refs_0_, ...), custom_call_target="tpu_custom_call" | custom-call | tf_op jit(solution)/shard_map/third/pallas_call | solution.py:559
  55.2 1.6 %collective-permute-start.16 = (f32[40,128]{1,0:T(8,128)S(1)}, f32[40,128]{1,0:T(8,128)S(1)}, u32[]{:S(2)}, u32[]{:S(2)}) collective-permute-start(f32[40,128]{1,0:T(8,128)S(1)} %get-tuple-element.41.refs_0_.sent.sent2), channel_id=1, source_target_pairs={{0,24},{8,16},{16,8},{24,0},{1,25},{9,17},{17,9},{25,1},{2,26},{10... | collective-permute-start | bytes 61448 | tf_op jit(solution)/shard_map/ppermute | solution.py:486
  56.8 0.5 collective-permute-start.15
  57.3 1.5 %collective-permute-start.14 = (f32[40,128]{1,0:T(8,128)S(1)}, f32[40,128]{1,0:T(8,128)S(1)}, u32[]{:S(2)}, u32[]{:S(2)}) collective-permute-start(f32[40,128]{1,0:T(8,128)S(1)} %get-tuple-element.41.refs_0_.sent.sent2), channel_id=1, source_target_pairs={{0,8},{8,0},{16,24},{24,16},{1,9},{9,1},{17,25},{25,17},{2,10},{10... | collective-permute-start | bytes 61448 | tf_op jit(solution)/shard_map/ppermute | solution.py:486
  58.8 1.2 %collective-permute-done.16.refs_3_ = f32[40,128]{1,0:T(8,128)S(1)} collective-permute-done((f32[40,128]{1,0:T(8,128)S(1)}, f32[40,128]{1,0:T(8,128)S(1)}, u32[]{:S(2)}, u32[]{:S(2)}) %collective-permute-start.16) | collective-permute-done | bytes 20512 | tf_op jit(solution)/shard_map/ppermute | solution.py:486
  59.9 0.6 collective-permute-done.15.refs_2_
  60.5 0.5 collective-permute-done.14.refs_1_
  61.0 2.6 %tiles.5 = (f32[4,40,128]{2,1,0:T(8,128)S(1)}, f32[4,40,128]{2,1,0:T(8,128)S(1)}) custom-call(bf16[256,160]{1,0:T(8,128)(2,1)S(1)} %get-tuple-element.31.gather, bf16[320,256]{1,0:T(8,128)(2,1)S(1)} %get-tuple-element.32.chosen_high, bf16[320,256]{1,0:T(8,128)(2,1)S(1)} %get-tuple-element.33.chosen_low, bf16[256,128,128]{2,1,0:T(8,128)(2,1)S(1)} %get-tuple-element.34.blocks, ...), custom_call_target="tpu_custom_call" | custom-call | tf_op jit(solution)/shard_map/tiles/pallas_call | solution.py:533
  63.7 0.1 collective-permute-start.17
  63.8 1.3 %collective-permute-done.17 = f32[4,40,128]{2,1,0:T(8,128)S(1)} collective-permute-done((f32[4,40,128]{2,1,0:T(8,128)S(1)}, f32[4,40,128]{2,1,0:T(8,128)S(1)}, u32[]{:S(2)}, u32[]{:S(2)}) %collective-permute-start.17) | collective-permute-done | bytes 81952 | tf_op jit(solution)/shard_map/ppermute | solution.py:486
  65.1 2.4 %collective-permute-start.20 = (f32[40,128]{1,0:T(8,128)S(1)}, f32[40,128]{1,0:T(8,128)S(1)}, u32[]{:S(2)}, u32[]{:S(2)}) collective-permute-start(f32[40,128]{1,0:T(8,128)S(1)} %get-tuple-element.48), channel_id=1, source_target_pairs={{0,6},{1,7},{2,4},{3,5},{4,2},{5,3},{6,0},{7,1},{8,14},{9,15},{10,... | collective-permute-start | bytes 61448 | tf_op jit(solution)/shard_map/ppermute | solution.py:486
  67.5 0.9 %collective-permute-start.19 = (f32[40,128]{1,0:T(8,128)S(1)}, f32[40,128]{1,0:T(8,128)S(1)}, u32[]{:S(2)}, u32[]{:S(2)}) collective-permute-start(f32[40,128]{1,0:T(8,128)S(1)} %get-tuple-element.49), channel_id=1, source_target_pairs={{0,4},{1,5},{2,6},{3,7},{4,0},{5,1},{6,2},{7,3},{8,12},{9,13},{10,... | collective-permute-start | bytes 61448 | tf_op jit(solution)/shard_map/ppermute | solution.py:486
  68.4 1.1 %collective-permute-start.18 = (f32[40,128]{1,0:T(8,128)S(1)}, f32[40,128]{1,0:T(8,128)S(1)}, u32[]{:S(2)}, u32[]{:S(2)}) collective-permute-start(f32[40,128]{1,0:T(8,128)S(1)} %get-tuple-element.50), channel_id=1, source_target_pairs={{0,2},{1,3},{2,0},{3,1},{4,6},{5,7},{6,4},{7,5},{8,10},{9,11},{10,... | collective-permute-start | bytes 61448 | tf_op jit(solution)/shard_map/ppermute | solution.py:486
  69.5 1.2 %collective-permute-done.20.refs_3_ = f32[40,128]{1,0:T(8,128)S(1)} collective-permute-done((f32[40,128]{1,0:T(8,128)S(1)}, f32[40,128]{1,0:T(8,128)S(1)}, u32[]{:S(2)}, u32[]{:S(2)}) %collective-permute-start.20) | collective-permute-done | bytes 20512 | tf_op jit(solution)/shard_map/ppermute | solution.py:486
  70.8 1.5 %collective-permute-done.19.refs_2_ = f32[40,128]{1,0:T(8,128)S(1)} collective-permute-done((f32[40,128]{1,0:T(8,128)S(1)}, f32[40,128]{1,0:T(8,128)S(1)}, u32[]{:S(2)}, u32[]{:S(2)}) %collective-permute-start.19) | collective-permute-done | bytes 20512 | tf_op jit(solution)/shard_map/ppermute | solution.py:486
  72.2 0.2 collective-permute-done.18.refs_1_
  72.4 0.1 fourth.1
  72.5 11.0 %all_to_all.11 = f32[32,1,128]{2,1,0:T(1,128)S(1)} all-to-all(f32[32,1,128]{2,1,0:T(1,128)S(1)} %bitcast.29), channel_id=1, replica_groups=mesh['row'=4,'col'=8] {'row','col'}, dimensions={0} | all-to-all | bytes 32768 | tf_op jit(solution)/shard_map/all_to_all | solution.py:578
  83.5 0.8 last.1
  (6 shorter events, 0.1 us)
Async XLA Ops:
  0.6 29.0 %copy-start = (f32[1,1,4608]{2,1,0:T(1,128)S(1)}, f32[1,1,4608]{2,1,0:T(1,128)}, u32[]{:S(2)}) copy-start(f32[1,1,4608]{2,1,0:T(1,128)} %rhs.7) | copy-start | bytes 55300
  0.6 29.0 %copy-start.1 = (f32[1,1,4608]{2,1,0:T(1,128)S(1)}, f32[1,1,4608]{2,1,0:T(1,128)}, u32[]{:S(2)}) copy-start(f32[1,1,4608]{2,1,0:T(1,128)} %friction.5) | copy-start | bytes 55300
  0.7 29.0 %copy-start.2 = (s32[1,1,24]{2,1,0:T(1,128)S(1)}, s32[1,1,24]{2,1,0:T(1,128)}, u32[]{:S(2)}) copy-start(s32[1,1,24]{2,1,0:T(1,128)} %sizes.3) | copy-start | bytes 292
  0.7 12.6 %copy-start.4 = (s32[1,1,256]{2,1,0:T(1,128)S(1)}, s32[1,1,256]{2,1,0:T(1,128)}, u32[]{:S(2)}) copy-start(s32[1,1,256]{2,1,0:T(1,128)} %tile_col.1) | copy-start | bytes 3076
  0.7 12.6 %copy-start.3 = (s32[1,1,256]{2,1,0:T(1,128)S(1)}, s32[1,1,256]{2,1,0:T(1,128)}, u32[]{:S(2)}) copy-start(s32[1,1,256]{2,1,0:T(1,128)} %tile_row.1) | copy-start | bytes 3076
  0.7 12.6 %copy-start.5 = (f32[1,1,256]{2,1,0:T(1,128)S(1)}, f32[1,1,256]{2,1,0:T(1,128)}, u32[]{:S(2)}) copy-start(f32[1,1,256]{2,1,0:T(1,128)} %scale.1) | copy-start | bytes 3076
  8.0 8.8 %collective-permute-start.2 = (f32[40,128]{1,0:T(8,128)S(1)}, f32[40,128]{1,0:T(8,128)S(1)}, u32[]{:S(2)}, u32[]{:S(2)}) collective-permute-start(f32[40,128]{1,0:T(8,128)S(1)} %get-tuple-element.30.refs_0_.refs_4_.sent0), channel_id=1, source_target_pairs={{0,24},{8,16},{16,8},{24,0},{1,25},{9,17},{17,9},{25,1},{2,26},{10... | collective-permute-start | bytes 61448 | tf_op jit(solution)/shard_map/ppermute | solution.py:486
  11.9 4.9 %collective-permute-start.1 = (f32[40,128]{1,0:T(8,128)S(1)}, f32[40,128]{1,0:T(8,128)S(1)}, u32[]{:S(2)}, u32[]{:S(2)}) collective-permute-start(f32[40,128]{1,0:T(8,128)S(1)} %get-tuple-element.30.refs_0_.refs_4_.sent0), channel_id=1, source_target_pairs={{0,16},{8,24},{16,0},{24,8},{1,17},{9,25},{17,1},{25,9},{2,18},{10... | collective-permute-start | bytes 61448 | tf_op jit(solution)/shard_map/ppermute | solution.py:486
  12.4 4.4 %collective-permute-start = (f32[40,128]{1,0:T(8,128)S(1)}, f32[40,128]{1,0:T(8,128)S(1)}, u32[]{:S(2)}, u32[]{:S(2)}) collective-permute-start(f32[40,128]{1,0:T(8,128)S(1)} %get-tuple-element.30.refs_0_.refs_4_.sent0), channel_id=1, source_target_pairs={{0,8},{8,0},{16,24},{24,16},{1,9},{9,1},{17,25},{25,17},{2,10},{10... | collective-permute-start | bytes 61448 | tf_op jit(solution)/shard_map/ppermute | solution.py:486
  19.5 1.3 %collective-permute-start.3 = (f32[4,40,128]{2,1,0:T(8,128)S(1)}, f32[4,40,128]{2,1,0:T(8,128)S(1)}, u32[]{:S(2)}, u32[]{:S(2)}) collective-permute-start(f32[4,40,128]{2,1,0:T(8,128)S(1)} %get-tuple-element.36), channel_id=1, source_target_pairs={{0,1},{1,0},{2,3},{3,2},{4,5},{5,4},{6,7},{7,6},{8,9},{9,8},{10,11... | collective-permute-start | bytes 245768 | tf_op jit(solution)/shard_map/ppermute | solution.py:486
  20.8 5.8 %collective-permute-start.6 = (f32[40,128]{1,0:T(8,128)S(1)}, f32[40,128]{1,0:T(8,128)S(1)}, u32[]{:S(2)}, u32[]{:S(2)}) collective-permute-start(f32[40,128]{1,0:T(8,128)S(1)} %get-tuple-element.56), channel_id=1, source_target_pairs={{0,6},{1,7},{2,4},{3,5},{4,2},{5,3},{6,0},{7,1},{8,14},{9,15},{10,... | collective-permute-start | bytes 61448 | tf_op jit(solution)/shard_map/ppermute | solution.py:486
  24.9 4.7 %collective-permute-start.5 = (f32[40,128]{1,0:T(8,128)S(1)}, f32[40,128]{1,0:T(8,128)S(1)}, u32[]{:S(2)}, u32[]{:S(2)}) collective-permute-start(f32[40,128]{1,0:T(8,128)S(1)} %get-tuple-element.57), channel_id=1, source_target_pairs={{0,4},{1,5},{2,6},{3,7},{4,0},{5,1},{6,2},{7,3},{8,12},{9,13},{10,... | collective-permute-start | bytes 61448 | tf_op jit(solution)/shard_map/ppermute | solution.py:486
  24.9 4.7 %collective-permute-start.4 = (f32[40,128]{1,0:T(8,128)S(1)}, f32[40,128]{1,0:T(8,128)S(1)}, u32[]{:S(2)}, u32[]{:S(2)}) collective-permute-start(f32[40,128]{1,0:T(8,128)S(1)} %get-tuple-element.58), channel_id=1, source_target_pairs={{0,2},{1,3},{2,0},{3,1},{4,6},{5,7},{6,4},{7,5},{8,10},{9,11},{10,... | collective-permute-start | bytes 61448 | tf_op jit(solution)/shard_map/ppermute | solution.py:486
  33.8 4.7 %collective-permute-start.9 = (f32[40,128]{1,0:T(8,128)S(1)}, f32[40,128]{1,0:T(8,128)S(1)}, u32[]{:S(2)}, u32[]{:S(2)}) collective-permute-start(f32[40,128]{1,0:T(8,128)S(1)} %get-tuple-element.37.refs_0_.refs_4_.sent1), channel_id=1, source_target_pairs={{0,24},{8,16},{16,8},{24,0},{1,25},{9,17},{17,9},{25,1},{2,26},{10... | collective-permute-start | bytes 61448 | tf_op jit(solution)/shard_map/ppermute | solution.py:486
  36.3 3.8 %collective-permute-start.8 = (f32[40,128]{1,0:T(8,128)S(1)}, f32[40,128]{1,0:T(8,128)S(1)}, u32[]{:S(2)}, u32[]{:S(2)}) collective-permute-start(f32[40,128]{1,0:T(8,128)S(1)} %get-tuple-element.37.refs_0_.refs_4_.sent1), channel_id=1, source_target_pairs={{0,16},{8,24},{16,0},{24,8},{1,17},{9,25},{17,1},{25,9},{2,18},{10... | collective-permute-start | bytes 61448 | tf_op jit(solution)/shard_map/ppermute | solution.py:486
  36.8 3.8 %collective-permute-start.7 = (f32[40,128]{1,0:T(8,128)S(1)}, f32[40,128]{1,0:T(8,128)S(1)}, u32[]{:S(2)}, u32[]{:S(2)}) collective-permute-start(f32[40,128]{1,0:T(8,128)S(1)} %get-tuple-element.37.refs_0_.refs_4_.sent1), channel_id=1, source_target_pairs={{0,8},{8,0},{16,24},{24,16},{1,9},{9,1},{17,25},{25,17},{2,10},{10... | collective-permute-start | bytes 61448 | tf_op jit(solution)/shard_map/ppermute | solution.py:486
  43.2 1.3 %collective-permute-start.10 = (f32[4,40,128]{2,1,0:T(8,128)S(1)}, f32[4,40,128]{2,1,0:T(8,128)S(1)}, u32[]{:S(2)}, u32[]{:S(2)}) collective-permute-start(f32[4,40,128]{2,1,0:T(8,128)S(1)} %get-tuple-element.40), channel_id=1, source_target_pairs={{0,1},{1,0},{2,3},{3,2},{4,5},{5,4},{6,7},{7,6},{8,9},{9,8},{10,11... | collective-permute-start | bytes 245768 | tf_op jit(solution)/shard_map/ppermute | solution.py:486
  44.6 5.8 %collective-permute-start.13 = (f32[40,128]{1,0:T(8,128)S(1)}, f32[40,128]{1,0:T(8,128)S(1)}, u32[]{:S(2)}, u32[]{:S(2)}) collective-permute-start(f32[40,128]{1,0:T(8,128)S(1)} %get-tuple-element.52), channel_id=1, source_target_pairs={{0,6},{1,7},{2,4},{3,5},{4,2},{5,3},{6,0},{7,1},{8,14},{9,15},{10,... | collective-permute-start | bytes 61448 | tf_op jit(solution)/shard_map/ppermute | solution.py:486
  46.1 4.7 %collective-permute-start.12 = (f32[40,128]{1,0:T(8,128)S(1)}, f32[40,128]{1,0:T(8,128)S(1)}, u32[]{:S(2)}, u32[]{:S(2)}) collective-permute-start(f32[40,128]{1,0:T(8,128)S(1)} %get-tuple-element.53), channel_id=1, source_target_pairs={{0,4},{1,5},{2,6},{3,7},{4,0},{5,1},{6,2},{7,3},{8,12},{9,13},{10,... | collective-permute-start | bytes 61448 | tf_op jit(solution)/shard_map/ppermute | solution.py:486
  46.8 4.3 %collective-permute-start.11 = (f32[40,128]{1,0:T(8,128)S(1)}, f32[40,128]{1,0:T(8,128)S(1)}, u32[]{:S(2)}, u32[]{:S(2)}) collective-permute-start(f32[40,128]{1,0:T(8,128)S(1)} %get-tuple-element.54), channel_id=1, source_target_pairs={{0,2},{1,3},{2,0},{3,1},{4,6},{5,7},{6,4},{7,5},{8,10},{9,11},{10,... | collective-permute-start | bytes 61448 | tf_op jit(solution)/shard_map/ppermute | solution.py:486
  55.2 4.7 %collective-permute-start.16 = (f32[40,128]{1,0:T(8,128)S(1)}, f32[40,128]{1,0:T(8,128)S(1)}, u32[]{:S(2)}, u32[]{:S(2)}) collective-permute-start(f32[40,128]{1,0:T(8,128)S(1)} %get-tuple-element.41.refs_0_.sent.sent2), channel_id=1, source_target_pairs={{0,24},{8,16},{16,8},{24,0},{1,25},{9,17},{17,9},{25,1},{2,26},{10... | collective-permute-start | bytes 61448 | tf_op jit(solution)/shard_map/ppermute | solution.py:486
  56.8 3.8 %collective-permute-start.15 = (f32[40,128]{1,0:T(8,128)S(1)}, f32[40,128]{1,0:T(8,128)S(1)}, u32[]{:S(2)}, u32[]{:S(2)}) collective-permute-start(f32[40,128]{1,0:T(8,128)S(1)} %get-tuple-element.41.refs_0_.sent.sent2), channel_id=1, source_target_pairs={{0,16},{8,24},{16,0},{24,8},{1,17},{9,25},{17,1},{25,9},{2,18},{10... | collective-permute-start | bytes 61448 | tf_op jit(solution)/shard_map/ppermute | solution.py:486
  57.3 3.8 %collective-permute-start.14 = (f32[40,128]{1,0:T(8,128)S(1)}, f32[40,128]{1,0:T(8,128)S(1)}, u32[]{:S(2)}, u32[]{:S(2)}) collective-permute-start(f32[40,128]{1,0:T(8,128)S(1)} %get-tuple-element.41.refs_0_.sent.sent2), channel_id=1, source_target_pairs={{0,8},{8,0},{16,24},{24,16},{1,9},{9,1},{17,25},{25,17},{2,10},{10... | collective-permute-start | bytes 61448 | tf_op jit(solution)/shard_map/ppermute | solution.py:486
  63.7 1.3 %collective-permute-start.17 = (f32[4,40,128]{2,1,0:T(8,128)S(1)}, f32[4,40,128]{2,1,0:T(8,128)S(1)}, u32[]{:S(2)}, u32[]{:S(2)}) collective-permute-start(f32[4,40,128]{2,1,0:T(8,128)S(1)} %get-tuple-element.45), channel_id=1, source_target_pairs={{0,1},{1,0},{2,3},{3,2},{4,5},{5,4},{6,7},{7,6},{8,9},{9,8},{10,11... | collective-permute-start | bytes 245768 | tf_op jit(solution)/shard_map/ppermute | solution.py:486
  65.1 5.7 %collective-permute-start.20 = (f32[40,128]{1,0:T(8,128)S(1)}, f32[40,128]{1,0:T(8,128)S(1)}, u32[]{:S(2)}, u32[]{:S(2)}) collective-permute-start(f32[40,128]{1,0:T(8,128)S(1)} %get-tuple-element.48), channel_id=1, source_target_pairs={{0,6},{1,7},{2,4},{3,5},{4,2},{5,3},{6,0},{7,1},{8,14},{9,15},{10,... | collective-permute-start | bytes 61448 | tf_op jit(solution)/shard_map/ppermute | solution.py:486
  67.5 4.7 %collective-permute-start.19 = (f32[40,128]{1,0:T(8,128)S(1)}, f32[40,128]{1,0:T(8,128)S(1)}, u32[]{:S(2)}, u32[]{:S(2)}) collective-permute-start(f32[40,128]{1,0:T(8,128)S(1)} %get-tuple-element.49), channel_id=1, source_target_pairs={{0,4},{1,5},{2,6},{3,7},{4,0},{5,1},{6,2},{7,3},{8,12},{9,13},{10,... | collective-permute-start | bytes 61448 | tf_op jit(solution)/shard_map/ppermute | solution.py:486
  68.4 4.0 %collective-permute-start.18 = (f32[40,128]{1,0:T(8,128)S(1)}, f32[40,128]{1,0:T(8,128)S(1)}, u32[]{:S(2)}, u32[]{:S(2)}) collective-permute-start(f32[40,128]{1,0:T(8,128)S(1)} %get-tuple-element.50), channel_id=1, source_target_pairs={{0,2},{1,3},{2,0},{3,1},{4,6},{5,7},{6,4},{7,5},{8,10},{9,11},{10,... | collective-permute-start | bytes 61448 | tf_op jit(solution)/shard_map/ppermute | solution.py:486

commit v9 on v8

--- a/solution.py
+++ b/solution.py
@@ -77,8 +77,6 @@
 
 def fetch(scalars, remote, blocks, sems):
     half = blocks.shape[1] // 2
-    for group in range(len(scalars) // 8):
-        leading(remote, blocks, sems, group).start()
     for f, (_, _, size) in enumerate(scalars):
 
         @pl.when(size > half)
@@ -229,6 +227,8 @@
     copies = [pltpu.make_async_copy(a, b, sems.at[i]) for i, (a, b) in enumerate(pairs)]
     for copy in copies:
         copy.start()
+    for group in range(blocks.shape[0] // 8):
+        leading(remote, blocks, block_sems, group).start()
     copies[0].wait()
     scalars = fault_scalars(sizes, blocks.shape[0])
     fetch(scalars, remote, blocks, block_sems)

time: 84.5 us -> 84.1 us (level)
  no operation moved by 1% of the time
where the time goes in v9:
time: 84.1 us; the launch traced here: 83.9 us
  Pallas kernels  27.6 us (33%)
  starting transfers between devices  25.5 us (30%)
  waiting for transfers between devices  18.2 us (22%)
  blocking collectives  11 us (13%)
  between operations  1.51 us (2%)
    ppermute x21, starting transfers between devices, exchange(): return lax.ppermute(value, axis, [(i, i ^ distance) for i in range(size)])  25.5 us
    ppermute x21, waiting for transfers between devices, exchange(): return lax.ppermute(value, axis, [(i, i ^ distance) for i in range(size)])  18.2 us
    all_to_all x1, blocking collectives, local(): sums = lax.all_to_all(sums, ('row', 'col'), 0, 0, tiled=True)  11 us
    pallas_call x3, Pallas kernels, apply_kernel(): pl.pallas_call(functools.partial(tiles_kernel, tiles % 8), out_shape=[hal...  7.92 us
    pallas_call x1, Pallas kernels, local(): pl.pallas_call(first_kernel, out_shape=[grid, pltpu.VMEM((faults, width,...  6.9 us
    pallas_call x1, Pallas kernels, local(): pl.pallas_call(second_kernel, out_shape=[grid, plain, grid], in_specs=[SM...  4.22 us
    pallas_call x1, Pallas kernels, local(): pl.pallas_call(third_kernel, out_shape=[grid, plain], in_specs=[SMEM, VME...  4.17 us
    pallas_call x1, Pallas kernels, local(): pl.pallas_call(functools.partial(prepare_kernel, (tiles, height, row_coun...  3.54 us
  transfers between devices with their start and end apart: 21, of which 17 were waited for; matrix products, arithmetic and copies ran while one was open for 0% of the time, Pallas kernels for 4%

profile of v9, /device:TPU:0, one launch (start us, length us, event | category | flops | bytes accessed | tf_op | source)
XLA Modules:
  0.0 83.9 jit_solution(18214122474349306943)
XLA Ops:
  0.6 0.0 copy-start
  0.6 0.0 copy-start.1
  0.7 0.0 copy-start.2
  0.7 0.0 copy-start.4
  0.7 0.0 copy-start.3
  0.7 0.0 copy-start.5
  0.7 6.9 %first.1 = (f32[40,128]{1,0:T(8,128)S(1)}, bf16[24,512,512]{2,1,0:T(8,128)(2,1)S(1)}, bf16[48,128]{1,0:T(8,128)(2,1)S(1)}, bf16[128,48]{1,0:T(8,128)(2,1)S(1)}, ...) custom-call(s32[1,1,24]{2,1,0:T(1,128)} %sizes.3, f32[1,1,4608]{2,1,0:T(1,128)} %rhs.7, f32[1,1,4608]{2,1,0:T(1,128)} %friction.5, ...), custom_call_target="tpu_custom_call" | custom-call | tf_op jit(solution)/shard_map/first/pallas_call | solution.py:491
  7.6 4.0 %collective-permute-start.2 = (f32[40,128]{1,0:T(8,128)S(1)}, f32[40,128]{1,0:T(8,128)S(1)}, u32[]{:S(2)}, u32[]{:S(2)}) collective-permute-start(f32[40,128]{1,0:T(8,128)S(1)} %get-tuple-element.30.refs_0_.refs_4_.sent0), channel_id=1, source_target_pairs={{0,24},{8,16},{16,8},{24,0},{1,25},{9,17},{17,9},{25,1},{2,26},{10... | collective-permute-start | bytes 61448 | tf_op jit(solution)/shard_map/ppermute | solution.py:486
  11.6 0.5 collective-permute-start.1
  12.1 0.1 collective-permute-start
  12.9 0.0 copy-done.4
  12.9 0.0 copy-done.3
  12.9 0.0 copy-done.5
  12.9 3.5 %prepare.1 = (bf16[256,128,128]{2,1,0:T(8,128)(2,1)S(1)}, bf16[256,160]{1,0:T(8,128)(2,1)S(1)}, bf16[320,256]{1,0:T(8,128)(2,1)S(1)}, bf16[320,256]{1,0:T(8,128)(2,1)S(1)}) custom-call(s32[24,128]{1,0:T(8,128)S(1)} %get-tuple-element.29.after.refs_3_, s32[1,1]{1,0:T(1,128)S(6)} %copy.12.counts, s32[1,1,256]{2,1,0:T(1,128)S(1)} %copy-done.3, ...), custom_call_target="tpu_custom_call" | custom-call | tf_op jit(solution)/shard_map/prepare/pallas_call | solution.py:516
  16.4 0.0 collective-permute-done.2.refs_3_
  16.4 0.0 collective-permute-done.1.refs_2_
  16.5 0.0 collective-permute-done.refs_1_
  16.5 2.6 %tiles.3 = (f32[4,40,128]{2,1,0:T(8,128)S(1)}, f32[4,40,128]{2,1,0:T(8,128)S(1)}) custom-call(bf16[256,160]{1,0:T(8,128)(2,1)S(1)} %get-tuple-element.31.gather, bf16[320,256]{1,0:T(8,128)(2,1)S(1)} %get-tuple-element.32.chosen_high, bf16[320,256]{1,0:T(8,128)(2,1)S(1)} %get-tuple-element.33.chosen_low, bf16[256,128,128]{2,1,0:T(8,128)(2,1)S(1)} %get-tuple-element.34.blocks, ...), custom_call_target="tpu_custom_call" | custom-call | tf_op jit(solution)/shard_map/tiles/pallas_call | solution.py:533
  19.1 0.1 collective-permute-start.3
  19.2 1.3 %collective-permute-done.3 = f32[4,40,128]{2,1,0:T(8,128)S(1)} collective-permute-done((f32[4,40,128]{2,1,0:T(8,128)S(1)}, f32[4,40,128]{2,1,0:T(8,128)S(1)}, u32[]{:S(2)}, u32[]{:S(2)}) %collective-permute-start.3) | collective-permute-done | bytes 81952 | tf_op jit(solution)/shard_map/ppermute | solution.py:486
  20.5 4.1 %collective-permute-start.6 = (f32[40,128]{1,0:T(8,128)S(1)}, f32[40,128]{1,0:T(8,128)S(1)}, u32[]{:S(2)}, u32[]{:S(2)}) collective-permute-start(f32[40,128]{1,0:T(8,128)S(1)} %get-tuple-element.56), channel_id=1, source_target_pairs={{0,6},{1,7},{2,4},{3,5},{4,2},{5,3},{6,0},{7,1},{8,14},{9,15},{10,... | collective-permute-start | bytes 61448 | tf_op jit(solution)/shard_map/ppermute | solution.py:486
  24.6 0.0 collective-permute-start.5
  24.6 0.6 collective-permute-start.4
  25.2 1.1 %collective-permute-done.6.refs_8_ = f32[40,128]{1,0:T(8,128)S(1)} collective-permute-done((f32[40,128]{1,0:T(8,128)S(1)}, f32[40,128]{1,0:T(8,128)S(1)}, u32[]{:S(2)}, u32[]{:S(2)}) %collective-permute-start.6) | collective-permute-done | bytes 20512 | tf_op jit(solution)/shard_map/ppermute | solution.py:486
  26.3 2.9 %collective-permute-done.5.refs_7_ = f32[40,128]{1,0:T(8,128)S(1)} collective-permute-done((f32[40,128]{1,0:T(8,128)S(1)}, f32[40,128]{1,0:T(8,128)S(1)}, u32[]{:S(2)}, u32[]{:S(2)}) %collective-permute-start.5) | collective-permute-done | bytes 20512 | tf_op jit(solution)/shard_map/ppermute | solution.py:486
  29.2 0.0 collective-permute-done.4.refs_6_
  29.2 0.0 copy-done
  29.2 0.0 copy-done.1
  29.2 0.0 copy-done.2
  29.3 4.2 %second.1 = (f32[40,128]{1,0:T(8,128)S(1)}, f32[36,128]{1,0:T(8,128)S(1)}, f32[40,128]{1,0:T(8,128)S(1)}) custom-call(s32[1,1,24]{2,1,0:T(1,128)S(1)} %copy-done.2, f32[1,1,4608]{2,1,0:T(1,128)S(1)} %copy-done, f32[1,1,4608]{2,1,0:T(1,128)S(1)} %copy-done.1, bf16[24,512,512]{2,1,0:T(8,128)(2,1)S(1)} %get-tuple-element.25.blocks, ...), custom_call_target="tpu_custom_call" | custom-call | tf_op jit(solution)/shard_map/second/pallas_call | solution.py:549
  33.5 2.5 %collective-permute-start.9 = (f32[40,128]{1,0:T(8,128)S(1)}, f32[40,128]{1,0:T(8,128)S(1)}, u32[]{:S(2)}, u32[]{:S(2)}) collective-permute-start(f32[40,128]{1,0:T(8,128)S(1)} %get-tuple-element.37.refs_0_.refs_4_.sent1), channel_id=1, source_target_pairs={{0,24},{8,16},{16,8},{24,0},{1,25},{9,17},{17,9},{25,1},{2,26},{10... | collective-permute-start | bytes 61448 | tf_op jit(solution)/shard_map/ppermute | solution.py:486
  35.9 0.5 collective-permute-start.8
  36.4 0.5 collective-permute-start.7
  37.0 1.2 %collective-permute-done.9.refs_3_ = f32[40,128]{1,0:T(8,128)S(1)} collective-permute-done((f32[40,128]{1,0:T(8,128)S(1)}, f32[40,128]{1,0:T(8,128)S(1)}, u32[]{:S(2)}, u32[]{:S(2)}) %collective-permute-start.9) | collective-permute-done | bytes 20512 | tf_op jit(solution)/shard_map/ppermute | solution.py:486
  38.2 1.6 %collective-permute-done.8.refs_2_ = f32[40,128]{1,0:T(8,128)S(1)} collective-permute-done((f32[40,128]{1,0:T(8,128)S(1)}, f32[40,128]{1,0:T(8,128)S(1)}, u32[]{:S(2)}, u32[]{:S(2)}) %collective-permute-start.8) | collective-permute-done | bytes 20512 | tf_op jit(solution)/shard_map/ppermute | solution.py:486
  39.7 0.5 collective-permute-done.7.refs_1_
  40.2 2.6 %tiles.4 = (f32[4,40,128]{2,1,0:T(8,128)S(1)}, f32[4,40,128]{2,1,0:T(8,128)S(1)}) custom-call(bf16[256,160]{1,0:T(8,128)(2,1)S(1)} %get-tuple-element.31.gather, bf16[320,256]{1,0:T(8,128)(2,1)S(1)} %get-tuple-element.32.chosen_high, bf16[320,256]{1,0:T(8,128)(2,1)S(1)} %get-tuple-element.33.chosen_low, bf16[256,128,128]{2,1,0:T(8,128)(2,1)S(1)} %get-tuple-element.34.blocks, ...), custom_call_target="tpu_custom_call" | custom-call | tf_op jit(solution)/shard_map/tiles/pallas_call | solution.py:533
  42.9 0.1 collective-permute-start.10
  42.9 1.3 %collective-permute-done.10 = f32[4,40,128]{2,1,0:T(8,128)S(1)} collective-permute-done((f32[4,40,128]{2,1,0:T(8,128)S(1)}, f32[4,40,128]{2,1,0:T(8,128)S(1)}, u32[]{:S(2)}, u32[]{:S(2)}) %collective-permute-start.10) | collective-permute-done | bytes 81952 | tf_op jit(solution)/shard_map/ppermute | solution.py:486
  44.2 1.5 %collective-permute-start.13 = (f32[40,128]{1,0:T(8,128)S(1)}, f32[40,128]{1,0:T(8,128)S(1)}, u32[]{:S(2)}, u32[]{:S(2)}) collective-permute-start(f32[40,128]{1,0:T(8,128)S(1)} %get-tuple-element.52), channel_id=1, source_target_pairs={{0,6},{1,7},{2,4},{3,5},{4,2},{5,3},{6,0},{7,1},{8,14},{9,15},{10,... | collective-permute-start | bytes 61448 | tf_op jit(solution)/shard_map/ppermute | solution.py:486
  45.8 0.6 collective-permute-start.12
  46.4 2.3 %collective-permute-start.11 = (f32[40,128]{1,0:T(8,128)S(1)}, f32[40,128]{1,0:T(8,128)S(1)}, u32[]{:S(2)}, u32[]{:S(2)}) collective-permute-start(f32[40,128]{1,0:T(8,128)S(1)} %get-tuple-element.54), channel_id=1, source_target_pairs={{0,2},{1,3},{2,0},{3,1},{4,6},{5,7},{6,4},{7,5},{8,10},{9,11},{10,... | collective-permute-start | bytes 61448 | tf_op jit(solution)/shard_map/ppermute | solution.py:486
  48.7 1.4 %collective-permute-done.13.refs_9_ = f32[40,128]{1,0:T(8,128)S(1)} collective-permute-done((f32[40,128]{1,0:T(8,128)S(1)}, f32[40,128]{1,0:T(8,128)S(1)}, u32[]{:S(2)}, u32[]{:S(2)}) %collective-permute-start.13) | collective-permute-done | bytes 20512 | tf_op jit(solution)/shard_map/ppermute | solution.py:486
  50.1 0.4 collective-permute-done.12.refs_8_
  50.5 0.2 collective-permute-done.11.refs_7_
  50.7 4.2 %third.1 = (f32[40,128]{1,0:T(8,128)S(1)}, f32[36,128]{1,0:T(8,128)S(1)}) custom-call(s32[1,1,24]{2,1,0:T(1,128)S(1)} %copy-done.2, f32[1,1,4608]{2,1,0:T(1,128)S(1)} %copy-done, f32[1,1,4608]{2,1,0:T(1,128)S(1)} %copy-done.1, bf16[24,512,512]{2,1,0:T(8,128)(2,1)S(1)} %get-tuple-element.25.blocks, bf16[48,128]{1,0:T(8,128)(2,1)S(1)} %get-tuple-element.26.refs_0_, ...), custom_call_target="tpu_custom_call" | custom-call | tf_op jit(solution)/shard_map/third/pallas_call | solution.py:559
  54.8 1.6 %collective-permute-start.16 = (f32[40,128]{1,0:T(8,128)S(1)}, f32[40,128]{1,0:T(8,128)S(1)}, u32[]{:S(2)}, u32[]{:S(2)}) collective-permute-start(f32[40,128]{1,0:T(8,128)S(1)} %get-tuple-element.41.refs_0_.sent.sent2), channel_id=1, source_target_pairs={{0,24},{8,16},{16,8},{24,0},{1,25},{9,17},{17,9},{25,1},{2,26},{10... | collective-permute-start | bytes 61448 | tf_op jit(solution)/shard_map/ppermute | solution.py:486
  56.4 0.5 collective-permute-start.15
  56.9 1.5 %collective-permute-start.14 = (f32[40,128]{1,0:T(8,128)S(1)}, f32[40,128]{1,0:T(8,128)S(1)}, u32[]{:S(2)}, u32[]{:S(2)}) collective-permute-start(f32[40,128]{1,0:T(8,128)S(1)} %get-tuple-element.41.refs_0_.sent.sent2), channel_id=1, source_target_pairs={{0,8},{8,0},{16,24},{24,16},{1,9},{9,1},{17,25},{25,17},{2,10},{10... | collective-permute-start | bytes 61448 | tf_op jit(solution)/shard_map/ppermute | solution.py:486
  58.4 1.2 %collective-permute-done.16.refs_3_ = f32[40,128]{1,0:T(8,128)S(1)} collective-permute-done((f32[40,128]{1,0:T(8,128)S(1)}, f32[40,128]{1,0:T(8,128)S(1)}, u32[]{:S(2)}, u32[]{:S(2)}) %collective-permute-start.16) | collective-permute-done | bytes 20512 | tf_op jit(solution)/shard_map/ppermute | solution.py:486
  59.6 0.6 collective-permute-done.15.refs_2_
  60.2 0.5 collective-permute-done.14.refs_1_
  60.7 2.6 %tiles.5 = (f32[4,40,128]{2,1,0:T(8,128)S(1)}, f32[4,40,128]{2,1,0:T(8,128)S(1)}) custom-call(bf16[256,160]{1,0:T(8,128)(2,1)S(1)} %get-tuple-element.31.gather, bf16[320,256]{1,0:T(8,128)(2,1)S(1)} %get-tuple-element.32.chosen_high, bf16[320,256]{1,0:T(8,128)(2,1)S(1)} %get-tuple-element.33.chosen_low, bf16[256,128,128]{2,1,0:T(8,128)(2,1)S(1)} %get-tuple-element.34.blocks, ...), custom_call_target="tpu_custom_call" | custom-call | tf_op jit(solution)/shard_map/tiles/pallas_call | solution.py:533
  63.3 0.1 collective-permute-start.17
  63.4 1.3 %collective-permute-done.17 = f32[4,40,128]{2,1,0:T(8,128)S(1)} collective-permute-done((f32[4,40,128]{2,1,0:T(8,128)S(1)}, f32[4,40,128]{2,1,0:T(8,128)S(1)}, u32[]{:S(2)}, u32[]{:S(2)}) %collective-permute-start.17) | collective-permute-done | bytes 81952 | tf_op jit(solution)/shard_map/ppermute | solution.py:486
  64.7 2.4 %collective-permute-start.20 = (f32[40,128]{1,0:T(8,128)S(1)}, f32[40,128]{1,0:T(8,128)S(1)}, u32[]{:S(2)}, u32[]{:S(2)}) collective-permute-start(f32[40,128]{1,0:T(8,128)S(1)} %get-tuple-element.48), channel_id=1, source_target_pairs={{0,6},{1,7},{2,4},{3,5},{4,2},{5,3},{6,0},{7,1},{8,14},{9,15},{10,... | collective-permute-start | bytes 61448 | tf_op jit(solution)/shard_map/ppermute | solution.py:486
  67.1 0.9 %collective-permute-start.19 = (f32[40,128]{1,0:T(8,128)S(1)}, f32[40,128]{1,0:T(8,128)S(1)}, u32[]{:S(2)}, u32[]{:S(2)}) collective-permute-start(f32[40,128]{1,0:T(8,128)S(1)} %get-tuple-element.49), channel_id=1, source_target_pairs={{0,4},{1,5},{2,6},{3,7},{4,0},{5,1},{6,2},{7,3},{8,12},{9,13},{10,... | collective-permute-start | bytes 61448 | tf_op jit(solution)/shard_map/ppermute | solution.py:486
  68.0 1.1 %collective-permute-start.18 = (f32[40,128]{1,0:T(8,128)S(1)}, f32[40,128]{1,0:T(8,128)S(1)}, u32[]{:S(2)}, u32[]{:S(2)}) collective-permute-start(f32[40,128]{1,0:T(8,128)S(1)} %get-tuple-element.50), channel_id=1, source_target_pairs={{0,2},{1,3},{2,0},{3,1},{4,6},{5,7},{6,4},{7,5},{8,10},{9,11},{10,... | collective-permute-start | bytes 61448 | tf_op jit(solution)/shard_map/ppermute | solution.py:486
  69.2 1.2 %collective-permute-done.20.refs_3_ = f32[40,128]{1,0:T(8,128)S(1)} collective-permute-done((f32[40,128]{1,0:T(8,128)S(1)}, f32[40,128]{1,0:T(8,128)S(1)}, u32[]{:S(2)}, u32[]{:S(2)}) %collective-permute-start.20) | collective-permute-done | bytes 20512 | tf_op jit(solution)/shard_map/ppermute | solution.py:486
  70.4 1.4 %collective-permute-done.19.refs_2_ = f32[40,128]{1,0:T(8,128)S(1)} collective-permute-done((f32[40,128]{1,0:T(8,128)S(1)}, f32[40,128]{1,0:T(8,128)S(1)}, u32[]{:S(2)}, u32[]{:S(2)}) %collective-permute-start.19) | collective-permute-done | bytes 20512 | tf_op jit(solution)/shard_map/ppermute | solution.py:486
  71.8 0.2 collective-permute-done.18.refs_1_
  72.0 0.1 fourth.1
  72.1 11.0 %all_to_all.11 = f32[32,1,128]{2,1,0:T(1,128)S(1)} all-to-all(f32[32,1,128]{2,1,0:T(1,128)S(1)} %bitcast.29), channel_id=1, replica_groups=mesh['row'=4,'col'=8] {'row','col'}, dimensions={0} | all-to-all | bytes 32768 | tf_op jit(solution)/shard_map/all_to_all | solution.py:578
  83.2 0.8 last.1
  (6 shorter events, 0.1 us)
Async XLA Ops:
  0.6 28.6 %copy-start = (f32[1,1,4608]{2,1,0:T(1,128)S(1)}, f32[1,1,4608]{2,1,0:T(1,128)}, u32[]{:S(2)}) copy-start(f32[1,1,4608]{2,1,0:T(1,128)} %rhs.7) | copy-start | bytes 55300
  0.6 28.6 %copy-start.1 = (f32[1,1,4608]{2,1,0:T(1,128)S(1)}, f32[1,1,4608]{2,1,0:T(1,128)}, u32[]{:S(2)}) copy-start(f32[1,1,4608]{2,1,0:T(1,128)} %friction.5) | copy-start | bytes 55300
  0.7 28.6 %copy-start.2 = (s32[1,1,24]{2,1,0:T(1,128)S(1)}, s32[1,1,24]{2,1,0:T(1,128)}, u32[]{:S(2)}) copy-start(s32[1,1,24]{2,1,0:T(1,128)} %sizes.3) | copy-start | bytes 292
  0.7 12.2 %copy-start.4 = (s32[1,1,256]{2,1,0:T(1,128)S(1)}, s32[1,1,256]{2,1,0:T(1,128)}, u32[]{:S(2)}) copy-start(s32[1,1,256]{2,1,0:T(1,128)} %tile_col.1) | copy-start | bytes 3076
  0.7 12.2 %copy-start.3 = (s32[1,1,256]{2,1,0:T(1,128)S(1)}, s32[1,1,256]{2,1,0:T(1,128)}, u32[]{:S(2)}) copy-start(s32[1,1,256]{2,1,0:T(1,128)} %tile_row.1) | copy-start | bytes 3076
  0.7 12.2 %copy-start.5 = (f32[1,1,256]{2,1,0:T(1,128)S(1)}, f32[1,1,256]{2,1,0:T(1,128)}, u32[]{:S(2)}) copy-start(f32[1,1,256]{2,1,0:T(1,128)} %scale.1) | copy-start | bytes 3076
  7.6 8.8 %collective-permute-start.2 = (f32[40,128]{1,0:T(8,128)S(1)}, f32[40,128]{1,0:T(8,128)S(1)}, u32[]{:S(2)}, u32[]{:S(2)}) collective-permute-start(f32[40,128]{1,0:T(8,128)S(1)} %get-tuple-element.30.refs_0_.refs_4_.sent0), channel_id=1, source_target_pairs={{0,24},{8,16},{16,8},{24,0},{1,25},{9,17},{17,9},{25,1},{2,26},{10... | collective-permute-start | bytes 61448 | tf_op jit(solution)/shard_map/ppermute | solution.py:486
  11.6 4.9 %collective-permute-start.1 = (f32[40,128]{1,0:T(8,128)S(1)}, f32[40,128]{1,0:T(8,128)S(1)}, u32[]{:S(2)}, u32[]{:S(2)}) collective-permute-start(f32[40,128]{1,0:T(8,128)S(1)} %get-tuple-element.30.refs_0_.refs_4_.sent0), channel_id=1, source_target_pairs={{0,16},{8,24},{16,0},{24,8},{1,17},{9,25},{17,1},{25,9},{2,18},{10... | collective-permute-start | bytes 61448 | tf_op jit(solution)/shard_map/ppermute | solution.py:486
  12.1 4.4 %collective-permute-start = (f32[40,128]{1,0:T(8,128)S(1)}, f32[40,128]{1,0:T(8,128)S(1)}, u32[]{:S(2)}, u32[]{:S(2)}) collective-permute-start(f32[40,128]{1,0:T(8,128)S(1)} %get-tuple-element.30.refs_0_.refs_4_.sent0), channel_id=1, source_target_pairs={{0,8},{8,0},{16,24},{24,16},{1,9},{9,1},{17,25},{25,17},{2,10},{10... | collective-permute-start | bytes 61448 | tf_op jit(solution)/shard_map/ppermute | solution.py:486
  19.1 1.3 %collective-permute-start.3 = (f32[4,40,128]{2,1,0:T(8,128)S(1)}, f32[4,40,128]{2,1,0:T(8,128)S(1)}, u32[]{:S(2)}, u32[]{:S(2)}) collective-permute-start(f32[4,40,128]{2,1,0:T(8,128)S(1)} %get-tuple-element.36), channel_id=1, source_target_pairs={{0,1},{1,0},{2,3},{3,2},{4,5},{5,4},{6,7},{7,6},{8,9},{9,8},{10,11... | collective-permute-start | bytes 245768 | tf_op jit(solution)/shard_map/ppermute | solution.py:486
  20.5 5.8 %collective-permute-start.6 = (f32[40,128]{1,0:T(8,128)S(1)}, f32[40,128]{1,0:T(8,128)S(1)}, u32[]{:S(2)}, u32[]{:S(2)}) collective-permute-start(f32[40,128]{1,0:T(8,128)S(1)} %get-tuple-element.56), channel_id=1, source_target_pairs={{0,6},{1,7},{2,4},{3,5},{4,2},{5,3},{6,0},{7,1},{8,14},{9,15},{10,... | collective-permute-start | bytes 61448 | tf_op jit(solution)/shard_map/ppermute | solution.py:486
  24.6 4.7 %collective-permute-start.5 = (f32[40,128]{1,0:T(8,128)S(1)}, f32[40,128]{1,0:T(8,128)S(1)}, u32[]{:S(2)}, u32[]{:S(2)}) collective-permute-start(f32[40,128]{1,0:T(8,128)S(1)} %get-tuple-element.57), channel_id=1, source_target_pairs={{0,4},{1,5},{2,6},{3,7},{4,0},{5,1},{6,2},{7,3},{8,12},{9,13},{10,... | collective-permute-start | bytes 61448 | tf_op jit(solution)/shard_map/ppermute | solution.py:486
  24.6 4.7 %collective-permute-start.4 = (f32[40,128]{1,0:T(8,128)S(1)}, f32[40,128]{1,0:T(8,128)S(1)}, u32[]{:S(2)}, u32[]{:S(2)}) collective-permute-start(f32[40,128]{1,0:T(8,128)S(1)} %get-tuple-element.58), channel_id=1, source_target_pairs={{0,2},{1,3},{2,0},{3,1},{4,6},{5,7},{6,4},{7,5},{8,10},{9,11},{10,... | collective-permute-start | bytes 61448 | tf_op jit(solution)/shard_map/ppermute | solution.py:486
  33.5 4.7 %collective-permute-start.9 = (f32[40,128]{1,0:T(8,128)S(1)}, f32[40,128]{1,0:T(8,128)S(1)}, u32[]{:S(2)}, u32[]{:S(2)}) collective-permute-start(f32[40,128]{1,0:T(8,128)S(1)} %get-tuple-element.37.refs_0_.refs_4_.sent1), channel_id=1, source_target_pairs={{0,24},{8,16},{16,8},{24,0},{1,25},{9,17},{17,9},{25,1},{2,26},{10... | collective-permute-start | bytes 61448 | tf_op jit(solution)/shard_map/ppermute | solution.py:486
  35.9 3.8 %collective-permute-start.8 = (f32[40,128]{1,0:T(8,128)S(1)}, f32[40,128]{1,0:T(8,128)S(1)}, u32[]{:S(2)}, u32[]{:S(2)}) collective-permute-start(f32[40,128]{1,0:T(8,128)S(1)} %get-tuple-element.37.refs_0_.refs_4_.sent1), channel_id=1, source_target_pairs={{0,16},{8,24},{16,0},{24,8},{1,17},{9,25},{17,1},{25,9},{2,18},{10... | collective-permute-start | bytes 61448 | tf_op jit(solution)/shard_map/ppermute | solution.py:486
  36.4 3.8 %collective-permute-start.7 = (f32[40,128]{1,0:T(8,128)S(1)}, f32[40,128]{1,0:T(8,128)S(1)}, u32[]{:S(2)}, u32[]{:S(2)}) collective-permute-start(f32[40,128]{1,0:T(8,128)S(1)} %get-tuple-element.37.refs_0_.refs_4_.sent1), channel_id=1, source_target_pairs={{0,8},{8,0},{16,24},{24,16},{1,9},{9,1},{17,25},{25,17},{2,10},{10... | collective-permute-start | bytes 61448 | tf_op jit(solution)/shard_map/ppermute | solution.py:486
  42.9 1.3 %collective-permute-start.10 = (f32[4,40,128]{2,1,0:T(8,128)S(1)}, f32[4,40,128]{2,1,0:T(8,128)S(1)}, u32[]{:S(2)}, u32[]{:S(2)}) collective-permute-start(f32[4,40,128]{2,1,0:T(8,128)S(1)} %get-tuple-element.40), channel_id=1, source_target_pairs={{0,1},{1,0},{2,3},{3,2},{4,5},{5,4},{6,7},{7,6},{8,9},{9,8},{10,11... | collective-permute-start | bytes 245768 | tf_op jit(solution)/shard_map/ppermute | solution.py:486
  44.2 5.8 %collective-permute-start.13 = (f32[40,128]{1,0:T(8,128)S(1)}, f32[40,128]{1,0:T(8,128)S(1)}, u32[]{:S(2)}, u32[]{:S(2)}) collective-permute-start(f32[40,128]{1,0:T(8,128)S(1)} %get-tuple-element.52), channel_id=1, source_target_pairs={{0,6},{1,7},{2,4},{3,5},{4,2},{5,3},{6,0},{7,1},{8,14},{9,15},{10,... | collective-permute-start | bytes 61448 | tf_op jit(solution)/shard_map/ppermute | solution.py:486
  45.8 4.7 %collective-permute-start.12 = (f32[40,128]{1,0:T(8,128)S(1)}, f32[40,128]{1,0:T(8,128)S(1)}, u32[]{:S(2)}, u32[]{:S(2)}) collective-permute-start(f32[40,128]{1,0:T(8,128)S(1)} %get-tuple-element.53), channel_id=1, source_target_pairs={{0,4},{1,5},{2,6},{3,7},{4,0},{5,1},{6,2},{7,3},{8,12},{9,13},{10,... | collective-permute-start | bytes 61448 | tf_op jit(solution)/shard_map/ppermute | solution.py:486
  46.4 4.3 %collective-permute-start.11 = (f32[40,128]{1,0:T(8,128)S(1)}, f32[40,128]{1,0:T(8,128)S(1)}, u32[]{:S(2)}, u32[]{:S(2)}) collective-permute-start(f32[40,128]{1,0:T(8,128)S(1)} %get-tuple-element.54), channel_id=1, source_target_pairs={{0,2},{1,3},{2,0},{3,1},{4,6},{5,7},{6,4},{7,5},{8,10},{9,11},{10,... | collective-permute-start | bytes 61448 | tf_op jit(solution)/shard_map/ppermute | solution.py:486
  54.8 4.7 %collective-permute-start.16 = (f32[40,128]{1,0:T(8,128)S(1)}, f32[40,128]{1,0:T(8,128)S(1)}, u32[]{:S(2)}, u32[]{:S(2)}) collective-permute-start(f32[40,128]{1,0:T(8,128)S(1)} %get-tuple-element.41.refs_0_.sent.sent2), channel_id=1, source_target_pairs={{0,24},{8,16},{16,8},{24,0},{1,25},{9,17},{17,9},{25,1},{2,26},{10... | collective-permute-start | bytes 61448 | tf_op jit(solution)/shard_map/ppermute | solution.py:486
  56.4 3.8 %collective-permute-start.15 = (f32[40,128]{1,0:T(8,128)S(1)}, f32[40,128]{1,0:T(8,128)S(1)}, u32[]{:S(2)}, u32[]{:S(2)}) collective-permute-start(f32[40,128]{1,0:T(8,128)S(1)} %get-tuple-element.41.refs_0_.sent.sent2), channel_id=1, source_target_pairs={{0,16},{8,24},{16,0},{24,8},{1,17},{9,25},{17,1},{25,9},{2,18},{10... | collective-permute-start | bytes 61448 | tf_op jit(solution)/shard_map/ppermute | solution.py:486
  56.9 3.8 %collective-permute-start.14 = (f32[40,128]{1,0:T(8,128)S(1)}, f32[40,128]{1,0:T(8,128)S(1)}, u32[]{:S(2)}, u32[]{:S(2)}) collective-permute-start(f32[40,128]{1,0:T(8,128)S(1)} %get-tuple-element.41.refs_0_.sent.sent2), channel_id=1, source_target_pairs={{0,8},{8,0},{16,24},{24,16},{1,9},{9,1},{17,25},{25,17},{2,10},{10... | collective-permute-start | bytes 61448 | tf_op jit(solution)/shard_map/ppermute | solution.py:486
  63.3 1.3 %collective-permute-start.17 = (f32[4,40,128]{2,1,0:T(8,128)S(1)}, f32[4,40,128]{2,1,0:T(8,128)S(1)}, u32[]{:S(2)}, u32[]{:S(2)}) collective-permute-start(f32[4,40,128]{2,1,0:T(8,128)S(1)} %get-tuple-element.45), channel_id=1, source_target_pairs={{0,1},{1,0},{2,3},{3,2},{4,5},{5,4},{6,7},{7,6},{8,9},{9,8},{10,11... | collective-permute-start | bytes 245768 | tf_op jit(solution)/shard_map/ppermute | solution.py:486
  64.7 5.7 %collective-permute-start.20 = (f32[40,128]{1,0:T(8,128)S(1)}, f32[40,128]{1,0:T(8,128)S(1)}, u32[]{:S(2)}, u32[]{:S(2)}) collective-permute-start(f32[40,128]{1,0:T(8,128)S(1)} %get-tuple-element.48), channel_id=1, source_target_pairs={{0,6},{1,7},{2,4},{3,5},{4,2},{5,3},{6,0},{7,1},{8,14},{9,15},{10,... | collective-permute-start | bytes 61448 | tf_op jit(solution)/shard_map/ppermute | solution.py:486
  67.1 4.7 %collective-permute-start.19 = (f32[40,128]{1,0:T(8,128)S(1)}, f32[40,128]{1,0:T(8,128)S(1)}, u32[]{:S(2)}, u32[]{:S(2)}) collective-permute-start(f32[40,128]{1,0:T(8,128)S(1)} %get-tuple-element.49), channel_id=1, source_target_pairs={{0,4},{1,5},{2,6},{3,7},{4,0},{5,1},{6,2},{7,3},{8,12},{9,13},{10,... | collective-permute-start | bytes 61448 | tf_op jit(solution)/shard_map/ppermute | solution.py:486
  68.0 4.0 %collective-permute-start.18 = (f32[40,128]{1,0:T(8,128)S(1)}, f32[40,128]{1,0:T(8,128)S(1)}, u32[]{:S(2)}, u32[]{:S(2)}) collective-permute-start(f32[40,128]{1,0:T(8,128)S(1)} %get-tuple-element.50), channel_id=1, source_target_pairs={{0,2},{1,3},{2,0},{3,1},{4,6},{5,7},{6,4},{7,5},{8,10},{9,11},{10,... | collective-permute-start | bytes 61448 | tf_op jit(solution)/shard_map/ppermute | solution.py:486
